TPU v7x, 32 devices: a whole 2x2x4 slice. The times are simulated.
32 devices in a mesh: dp: 8 (over y, x, core), tensor: 4 (over z).
Axes of the slice: x: 2, y: 2, z: 4, core: 2. Of those that a mesh axis runs over, the one named last changes fastest.
Arguments:
- block_in: bfloat16 [16384, 1024], P(('dp', 'tensor')), may hold values from -48 to 48
- segments: int32 [8, 2048], P('dp'), may hold values from 0 to 5, never falling along the last dimension, each value on 1 to 800 neighbouring positions
- norm_gain: float32 [1024], replicated, may hold values from 0.1 to 1.9
- ema_rate: float32 [16, 1024], replicated, may hold values from 0.0005 to 0.033
- ema_angle: float32 [16, 1024], replicated, may hold values from -3.140625 to 3.140625
- ema_input: float32 [16, 1024], replicated, may hold values from -4 to 4
- ema_output: float32 [2, 16, 1024], replicated, may hold values from -1 to 1
- ema_skip: float32 [1024], replicated, may hold values from -2 to 2
- w_shared: float32 [1024, 256], P('dp'), may hold values from -0.1875 to 0.1875
- query_gain: float32 [256], replicated, may hold values from 0.1 to 1.9
- query_bias: float32 [256], replicated, may hold values from -2 to 2
- key_gain: float32 [256], replicated, may hold values from 0.1 to 1.9
- w_value: float32 [1024, 2048], P('dp', 'tensor'), may hold values from -0.1875 to 0.1875
- w_gate: float32 [1024, 2048], P('dp', 'tensor'), may hold values from -0.1875 to 0.1875
- w_out: float32 [2048, 1024], P('tensor', 'dp'), may hold values from -0.5 to 0.5
- ffn_gain: float32 [1024], replicated, may hold values from 0.1 to 1.9
- w_swish: float32 [1024, 2560], P('dp', 'tensor'), may hold values from -0.1875 to 0.1875
- w_up: float32 [1024, 2560], P('dp', 'tensor'), may hold values from -0.1875 to 0.1875
- w_down: float32 [2560, 1024], P('tensor', 'dp'), may hold values from -0.25 to 0.25
- out_grad: bfloat16 [16384, 1024], P(('dp', 'tensor')), may hold values from -7.2 to 7.2
Outputs:
- block_out: bfloat16 [16384, 1024], P(('dp', 'tensor'))
- in_grad: float32 [16384, 1024], P(('dp', 'tensor'))
- grad_norm_gain: float32 [1024], replicated
- grad_ema_rate: float32 [16, 1024], replicated
- grad_ema_angle: float32 [16, 1024], replicated
- grad_ema_input: float32 [16, 1024], replicated
- grad_ema_output: float32 [2, 16, 1024], replicated
- grad_ema_skip: float32 [1024], replicated
- grad_shared: float32 [1024, 256], P('dp')
- grad_query_gain: float32 [256], replicated
- grad_query_bias: float32 [256], replicated
- grad_key_gain: float32 [256], replicated
- grad_value: float32 [1024, 2048], P('dp', 'tensor')
- grad_gate: float32 [1024, 2048], P('dp', 'tensor')
- grad_out: float32 [2048, 1024], P('tensor', 'dp')
- grad_ffn_gain: float32 [1024], replicated
- grad_swish: float32 [1024, 2560], P('dp', 'tensor')
- grad_up: float32 [1024, 2560], P('dp', 'tensor')
- grad_down: float32 [2560, 1024], P('tensor', 'dp')
Inputs may be any that keep to these rules, and one draw needn't show every extreme that they name: `segments`: in each row of 2048 positions the document numbers never fall, and each document spans 1 to 800 positions.
All inputs are finite; a program needn't handle non-finite values.
Results may differ from a plain program's by a relative error of at most 0.02.
Values may be sent and summed in bfloat16 or wider, within the bound.
A program may use at most 576 MiB of HBM per device.

v0:
```python
from functools import partial
import math

import jax
import jax.numpy as jnp
from jax import lax
from jax.sharding import PartitionSpec as P

EMA_BLOCK = 128
TN_GROUPS = 16


EPSILON = 1e-05
HIGHEST = lax.Precision.HIGHEST


def silu_of(values_in):
    return values_in * jax.nn.sigmoid(values_in)


def silu_slope(values_in):
    logistic = jax.nn.sigmoid(values_in)
    return logistic * (1.0 + values_in * (1.0 - logistic))


def prefix_reset(flags, values_in):

    def prefix_combine(earlier, later):
        return (jnp.maximum(earlier[0], later[0]), later[1] + (1.0 - later[0]) * earlier[1])

    return lax.associative_scan(prefix_combine, (flags, values_in), axis=0)[1]


def step_norm(inputs, norm_scale, seg_ids, group_count):
    seq_length, features = inputs.shape
    group_width = features // group_count
    grouped = inputs.reshape(seq_length, group_count, group_width)
    sums_first = jnp.sum(grouped, axis=2)
    sums_second = jnp.sum(grouped * grouped, axis=2)
    starts = jnp.concatenate(
        [jnp.ones((1,), jnp.float32), (seg_ids[1:] != seg_ids[:-1]).astype(jnp.float32)]
    )[:, None]
    counter = jnp.ones((seq_length, 1), jnp.float32)
    running = prefix_reset(starts, jnp.concatenate([sums_first, sums_second, counter], axis=1))
    entries = running[:, 2 * group_count :] * group_width
    average = running[:, :group_count] / entries
    spread = running[:, group_count : 2 * group_count] / entries - average * average
    centred = (grouped - average[:, :, None]) * lax.rsqrt(spread + EPSILON)[:, :, None]
    return centred.reshape(seq_length, features) * norm_scale


def rms_norm(inputs, norm_scale):
    return (
        inputs * lax.rsqrt(jnp.mean(inputs * inputs, axis=1, keepdims=True) + EPSILON) * norm_scale
    )


def ema_apply(hidden, decay_rate, turn_angle, feed_gain, read_gain, skip_gain, seg_ids):
    seq_length, channels = hidden.shape
    ema_dims = decay_rate.shape[0]
    block_len = EMA_BLOCK
    block_count = seq_length // block_len
    offsets = jnp.arange(block_len).astype(jnp.float32)[:, None, None]
    grow = jnp.exp(decay_rate * offsets)
    shrink = jnp.exp(-decay_rate * offsets)
    cosine = jnp.cos(turn_angle * offsets)
    sine_part = jnp.sin(turn_angle * offsets)
    feed = feed_gain * jnp.sqrt(1.0 - jnp.exp(-2.0 * decay_rate))
    tiled = hidden.reshape(block_count, block_len, 1, channels)
    drive_real = tiled * (feed * grow * cosine)
    drive_imag = tiled * (-feed * grow * sine_part)
    seg_blocks = seg_ids.reshape(block_count, block_len)
    lower = jnp.arange(block_len)[:, None] >= jnp.arange(block_len)[None, :]
    same_doc = seg_blocks[:, :, None] == seg_blocks[:, None, :]
    within = jnp.logical_and(same_doc, lower[None]).astype(jnp.float32)
    stacked = jnp.stack([drive_real, drive_imag], axis=2).reshape(
        block_count, block_len, 2 * ema_dims * channels
    )
    inner = jnp.einsum("nts,nsk->ntk", within, stacked, precision=HIGHEST)
    inner = inner.reshape(block_count, block_len, 2, ema_dims, channels)
    inner_real = inner[:, :, 0]
    inner_imag = inner[:, :, 1]
    prior = jnp.concatenate([jnp.full((1,), -1, jnp.int32), seg_blocks[:-1, -1]])
    linked = (seg_blocks == prior[:, None]).astype(jnp.float32)
    power_real = shrink * cosine
    power_imag = shrink * sine_part
    end_real = power_real[-1] * inner_real[:, -1] - power_imag[-1] * inner_imag[:, -1]
    end_imag = power_real[-1] * inner_imag[:, -1] + power_imag[-1] * inner_real[:, -1]
    whole_mod = jnp.exp(-decay_rate * block_len)
    carry_real = (whole_mod * jnp.cos(turn_angle * block_len))[None] * linked[:, -1, None, None]
    carry_imag = (whole_mod * jnp.sin(turn_angle * block_len))[None] * linked[:, -1, None, None]

    def ema_combine(earlier, later):
        return (
            later[0] * earlier[0] - later[1] * earlier[1],
            later[0] * earlier[1] + later[1] * earlier[0],
            later[0] * earlier[2] - later[1] * earlier[3] + later[2],
            later[0] * earlier[3] + later[1] * earlier[2] + later[3],
        )

    states = lax.associative_scan(ema_combine, (carry_real, carry_imag, end_real, end_imag), axis=0)
    zero_state = jnp.zeros((1, ema_dims, channels), jnp.float32)
    before_real = jnp.concatenate([zero_state, states[2][:-1]], axis=0)
    before_imag = jnp.concatenate([zero_state, states[3][:-1]], axis=0)
    step_real = jnp.exp(-decay_rate) * jnp.cos(turn_angle)
    step_imag = jnp.exp(-decay_rate) * jnp.sin(turn_angle)
    push_real = step_real * before_real - step_imag * before_imag
    push_imag = step_real * before_imag + step_imag * before_real
    link_full = linked[:, :, None, None]
    total_real = inner_real + link_full * push_real[:, None]
    total_imag = inner_imag + link_full * push_imag[:, None]
    state_real = power_real * total_real - power_imag * total_imag
    state_imag = power_real * total_imag + power_imag * total_real
    mixed = jnp.sum(read_gain[0] * state_real - read_gain[1] * state_imag, axis=2)
    return mixed.reshape(seq_length, channels) + skip_gain * hidden


def ema_mixed(hidden, decay_rate, turn_angle, feed_gain, read_gain, skip_gain, seg_ids):
    return silu_of(
        ema_apply(hidden, decay_rate, turn_angle, feed_gain, read_gain, skip_gain, seg_ids)
    )


def block_mask(positions, seg_ids, row_start, block_len):
    query_pos = row_start + jnp.arange(block_len, dtype=jnp.int32)
    query_seg = lax.dynamic_slice_in_dim(seg_ids, row_start, block_len, 0)
    return jnp.logical_and(
        positions[None, :] <= query_pos[:, None], seg_ids[None, :] == query_seg[:, None]
    )


def attend_forward(queries, keys_in, values_in, seg_ids):
    seq_length, head_dim = queries.shape
    block_len = min(512, seq_length)
    score_scale = 1.0 / math.sqrt(head_dim)
    positions = jnp.arange(seq_length, dtype=jnp.int32)

    def one_block(block_index):
        row_start = block_index * block_len
        query_rows = lax.dynamic_slice_in_dim(queries, row_start, block_len, 0)
        allowed = block_mask(positions, seg_ids, row_start, block_len)
        scores = (
            jnp.einsum("qd,kd->qk", query_rows, keys_in, preferred_element_type=jnp.float32)
            * score_scale
        )
        masked = jnp.where(allowed, scores, -1e30)
        row_peak = jnp.max(masked, axis=1, keepdims=True)
        raw_weights = jnp.exp(masked - row_peak)
        row_total = jnp.sum(raw_weights, axis=1, keepdims=True)
        attn_probs = (raw_weights / row_total).astype(jnp.bfloat16)
        rows_out = jnp.dot(attn_probs, values_in, preferred_element_type=jnp.float32)
        return (rows_out, (row_peak + jnp.log(row_total))[:, 0])

    block_outs, log_totals = lax.map(
        one_block, jnp.arange(seq_length // block_len, dtype=jnp.int32)
    )
    return (block_outs.reshape(seq_length, values_in.shape[1]), log_totals.reshape(seq_length))


def attend_backward(queries, keys_in, values_in, seg_ids, log_totals, grad_rows):
    seq_length, head_dim = queries.shape
    block_len = min(512, seq_length)
    score_scale = 1.0 / math.sqrt(head_dim)
    positions = jnp.arange(seq_length, dtype=jnp.int32)

    def one_block(carry, block_index):
        key_acc, value_acc = carry
        row_start = block_index * block_len
        query_rows = lax.dynamic_slice_in_dim(queries, row_start, block_len, 0)
        grad_block = lax.dynamic_slice_in_dim(grad_rows, row_start, block_len, 0)
        total_rows = lax.dynamic_slice_in_dim(log_totals, row_start, block_len, 0)
        allowed = block_mask(positions, seg_ids, row_start, block_len)
        scores = (
            jnp.einsum("qd,kd->qk", query_rows, keys_in, preferred_element_type=jnp.float32)
            * score_scale
        )
        masked = jnp.where(allowed, scores, -1e30)
        attn_probs = jnp.exp(masked - total_rows[:, None])
        grad_probs = jnp.einsum(
            "qv,kv->qk", grad_block, values_in, preferred_element_type=jnp.float32
        )
        centre = jnp.sum(attn_probs * grad_probs, axis=1, keepdims=True)
        grad_scores = (attn_probs * (grad_probs - centre)).astype(jnp.bfloat16)
        query_grad = jnp.dot(grad_scores, keys_in, preferred_element_type=jnp.float32) * score_scale
        key_acc = (
            key_acc
            + jnp.einsum("qk,qd->kd", grad_scores, query_rows, preferred_element_type=jnp.float32)
            * score_scale
        )
        value_acc = value_acc + jnp.einsum(
            "qk,qv->kv",
            attn_probs.astype(jnp.bfloat16),
            grad_block,
            preferred_element_type=jnp.float32,
        )
        return ((key_acc, value_acc), query_grad)

    start_carry = (
        jnp.zeros((seq_length, head_dim), jnp.float32),
        jnp.zeros(values_in.shape, jnp.float32),
    )
    (key_grad, value_grad), query_grads = lax.scan(
        one_block, start_carry, jnp.arange(seq_length // block_len, dtype=jnp.int32)
    )
    return (query_grads.reshape(seq_length, head_dim), key_grad, value_grad)


def fetch_weights(w_shared, w_value, w_gate, w_out, w_swish, w_up, w_down):
    return (
        lax.all_gather(w_shared.astype(jnp.bfloat16), "dp", axis=0, tiled=True),
        lax.all_gather(w_value.astype(jnp.bfloat16), "dp", axis=0, tiled=True),
        lax.all_gather(w_gate.astype(jnp.bfloat16), "dp", axis=0, tiled=True),
        lax.all_gather(w_out.astype(jnp.bfloat16), "dp", axis=1, tiled=True),
        lax.all_gather(w_swish.astype(jnp.bfloat16), "dp", axis=0, tiled=True),
        lax.all_gather(w_up.astype(jnp.bfloat16), "dp", axis=0, tiled=True),
        lax.all_gather(w_down.astype(jnp.bfloat16), "dp", axis=1, tiled=True),
    )


def on_device(
    block_in,
    segments,
    norm_gain,
    ema_rate,
    ema_angle,
    ema_input,
    ema_output,
    ema_skip,
    w_shared,
    query_gain,
    query_bias,
    key_gain,
    w_value,
    w_gate,
    w_out,
    ffn_gain,
    w_swish,
    w_up,
    w_down,
    out_grad,
):
    tensor_size = lax.axis_size("tensor")
    tensor_rank = lax.axis_index("tensor")
    features = block_in.shape[1]
    own_width = features // tensor_size
    own_start = tensor_rank * own_width
    matrices = fetch_weights(w_shared, w_value, w_gate, w_out, w_swish, w_up, w_down)
    shared_b, value_b, gate_b, out_b, swish_b, up_b, down_b = matrices
    gathered_in = lax.all_gather(block_in, "tensor", axis=0, tiled=True).astype(jnp.float32)
    rate_own = lax.dynamic_slice_in_dim(ema_rate, own_start, own_width, 1)
    angle_own = lax.dynamic_slice_in_dim(ema_angle, own_start, own_width, 1)
    input_own = lax.dynamic_slice_in_dim(ema_input, own_start, own_width, 1)
    output_own = lax.dynamic_slice_in_dim(ema_output, own_start, own_width, 2)
    skip_own = lax.dynamic_slice_in_dim(ema_skip, own_start, own_width, 0)
    normed_parts, norm_pulls, mixed_parts, ema_pulls = ([], [], [], [])
    member = 0
    seg_ids = segments[member]
    normed_seq, norm_pull = jax.vjp(
        partial(step_norm, seg_ids=seg_ids, group_count=TN_GROUPS), gathered_in, norm_gain
    )
    hidden_own = lax.dynamic_slice_in_dim(normed_seq, own_start, own_width, 1)
    mixed_seq, ema_pull = jax.vjp(
        partial(ema_mixed, seg_ids=seg_ids),
        hidden_own,
        rate_own,
        angle_own,
        input_own,
        output_own,
        skip_own,
    )
    normed_parts.append(normed_seq)
    norm_pulls.append(norm_pull)
    mixed_parts.append(mixed_seq)
    ema_pulls.append(ema_pull)
    normed_b = normed_parts[0].astype(jnp.bfloat16)
    mixed_own = mixed_parts[0].astype(jnp.bfloat16)
    mixed_full = lax.all_gather(mixed_own, "tensor", axis=1, tiled=True)
    latent = jnp.dot(mixed_full, shared_b, preferred_element_type=jnp.float32)
    queries = (latent * query_gain + query_bias).astype(jnp.bfloat16)
    keys_in = (latent * key_gain).astype(jnp.bfloat16)
    value_pre = jnp.dot(normed_b, value_b, preferred_element_type=jnp.float32)
    values_in = silu_of(value_pre).astype(jnp.bfloat16)
    gate_pre = jnp.dot(mixed_full, gate_b, preferred_element_type=jnp.float32)
    gate_act = silu_of(gate_pre)
    attended_parts, total_parts = ([], [])
    member = 0
    attended_seq, totals_seq = attend_forward(queries, keys_in, values_in, segments[member])
    attended_parts.append(attended_seq)
    total_parts.append(totals_seq)
    attended = attended_parts[0]
    mixed_gate = (gate_act * attended).astype(jnp.bfloat16)
    residual = block_in.astype(jnp.float32) + lax.psum_scatter(
        jnp.dot(mixed_gate, out_b, preferred_element_type=jnp.float32).astype(jnp.bfloat16),
        "tensor",
        scatter_dimension=0,
        tiled=True,
    ).astype(jnp.float32)
    norm_in, ffn_pull = jax.vjp(rms_norm, residual, ffn_gain)
    norm_full = lax.all_gather(norm_in.astype(jnp.bfloat16), "tensor", axis=0, tiled=True)
    swish_pre = jnp.dot(norm_full, swish_b, preferred_element_type=jnp.float32)
    up_pre = jnp.dot(norm_full, up_b, preferred_element_type=jnp.float32)
    swish_act = silu_of(swish_pre)
    hidden_b = (swish_act * up_pre).astype(jnp.bfloat16)
    block_out = residual + lax.psum_scatter(
        jnp.dot(hidden_b, down_b, preferred_element_type=jnp.float32).astype(jnp.bfloat16),
        "tensor",
        scatter_dimension=0,
        tiled=True,
    ).astype(jnp.float32)
    matrices = fetch_weights(w_shared, w_value, w_gate, w_out, w_swish, w_up, w_down)
    shared_b, value_b, gate_b, out_b, swish_b, up_b, down_b = matrices
    grad_full = lax.all_gather(out_grad, "tensor", axis=0, tiled=True)
    grad_hidden = jnp.einsum("rd,fd->rf", grad_full, down_b, preferred_element_type=jnp.float32)
    grad_down = jnp.einsum("rf,rd->fd", hidden_b, grad_full, preferred_element_type=jnp.float32)
    grad_swish_pre = (grad_hidden * up_pre * silu_slope(swish_pre)).astype(jnp.bfloat16)
    grad_up_pre = (grad_hidden * swish_act).astype(jnp.bfloat16)
    grad_swish = jnp.einsum(
        "rd,rf->df", norm_full, grad_swish_pre, preferred_element_type=jnp.float32
    )
    grad_up = jnp.einsum("rd,rf->df", norm_full, grad_up_pre, preferred_element_type=jnp.float32)
    grad_norm_in = lax.psum_scatter(
        (
            jnp.einsum("rf,df->rd", grad_swish_pre, swish_b, preferred_element_type=jnp.float32)
            + jnp.einsum("rf,df->rd", grad_up_pre, up_b, preferred_element_type=jnp.float32)
        ).astype(jnp.bfloat16),
        "tensor",
        scatter_dimension=0,
        tiled=True,
    ).astype(jnp.float32)
    grad_residual_part, grad_ffn_gain = ffn_pull(grad_norm_in)
    grad_residual = out_grad.astype(jnp.float32) + grad_residual_part
    branch_grad = lax.all_gather(grad_residual.astype(jnp.bfloat16), "tensor", axis=0, tiled=True)
    grad_mixed = jnp.einsum("rd,vd->rv", branch_grad, out_b, preferred_element_type=jnp.float32)
    grad_out = jnp.einsum("rv,rd->vd", mixed_gate, branch_grad, preferred_element_type=jnp.float32)
    grad_attended = (grad_mixed * gate_act).astype(jnp.bfloat16)
    grad_gate_pre = (grad_mixed * attended * silu_slope(gate_pre)).astype(jnp.bfloat16)
    query_parts, key_parts, value_parts = ([], [], [])
    member = 0
    query_seq, key_seq, value_seq = attend_backward(
        queries, keys_in, values_in, segments[member], total_parts[member], grad_attended
    )
    query_parts.append(query_seq)
    key_parts.append(key_seq)
    value_parts.append(value_seq)
    grad_queries = query_parts[0]
    grad_keys = key_parts[0]
    grad_values = value_parts[0]
    grad_value_pre = (grad_values * silu_slope(value_pre)).astype(jnp.bfloat16)
    grad_value = jnp.einsum(
        "rd,rv->dv", normed_b, grad_value_pre, preferred_element_type=jnp.float32
    )
    grad_gate = jnp.einsum(
        "rd,rv->dv", mixed_full, grad_gate_pre, preferred_element_type=jnp.float32
    )
    grad_query_gain = jnp.sum(latent * grad_queries, axis=0)
    grad_query_bias = jnp.sum(grad_queries, axis=0)
    grad_key_gain = jnp.sum(latent * grad_keys, axis=0)
    grad_latent = lax.psum(
        (grad_queries * query_gain + grad_keys * key_gain).astype(jnp.bfloat16), "tensor"
    )
    grad_shared = jnp.einsum(
        "rd,rz->dz", mixed_full, grad_latent, preferred_element_type=jnp.float32
    )
    shared_own = lax.dynamic_slice_in_dim(shared_b, own_start, own_width, 0)
    gate_part = lax.psum_scatter(
        jnp.einsum("rv,dv->rd", grad_gate_pre, gate_b, preferred_element_type=jnp.float32).astype(
            jnp.bfloat16
        ),
        "tensor",
        scatter_dimension=1,
        tiled=True,
    ).astype(jnp.float32)
    grad_mixed_own = gate_part + jnp.einsum(
        "rz,dz->rd", grad_latent, shared_own, preferred_element_type=jnp.float32
    )
    grad_value_in = jnp.einsum(
        "rv,dv->rd", grad_value_pre, value_b, preferred_element_type=jnp.float32
    )
    member = 0
    hidden_grad, rate_grad, angle_grad, input_grad_part, output_grad, skip_grad = ema_pulls[member](
        grad_mixed_own
    )
    full_seq = grad_value_in
    own_cols = lax.dynamic_slice_in_dim(full_seq, own_start, own_width, 1) + hidden_grad
    full_seq = lax.dynamic_update_slice_in_dim(full_seq, own_cols, own_start, 1)
    rows_grad, gain_grad = norm_pulls[member](full_seq)
    in_grad = grad_residual + lax.psum_scatter(
        rows_grad.astype(jnp.bfloat16), "tensor", scatter_dimension=0, tiled=True
    ).astype(jnp.float32)
    rate_full = lax.dynamic_update_slice_in_dim(jnp.zeros_like(ema_rate), rate_grad, own_start, 1)
    angle_full = lax.dynamic_update_slice_in_dim(
        jnp.zeros_like(ema_angle), angle_grad, own_start, 1
    )
    input_full = lax.dynamic_update_slice_in_dim(
        jnp.zeros_like(ema_input), input_grad_part, own_start, 1
    )
    output_full = lax.dynamic_update_slice_in_dim(
        jnp.zeros_like(ema_output), output_grad, own_start, 2
    )
    skip_full = lax.dynamic_update_slice_in_dim(jnp.zeros_like(ema_skip), skip_grad, own_start, 0)
    small_sums = lax.psum(
        (
            gain_grad,
            rate_full,
            angle_full,
            input_full,
            output_full,
            skip_full,
            grad_query_gain,
            grad_query_bias,
            grad_key_gain,
            grad_ffn_gain,
        ),
        ("dp", "tensor"),
    )
    large_sums = (
        lax.psum_scatter(grad_shared, "dp", scatter_dimension=0, tiled=True),
        lax.psum_scatter(grad_value, "dp", scatter_dimension=0, tiled=True),
        lax.psum_scatter(grad_gate, "dp", scatter_dimension=0, tiled=True),
        lax.psum_scatter(grad_out, "dp", scatter_dimension=1, tiled=True),
        lax.psum_scatter(grad_swish, "dp", scatter_dimension=0, tiled=True),
        lax.psum_scatter(grad_up, "dp", scatter_dimension=0, tiled=True),
        lax.psum_scatter(grad_down, "dp", scatter_dimension=1, tiled=True),
    )
    return (
        block_out.astype(jnp.bfloat16),
        in_grad,
        small_sums[0],
        small_sums[1],
        small_sums[2],
        small_sums[3],
        small_sums[4],
        small_sums[5],
        large_sums[0],
        small_sums[6],
        small_sums[7],
        small_sums[8],
        large_sums[1],
        large_sums[2],
        large_sums[3],
        small_sums[9],
        large_sums[4],
        large_sums[5],
        large_sums[6],
    )


def solution(mesh):
    return jax.shard_map(
        on_device,
        mesh=mesh,
        in_specs=(
            P(("dp", "tensor"), None),
            P("dp", None),
            P(),
            P(),
            P(),
            P(),
            P(),
            P(),
            P("dp", None),
            P(),
            P(),
            P(),
            P("dp", "tensor"),
            P("dp", "tensor"),
            P("tensor", "dp"),
            P(),
            P("dp", "tensor"),
            P("dp", "tensor"),
            P("tensor", "dp"),
            P(("dp", "tensor"), None),
        ),
        out_specs=(
            P(("dp", "tensor"), None),
            P(("dp", "tensor"), None),
            P(),
            P(),
            P(),
            P(),
            P(),
            P(),
            P("dp", None),
            P(),
            P(),
            P(),
            P("dp", "tensor"),
            P("dp", "tensor"),
            P("tensor", "dp"),
            P(),
            P("dp", "tensor"),
            P("dp", "tensor"),
            P("tensor", "dp"),
        ),
        check_vma=False,
    )
```

profile of v0, /device:TPU:0, one launch (start us, length us, event | category | flops | bytes accessed | tf_op | source)
XLA Modules:
  0.0 2549.3 jit_solution(11950563016818471883)
XLA Ops:
  25.8 9.4 fusion.57
  40.1 53.0 %all-gather.12.cloned.1.call-done = bf16[2048,1024]{1,0:T(8,128)(2,1)} async-done(((bf16[512,1024]{1,0:T(8,128)(2,1)}), bf16[2048,1024]{1,0:T(8,128)(2,1)}) %all-gather.12.cloned.1.call-update) | async-done | bytes 4194320 | tf_op jit(solution)/shard_map/all_gather | solution.py:249
  93.1 7.2 copy.244
  112.0 7.1 slice.632
  170.7 9.3 copy.245
  184.4 9.3 copy.246
  193.6 13.5 broadcast_multiply_fusion.3
  209.3 21.8 broadcast_multiply_fusion.1
  231.2 43.6 %pad_maximum_fusion = f32[16,128,2,16,256]{4,3,2,1,0:T(8,128)} fusion(f32[16,128,1,16,256]{4,3,2,1,0:T(8,128)} %get-tuple-element.388, f32[16,128,1,16,256]{4,3,2,1,0:T(8,128)} %get-tuple-element.387), kind=kLoop, calls=%fused_computation.41 | loop fusion | flops 16777216 | bytes 134217728 | tf_op jit(solution)/shard_map/jvp()/stack | solution.py:76
  274.8 71.4 %reshape.370 = f32[16,128,8192]{2,1,0:T(8,128)} reshape(f32[16,128,2,16,256]{4,3,2,1,0:T(8,128)} %pad_maximum_fusion) | data formatting | bytes 134217728 | tf_op jit(solution)/shard_map/jvp()/reshape | solution.py:76
  346.2 54.8 %fusion.89 = f32[16,128,8192]{2,1,0:T(8,128)} fusion(f32[16,128,8192]{2,1,0:T(8,128)} %reshape.370, s32[16,128]{1,0:T(8,128)S(1)} %bitcast.295, pred[128,128]{0,1:T(8,128)(4,1)S(1)} %iota_compare_fusion.2), kind=kOutput, calls=%fused_computation.181 | convolution fusion | flops 25770328064 | bytes 134242304 | tf_op jit(solution)/shard_map/jvp(nts,nsk->ntk)/dot_general | solution.py:79
  401.0 45.4 %copy.269 = f32[256,8,32,256]{3,2,1,0:T(8,128)} copy(f32[256,8,32,256]{3,1,2,0:T(8,128)} %bitcast.73) | data formatting | bytes 134217728
  446.4 43.0 %fusion.147 = (f32[16,128,1,16,256]{4,3,2,1,0:T(8,128)}, f32[16,128,1,16,256]{4,3,2,1,0:T(8,128)}) fusion(f32[16,128,2,16,256]{4,3,2,1,0:T(8,128)} %bitcast.75), kind=kLoop, calls=%fused_computation.484 | loop fusion | bytes 134217728 | tf_op jit(solution)/shard_map/jvp()/slice | solution.py:82
  489.4 43.0 %copy_bitcast_fusion = (f32[16,128,16,256]{3,2,0,1:T(8,128)}, f32[16,128,16,256]{3,2,0,1:T(8,128)}) fusion(f32[16,128,1,16,256]{4,3,2,1,0:T(8,128)} %get-tuple-element.368, f32[16,128,1,16,256]{4,3,2,1,0:T(8,128)} %get-tuple-element.369), kind=kLoop, calls=%fused_computation.66 | loop fusion | bytes 134217728 | tf_op jit(solution)/shard_map/jvp()/squeeze | solution.py:82
  558.0 27.0 %subtract_reduce_fusion = f32[16,128,256]{2,0,1:T(8,128)S(1)} fusion(f32[16,256]{1,0:T(8,128)S(1)} %copy-done.114, f32[16,256]{1,0:T(8,128)S(1)} %copy-done.112, f32[16,16,256]{2,1,0:T(8,128)S(1)} %get-tuple-element.399, f32[128,16,256]{2,1,0:T(8,128)} %copy-done.10, f32[16,16,256]{2,1,0:T(8,128)S(1)} %get-tuple-element.398, f32[16,128]{0,1:T(8,128)S(1)} %copy-done.80, ...), kind=kLoop, calls=%fused_computation.74 | loop fusion | flops 116916224 | bytes 73965568 | tf_op jit(solution)/shard_map/jvp()/reduce_sum | solution.py:114
  592.1 9.9 all_gather.46
  602.0 9.4 multiply_convert_fusion.6
  611.4 58.4 %all-gather.14.cloned.1.call-done = bf16[2048,1024]{1,0:T(8,128)(2,1)} async-done(((bf16[2048,256]{1,0:T(8,128)(2,1)}), bf16[2048,1024]{1,0:T(8,128)(2,1)}) %all-gather.14.cloned.1.call-update) | async-done | bytes 4194320 | tf_op jit(solution)/shard_map/all_gather | solution.py:277
  674.6 42.9 %while.28 = (s32[]{:T(128)}, f32[4,512,512]{2,1,0:T(8,128)}, f32[4,512]{1,0:T(4,128)S(1)}, s32[4]{0:T(128)S(1)}, s32[1,2048]{1,0:T(1,128)S(1)}, /*index=5*/s32[2...) while((s32[]{:T(128)}, f32[4,512,512]{2,1,0:T(8,128)}, ...), condition=%wide.region_6.7_spmd.clone, body=%wide.region_3.6_spmd.clone.sunk | while | flops 1622147072 | bytes 33856228 | solution.py:154
  717.5 10.0 fusion.49
  735.4 73.5 %reduce-scatter.13.cloned.1.call-done = bf16[512,1024]{1,0:T(8,128)(2,1)} async-done(((bf16[2048,1024]{1,0:T(8,128)(2,1)}), bf16[512,1024]{1,0:T(8,128)(2,1)}) %reduce-scatter.13.cloned.1.call-update) | async-done | bytes 1048592 | tf_op jit(solution)/shard_map/reduce_scatter | solution.py:292
  816.0 20.1 all-gather.24.cloned.1.call-done
  836.1 83.0 %all-gather.22.cloned.1.call-done = bf16[2048,1024]{1,0:T(8,128)(2,1)} async-done(((bf16[512,1024]{1,0:T(8,128)(2,1)}), bf16[2048,1024]{1,0:T(8,128)(2,1)}) %all-gather.22.cloned.1.call-update) | async-done | bytes 4194320 | tf_op jit(solution)/shard_map/all_gather | solution.py:299
  919.1 8.3 fusion.186
  927.5 16.9 all-gather.26.cloned.1.call-done
  944.3 8.4 fusion.187
  952.8 18.2 all-gather.28.cloned.1.call-done
  971.0 82.5 %all-gather.30.cloned.1.call-done = bf16[2048,1024]{1,0:T(8,128)(2,1)} async-done(((bf16[512,1024]{1,0:T(8,128)(2,1)}), bf16[2048,1024]{1,0:T(8,128)(2,1)}) %all-gather.30.cloned.1.call-update) | async-done | bytes 4194320 | tf_op jit(solution)/shard_map/all_gather | solution.py:312
  1053.4 10.4 multiply_convert_fusion.1
  1072.6 75.4 %reduce-scatter.17.cloned.1.call-done = bf16[512,1024]{1,0:T(8,128)(2,1)} async-done(((bf16[2048,1024]{1,0:T(8,128)(2,1)}), bf16[512,1024]{1,0:T(8,128)(2,1)}) %reduce-scatter.17.cloned.1.call-update) | async-done | bytes 1048592 | tf_op jit(solution)/shard_map/reduce_scatter | solution.py:321
  1154.7 81.1 %all-gather.32.cloned.1.call-done = bf16[2048,1024]{1,0:T(8,128)(2,1)} async-done(((bf16[512,1024]{1,0:T(8,128)(2,1)}), bf16[2048,1024]{1,0:T(8,128)(2,1)}) %all-gather.32.cloned.1.call-update) | async-done | bytes 4194320 | tf_op jit(solution)/shard_map/all_gather | solution.py:332
  1235.8 11.3 fusion.51
  1247.1 73.3 %while.29 = (s32[]{:T(128)}, f32[2048,256]{1,0:T(8,128)S(1)}, f32[2048,512]{1,0:T(8,128)}, f32[4,512,256]{2,1,0:T(8,128)}, s32[4]{0:T(128)S(1)}, /*index=5*/s32[...) while((s32[]{:T(128)}, f32[2048,256]{1,0:T(8,128)S(1)}, ...), condition=%wide.region_14.15_spmd.clone, body=%wide.region_12.14_spmd.clone.sunk | while | flops 3774480384 | bytes 109081472 | solution.py:202
  1272.5 7.0 select_add_fusion.2
  1291.1 7.0 select_add_fusion.2
  1309.7 7.0 select_add_fusion.2
  1351.5 23.9 all-reduce.168.cloned.1.call-done
  1375.3 78.4 %reduce-scatter.19.cloned.1.call-done = bf16[2048,256]{1,0:T(8,128)(2,1)} async-done(((bf16[2048,1024]{1,0:T(8,128)(2,1)}), bf16[2048,256]{1,0:T(8,128)(2,1)}) %reduce-scatter.19.cloned.1.call-update) | async-done | bytes 1048592 | tf_op jit(solution)/shard_map/reduce_scatter | solution.py:365
  1461.8 50.9 %multiply_reduce_fusion.2 = (f32[16,256]{1,0:T(8,128)}, f32[16,256]{1,0:T(8,128)}, f32[128,16,256]{2,1,0:T(8,128)}, f32[128,16,256]{2,1,0:T(8,128)}, f32[128,16,...) fusion(f32[16,128,256]{2,0,1:T(8,128)} %copy.253, ...), kind=kLoop, calls=%fused_computation.69 | loop fusion | flops 291364864 | bytes 85008384 | tf_op jit(solution)/shard_map/transpose(jvp())/reduce_sum | solution.py:114
  1597.1 27.2 %fusion.35 = (f32[16,128,1,16,256]{4,3,0,1,2:T(8,128)}, f32[16,128,1,16,256]{4,3,0,1,2:T(8,128)}) fusion(f32[16,1,16,256]{3,2,0,1:T(8,128)S(1)} %get-tuple-element.427, f32[16,1,16,256]{3,2,0,1:T(8,128)S(1)} %get-tuple-element.492, f32[16,128,256]{2,0,1:T(8,128)} %copy.254, f32[16,128,256]{2,0,1:T(8,128)} %copy.253, f32[16,256]{1,0:T(8,128)} %get-tuple-element.457, ...), kind=kLoop, calls=%fused_computation.56 | loop fusion | flops 109051904 | bytes 76578816 | tf_op jit(solution)/shard_map/transpose(jvp())/broadcast_in_dim | solution.py:82
  1624.3 44.9 %pad_add_fusion = f32[16,128,2,16,256]{4,3,0,1,2:T(8,128)} fusion(f32[16,128,1,16,256]{4,3,0,1,2:T(8,128)} %get-tuple-element.376, f32[16,128,1,16,256]{4,3,0,1,2:T(8,128)} %get-tuple-element.375), kind=kLoop, calls=%fused_computation.42 | loop fusion | flops 16777216 | bytes 134217728 | tf_op jit(solution)/shard_map/transpose(jvp())/add_any | solution.py:81
  1669.2 69.2 %copy.255 = f32[16,128,2,16,256]{1,4,3,2,0:T(8,128)} copy(f32[16,128,2,16,256]{4,3,0,1,2:T(8,128)} %pad_add_fusion) | data formatting | bytes 134217728 | tf_op jit(solution)/shard_map/transpose(jvp())/add_any | solution.py:81
  1738.5 54.6 %fusion.88 = f32[16,128,8192]{2,1,0:T(8,128)} fusion(f32[16,128,8192]{1,2,0:T(8,128)} %bitcast.47, s32[16,128]{1,0:T(8,128)S(1)} %bitcast.300, pred[128,128]{0,1:T(8,128)(4,1)S(1)} %copy-done.66), kind=kOutput, calls=%fused_computation.180 | convolution fusion | flops 25770328064 | bytes 134242304 | tf_op jit(solution)/shard_map/transpose(jvp(nts,nsk->ntk))/dot_general | solution.py:79
  1793.0 46.0 %copy.271 = f32[256,8,32,256]{3,2,1,0:T(8,128)} copy(f32[256,8,32,256]{3,1,2,0:T(8,128)} %bitcast.79) | data formatting | bytes 134217728
  1839.0 32.4 %multiply_reduce_fusion.3 = (f32[128,16,256]{2,1,0:T(8,128)}, f32[128,16,256]{2,1,0:T(8,128)}, f32[16,128,256]{2,1,0:T(8,128)S(1)}, f32[16,128,256]{2,1,0:T(8,128)S(1)}) fusion(f32[16,128,2,16,256]{4,3,2,1,0:T(8,128)} %bitcast.81, f32[16,128,256]{2,1,0:T(8,128)S(1)} %bitcast.290, f32[128,16,256]{2,1,0:T(8,128)} %get-tuple-element.537, ...), kind=kLoop, calls=%fused_computation.70 | loop fusion | flops 65011712 | bytes 81788928 | tf_op jit(solution)/shard_map/transpose(jvp())/reduce_sum | solution.py:70
  1883.8 9.2 copy.260
  1893.0 7.2 multiply_reduce_fusion.8
  1963.6 9.2 copy.261
  1977.2 9.2 copy.262
  1986.4 19.2 multiply_reduce_fusion.7
  2005.7 8.2 fusion.194
  2014.2 7.1 fusion.193
  2021.4 7.5 fusion.195
  2046.7 7.1 fusion.82
  2057.4 14.0 fusion.74
  2073.1 40.9 %all-reduce.163 = (f32[1024]{0:T(1024)}, f32[1024]{0:T(1024)}, f32[256]{0:T(256)}, f32[256]{0:T(256)}, f32[256]{0:T(256)}, /*index=5*/f32[1024]{0:T(1024)}) all-reduce(f32[1024]{0:T(1024)S(1)} %get-tuple-element.370, f32[1024]{0:T(1024)S(1)} %dynamic_update_slice.35, ...), channel_id=1, replica_groups=mesh['dp'=8,'tensor'=4] {'dp','tensor'}, use_global_device_ids=true, to_apply=%region_27.28 | all-reduce | flops 3840 | bytes 30720 | tf_op jit(solution)/shard_map/psum | solution.py:401
  2118.7 13.0 reduce-scatter.33.cloned.1.call-done
  2131.7 47.6 %reduce-scatter.31.cloned.1.call-done = f32[128,640]{1,0:T(8,128)} async-done(((f32[1024,640]{1,0:T(8,128)}), f32[128,640]{1,0:T(8,128)}) %reduce-scatter.31.cloned.1.call-update) | async-done | bytes 327696 | tf_op jit(solution)/shard_map/reduce_scatter | solution.py:421
  2179.2 47.4 %reduce-scatter.35.cloned.1.call-done = f32[640,128]{1,0:T(8,128)} async-done(((f32[640,1024]{1,0:T(8,128)}), f32[640,128]{1,0:T(8,128)}) %reduce-scatter.35.cloned.1.call-update) | async-done | bytes 327696 | tf_op jit(solution)/shard_map/reduce_scatter | solution.py:423
  2226.6 39.8 %reduce-scatter.23.cloned.1.call-done = f32[128,256]{1,0:T(8,128)} async-done(((f32[1024,256]{1,0:T(8,128)}), f32[128,256]{1,0:T(8,128)}) %reduce-scatter.23.cloned.1.call-update) | async-done | bytes 131088 | tf_op jit(solution)/shard_map/reduce_scatter | solution.py:417
  2266.4 45.1 %reduce-scatter.29.cloned.1.call-done = f32[512,128]{1,0:T(8,128)} async-done(((f32[512,1024]{1,0:T(8,128)}), f32[512,128]{1,0:T(8,128)}) %reduce-scatter.29.cloned.1.call-update) | async-done | bytes 262160 | tf_op jit(solution)/shard_map/reduce_scatter | solution.py:420
  2311.5 45.5 %reduce-scatter.27.cloned.1.call-done = f32[128,512]{1,0:T(8,128)} async-done(((f32[1024,512]{1,0:T(8,128)}), f32[128,512]{1,0:T(8,128)}) %reduce-scatter.27.cloned.1.call-update) | async-done | bytes 262160 | tf_op jit(solution)/shard_map/reduce_scatter | solution.py:419
  2357.0 45.0 %reduce-scatter.25.cloned.1.call-done = f32[128,512]{1,0:T(8,128)} async-done(((f32[1024,512]{1,0:T(8,128)}), f32[128,512]{1,0:T(8,128)}) %reduce-scatter.25.cloned.1.call-update) | async-done | bytes 262160 | tf_op jit(solution)/shard_map/reduce_scatter | solution.py:418
  2401.9 134.6 %all-reduce.170.cloned.1.call-done = (f32[16,1024]{1,0:T(8,128)}, f32[16,1024]{1,0:T(8,128)}, f32[16,1024]{1,0:T(8,128)}, f32[2,16,1024]{2,1,0:T(8,128)}) async-done(((f32[16,1024]{1,0:T(8,128)}, f32[16,1024]{1,0:T(8,128)}, f32[16,1024]{1,0:T(8,128)}, f32[2,16,1024]{2,1,0:T(8,128)}), (f32[16,1024]{1,0:T(8,128)}, f32[16,1024]{1,0:T(8,128)}, f32[16,1024]{1,0:T(8,128)}, ...) | async-done | bytes 327696 | tf_op jit(solution)/shard_map/psum | solution.py:401
  (1050 shorter events, 482.6 us)
Async XLA Ops:
  7.2 85.9 %all-gather.12.cloned.1.call-start = ((), (), s32[]{:S(2)}) async-start(), calls=%async_computation.12 | async-start | bytes 5242880 | tf_op jit(solution)/shard_map/all_gather | solution.py:249
  7.9 594.1 %all-gather.18.cloned.1.call-start = ((), (), s32[]{:S(2)}) async-start(), calls=%async_computation.15 | async-start | bytes 1179648 | tf_op jit(solution)/shard_map/all_gather | solution.py:211
  9.6 660.2 %all-gather.14.cloned.1.call-start = ((), (), s32[]{:S(2)}) async-start(), calls=%async_computation.13 | async-start | bytes 5242880 | tf_op jit(solution)/shard_map/all_gather | solution.py:277
  11.1 107.9 %copy-start.155 = (f32[1024,1]{0,1:T(1,128)}, f32[1024,1]{0,1:T(1,128)S(1)}, u32[]{:S(2)}) copy-start(f32[1024,1]{0,1:T(1,128)S(1)} %get-tuple-element.543) | copy-start | bytes 12292
  11.6 112.2 %copy-start.162 = (f32[512,1]{0,1:T(1,128)}, f32[512,1]{0,1:T(1,128)S(1)}, u32[]{:S(2)}) copy-start(f32[512,1]{0,1:T(1,128)S(1)} %get-tuple-element.545) | copy-start | bytes 6148
  12.1 114.4 %copy-start.171 = (f32[256,1]{0,1:T(1,128)}, f32[256,1]{0,1:T(1,128)S(1)}, u32[]{:S(2)}) copy-start(f32[256,1]{0,1:T(1,128)S(1)} %get-tuple-element.547) | copy-start | bytes 3076
  12.5 115.4 %copy-start.179 = (f32[128]{0:T(128)}, f32[128]{0:T(128)S(1)}, u32[]{:S(2)}) copy-start(f32[128]{0:T(128)S(1)} %get-tuple-element.563) | copy-start | bytes 1540
  12.9 115.9 %copy-start.181 = (f32[64]{0:T(128)}, f32[64]{0:T(128)S(1)}, u32[]{:S(2)}) copy-start(f32[64]{0:T(128)S(1)} %get-tuple-element.561) | copy-start | bytes 772
  13.1 116.2 %copy-start.183 = (f32[32]{0:T(128)}, f32[32]{0:T(128)S(1)}, u32[]{:S(2)}) copy-start(f32[32]{0:T(128)S(1)} %get-tuple-element.559) | copy-start | bytes 388
  13.4 116.3 %copy-start.185 = (f32[16]{0:T(128)}, f32[16]{0:T(128)S(1)}, u32[]{:S(2)}) copy-start(f32[16]{0:T(128)S(1)} %get-tuple-element.557) | copy-start | bytes 196
  13.6 116.4 %copy-start.187 = (f32[8]{0:T(128)}, f32[8]{0:T(128)S(1)}, u32[]{:S(2)}) copy-start(f32[8]{0:T(128)S(1)} %get-tuple-element.555) | copy-start | bytes 100
  13.8 116.4 %copy-start.189 = (f32[4]{0:T(128)}, f32[4]{0:T(128)S(1)}, u32[]{:S(2)}) copy-start(f32[4]{0:T(128)S(1)} %get-tuple-element.553) | copy-start | bytes 52
  16.1 330.1 %copy-start.65 = (pred[128,128]{0,1:T(8,128)(4,1)}, pred[128,128]{0,1:T(8,128)(4,1)S(1)}, u32[]{:S(2)}) copy-start(pred[128,128]{0,1:T(8,128)(4,1)S(1)} %iota_compare_fusion.2) | copy-start | bytes 49156
  18.8 123.9 %copy-start.191 = (f32[2]{0:T(128)}, f32[2]{0:T(128)S(1)}, u32[]{:S(2)}) copy-start(f32[2]{0:T(128)S(1)} %get-tuple-element.551) | copy-start | bytes 28
  20.7 122.5 %copy-start.200 = (f32[3]{0:T(128)}, f32[3]{0:T(128)S(1)}, u32[]{:S(2)}) copy-start(f32[3]{0:T(128)S(1)} %subtract_bitcast_fusion.2) | copy-start | bytes 40
  20.7 122.9 %copy-start.202 = (f32[7]{0:T(128)}, f32[7]{0:T(128)S(1)}, u32[]{:S(2)}) copy-start(f32[7]{0:T(128)S(1)} %subtract_bitcast_fusion.4) | copy-start | bytes 88
  20.7 123.1 %copy-start.204 = (f32[15]{0:T(128)}, f32[15]{0:T(128)S(1)}, u32[]{:S(2)}) copy-start(f32[15]{0:T(128)S(1)} %subtract_bitcast_fusion.6) | copy-start | bytes 184
  20.8 123.8 %copy-start.206 = (f32[31]{0:T(128)}, f32[31]{0:T(128)S(1)}, u32[]{:S(2)}) copy-start(f32[31]{0:T(128)S(1)} %subtract_bitcast_fusion.8) | copy-start | bytes 376
  20.8 124.1 %copy-start.208 = (f32[63]{0:T(128)}, f32[63]{0:T(128)S(1)}, u32[]{:S(2)}) copy-start(f32[63]{0:T(128)S(1)} %subtract_bitcast_fusion.10) | copy-start | bytes 760
  20.8 125.7 %copy-start.210 = (f32[127]{0:T(128)}, f32[127]{0:T(128)S(1)}, u32[]{:S(2)}) copy-start(f32[127]{0:T(128)S(1)} %subtract_bitcast_fusion.12) | copy-start | bytes 1528
  20.8 126.6 %copy-start.167 = (f32[255,1]{0,1:T(1,128)}, f32[255,1]{0,1:T(1,128)S(1)}, u32[]{:S(2)}) copy-start(f32[255,1]{0,1:T(1,128)S(1)} %broadcast_subtract_fusion.5) | copy-start | bytes 3064
  20.8 131.6 %copy-start.160 = (f32[511,1]{0,1:T(1,128)}, f32[511,1]{0,1:T(1,128)S(1)}, u32[]{:S(2)}) copy-start(f32[511,1]{0,1:T(1,128)S(1)} %broadcast_subtract_fusion.3) | copy-start | bytes 6136
  20.9 134.1 %copy-start.153 = (f32[1023,1]{0,1:T(1,128)}, f32[1023,1]{0,1:T(1,128)S(1)}, u32[]{:S(2)}) copy-start(f32[1023,1]{0,1:T(1,128)S(1)} %broadcast_subtract_fusion.1) | copy-start | bytes 12280
  35.3 173.7 %copy-start.15 = (f32[128,16,256]{2,1,0:T(8,128)}, f32[128,16,256]{2,1,0:T(8,128)S(1)}, u32[]{:S(2)}) copy-start(f32[128,16,256]{2,1,0:T(8,128)S(1)} %get-tuple-element.536) | copy-start | bytes 6291460
  274.8 71.4 %copy-start.27 = (s32[1,2048]{1,0:T(1,128)S(1)}, s32[1,2048]{1,0:T(1,128)}, u32[]{:S(2)}) copy-start(s32[1,2048]{1,0:T(1,128)} %param.25) | copy-start | bytes 24580
  590.5 127.0 %all-gather.16.cloned.1.call-start = ((), (), s32[]{:S(2)}) async-start(), calls=%async_computation.14 | async-start | bytes 1179648 | tf_op jit(solution)/shard_map/all_gather | solution.py:212
  591.2 136.3 %all-gather.20.cloned.1.call-start = ((), (), s32[]{:S(2)}) async-start(), calls=%async_computation.16 | async-start | bytes 1179648 | tf_op jit(solution)/shard_map/all_gather | solution.py:213
  592.0 216.9 %reduce-scatter.13.cloned.1.call-start = ((), (), s32[]{:S(2)}) async-start(), calls=%async_computation.17 | async-start | bytes 5242880 | tf_op jit(solution)/shard_map/reduce_scatter | solution.py:292
  602.0 67.8 %copy-start.51 = (bf16[1024,256]{1,0:T(8,128)(2,1)}, bf16[1024,256]{1,0:T(8,128)(2,1)S(1)}, u32[]{:S(2)}) copy-start(bf16[1024,256]{1,0:T(8,128)(2,1)S(1)} %all_gather.46) | copy-start | bytes 1572868
  602.0 67.8 %copy-start.173 = (f32[256]{0:T(256)S(1)}, f32[256]{0:T(256)}, u32[]{:S(2)}) copy-start(f32[256]{0:T(256)} %param.35) | copy-start | bytes 3076
  602.0 67.8 %copy-start.175 = (f32[256]{0:T(256)S(1)}, f32[256]{0:T(256)}, u32[]{:S(2)}) copy-start(f32[256]{0:T(256)} %param.33) | copy-start | bytes 3076
  602.0 67.8 %copy-start.195 = (f32[256]{0:T(256)S(1)}, f32[256]{0:T(256)}, u32[]{:S(2)}) copy-start(f32[256]{0:T(256)} %param.34) | copy-start | bytes 3076
  733.7 75.2 %copy-start.5 = (bf16[512,1024]{1,0:T(8,128)(2,1)S(1)}, bf16[512,1024]{1,0:T(8,128)(2,1)}, u32[]{:S(2)}) copy-start(bf16[512,1024]{1,0:T(8,128)(2,1)} %param.24) | copy-start | bytes 3145732
  733.7 76.9 %copy-start.147 = (f32[1024]{0:T(1024)S(1)}, f32[1024]{0:T(1024)}, u32[]{:S(2)}) copy-start(f32[1024]{0:T(1024)} %param.39) | copy-start | bytes 12292
  733.7 79.5 %copy-start.95 = (f32[128,640]{1,0:T(8,128)S(1)}, f32[128,640]{1,0:T(8,128)}, u32[]{:S(2)}) copy-start(f32[128,640]{1,0:T(8,128)} %param.41) | copy-start | bytes 983044
  733.7 80.3 %copy-start.96 = (f32[640,128]{1,0:T(8,128)S(1)}, f32[640,128]{1,0:T(8,128)}, u32[]{:S(2)}) copy-start(f32[640,128]{1,0:T(8,128)} %param.42) | copy-start | bytes 983044
  733.8 102.4 %all-gather.24.cloned.1.call-start = ((), (), s32[]{:S(2)}) async-start(), calls=%async_computation.19 | async-start | bytes 1474560 | tf_op jit(solution)/shard_map/all_gather | solution.py:214
  735.4 183.7 %all-gather.22.cloned.1.call-start = ((), (), s32[]{:S(2)}) async-start(), calls=%async_computation.18 | async-start | bytes 5242880 | tf_op jit(solution)/shard_map/all_gather | solution.py:299
  810.6 340.2 %copy-start.151 = (f32[512]{0:T(512)}, f32[512]{0:T(512)S(1)}, u32[]{:S(2)}) copy-start(f32[512]{0:T(512)S(1)} %fusion.132) | copy-start | bytes 6148
  813.2 131.1 %all-gather.26.cloned.1.call-start = ((), (), s32[]{:S(2)}) async-start(), calls=%async_computation.20 | async-start | bytes 1474560 | tf_op jit(solution)/shard_map/all_gather | solution.py:215
  814.0 157.0 %all-gather.28.cloned.1.call-start = ((), (), s32[]{:S(2)}) async-start(), calls=%async_computation.21 | async-start | bytes 1474560 | tf_op jit(solution)/shard_map/all_gather | solution.py:216
  814.7 238.7 %all-gather.30.cloned.1.call-start = ((), (), s32[]{:S(2)}) async-start(), calls=%async_computation.23 | async-start | bytes 5242880 | tf_op jit(solution)/shard_map/all_gather | solution.py:312
  815.5 332.5 %reduce-scatter.17.cloned.1.call-start = ((), (), s32[]{:S(2)}) async-start(), calls=%async_computation.24 | async-start | bytes 5242880 | tf_op jit(solution)/shard_map/reduce_scatter | solution.py:321
  952.8 111.1 %copy-start.213 = (bf16[1024,640]{1,0:T(8,128)(2,1)S(1)}, bf16[1024,640]{1,0:T(8,128)(2,1)}, u32[]{:S(2)}) copy-start(bf16[1024,640]{1,0:T(8,128)(2,1)} %all-gather.24.cloned.1.call-done) | copy-start | bytes 3932164
  1072.5 75.5 %copy-start.11 = (bf16[512,1024]{1,0:T(8,128)(2,1)S(1)}, bf16[512,1024]{1,0:T(8,128)(2,1)}, u32[]{:S(2)}) copy-start(bf16[512,1024]{1,0:T(8,128)(2,1)} %reduce-scatter.13.cloned.1.call-done) | copy-start | bytes 3145732
  1072.5 78.9 %copy-start.19 = (bf16[512,1024]{1,0:T(8,128)(2,1)S(1)}, bf16[512,1024]{1,0:T(8,128)(2,1)}, u32[]{:S(2)}) copy-start(bf16[512,1024]{1,0:T(8,128)(2,1)} %param.43) | copy-start | bytes 3145732
  1072.5 163.3 %all-gather.32.cloned.1.call-start = ((), (), s32[]{:S(2)}) async-start(), calls=%async_computation.25 | async-start | bytes 5242880 | tf_op jit(solution)/shard_map/all_gather | solution.py:332
  1154.4 220.9 %all-reduce.168.cloned.1.call-start = ((), (), s32[]{:S(2)}) async-start(), calls=%async_computation.27 | async-start | bytes 2097152 | tf_op jit(solution)/shard_map/psum | solution.py:358
  1247.1 73.3 %copy-start.174 = (f32[256]{0:T(256)S(1)}, f32[256]{0:T(256)}, u32[]{:S(2)}) copy-start(f32[256]{0:T(256)} %param.35) | copy-start | bytes 3076
  1247.1 73.3 %copy-start.176 = (f32[256]{0:T(256)S(1)}, f32[256]{0:T(256)}, u32[]{:S(2)}) copy-start(f32[256]{0:T(256)} %param.33) | copy-start | bytes 3076
  1324.8 128.9 %reduce-scatter.19.cloned.1.call-start = ((), (), s32[]{:S(2)}) async-start(), calls=%async_computation.26 | async-start | bytes 5242880 | tf_op jit(solution)/shard_map/reduce_scatter | solution.py:365
  1331.2 782.8 %reduce-scatter.15.cloned.1.call-start = ((), (), s32[]{:S(2)}) async-start(), calls=%async_computation.22 | async-start | bytes 5242880 | tf_op jit(solution)/shard_map/reduce_scatter | solution.py:304
  1339.3 774.8 %reduce-scatter.21.cloned.1.call-start = ((), (), s32[]{:S(2)}) async-start(), calls=%async_computation.28 | async-start | bytes 5242880 | tf_op jit(solution)/shard_map/reduce_scatter | solution.py:387
  1345.8 108.0 %copy-start.52 = (f32[2048,256]{1,0:T(8,128)S(1)}, f32[2048,256]{1,0:T(8,128)}, u32[]{:S(2)}) copy-start(f32[2048,256]{1,0:T(8,128)} %get-tuple-element.340) | copy-start | bytes 6291460
  1669.2 69.3 %copy-start.30 = (s32[2048]{0:T(1024)S(1)}, s32[2048]{0:T(1024)}, u32[]{:S(2)}) copy-start(s32[2048]{0:T(1024)} %copy-done.29) | copy-start | bytes 24580
  1669.2 69.3 %copy-start.66 = (pred[128,128]{0,1:T(8,128)(4,1)S(1)}, pred[128,128]{0,1:T(8,128)(4,1)}, u32[]{:S(2)}) copy-start(pred[128,128]{0,1:T(8,128)(4,1)} %copy-done.65) | copy-start | bytes 49156
  2005.7 126.0 %reduce-scatter.33.cloned.1.call-start = ((), (), s32[]{:S(2)}) async-start(), calls=%async_computation.34 | async-start | bytes 2949120 | tf_op jit(solution)/shard_map/reduce_scatter | solution.py:422
  2013.9 165.3 %reduce-scatter.31.cloned.1.call-start = ((), (), s32[]{:S(2)}) async-start(), calls=%async_computation.33 | async-start | bytes 2949120 | tf_op jit(solution)/shard_map/reduce_scatter | solution.py:421
  2021.4 205.3 %reduce-scatter.35.cloned.1.call-start = ((), (), s32[]{:S(2)}) async-start(), calls=%async_computation.35 | async-start | bytes 2949120 | tf_op jit(solution)/shard_map/reduce_scatter | solution.py:423
  2029.0 237.5 %reduce-scatter.23.cloned.1.call-start = ((), (), s32[]{:S(2)}) async-start(), calls=%async_computation.29 | async-start | bytes 1179648 | tf_op jit(solution)/shard_map/reduce_scatter | solution.py:417
  2033.6 277.9 %reduce-scatter.29.cloned.1.call-start = ((), (), s32[]{:S(2)}) async-start(), calls=%async_computation.32 | async-start | bytes 2359296 | tf_op jit(solution)/shard_map/reduce_scatter | solution.py:420
  2039.6 317.4 %reduce-scatter.27.cloned.1.call-start = ((), (), s32[]{:S(2)}) async-start(), calls=%async_computation.31 | async-start | bytes 2359296 | tf_op jit(solution)/shard_map/reduce_scatter | solution.py:419
  2046.4 355.5 %reduce-scatter.25.cloned.1.call-start = ((), (), s32[]{:S(2)}) async-start(), calls=%async_computation.30 | async-start | bytes 2359296 | tf_op jit(solution)/shard_map/reduce_scatter | solution.py:418
  2054.0 482.5 %all-reduce.170.cloned.1.call-start = ((), (), s32[]{:S(2)}) async-start(), calls=%async_computation.36 | async-start | bytes 655360 | tf_op jit(solution)/shard_map/psum | solution.py:401
  (204 other events, 2623.4 us)
Sparse Core Ops, SparseCore 0:
  9.6 83.4 all-gather.11
  95.5 22.0 all-gather.17
  590.6 79.1 all-gather.13
  672.1 21.6 all-gather.15
  695.5 23.5 all-gather.19
  733.9 75.0 reduce-scatter.12
  811.0 25.1 all-gather.23
  838.3 80.7 all-gather.21
  921.2 23.1 all-gather.25
  946.2 24.7 all-gather.27
  972.6 80.7 all-gather.29
  1072.6 75.2 reduce-scatter.16
  1154.5 81.2 all-gather.31
  1324.9 50.3 all-reduce.167
  1377.6 76.1 reduce-scatter.18
  1455.9 77.2 reduce-scatter.14
  2005.8 77.4 reduce-scatter.20
  2087.1 44.5 reduce-scatter.32
  2135.6 43.6 reduce-scatter.30
  2183.0 43.6 reduce-scatter.34
  2230.4 35.9 reduce-scatter.22
  2270.3 41.1 reduce-scatter.28
  2315.7 41.2 reduce-scatter.26
  2360.7 41.1 reduce-scatter.24
  2409.4 127.0 all-reduce.169
where the time goes:
time: 2560 us; the launch traced here: 2550 us
  waiting for transfers between devices  1080 us (42%)
  local copies, waits for them, and re-layouts  639 us (25%)
  other arithmetic  400 us (16%)
  matrix products  347 us (14%)
  blocking collectives  50.8 us (2%)
    psum x1, waiting for transfers between devices, on_device(): lax.psum((gain_grad, rate_full, angle_full, input_full, output_full, skip...  135 us
    unnamed x445, local copies, waits for them, and re-layouts  117 us
    dot_general x2, matrix products, ema_apply(): inner = jnp.einsum('nts,nsk->ntk', within, stacked, precision=HIGHEST)  109 us
    all_gather x1, waiting for transfers between devices, on_device(): lax.all_gather(norm_in.astype(jnp.bfloat16), 'tensor', axis=0, tiled=True)  83 us
    all_gather x1, waiting for transfers between devices, on_device(): grad_full = lax.all_gather(out_grad, 'tensor', axis=0, tiled=True)  82.5 us
    all_gather x1, waiting for transfers between devices, on_device(): lax.all_gather(grad_residual.astype(jnp.bfloat16), 'tensor', axis=0, tile...  81.1 us
    reduce_scatter x1, waiting for transfers between devices, on_device(): lax.psum_scatter(jnp.einsum('rv,dv->rd', grad_gate_pre, gate_b, preferred...  78.4 us
    reduce_scatter x1, waiting for transfers between devices, on_device(): lax.psum_scatter((jnp.einsum('rf,df->rd', grad_swish_pre, swish_b, prefer...  75.4 us
  transfers between devices with their start and end apart: 25, of which 20 were waited for; matrix products, arithmetic and copies ran while one was open for 49% of the time, Pallas kernels for 0%

commit v1 on v0

v1 whole, which is shorter than its diff:
```python
import functools
import math

import jax
import jax.numpy as jnp
from jax import lax
from jax.experimental import pallas as pl
from jax.experimental.pallas import tpu as pltpu
from jax.sharding import PartitionSpec as P

TN_GROUPS = 16
EPSILON = 1e-05
REACH = 800
STEP = 16
LANES = 128
F32 = jnp.float32
BF16 = jnp.bfloat16
HIGHEST = lax.Precision.HIGHEST
BOTH = ("dp", "tensor")


def dot32(a, b, dims=((1,), (0,)), precision=None):
    return lax.dot_general(a, b, (dims, ((), ())), precision=precision, preferred_element_type=F32)


NT = ((1,), (1,))
TN = ((0,), (0,))


def silu_of(v):
    return v * jax.nn.sigmoid(v)


def silu_slope(v):
    sg = jax.nn.sigmoid(v)
    return sg * (1.0 + v * (1.0 - sg))


def broadcast_row(ref, row):
    return ref[pl.ds(row, 8, stride=0), :]


def rotate(x, shift):
    return pltpu.roll(x, shift % 8, axis=0)


def ema_enter(rows, dims, h_ref, kend_ref, br_ref, bi_ref, qs_ref, cont_ref, mk_ref, l_ref, end_ref, hm):
    groups = rows // (8 * STEP)
    for g in range(groups):
        for i in range(STEP):
            at = g * STEP + i
            h = h_ref[pl.ds(at, 8, stride=groups * STEP), :]
            hm[at] = h * kend_ref[at]

    def quad(jq, carry):
        for half in range(2):
            acc = [[None] * 4 for _ in range(groups)]
            for i in range(STEP):
                cr = [broadcast_row(br_ref, i * dims + jq * 4 + half * 2 + k) for k in range(2)]
                ci = [broadcast_row(bi_ref, i * dims + jq * 4 + half * 2 + k) for k in range(2)]
                for g in range(groups):
                    h = hm[g * STEP + i]
                    terms = [cr[0] * h, ci[0] * h, cr[1] * h, ci[1] * h]
                    acc[g] = terms if i == 0 else [a + t for a, t in zip(acc[g], terms)]
            for g in range(groups):
                for k in range(2):
                    j = jq * 4 + half * 2 + k
                    l_ref[(g * dims + j) * 2] = acc[g][2 * k]
                    l_ref[(g * dims + j) * 2 + 1] = acc[g][2 * k + 1]
        return carry

    lax.fori_loop(0, dims // 4, quad, 0)

    def one(j, carry):
        zero = jnp.zeros((8, LANES), F32)
        states = scan_states(groups, dims, j, l_ref, qs_ref, cont_ref, mk_ref, zero, zero)
        end_ref[pl.ds(2 * j, 1), :] = states[1][0][7:8]
        end_ref[pl.ds(2 * j + 1, 1), :] = states[1][1][7:8]
        return carry

    lax.fori_loop(0, dims, one, 0)


def scan_states(groups, dims, j, l_ref, qs_ref, cont_ref, mk_ref, inr, ini):
    qr, qi = broadcast_row(qs_ref, 2 * j), broadcast_row(qs_ref, 2 * j + 1)
    part = [(l_ref[(g * dims + j) * 2], l_ref[(g * dims + j) * 2 + 1]) for g in range(groups)]

    def through(sr, si):
        starts = []
        for g in range(groups):
            starts.append((sr, si))
            keep = cont_ref[g]
            sr, si = (
                keep * (qr * sr - qi * si) + part[g][0],
                keep * (qr * si + qi * sr) + part[g][1],
            )
        return starts, sr, si

    _, er, ei = through(inr, ini)
    for k in range(3):
        wr = broadcast_row(qs_ref, 2 * dims * (k + 1) + 2 * j)
        wi = broadcast_row(qs_ref, 2 * dims * (k + 1) + 2 * j + 1)
        pr, pi = rotate(er, 1 << k), rotate(ei, 1 << k)
        keep = mk_ref[k]
        er, ei = er + keep * (wr * pr - wi * pi), ei + keep * (wr * pi + wi * pr)
    first = lax.broadcasted_iota(jnp.int32, (8, LANES), 0) == 0
    sr = jnp.where(first, inr, rotate(er, 1))
    si = jnp.where(first, ini, rotate(ei, 1))
    starts, _, _ = through(sr, si)
    return starts, (er, ei)


def ema_read(
    rows, dims, h_ref, seg_ref, k0_ref, ar_ref, ai_ref, kd_ref, qs_ref, cont_ref, mk_ref, l_ref, in_ref, skip_ref,
    e_ref, m_ref, s_ref, hs
):
    groups = rows // (8 * STEP)
    first = lax.broadcasted_iota(jnp.int32, (8, LANES), 0) == 0

    def one(j, carry):
        inr = jnp.where(first, broadcast_row(in_ref, 2 * j), 0.0)
        ini = jnp.where(first, broadcast_row(in_ref, 2 * j + 1), 0.0)
        starts, _ = scan_states(groups, dims, j, l_ref, qs_ref, cont_ref, mk_ref, inr, ini)
        for g in range(groups):
            s_ref[(g * dims + j) * 2] = starts[g][0]
            s_ref[(g * dims + j) * 2 + 1] = starts[g][1]
        return carry

    lax.fori_loop(0, dims, one, 0)
    for g in range(groups):
        for i in range(STEP):
            at = g * STEP + i
            hs[at] = h_ref[pl.ds(at, 8, stride=groups * STEP), :]

    block = 4

    def some(iq, carry):
        acc = [[None] * block for _ in range(groups)]
        for j in range(dims):
            states = [(s_ref[(g * dims + j) * 2], s_ref[(g * dims + j) * 2 + 1]) for g in range(groups)]
            for i in range(block):
                cr = broadcast_row(ar_ref, (iq * block + i) * dims + j)
                ci = broadcast_row(ai_ref, (iq * block + i) * dims + j)
                for g in range(groups):
                    term = cr * states[g][0] - ci * states[g][1]
                    acc[g][i] = term if j == 0 else acc[g][i] + term
        for g in range(groups):
            for i in range(block):
                at = g * STEP + iq * block + i
                hs[groups * STEP + at] = acc[g][i] * k0_ref[at]
        return carry

    lax.fori_loop(0, STEP // block, some, 0)
    taps = [jnp.broadcast_to(kd_ref[d : d + 1, :], (8, LANES)) for d in range(STEP)]
    skip = jnp.broadcast_to(skip_ref[...], (8, LANES))
    tap0 = taps[0] + skip
    for g in range(groups):
        for i in range(STEP):
            at = g * STEP + i
            seg = seg_ref[at]
            out = hs[groups * STEP + at] + tap0 * hs[at]
            for s in range(i):
                src = g * STEP + s
                out = out + taps[i - s] * jnp.where(seg_ref[src] == seg, hs[src], 0.0)
            e_ref[pl.ds(at, 8, stride=groups * STEP), :] = out
    e = e_ref[...]
    m_ref[...] = silu_of(e).astype(m_ref.dtype)


def reverse_states(groups, dims, j, g_ref, qs_ref, cont_ref, mkr_ref, inr, ini):
    qr, qi = broadcast_row(qs_ref, 2 * j), broadcast_row(qs_ref, 2 * j + 1)
    part = [(g_ref[(g * dims + j) * 2], g_ref[(g * dims + j) * 2 + 1]) for g in range(groups)]

    def through(yr, yi):
        ends = [None] * groups
        for g in reversed(range(groups)):
            ends[g] = (yr, yi)
            keep = cont_ref[g]
            yr, yi = (
                keep * (qr * yr + qi * yi) + part[g][0],
                keep * (qr * yi - qi * yr) + part[g][1],
            )
        return ends, yr, yi

    _, fr, fi = through(inr, ini)
    for k in range(3):
        wr = broadcast_row(qs_ref, 2 * dims * (k + 1) + 2 * j)
        wi = broadcast_row(qs_ref, 2 * dims * (k + 1) + 2 * j + 1)
        pr, pi = rotate(fr, -(1 << k)), rotate(fi, -(1 << k))
        keep = mkr_ref[k]
        fr, fi = fr + keep * (wr * pr + wi * pi), fi + keep * (wr * pi - wi * pr)
    last = lax.broadcasted_iota(jnp.int32, (8, LANES), 0) == 7
    yr = jnp.where(last, inr, rotate(fr, -1))
    yi = jnp.where(last, ini, rotate(fi, -1))
    ends, _, _ = through(yr, yi)
    return ends, (fr, fi)


def ema_leave(rows, dims, de_ref, k0_ref, ar_ref, ai_ref, qs_ref, cont_ref, mkr_ref, g_ref, head_ref, dm):
    groups = rows // (8 * STEP)
    for g in range(groups):
        for i in range(STEP):
            at = g * STEP + i
            dm[at] = de_ref[pl.ds(at, 8, stride=groups * STEP), :] * k0_ref[at]

    def quad(jq, carry):
        for half in range(2):
            acc = [[None] * 4 for _ in range(groups)]
            for i in range(STEP):
                cr = [broadcast_row(ar_ref, i * dims + jq * 4 + half * 2 + k) for k in range(2)]
                ci = [broadcast_row(ai_ref, i * dims + jq * 4 + half * 2 + k) for k in range(2)]
                for g in range(groups):
                    d = dm[g * STEP + i]
                    terms = [cr[0] * d, ci[0] * d, cr[1] * d, ci[1] * d]
                    acc[g] = terms if i == 0 else [a + t for a, t in zip(acc[g], terms)]
            for g in range(groups):
                for k in range(2):
                    j = jq * 4 + half * 2 + k
                    g_ref[(g * dims + j) * 2] = acc[g][2 * k]
                    g_ref[(g * dims + j) * 2 + 1] = -acc[g][2 * k + 1]
        return carry

    lax.fori_loop(0, dims // 4, quad, 0)

    def one(j, carry):
        zero = jnp.zeros((8, LANES), F32)
        _, heads = reverse_states(groups, dims, j, g_ref, qs_ref, cont_ref, mkr_ref, zero, zero)
        head_ref[pl.ds(2 * j, 1), :] = heads[0][0:1]
        head_ref[pl.ds(2 * j + 1, 1), :] = heads[1][0:1]
        return carry

    lax.fori_loop(0, dims, one, 0)


def ema_grads(
    rows, dims, h_ref, de_ref, seg_ref, kend_ref, rk0_ref, rkend_ref, br_ref, bi_ref, kd_ref, qs_ref, cont_ref,
    mkr_ref, g_ref, in_ref, s_ref, skip_ref, dh_ref, ga_ref, gb_ref, gk_ref, gq_ref, gs_ref, hs, ds, la
):
    groups = rows // (8 * STEP)
    last = lax.broadcasted_iota(jnp.int32, (8, LANES), 0) == 7

    def one(j, carry):
        inr = jnp.where(last, broadcast_row(in_ref, 2 * j), 0.0)
        ini = jnp.where(last, broadcast_row(in_ref, 2 * j + 1), 0.0)
        ends, _ = reverse_states(groups, dims, j, g_ref, qs_ref, cont_ref, mkr_ref, inr, ini)
        qr = jnp.zeros((8, LANES), F32)
        qi = jnp.zeros((8, LANES), F32)
        for g in range(groups):
            yr, yi = ends[g]
            la[(g * dims + j) * 2] = yr
            la[(g * dims + j) * 2 + 1] = yi
            keep = cont_ref[g]
            sr, si = s_ref[(g * dims + j) * 2], s_ref[(g * dims + j) * 2 + 1]
            qr = qr + keep * (yr * sr + yi * si)
            qi = qi + keep * (yi * sr - yr * si)
        gq_ref[pl.ds(2 * j, 1), :] = jnp.sum(qr, axis=0, keepdims=True)
        gq_ref[pl.ds(2 * j + 1, 1), :] = jnp.sum(qi, axis=0, keepdims=True)
        return carry

    lax.fori_loop(0, dims, one, 0)
    total = jnp.zeros((8, LANES), F32)
    for g in range(groups):
        for i in range(STEP):
            at = g * STEP + i
            h = h_ref[pl.ds(at, 8, stride=groups * STEP), :]
            d = de_ref[pl.ds(at, 8, stride=groups * STEP), :]
            hs[at] = h
            ds[at] = d
            total = total + h * d
    gs_ref[...] = jnp.sum(total, axis=0, keepdims=True)
    block = 4

    def some(iq, carry):
        acc = [[None] * block for _ in range(groups)]
        for j in range(dims):
            ends = [(la[(g * dims + j) * 2], la[(g * dims + j) * 2 + 1]) for g in range(groups)]
            for i in range(block):
                cr = broadcast_row(br_ref, (iq * block + i) * dims + j)
                ci = broadcast_row(bi_ref, (iq * block + i) * dims + j)
                for g in range(groups):
                    term = cr * ends[g][0] + ci * ends[g][1]
                    acc[g][i] = term if j == 0 else acc[g][i] + term
        for g in range(groups):
            for i in range(block):
                at = g * STEP + iq * block + i
                hs[groups * STEP + at] = acc[g][i] * kend_ref[at]
        return carry

    lax.fori_loop(0, STEP // block, some, 0)
    taps = [jnp.broadcast_to(kd_ref[d : d + 1, :], (8, LANES)) for d in range(STEP)]
    skip = jnp.broadcast_to(skip_ref[...], (8, LANES))
    tap0 = taps[0] + skip
    kacc = [jnp.zeros((8, LANES), F32) for _ in range(STEP)]
    kacc[0] = total
    for g in range(groups):
        for s in range(STEP):
            at = g * STEP + s
            seg = seg_ref[at]
            h = hs[at]
            out = hs[groups * STEP + at] + tap0 * ds[at]
            for t in range(s + 1, STEP):
                d = jnp.where(seg_ref[g * STEP + t] == seg, ds[g * STEP + t], 0.0)
                out = out + taps[t - s] * d
                kacc[t - s] = kacc[t - s] + h * d
            dh_ref[pl.ds(at, 8, stride=groups * STEP), :] = out
    for d in range(STEP):
        gk_ref[d : d + 1, :] = jnp.sum(kacc[d], axis=0, keepdims=True)

    def tables(jq, carry):
        width = 4

        def chunk(n, acc):
            sub, g = n // groups, n % groups
            base = pl.multiple_of(n * STEP, STEP)
            d = de_ref[pl.ds(base, STEP), :] * rk0_ref[pl.ds(base, STEP), :]
            h = h_ref[pl.ds(base, STEP), :] * rkend_ref[pl.ds(base, STEP), :]
            out = []
            for k in range(width):
                at = (g * dims + jq * width + k) * 2
                sr = s_ref[at, pl.ds(sub, STEP, stride=0), :]
                si = s_ref[at + 1, pl.ds(sub, STEP, stride=0), :]
                yr = la[at, pl.ds(sub, STEP, stride=0), :]
                yi = la[at + 1, pl.ds(sub, STEP, stride=0), :]
                a0, a1, b0, b1 = acc[4 * k : 4 * k + 4]
                out += [a0 + d * sr, a1 - d * si, b0 + h * yr, b1 + h * yi]
            return tuple(out)

        zero = jnp.zeros((STEP, LANES), F32)
        acc = lax.fori_loop(0, 8 * groups, chunk, (zero,) * (4 * width))
        for k in range(width):
            j = jq * width + k
            ga_ref[2 * j] = acc[4 * k]
            ga_ref[2 * j + 1] = acc[4 * k + 1]
            gb_ref[2 * j] = acc[4 * k + 2]
            gb_ref[2 * j + 1] = acc[4 * k + 3]
        return carry

    lax.fori_loop(0, dims // 4, tables, 0)


def col(rows):
    return pl.BlockSpec((rows, LANES), lambda i: (0, i))


def col3(a, b):
    return pl.BlockSpec((a, b, LANES), lambda i: (0, 0, i))


def whole(*shape):
    return pl.BlockSpec(shape, lambda i: (0,) * len(shape))


def ema_call(body, rows, dims, width, ins, outs, scratch, name, flops):
    specs = [s for _, s in ins]
    return pl.pallas_call(
        functools.partial(body, rows, dims),
        grid=(width // LANES,),
        in_specs=specs,
        out_specs=[s for _, s in outs],
        out_shape=[o for o, _ in outs],
        scratch_shapes=scratch,
        compiler_params=pltpu.CompilerParams(vmem_limit_bytes=48 << 20),
        cost_estimate=pl.CostEstimate(flops=flops, bytes_accessed=16 << 20, transcendentals=0),
        name=name,
    )(*[a for a, _ in ins])


def powers(rate, angle, first, count, axis):
    n = (first + jnp.arange(count)).astype(F32)
    n = n[:, None, None] if axis == 0 else n[None, :, None]
    rate, angle = jnp.expand_dims(rate, axis), jnp.expand_dims(angle, axis)
    size = jnp.exp(-rate * n)
    return size * jnp.cos(angle * n), size * jnp.sin(angle * n)


def ema_tables(rate, angle, feed_gain, read_gain, axis):
    feed = feed_gain * jnp.sqrt(1.0 - jnp.exp(-2.0 * rate))
    pr, pi = powers(rate, angle, 0, STEP + 1, axis)
    low = functools.partial(lax.slice_in_dim, start_index=0, limit_index=STEP, axis=axis)
    high = functools.partial(lax.slice_in_dim, start_index=1, limit_index=STEP + 1, axis=axis)
    e0, e1, f = (jnp.expand_dims(v, axis) for v in (read_gain[0], read_gain[1], feed))
    hr, hi, lr, li = high(pr), high(pi), low(pr), low(pi)
    ar, ai = e0 * hr - e1 * hi, e0 * hi + e1 * hr
    br, bi = jnp.flip(f * lr, axis), jnp.flip(f * li, axis)
    taps = jnp.sum(f * (e0 * lr - e1 * li), axis=1 - axis)
    top = functools.partial(lax.index_in_dim, index=STEP, axis=axis, keepdims=False)
    return ar, ai, br, bi, taps, top(pr), top(pi)


def power_of(rate, angle, n):
    size = jnp.exp(-rate * n)
    return size * jnp.cos(angle * n), size * jnp.sin(angle * n)


def spread(v):
    return jnp.broadcast_to(v[..., None], v.shape + (LANES,))


def row_masks(seg, before):
    rows = seg.shape[0]
    groups = rows // (8 * STEP)
    cube = seg.reshape(8, groups, STEP)
    chunk_last = cube[:, :, -1]
    prior = jnp.concatenate([before[None], chunk_last.reshape(-1)[:-1]]).reshape(8, groups)
    keep0 = (cube == prior[:, :, None]).astype(F32)
    kend = (cube == chunk_last[:, :, None]).astype(F32)
    order = lambda v: spread(v.transpose(1, 2, 0).reshape(groups * STEP, 8))
    cont = spread((chunk_last == prior).astype(F32).transpose(1, 0))
    ends = jnp.concatenate([before[None], chunk_last[:, -1]])
    sub = jnp.arange(8)
    ahead, behind = [], []
    for k in range(3):
        w = 1 << k
        a = jnp.take(ends, jnp.maximum(sub + 1 - w, 0))
        ahead.append(((ends[1:] == a) & (sub >= w)).astype(F32))
        b = jnp.take(ends, jnp.minimum(sub + w, 8))
        behind.append(((ends[:8] == b) & (sub + w <= 7)).astype(F32))
    return dict(
        seg=order(cube.astype(F32)), keep0=order(keep0), kend=order(kend), cont=cont,
        mk=spread(jnp.stack(ahead)), mkr=spread(jnp.stack(behind)),
        rk0=spread(keep0.reshape(rows)), rkend=spread(kend.reshape(rows)),
    )


def on_device(
    block_in, segments, norm_gain, ema_rate, ema_angle, ema_input, ema_output, ema_skip, w_shared, query_gain,
    query_bias, key_gain, w_value, w_gate, w_out, ffn_gain, w_swish, w_up, w_down, out_grad,
):
    parts = lax.axis_size("tensor")
    replicas = lax.axis_size("dp")
    rank = lax.axis_index("tensor")
    rows, width = block_in.shape
    dims = ema_rate.shape[0]
    length = segments.shape[1]
    groups = TN_GROUPS
    span = width // groups
    latent_width = w_shared.shape[1]
    value_width = w_value.shape[1] * parts
    ffn_width = w_swish.shape[1] * parts
    depth = w_value.shape[0]
    hops = [min(rows, REACH - h * rows) for h in range(-(-REACH // rows))]
    halo = sum(hops)

    def from_earlier(x, hop):
        return lax.ppermute(x, "tensor", [(i, i + hop) for i in range(parts - hop)])

    def from_later(x, hop):
        return lax.ppermute(x, "tensor", [(i + hop, i) for i in range(parts - hop)])

    def halo_of(x):
        pieces = [from_earlier(x[rows - n :], h + 1) for h, n in enumerate(hops)]
        return jnp.concatenate(pieces[::-1] + [x], axis=0)

    def give_back(x):
        total = x[halo:].astype(F32)
        end = halo
        for h, n in enumerate(hops):
            got = from_later(x[end - n : end].astype(BF16), h + 1).astype(F32)
            total = total.at[rows - n :].add(got)
            end -= n
        return total

    piece = depth // parts
    shared_piece = lax.dynamic_slice_in_dim(w_shared, rank * piece, piece, 0)
    low = lambda w: w.astype(BF16)
    vw, fw = value_width // parts, ffn_width // parts
    pack_a = jnp.concatenate([low(w_value), low(w_gate), low(w_out.T)], axis=0)
    pack_f = jnp.concatenate([low(w_swish), low(w_up), low(w_down.T)], axis=0)
    all_s = lax.all_gather(low(shared_piece), BOTH, axis=0, tiled=True)
    all_a = lax.all_gather(pack_a, BOTH, axis=0).reshape(replicas, parts, 3, depth, vw)
    all_f = lax.all_gather(pack_f, BOTH, axis=0).reshape(replicas, parts, 3, depth, fw)
    flat = lambda w, k: w[:, :, k].transpose(0, 2, 1, 3).reshape(width, -1)
    value_b, gate_b, out_t = (flat(all_a, k) for k in range(3))
    swish_b, up_b, down_t = (flat(all_f, k) for k in range(3))
    shared_b = all_s

    seg_all = segments[0]
    padded = jnp.concatenate([jnp.full((halo,), -1, jnp.int32), seg_all, jnp.full((halo,), -2, jnp.int32)])
    near = lax.dynamic_slice_in_dim(padded, rank * rows, halo + rows + halo, 0)
    seg_keys = near[: halo + rows]
    seg = near[halo : halo + rows]
    before = near[halo - 1]
    masks = row_masks(seg, before)
    index = rank * rows + jnp.arange(rows, dtype=jnp.int32)
    start = jnp.sum((seg_all[None, :] < seg[:, None]).astype(jnp.int32), axis=1)
    count = (index - start + 1).astype(F32)[:, None] * span
    tri = jnp.arange(rows)
    same = seg[:, None] == seg[None, :]
    lower = (same & (tri[:, None] >= tri[None, :])).astype(F32)
    link1 = (seg[0] == before).astype(F32)
    link2 = (before == near[halo - rows - 1]).astype(F32)
    last = seg[-1]
    next1 = (near[halo + rows] == last).astype(F32)
    next2 = ((near[halo + 2 * rows - 1] == last) & (near[halo + 2 * rows] == last)).astype(F32) if halo > rows else 0.0
    heads = (seg == before).astype(F32)[:, None]
    tails = (seg == last).astype(F32)[:, None]

    x = block_in.astype(F32)
    gather = (jnp.arange(width)[:, None] // span == jnp.arange(groups)[None, :]).astype(F32)
    sums_of = lambda v: dot32(v, gather, precision=HIGHEST)
    spread_of = lambda v: dot32(v, gather, NT, precision=HIGHEST)
    sums = jnp.concatenate([dot32(block_in, gather.astype(BF16)), sums_of(x * x)], axis=1)
    running = dot32(lower, sums, precision=HIGHEST)
    tail = running[-1:]
    carry = from_earlier(tail, 1) + link2 * from_earlier(tail, 2)
    running = running + heads * carry
    mean = running[:, :groups] / count
    var = running[:, groups:] / count - mean * mean
    rho = lax.rsqrt(var + EPSILON)
    mean_full, rho_full = spread_of(mean), spread_of(rho)
    centred = (x - mean_full) * rho_full
    hidden = centred * norm_gain
    hidden_b = low(hidden)

    ar, ai, br, bi, taps, qr, qi = ema_tables(ema_rate, ema_angle, ema_input, ema_output, 0)
    stack2 = lambda r, i: jnp.stack([r, i], axis=1).reshape(2 * dims, width)
    sub_rows = rows // 8
    scales = jnp.concatenate(
        [stack2(qr, qi)] + [stack2(*power_of(ema_rate, ema_angle, float(sub_rows << k))) for k in range(3)]
    )
    flat2 = lambda v: v.reshape(STEP * dims, width)
    ar, ai, br, bi = flat2(ar), flat2(ai), flat2(br), flat2(bi)
    skip = ema_skip[None]
    gcount = rows // (8 * STEP)
    nstate = gcount * dims * 2
    at_rows = gcount * STEP
    state_shape = (jax.ShapeDtypeStruct((nstate, 8, width), F32), col3(nstate, 8))
    edge_shape = (jax.ShapeDtypeStruct((2 * dims, width), F32), col(2 * dims))
    table = col(STEP * dims)
    mask_spec = whole(at_rows, 8, LANES)
    cont_spec, mk_spec = whole(gcount, 8, LANES), whole(3, 8, LANES)
    qs_spec = col(8 * dims)
    vm = lambda n: pltpu.VMEM((n, 8, LANES), F32)
    mac = rows * width * dims * 4
    entering, end = ema_call(
        ema_enter, rows, dims, width,
        [(hidden, col(rows)), (masks["kend"], mask_spec), (br, table), (bi, table), (scales, qs_spec),
         (masks["cont"], cont_spec), (masks["mk"], mk_spec)],
        [state_shape, edge_shape], [vm(at_rows)], "ema_enter", mac,
    )
    whole_r, whole_i = power_of(ema_rate, ema_angle, float(rows))

    def turned(v, sign):
        v = v.reshape(dims, 2, width)
        r, i = v[:, 0], v[:, 1]
        wi = sign * whole_i
        return stack2(whole_r * r - wi * i, whole_r * i + wi * r)

    state_in = from_earlier(end, 1) + link2 * turned(from_earlier(end, 2), 1.0)
    ema_out, mixed, states = ema_call(
        ema_read, rows, dims, width,
        [(hidden, col(rows)), (masks["seg"], mask_spec), (masks["keep0"], mask_spec), (ar, table), (ai, table),
         (taps, col(STEP)), (scales, qs_spec), (masks["cont"], cont_spec), (masks["mk"], mk_spec),
         (entering, col3(nstate, 8)), (state_in, col(2 * dims)), (skip, col(1))],
        [(jax.ShapeDtypeStruct((rows, width), F32), col(rows)), (jax.ShapeDtypeStruct((rows, width), BF16), col(rows)),
         state_shape],
        [vm(2 * at_rows)], "ema_read", mac,
    )

    hidden_near = halo_of(hidden_b)
    latent = dot32(mixed, shared_b)
    queries = low(latent * query_gain + query_bias)
    keys_own = low(latent * key_gain)
    keys_near = halo_of(keys_own)
    value_pre = dot32(hidden_near, value_b)
    values = low(silu_of(value_pre))
    gate_pre = dot32(mixed, gate_b)
    gate_act = silu_of(gate_pre)
    scale = 1.0 / math.sqrt(latent_width)
    key_at = jnp.arange(halo + rows, dtype=jnp.int32)
    allowed = (key_at[None, :] <= halo + tri[:, None]) & (seg_keys[None, :] == seg[:, None])
    scores = jnp.where(allowed, dot32(queries, keys_near, NT) * scale, -1e30)
    peak = jnp.max(scores, axis=1, keepdims=True)
    raw = jnp.exp(scores - peak)
    probs = raw / jnp.sum(raw, axis=1, keepdims=True)
    probs_b = low(probs)
    attended = dot32(probs_b, values)
    gated = low(gate_act * attended)
    residual = x + dot32(gated, out_t, NT)

    rr = lax.rsqrt(jnp.mean(residual * residual, axis=1, keepdims=True) + EPSILON)
    nh = residual * rr
    norm_in = low(nh * ffn_gain)
    swish_pre = dot32(norm_in, swish_b)
    up_pre = dot32(norm_in, up_b)
    swish_act = silu_of(swish_pre)
    inner = low(swish_act * up_pre)
    block_out = low(residual + dot32(inner, down_t, NT))

    grad_inner = dot32(out_grad, down_t)
    grad_swish_pre = low(grad_inner * up_pre * silu_slope(swish_pre))
    grad_up_pre = low(grad_inner * swish_act)

    def shards(g):
        return low(g).reshape(replicas, depth, parts, -1).transpose(0, 2, 1, 3)

    def summed(pieces):
        g = jnp.concatenate(pieces, axis=2)
        g = lax.psum_scatter(g, "dp", scatter_dimension=0, tiled=False)
        return lax.psum_scatter(g, "tensor", scatter_dimension=0, tiled=False).astype(F32)

    ffn_sum = summed([
        shards(dot32(norm_in, grad_swish_pre, TN)),
        shards(dot32(norm_in, grad_up_pre, TN)),
        shards(dot32(out_grad, inner, TN)),
    ])
    grad_nn = dot32(grad_swish_pre, swish_b, NT) + dot32(grad_up_pre, up_b, NT)
    grad_ffn_gain = jnp.sum(nh * grad_nn, axis=0)
    scaled = grad_nn * ffn_gain
    grad_residual = out_grad.astype(F32) + rr * (scaled - nh * jnp.mean(nh * scaled, axis=1, keepdims=True))
    branch = low(grad_residual)

    grad_gated = dot32(branch, out_t)
    grad_attended = low(grad_gated * gate_act)
    grad_gate_pre = low(grad_gated * attended * silu_slope(gate_pre))
    grad_probs = dot32(grad_attended, values, NT)
    centre = jnp.sum(probs * grad_probs, axis=1, keepdims=True)
    grad_scores = low(probs * (grad_probs - centre))
    grad_queries = dot32(grad_scores, keys_near) * scale
    grad_keys = give_back(dot32(grad_scores, queries, TN) * scale)
    grad_value_pre = low(dot32(probs_b, grad_attended, TN) * silu_slope(value_pre))
    grad_hidden = give_back(dot32(grad_value_pre, value_b, NT))
    grad_query_gain = jnp.sum(latent * grad_queries, axis=0)
    grad_query_bias = jnp.sum(grad_queries, axis=0)
    grad_key_gain = jnp.sum(latent * grad_keys, axis=0)
    grad_latent = low(grad_queries * query_gain + grad_keys * key_gain)
    grad_shared = low(dot32(mixed, grad_latent, TN)).reshape(replicas, parts, -1, vw)
    attn_sum = summed([
        shards(dot32(hidden_near, grad_value_pre, TN)),
        shards(dot32(mixed, grad_gate_pre, TN)),
        shards(dot32(branch, gated, TN)),
        grad_shared,
    ])
    grad_ema = (dot32(grad_latent, shared_b, NT) + dot32(grad_gate_pre, gate_b, NT)) * silu_slope(ema_out)

    pulls, head = ema_call(
        ema_leave, rows, dims, width,
        [(grad_ema, col(rows)), (masks["keep0"], mask_spec), (ar, table), (ai, table), (scales, qs_spec),
         (masks["cont"], cont_spec), (masks["mkr"], mk_spec)],
        [state_shape, edge_shape], [vm(at_rows)], "ema_leave", mac,
    )
    cross = (near[halo + 2 * rows - 1] == last).astype(F32)
    pull_in = from_later(head, 1) + cross * turned(from_later(head, 2), -1.0)
    grad_hidden_ema, grad_a, grad_b, grad_taps, grad_q, grad_skip = ema_call(
        ema_grads, rows, dims, width,
        [(hidden, col(rows)), (grad_ema, col(rows)), (masks["seg"], mask_spec), (masks["kend"], mask_spec),
         (masks["rk0"], whole(rows, LANES)), (masks["rkend"], whole(rows, LANES)), (br, table), (bi, table),
         (taps, col(STEP)), (scales, qs_spec), (masks["cont"], cont_spec), (masks["mkr"], mk_spec),
         (pulls, col3(nstate, 8)), (pull_in, col(2 * dims)), (states, col3(nstate, 8)), (skip, col(1))],
        [(jax.ShapeDtypeStruct((rows, width), F32), col(rows)),
         (jax.ShapeDtypeStruct((2 * dims, STEP, width), F32), col3(2 * dims, STEP)),
         (jax.ShapeDtypeStruct((2 * dims, STEP, width), F32), col3(2 * dims, STEP)),
         (jax.ShapeDtypeStruct((STEP, width), F32), col(STEP)), edge_shape,
         (jax.ShapeDtypeStruct((1, width), F32), col(1))],
        [vm(2 * at_rows), vm(at_rows), vm(nstate)], "ema_grads", 3 * mac,
    )
    four = lambda v: v.reshape(dims, 2, STEP, width)
    ga, gb, gq = four(grad_a), four(grad_b), grad_q.reshape(dims, 2, width)
    _, table_pull = jax.vjp(functools.partial(ema_tables, axis=1), ema_rate, ema_angle, ema_input, ema_output)
    rate_grad, angle_grad, input_grad, output_grad = table_pull(
        (ga[:, 0], ga[:, 1], gb[:, 0], gb[:, 1], grad_taps, gq[:, 0], gq[:, 1])
    )

    grad_hidden = grad_hidden + grad_hidden_ema
    gain_grad = jnp.sum(centred * grad_hidden, axis=0)
    spread_grad = grad_hidden * norm_gain
    sum_a = rho * sums_of(spread_grad)
    sum_b = sums_of(spread_grad * (x - mean_full))
    cube = sum_b * rho * rho * rho
    push = jnp.concatenate([(cube * mean - sum_a) / count, -cube / (2.0 * count)], axis=1)
    backed = dot32(lower, push, TN, precision=HIGHEST)
    first = backed[:1]
    carry = next1 * from_later(first, 1) + next2 * from_later(first, 2)
    backed = backed + tails * carry
    grad_x = spread_grad * rho_full + spread_of(backed[:, :groups]) + 2.0 * x * spread_of(backed[:, groups:])
    in_grad = grad_residual + grad_x

    small = [gain_grad, rate_grad, angle_grad, input_grad, output_grad, grad_skip, grad_query_gain,
             grad_query_bias, grad_key_gain, grad_ffn_gain]
    sizes = [v.size for v in small]
    total = sum(sizes)
    members = parts * replicas
    unit = members * 8 * LANES
    packed = jnp.concatenate([v.reshape(-1) for v in small] + [jnp.zeros((-total % unit,), F32)])
    packed = packed.reshape(members * 8, -1)
    packed = lax.psum_scatter(packed, BOTH, scatter_dimension=0, tiled=True)
    packed = lax.all_gather(packed, BOTH, axis=0, tiled=True).reshape(-1)
    small_sums, at = [], 0
    for n in sizes:
        small_sums.append(packed[at : at + n])
        at += n
    shape = lambda k, like: small_sums[k].reshape(like.shape)

    shared_sum = lax.all_gather(attn_sum[3 * depth :].reshape(piece, latent_width), "tensor", axis=0, tiled=True)
    cut = lambda g, k: g[k * depth : (k + 1) * depth]
    return (
        block_out, in_grad, shape(0, norm_gain), shape(1, ema_rate), shape(2, ema_angle), shape(3, ema_input),
        shape(4, ema_output), shape(5, ema_skip), shared_sum, shape(6, query_gain), shape(7, query_bias),
        shape(8, key_gain), cut(attn_sum, 0), cut(attn_sum, 1), cut(attn_sum, 2).T, shape(9, ffn_gain),
        cut(ffn_sum, 0), cut(ffn_sum, 1), cut(ffn_sum, 2).T,
    )


def solution(mesh):
    rows, dp, copy = P(BOTH, None), P("dp", None), P()
    wide, tall = P("dp", "tensor"), P("tensor", "dp")
    return jax.shard_map(
        on_device,
        mesh=mesh,
        in_specs=(
            rows, dp, copy, copy, copy, copy, copy, copy, dp, copy, copy, copy, wide, wide, tall, copy, wide, wide,
            tall, rows,
        ),
        out_specs=(
            rows, rows, copy, copy, copy, copy, copy, copy, dp, copy, copy, copy, wide, wide, tall, copy, wide, wide,
            tall,
        ),
        check_vma=False,
    )
```

time: 2560 us -> 974 us (0.38)
  waiting for transfers between devices: 1080 us -> 189 us
  local copies, waits for them, and re-layouts: 639 us -> 231 us
  other arithmetic: 400 us -> 79.1 us
  matrix products: 347 us -> 146 us
  blocking collectives: 50.8 us -> 166 us
  Pallas kernels: 0 us -> 94.6 us
  starting transfers between devices: 2.58 us -> 38.7 us
    reduce_scatter x12 -> x4, waiting for transfers between devices: 511 us -> 0.04 us  [the longest x2 0.03 us: summed(): g = lax.psum_scatter(g, 'dp', scatter_dimension=0, tiled=False)]
    all_gather x11 -> x2, waiting for transfers between devices: 413 us -> 0.01 us  [the longest x1 0.01 us: on_device(): lax.all_gather(pack_a, BOTH, axis=0).reshape(replicas, parts, 3, depth, vw)]
    dot_general x51 -> x37, matrix products: 347 us -> 146 us  [dot32(): lax.dot_general(a, b, (dims, ((), ())), precision=precision, preferred_el...]
    reduce_sum x20 -> x6, other arithmetic: 176 us -> 16.2 us  [the longest x1 7.89 us: powers(): return (size * jnp.cos(angle * n), size * jnp.sin(angle * n))]
    psum x2 -> x0, waiting for transfers between devices: 158 us -> none  [the longest x1 135 us: on_device(): lax.psum((gain_grad, rate_full, angle_full, input_full, output_full, skip...]
    all_gather x1 -> x3, blocking collectives: 9.88 us -> 166 us  [the longest x1 77.7 us: on_device(): all_s = lax.all_gather(low(shared_piece), BOTH, axis=0, tiled=True)]
    pad x105 -> x0, local copies, waits for them, and re-layouts: 123 us -> none  [the longest x46 71.7 us: ema_apply(): lax.associative_scan(ema_combine, (carry_real, carry_imag, end_real, end_...]
    unnamed x25 -> x8, waiting for transfers between devices: 1.74 us -> 109 us
  transfers between devices with their start and end apart: 25 -> 23, of which waited for: 20 -> 8; matrix products, arithmetic and copies ran while one was open for 49% -> 34% of each run, Pallas kernels for 0% -> 10%
where the time goes in v1:
time: 974 us; the launch traced here: 967 us
  local copies, waits for them, and re-layouts  231 us (24%)
  waiting for transfers between devices  189 us (19%)
  blocking collectives  166 us (17%)
  matrix products  146 us (15%)
  Pallas kernels  94.6 us (10%)
  other arithmetic  79.1 us (8%)
  starting transfers between devices  38.7 us (4%)
  between operations  22 us (2%)
    dot_general x37, matrix products, dot32(): lax.dot_general(a, b, (dims, ((), ())), precision=precision, preferred_el...  146 us
    unnamed x8, waiting for transfers between devices  109 us
    pallas_call x4, Pallas kernels, ema_call(): pl.pallas_call(functools.partial(body, rows, dims), grid=(width // LANES,...  94.6 us
    reshape x11, local copies, waits for them, and re-layouts, shards(): return low(g).reshape(replicas, depth, parts, -1).transpose(0, 2, 1, 3)  79.3 us
    all_gather x1, blocking collectives, on_device(): all_s = lax.all_gather(low(shared_piece), BOTH, axis=0, tiled=True)  77.7 us
    all_gather x1, blocking collectives, on_device(): packed = lax.all_gather(packed, BOTH, axis=0, tiled=True).reshape(-1)  74.2 us
    transpose x8, local copies, waits for them, and re-layouts, on_device(): flat = lambda w, k: w[:, :, k].transpose(0, 2, 1, 3).reshape(width, -1)  70.2 us
    ppermute x8, waiting for transfers between devices, from_later(): return lax.ppermute(x, 'tensor', [(i + hop, i) for i in range(parts - hop)])  59.1 us
  transfers between devices with their start and end apart: 23, of which 8 were waited for; matrix products, arithmetic and copies ran while one was open for 34% of the time, Pallas kernels for 10%

profile of v1, /device:TPU:0, one launch (start us, length us, event | category | flops | bytes accessed | tf_op | source)
XLA Modules:
  0.0 966.8 jit_solution(14455108799892925848)
XLA Ops:
  18.6 5.5 collective-permute-start
  24.1 4.7 collective-permute-start.1
  34.2 5.7 fusion.61
  50.5 5.4 rev.14
  74.8 12.6 %ema_enter.1 = (f32[128,8,1024]{2,1,0:T(8,128)}, f32[32,1024]{1,0:T(8,128)S(1)}) custom-call(f32[512,1024]{1,0:T(8,128)S(1)} %get-tuple-element.193.h_ref, f32[64,8,128]{2,1,0:T(8,128)S(1)} %broadcast_in_dim.55.kend_ref, f32[256,1024]{1,0:T(8,128)S(1)} %bitcast.336, f32[256,1024]{1,0:T(8,128)S(1)} %bitcast.342, ...), custom_call_target="tpu_custom_call" | custom-call | flops 33554432 | bytes 16777216 | tf_op jit(solution)/shard_map/ema_enter/pallas_call | solution.py:355
  88.9 77.7 %all_gather.23 = bf16[1024,256]{1,0:T(8,128)(2,1)S(1)} all-gather(bf16[32,256]{1,0:T(8,128)(2,1)S(1)} %copy-done.93), channel_id=1, replica_groups=mesh['dp'=8,'tensor'=4] {'dp','tensor'}, dimensions={0}, use_global_device_ids=true | all-gather | bytes 540672 | tf_op jit(solution)/shard_map/all_gather | solution.py:469
  166.6 4.0 collective-permute-start.2
  171.4 4.2 collective-permute-done.2
  178.5 18.6 %ema_read.1 = (f32[512,1024]{1,0:T(8,128)}, bf16[512,1024]{1,0:T(8,128)(2,1)S(1)}, f32[128,8,1024]{2,1,0:T(8,128)}) custom-call(f32[512,1024]{1,0:T(8,128)} %copy-done.2, f32[64,8,128]{2,1,0:T(8,128)S(1)} %broadcast_in_dim.47.seg_ref, f32[64,8,128]{2,1,0:T(8,128)S(1)} %broadcast_in_dim.50.k0_ref, f32[256,1024]{1,0:T(8,128)S(1)} %bitcast.338, ...), custom_call_target="tpu_custom_call" | custom-call | flops 33554432 | bytes 16777216 | tf_op jit(solution)/shard_map/ema_read/pallas_call | solution.py:355
  197.7 4.4 collective-permute-start.5
  211.4 9.2 collective-permute-done.4
  223.4 9.7 %slice_bitcast_fusion.3 = (bf16[8,128,4,512]{3,1,2,0:T(8,128)(2,1)}, bf16[8,128,4,512]{3,1,2,0:T(8,128)(2,1)}, bf16[8,128,4,512]{3,1,2,0:T(8,128)(2,1)}) fusion(bf16[8,4,3,128,512]{4,3,2,1,0:T(8,128)(2,1)} %bitcast.355), kind=kLoop, calls=%fused_computation.57 | loop fusion | bytes 25165824 | tf_op jit(solution)/shard_map/transpose | solution.py:472
  233.1 7.6 copy.172
  240.7 7.6 copy.173
  248.3 7.6 copy.174
  255.9 4.7 fusion.32
  260.6 7.5 collective-permute-done.6
  268.1 11.7 %multiply_convert_fusion.1 = (bf16[1312,2048]{1,0:T(8,128)(2,1)S(1)}, f32[1312,2048]{1,0:T(8,128)}) fusion(bf16[256,8,8,128]{3,2,1,0:T(8,128)(2,1)S(1)} %bitcast.364, bf16[512,1024]{1,0:T(8,128)(2,1)S(1)} %copy-done.55, bf16[512,1024]{1,0:T(8,128)(2,1)} %collective-permute-done.7, bf16[288,1024]{1,0:T(8,128)(2,1)} %collective-permute-done.6), kind=kOutput, calls=%fused_computation.9 | convolution fusion | flops 5524422656 | bytes 23003136 | tf_op jit(solution)/shard_map/dot_general | solution.py:23
  279.9 5.6 multiply_convert_fusion.5
  290.5 10.6 %slice_bitcast_fusion = (bf16[8,128,4,640]{3,1,2,0:T(8,128)(2,1)}, bf16[8,128,4,640]{3,1,2,0:T(8,128)(2,1)}, bf16[8,128,4,640]{3,1,2,0:T(8,128)(2,1)}) fusion(bf16[8,4,3,128,640]{4,3,2,1,0:T(8,128)(2,1)} %bitcast.354), kind=kLoop, calls=%fused_computation.26 | loop fusion | bytes 31457280 | tf_op jit(solution)/shard_map/transpose | solution.py:472
  301.1 9.0 copy.178
  310.1 9.0 copy.176
  319.1 9.0 copy.177
  328.2 5.5 fusion
  333.7 4.7 fusion.10
  338.4 8.4 fusion.13
  346.8 5.6 fusion.4
  352.4 3.8 multiply_reduce_fusion.1
  359.1 7.0 multiply_convert_fusion.3
  373.8 4.4 convolution_convert_fusion.3
  378.2 6.6 multiply_convert_fusion
  387.4 8.2 reshape.519
  395.6 5.4 copy.311
  401.0 10.1 %convolution_convert_fusion.5 = bf16[1024,2048]{1,0:T(8,128)(2,1)} fusion(bf16[1312,2048]{1,0:T(8,128)(2,1)S(1)} %copy-done.129, bf16[512,1024]{1,0:T(8,128)(2,1)S(1)} %copy-done.56, bf16[512,1024]{1,0:T(8,128)(2,1)} %collective-permute-done.7, bf16[288,1024]{1,0:T(8,128)(2,1)} %collective-permute-done.6), kind=kOutput, calls=%fused_computation.71 | convolution fusion | flops 5513084928 | bytes 12255232 | tf_op jit(solution)/shard_map/dot_general | solution.py:23
  411.2 4.4 convolution_convert_fusion.4
  415.6 7.8 reshape.518
  423.3 5.2 copy.312
  428.6 7.8 reshape.517
  436.4 5.5 copy.313
  444.5 11.6 %pad_maximum_fusion.1 = bf16[8,4,400,512]{3,2,1,0:T(8,128)(2,1)} fusion(bf16[8,4,16,512]{3,2,1,0:T(8,128)(2,1)S(1)} %reshape.520, bf16[8,4,128,512]{3,2,1,0:T(8,128)(2,1)} %bitcast.351, bf16[8,4,128,512]{3,2,1,0:T(8,128)(2,1)} %bitcast.352, bf16[8,4,128,512]{3,2,1,0:T(8,128)(2,1)} %bitcast.353), kind=kLoop, calls=%fused_computation.7 | loop fusion | flops 52428800 | bytes 26214400 | tf_op jit(solution)/shard_map/concatenate | solution.py:598
  457.3 5.0 fusion.43
  466.0 8.9 copy.192
  475.0 6.4 convolution_convert_fusion.1
  481.4 10.4 %reshape.523 = bf16[8,128,4,640]{3,2,1,0:T(4,128)(2,1)} reshape(bf16[1024,2560]{1,0:T(8,128)(2,1)} %convolution_convert_fusion.1) | data formatting | bytes 10485760 | tf_op jit(solution)/shard_map/reshape | solution.py:595
  491.8 6.5 copy.309
  498.3 4.7 convolution_convert_fusion.2
  503.0 9.9 %reshape.522 = bf16[8,128,4,640]{3,2,1,0:T(4,128)(2,1)} reshape(bf16[1024,2560]{1,0:T(8,128)(2,1)} %convolution_convert_fusion.2) | data formatting | bytes 10485760 | tf_op jit(solution)/shard_map/reshape | solution.py:595
  516.5 11.4 %pad_maximum_fusion = bf16[8,4,384,640]{3,2,1,0:T(8,128)(2,1)} fusion(bf16[8,4,128,640]{3,2,1,0:T(8,128)(2,1)} %bitcast.348, bf16[8,4,128,640]{3,2,1,0:T(8,128)(2,1)} %bitcast.349, bf16[8,4,128,640]{3,2,1,0:T(8,128)(2,1)S(1)} %bitcast.350), kind=kLoop, calls=%fused_computation.6 | loop fusion | flops 47185920 | bytes 31457280 | tf_op jit(solution)/shard_map/concatenate | solution.py:598
  531.9 7.4 fusion.47
  539.3 5.2 fusion.30
  547.7 12.7 %ema_leave.1 = (f32[128,8,1024]{2,1,0:T(8,128)}, f32[32,1024]{1,0:T(8,128)S(1)}) custom-call(f32[512,1024]{1,0:T(8,128)S(1)} %multiply_multiply_fusion.de_ref, f32[64,8,128]{2,1,0:T(8,128)S(1)} %copy-done.17, f32[256,1024]{1,0:T(8,128)S(1)} %bitcast.339, f32[256,1024]{1,0:T(8,128)S(1)} %bitcast.341, ...), custom_call_target="tpu_custom_call" | custom-call | flops 33554432 | bytes 16777216 | tf_op jit(solution)/shard_map/ema_leave/pallas_call | solution.py:355
  561.6 9.1 fusion.158
  576.7 9.7 %collective-permute-done.13 = f32[32,1024]{1,0:T(8,128)} collective-permute-done((f32[32,1024]{1,0:T(8,128)S(1)}, f32[32,1024]{1,0:T(8,128)}, u32[]{:S(2)}, u32[]{:S(2)}) %collective-permute-start.13) | collective-permute-done | bytes 131104 | tf_op jit(solution)/shard_map/ppermute | solution.py:448
  592.6 26.8 %collective-permute-done.12 = f32[32,1024]{1,0:T(8,128)} collective-permute-done((f32[32,1024]{1,0:T(8,128)S(1)}, f32[32,1024]{1,0:T(8,128)}, u32[]{:S(2)}, u32[]{:S(2)}) %collective-permute-start.12) | collective-permute-done | bytes 131104 | tf_op jit(solution)/shard_map/ppermute | solution.py:448
  620.8 50.7 %ema_grads.1 = (f32[512,1024]{1,0:T(8,128)S(1)}, f32[32,16,1024]{2,1,0:T(8,128)}, f32[32,16,1024]{2,1,0:T(8,128)}, f32[16,1024]{1,0:T(8,128)S(1)}, f32[32,1024]{1,0:T(8,128)S(1)}, /*index=5*/f32[1,1024]{1,0:T(1,128)S(1)}) custom-call(f32[512,1024]{1,0:T(8,128)} %copy-done.2, f32[512,1024]{1,0:T(8,128)} %copy-done.3, f32[64,8,128]{2,1,0:T(8,128)S(1)} %copy-done.15, ...), custom_call_target="tpu_custom_call" | custom-call | flops 100663296 | bytes 16777216 | tf_op jit(solution)/shard_map/ema_grads/pallas_call | solution.py:355
  676.1 5.5 rev.16
  681.6 5.2 rev.17
  688.6 4.7 multiply_reduce_fusion.8
  693.4 7.9 fusion.70
  718.6 6.5 add_convert_fusion
  725.1 19.5 %collective-permute-done.15 = f32[1,32]{0,1:T(8,128)S(1)} collective-permute-done((f32[1,32]{0,1:T(8,128)S(1)}, f32[1,32]{0,1:T(8,128)S(1)}, u32[]{:S(2)}, u32[]{:S(2)}) %collective-permute-start.15) | collective-permute-done | bytes 160 | tf_op jit(solution)/shard_map/ppermute | solution.py:448
  752.3 108.5 %all-reduce.11.cloned.1.call-done = f32[256,384]{1,0:T(8,128)} async-done(((f32[256,384]{1,0:T(8,128)}), f32[256,384]{1,0:T(8,128)}) %all-reduce.11.cloned.1.call-update) | async-done | bytes 393232
  861.5 74.2 %all_gather.26 = f32[256,384]{1,0:T(8,128)S(1)} all-gather(f32[8,384]{1,0:T(8,128)S(1)} %constant_dynamic-slice_fusion), channel_id=1, replica_groups=mesh['dp'=8,'tensor'=4] {'dp','tensor'}, dimensions={0}, use_global_device_ids=true | all-gather | bytes 405504 | tf_op jit(solution)/shard_map/all_gather | solution.py:687
  939.1 14.1 %all_gather.27 = f32[128,256]{1,0:T(8,128)S(1)} all-gather(f32[32,256]{1,0:T(8,128)S(1)} %reshape.521), channel_id=1, replica_groups=mesh['dp'=8,'tensor'=4] {'tensor'}, dimensions={0}, use_global_device_ids=true | all-gather | bytes 163840 | tf_op jit(solution)/shard_map/all_gather | solution.py:694
  (514 shorter events, 150.0 us)
Async XLA Ops:
  7.2 52.1 %copy-start = (f32[128,256]{1,0:T(8,128)S(1)}, f32[128,256]{1,0:T(8,128)}, u32[]{:S(2)}) copy-start(f32[128,256]{1,0:T(8,128)} %param.42) | copy-start | bytes 393220
  7.2 216.1 %all-gather.5.cloned.1.call-start = ((), (), s32[]{:S(2)}) async-start(), calls=%async_computation.8 | async-start | bytes 12976128 | tf_op jit(solution)/shard_map/all_gather | solution.py:470
  11.2 279.3 %all-gather.7.cloned.1.call-start = ((), (), s32[]{:S(2)}) async-start(), calls=%async_computation.9 | async-start | bytes 16220160 | tf_op jit(solution)/shard_map/all_gather | solution.py:471
  12.5 20.8 %copy-start.89 = (f32[2,16,1024]{2,1,0:T(8,128)S(1)}, f32[2,16,1024]{2,1,0:T(8,128)}, u32[]{:S(2)}) copy-start(f32[2,16,1024]{2,1,0:T(8,128)} %param.40) | copy-start | bytes 393220
  12.5 20.9 %copy-start.61 = (f32[16,1024]{1,0:T(8,128)S(1)}, f32[16,1024]{1,0:T(8,128)}, u32[]{:S(2)}) copy-start(f32[16,1024]{1,0:T(8,128)} %param.38) | copy-start | bytes 196612
  12.5 20.9 %copy-start.80 = (f32[16,1024]{1,0:T(8,128)S(1)}, f32[16,1024]{1,0:T(8,128)}, u32[]{:S(2)}) copy-start(f32[16,1024]{1,0:T(8,128)} %param.37) | copy-start | bytes 196612
  12.5 20.8 %copy-start.86 = (f32[16,1024]{1,0:T(8,128)S(1)}, f32[16,1024]{1,0:T(8,128)}, u32[]{:S(2)}) copy-start(f32[16,1024]{1,0:T(8,128)} %param.39) | copy-start | bytes 196612
  13.4 694.4 %reduce-scatter.5.cloned.1.call-start = ((), (), s32[]{:S(2)}) async-start(), calls=%async_computation.4 | async-start | bytes 14745600 | tf_op jit(solution)/shard_map/reduce_scatter | solution.py:599
  14.2 56.7 %copy-start.84 = (s32[1024]{0:T(1024)}, s32[1024]{0:T(1024)S(1)}, u32[]{:S(2)}) copy-start(s32[1024]{0:T(1024)S(1)} %add_select_fusion) | copy-start | bytes 12292
  15.5 205.1 %copy-start.98 = (s32[512]{0:T(512)}, s32[512]{0:T(512)S(1)}, u32[]{:S(2)}) copy-start(s32[512]{0:T(512)S(1)} %get-tuple-element.188) | copy-start | bytes 6148
  18.6 49.1 %collective-permute-start = (f32[1,32]{0,1:T(8,128)}, f32[1,32]{0,1:T(8,128)}, u32[]{:S(2)}, u32[]{:S(2)}) collective-permute-start(f32[1,32]{0,1:T(8,128)} %slice.405), channel_id=1, source_target_pairs={{0,1},{1,2},{2,3},{4,5},{5,6},{6,7},{8,9},{9,10},{10,11},{12,13},{... | collective-permute-start | bytes 392 | tf_op jit(solution)/shard_map/ppermute | solution.py:445
  24.1 43.6 %collective-permute-start.1 = (f32[1,32]{0,1:T(8,128)}, f32[1,32]{0,1:T(8,128)}, u32[]{:S(2)}, u32[]{:S(2)}) collective-permute-start(f32[1,32]{0,1:T(8,128)} %slice.405), channel_id=1, source_target_pairs={{0,2},{1,3},{4,6},{5,7},{8,10},{9,11},{12,14},{13,15},{16,18},{17,... | collective-permute-start | bytes 392 | tf_op jit(solution)/shard_map/ppermute | solution.py:445
  41.6 134.4 %copy-start.22 = (f32[16,1024]{1,0:T(8,128)}, f32[16,1024]{1,0:T(8,128)S(1)}, u32[]{:S(2)}) copy-start(f32[16,1024]{1,0:T(8,128)S(1)} %get-tuple-element.206.kd_ref) | copy-start | bytes 196612
  74.5 92.1 %copy-start.2 = (f32[512,1024]{1,0:T(8,128)}, f32[512,1024]{1,0:T(8,128)S(1)}, u32[]{:S(2)}) copy-start(f32[512,1024]{1,0:T(8,128)S(1)} %get-tuple-element.193.h_ref) | copy-start | bytes 6291460
  74.5 133.9 %copy-start.54 = (bf16[512,1024]{1,0:T(8,128)(2,1)}, bf16[512,1024]{1,0:T(8,128)(2,1)S(1)}, u32[]{:S(2)}) copy-start(bf16[512,1024]{1,0:T(8,128)(2,1)S(1)} %get-tuple-element.192) | copy-start | bytes 3145732
  74.6 472.6 %copy-start.24 = (f32[4,8,128]{2,1,0:T(8,128)}, f32[4,8,128]{2,1,0:T(8,128)S(1)}, u32[]{:S(2)}) copy-start(f32[4,8,128]{2,1,0:T(8,128)S(1)} %broadcast_in_dim.51.cont_ref) | copy-start | bytes 49156
  74.8 91.8 %copy-start.12 = (f32[64,8,128]{2,1,0:T(8,128)}, f32[64,8,128]{2,1,0:T(8,128)S(1)}, u32[]{:S(2)}) copy-start(f32[64,8,128]{2,1,0:T(8,128)S(1)} %broadcast_in_dim.55.kend_ref) | copy-start | bytes 786436
  87.4 88.6 %copy-start.26 = (f32[1024]{0:T(1024)S(1)}, f32[1024]{0:T(1024)}, u32[]{:S(2)}) copy-start(f32[1024]{0:T(1024)} %param.41) | copy-start | bytes 12292
  87.4 83.2 %collective-permute-start.3 = (f32[32,1024]{1,0:T(8,128)S(1)}, f32[32,1024]{1,0:T(8,128)S(1)}, u32[]{:S(2)}, u32[]{:S(2)}) collective-permute-start(f32[32,1024]{1,0:T(8,128)S(1)} %get-tuple-element.98), channel_id=1, source_target_pairs={{0,2},{1,3},{4,6},{5,7},{8,10},{9,11},{12,14},{13,15},{16,18},{17,... | collective-permute-start | bytes 393224 | tf_op jit(solution)/shard_map/ppermute | solution.py:445
  166.6 30.6 %copy-start.48 = (bf16[1024,256]{1,0:T(8,128)(2,1)}, bf16[1024,256]{1,0:T(8,128)(2,1)S(1)}, u32[]{:S(2)}) copy-start(bf16[1024,256]{1,0:T(8,128)(2,1)S(1)} %all_gather.23) | copy-start | bytes 1572868
  166.6 9.0 collective-permute-start.2
  171.1 26.0 %copy-start.77 = (f32[16,1024]{1,0:T(8,128)}, f32[16,1024]{1,0:T(8,128)S(1)}, u32[]{:S(2)}) copy-start(f32[16,1024]{1,0:T(8,128)S(1)} %get-tuple-element.190) | copy-start | bytes 196612
  175.8 21.3 %copy-start.14 = (f32[64,8,128]{2,1,0:T(8,128)}, f32[64,8,128]{2,1,0:T(8,128)S(1)}, u32[]{:S(2)}) copy-start(f32[64,8,128]{2,1,0:T(8,128)S(1)} %broadcast_in_dim.47.seg_ref) | copy-start | bytes 786436
  175.9 21.2 %copy-start.16 = (f32[64,8,128]{2,1,0:T(8,128)}, f32[64,8,128]{2,1,0:T(8,128)S(1)}, u32[]{:S(2)}) copy-start(f32[64,8,128]{2,1,0:T(8,128)S(1)} %broadcast_in_dim.50.k0_ref) | copy-start | bytes 786436
  178.5 18.7 %copy-start.113 = (f32[256]{0:T(256)S(1)}, f32[256]{0:T(256)}, u32[]{:S(2)}) copy-start(f32[256]{0:T(256)} %param.45) | copy-start | bytes 3076
  178.5 27.0 %copy-start.110 = (f32[256]{0:T(256)S(1)}, f32[256]{0:T(256)}, u32[]{:S(2)}) copy-start(f32[256]{0:T(256)} %param.43) | copy-start | bytes 3076
  178.5 27.5 %copy-start.95 = (s32[3648]{0:T(1024)S(1)}, s32[3648]{0:T(1024)}, u32[]{:S(2)}) copy-start(s32[3648]{0:T(1024)} %copy-done.94) | copy-start | bytes 43780
  197.1 58.8 %copy-start.20 = (bf16[512,1024]{1,0:T(8,128)(2,1)}, bf16[512,1024]{1,0:T(8,128)(2,1)S(1)}, u32[]{:S(2)}) copy-start(bf16[512,1024]{1,0:T(8,128)(2,1)S(1)} %get-tuple-element.99) | copy-start | bytes 3145732
  197.1 23.5 %copy-start.112 = (f32[256]{0:T(256)S(1)}, f32[256]{0:T(256)}, u32[]{:S(2)}) copy-start(f32[256]{0:T(256)} %param.44) | copy-start | bytes 3076
  197.6 23.8 %copy-start.57 = (f32[512,256]{1,0:T(8,128)}, f32[512,256]{1,0:T(8,128)S(1)}, u32[]{:S(2)}) copy-start(f32[512,256]{1,0:T(8,128)S(1)} %get-tuple-element.285) | copy-start | bytes 1572868
  197.6 23.8 %copy-start.70 = (bf16[512,256]{1,0:T(8,128)(2,1)}, bf16[512,256]{1,0:T(8,128)(2,1)S(1)}, u32[]{:S(2)}) copy-start(bf16[512,256]{1,0:T(8,128)(2,1)S(1)} %get-tuple-element.284) | copy-start | bytes 786436
  197.7 23.0 %collective-permute-start.5 = (bf16[512,256]{1,0:T(8,128)(2,1)S(1)}, bf16[512,256]{1,0:T(8,128)(2,1)S(1)}, u32[]{:S(2)}, u32[]{:S(2)}) collective-permute-start(bf16[512,256]{1,0:T(8,128)(2,1)S(1)} %get-tuple-element.284), channel_id=1, source_target_pairs={{0,1},{1,2},{2,3},{4,5},{5,6},{6,7},{8,9},{9,10},{10,11},{12,13},{... | collective-permute-start | bytes 786440 | tf_op jit(solution)/shard_map/ppermute | solution.py:445
  202.1 18.5 %collective-permute-start.4 = (bf16[288,256]{1,0:T(8,128)(2,1)S(1)}, bf16[288,256]{1,0:T(8,128)(2,1)S(1)}, u32[]{:S(2)}, u32[]{:S(2)}) collective-permute-start(bf16[288,256]{1,0:T(8,128)(2,1)S(1)} %slice.418), channel_id=1, source_target_pairs={{0,2},{1,3},{4,6},{5,7},{8,10},{9,11},{12,14},{13,15},{16,18},{17,... | collective-permute-start | bytes 442376 | tf_op jit(solution)/shard_map/ppermute | solution.py:445
  206.1 62.0 %collective-permute-start.7 = (bf16[512,1024]{1,0:T(8,128)(2,1)S(1)}, bf16[512,1024]{1,0:T(8,128)(2,1)}, u32[]{:S(2)}, u32[]{:S(2)}) collective-permute-start(bf16[512,1024]{1,0:T(8,128)(2,1)S(1)} %get-tuple-element.192), channel_id=1, source_target_pairs={{0,1},{1,2},{2,3},{4,5},{5,6},{6,7},{8,9},{9,10},{10,11},{12,13},{... | collective-permute-start | bytes 3145736 | tf_op jit(solution)/shard_map/ppermute | solution.py:445
  209.3 58.9 %collective-permute-start.6 = (bf16[288,1024]{1,0:T(8,128)(2,1)}, bf16[288,1024]{1,0:T(8,128)(2,1)}, u32[]{:S(2)}, u32[]{:S(2)}) collective-permute-start(bf16[288,1024]{1,0:T(8,128)(2,1)} %slice.419), channel_id=1, source_target_pairs={{0,2},{1,3},{4,6},{5,7},{8,10},{9,11},{12,14},{13,15},{16,18},{17,... | collective-permute-start | bytes 1769480 | tf_op jit(solution)/shard_map/ppermute | solution.py:445
  260.6 19.2 %copy-start.126 = (f32[512,2048]{1,0:T(8,128)}, f32[512,2048]{1,0:T(8,128)S(1)}, u32[]{:S(2)}) copy-start(f32[512,2048]{1,0:T(8,128)S(1)} %fusion.32) | copy-start | bytes 12582916
  356.8 17.0 %copy-start.40 = (f32[512,1024]{1,0:T(8,128)}, f32[512,1024]{1,0:T(8,128)S(1)}, u32[]{:S(2)}) copy-start(f32[512,1024]{1,0:T(8,128)S(1)} %multiply_add_fusion) | copy-start | bytes 6291460
  384.8 57.2 %collective-permute-start.10 = (bf16[512,256]{1,0:T(8,128)(2,1)}, bf16[512,256]{1,0:T(8,128)(2,1)S(1)}, u32[]{:S(2)}, u32[]{:S(2)}) collective-permute-start(bf16[512,256]{1,0:T(8,128)(2,1)} %slice.430), channel_id=1, source_target_pairs={{1,0},{2,1},{3,2},{5,4},{6,5},{7,6},{9,8},{10,9},{11,10},{13,12},{... | collective-permute-start | bytes 786440 | tf_op jit(solution)/shard_map/ppermute | solution.py:448
  386.1 57.0 %collective-permute-start.11 = (bf16[288,256]{1,0:T(8,128)(2,1)S(1)}, bf16[288,256]{1,0:T(8,128)(2,1)S(1)}, u32[]{:S(2)}, u32[]{:S(2)}) collective-permute-start(bf16[288,256]{1,0:T(8,128)(2,1)S(1)} %slice.432), channel_id=1, source_target_pairs={{2,0},{3,1},{6,4},{7,5},{10,8},{11,9},{14,12},{15,13},{18,16},{19,... | collective-permute-start | bytes 442376 | tf_op jit(solution)/shard_map/ppermute | solution.py:448
  456.1 254.8 %reduce-scatter.9.cloned.1.call-start = ((), (), s32[]{:S(2)}) async-start(), calls=%async_computation.6 | async-start | bytes 17694720 | tf_op jit(solution)/shard_map/reduce_scatter | solution.py:599
  528.0 332.9 %all-reduce.11.cloned.1.call-start = ((), (), s32[]{:S(2)}) async-start(), calls=%async_computation.10 | async-start | bytes 786432
  547.1 23.7 %copy-start.3 = (f32[512,1024]{1,0:T(8,128)}, f32[512,1024]{1,0:T(8,128)S(1)}, u32[]{:S(2)}) copy-start(f32[512,1024]{1,0:T(8,128)S(1)} %multiply_multiply_fusion.de_ref) | copy-start | bytes 6291460
  560.3 26.1 %collective-permute-start.13 = (f32[32,1024]{1,0:T(8,128)S(1)}, f32[32,1024]{1,0:T(8,128)}, u32[]{:S(2)}, u32[]{:S(2)}) collective-permute-start(f32[32,1024]{1,0:T(8,128)S(1)} %get-tuple-element.102), channel_id=1, source_target_pairs={{2,0},{3,1},{6,4},{7,5},{10,8},{11,9},{14,12},{15,13},{18,16},{19,... | collective-permute-start | bytes 393224 | tf_op jit(solution)/shard_map/ppermute | solution.py:448
  570.8 18.5 %copy-start.78 = (f32[16,1024]{1,0:T(8,128)S(1)}, f32[16,1024]{1,0:T(8,128)}, u32[]{:S(2)}) copy-start(f32[16,1024]{1,0:T(8,128)} %copy-done.77) | copy-start | bytes 196612
  570.8 49.7 %copy-start.104 = (f32[512]{0:T(512)S(1)}, f32[512]{0:T(512)}, u32[]{:S(2)}) copy-start(f32[512]{0:T(512)} %get-tuple-element.273) | copy-start | bytes 6148
  570.8 49.9 %copy-start.103 = (f32[512]{0:T(512)S(1)}, f32[512]{0:T(512)}, u32[]{:S(2)}) copy-start(f32[512]{0:T(512)} %get-tuple-element.272) | copy-start | bytes 6148
  570.8 50.0 %copy-start.5 = (f32[16,16,1024]{2,1,0:T(8,128)S(1)}, f32[16,16,1024]{2,1,0:T(8,128)}, u32[]{:S(2)}) copy-start(f32[16,16,1024]{2,1,0:T(8,128)} %copy.166) | copy-start | bytes 3145732
  570.8 50.0 %copy-start.11 = (f32[16,16,1024]{2,1,0:T(8,128)S(1)}, f32[16,16,1024]{2,1,0:T(8,128)}, u32[]{:S(2)}) copy-start(f32[16,16,1024]{2,1,0:T(8,128)} %copy-done.10) | copy-start | bytes 3145732
  570.8 50.0 %copy-start.13 = (f32[64,8,128]{2,1,0:T(8,128)S(1)}, f32[64,8,128]{2,1,0:T(8,128)}, u32[]{:S(2)}) copy-start(f32[64,8,128]{2,1,0:T(8,128)} %copy-done.12) | copy-start | bytes 786436
  570.8 50.0 %copy-start.15 = (f32[64,8,128]{2,1,0:T(8,128)S(1)}, f32[64,8,128]{2,1,0:T(8,128)}, u32[]{:S(2)}) copy-start(f32[64,8,128]{2,1,0:T(8,128)} %copy-done.14) | copy-start | bytes 786436
  570.8 50.0 %copy-start.23 = (f32[16,1024]{1,0:T(8,128)S(1)}, f32[16,1024]{1,0:T(8,128)}, u32[]{:S(2)}) copy-start(f32[16,1024]{1,0:T(8,128)} %copy-done.22) | copy-start | bytes 196612
  570.8 50.0 %copy-start.25 = (f32[4,8,128]{2,1,0:T(8,128)S(1)}, f32[4,8,128]{2,1,0:T(8,128)}, u32[]{:S(2)}) copy-start(f32[4,8,128]{2,1,0:T(8,128)} %copy-done.24) | copy-start | bytes 49156
  570.8 50.0 %copy-start.27 = (f32[1024]{0:T(1024)S(1)}, f32[1024]{0:T(1024)}, u32[]{:S(2)}) copy-start(f32[1024]{0:T(1024)} %param.41) | copy-start | bytes 12292
  572.8 128.8 %collective-permute-start.8 = (bf16[512,1024]{1,0:T(8,128)(2,1)}, bf16[512,1024]{1,0:T(8,128)(2,1)}, u32[]{:S(2)}, u32[]{:S(2)}) collective-permute-start(bf16[512,1024]{1,0:T(8,128)(2,1)} %slice.426), channel_id=1, source_target_pairs={{1,0},{2,1},{3,2},{5,4},{6,5},{7,6},{9,8},{10,9},{11,10},{13,12},{... | collective-permute-start | bytes 3145736 | tf_op jit(solution)/shard_map/ppermute | solution.py:448
  574.1 129.8 %collective-permute-start.9 = (bf16[288,1024]{1,0:T(8,128)(2,1)}, bf16[288,1024]{1,0:T(8,128)(2,1)}, u32[]{:S(2)}, u32[]{:S(2)}) collective-permute-start(bf16[288,1024]{1,0:T(8,128)(2,1)} %slice.428), channel_id=1, source_target_pairs={{2,0},{3,1},{6,4},{7,5},{10,8},{11,9},{14,12},{15,13},{18,16},{19,... | collective-permute-start | bytes 1769480 | tf_op jit(solution)/shard_map/ppermute | solution.py:448
  575.4 44.0 %collective-permute-start.12 = (f32[32,1024]{1,0:T(8,128)S(1)}, f32[32,1024]{1,0:T(8,128)}, u32[]{:S(2)}, u32[]{:S(2)}) collective-permute-start(f32[32,1024]{1,0:T(8,128)S(1)} %get-tuple-element.102), channel_id=1, source_target_pairs={{1,0},{2,1},{3,2},{5,4},{6,5},{7,6},{9,8},{10,9},{11,10},{13,12},{... | collective-permute-start | bytes 393224 | tf_op jit(solution)/shard_map/ppermute | solution.py:448
  707.7 230.7 %reduce-scatter.7.cloned.1.call-start = ((), (), s32[]{:S(2)}) async-start(), calls=%async_computation.5 | async-start | bytes 2048000 | tf_op jit(solution)/shard_map/reduce_scatter | solution.py:600
  708.3 247.8 %reduce-scatter.11.cloned.1.call-start = ((), (), s32[]{:S(2)}) async-start(), calls=%async_computation.7 | async-start | bytes 2457600 | tf_op jit(solution)/shard_map/reduce_scatter | solution.py:600
  715.7 32.1 %copy-start.102 = (f32[512]{0:T(512)S(1)}, f32[512]{0:T(512)}, u32[]{:S(2)}) copy-start(f32[512]{0:T(512)} %get-tuple-element.187) | copy-start | bytes 6148
  715.7 28.9 %collective-permute-start.15 = (f32[1,32]{0,1:T(8,128)S(1)}, f32[1,32]{0,1:T(8,128)S(1)}, u32[]{:S(2)}, u32[]{:S(2)}) collective-permute-start(f32[1,32]{0,1:T(8,128)S(1)} %slice.435), channel_id=1, source_target_pairs={{2,0},{3,1},{6,4},{7,5},{10,8},{11,9},{14,12},{15,13},{18,16},{19,... | collective-permute-start | bytes 392 | tf_op jit(solution)/shard_map/ppermute | solution.py:448
  717.0 30.7 %collective-permute-start.14 = (f32[1,32]{0,1:T(8,128)S(1)}, f32[1,32]{0,1:T(8,128)S(1)}, u32[]{:S(2)}, u32[]{:S(2)}) collective-permute-start(f32[1,32]{0,1:T(8,128)S(1)} %slice.435), channel_id=1, source_target_pairs={{1,0},{2,1},{3,2},{5,4},{6,5},{7,6},{9,8},{10,9},{11,10},{13,12},{... | collective-permute-start | bytes 392 | tf_op jit(solution)/shard_map/ppermute | solution.py:448
  718.6 30.5 %copy-start.36 = (bf16[512,1024]{1,0:T(8,128)(2,1)S(1)}, bf16[512,1024]{1,0:T(8,128)(2,1)}, u32[]{:S(2)}) copy-start(bf16[512,1024]{1,0:T(8,128)(2,1)} %param.34) | copy-start | bytes 3145732
  718.6 30.5 %copy-start.41 = (f32[512,1024]{1,0:T(8,128)S(1)}, f32[512,1024]{1,0:T(8,128)}, u32[]{:S(2)}) copy-start(f32[512,1024]{1,0:T(8,128)} %copy-done.40) | copy-start | bytes 6291460
  725.1 24.0 %copy-start.31 = (f32[512,1024]{1,0:T(8,128)S(1)}, f32[512,1024]{1,0:T(8,128)}, u32[]{:S(2)}) copy-start(f32[512,1024]{1,0:T(8,128)} %copy-done.30) | copy-start | bytes 6291460
  (97 other events, 560.2 us)
Sparse Core Ops, SparseCore 0:
  11.4 100.3 all-gather.4
  114.6 135.6 all-gather.6
  456.2 113.2 reduce-scatter.4
  572.9 109.1 reduce-scatter.8
  707.8 152.9 all-reduce.10
  863.1 38.4 reduce-scatter.6
  903.9 44.1 reduce-scatter.10

commit v2 on v1

v2 whole, which is shorter than its diff:
```python
import functools
import math

import jax
import jax.numpy as jnp
from jax import lax
from jax.experimental import pallas as pl
from jax.experimental.pallas import tpu as pltpu
from jax.experimental.layout import Layout, with_layout_constraint
from jax.sharding import PartitionSpec as P

TN_GROUPS = 16
EPSILON = 1e-05
REACH = 800
STEP = 16
LANES = 128
F32 = jnp.float32
BF16 = jnp.bfloat16
HIGHEST = lax.Precision.HIGHEST
BOTH = ("dp", "tensor")


def dot32(a, b, dims=((1,), (0,)), precision=None):
    return lax.dot_general(a, b, (dims, ((), ())), precision=precision, preferred_element_type=F32)


NT = ((1,), (1,))
TN = ((0,), (0,))


def silu_of(v):
    return v * jax.nn.sigmoid(v)


def silu_slope(v):
    sg = jax.nn.sigmoid(v)
    return sg * (1.0 + v * (1.0 - sg))


def broadcast_row(ref, row):
    return ref[pl.ds(row, 8, stride=0), :]


def rotate(x, shift):
    return pltpu.roll(x, shift % 8, axis=0)


def times(ar, ai, br, bi):
    return ar * br - ai * bi, ar * bi + ai * br


def power_list(dims, q_ref):
    qr, qi = q_ref[:dims], q_ref[dims:]
    out = [(jnp.ones_like(qr), jnp.zeros_like(qr))]
    for n in range(STEP):
        out.append(times(*out[-1], qr, qi))
    return out


def fill_scales(groups, dims, pw, qs):
    step = pw[STEP]
    qs[:dims], qs[dims : 2 * dims] = step
    turn = step
    for _ in range(groups - 1):
        turn = times(*turn, *step)
    for k in range(3):
        base = 2 * dims * (k + 1)
        qs[base : base + dims], qs[base + dims : base + 2 * dims] = turn
        turn = times(*turn, *turn)
    return turn


def fill_read(dims, pw, e_ref, ta):
    e0, e1 = e_ref[:dims], e_ref[dims:]
    for i in range(STEP):
        ta[0, i * dims : (i + 1) * dims], ta[1, i * dims : (i + 1) * dims] = times(e0, e1, *pw[i + 1])


def fill_feed(dims, pw, f_ref, tb):
    f = f_ref[...]
    for i in range(STEP):
        r, m = pw[STEP - 1 - i]
        tb[0, i * dims : (i + 1) * dims], tb[1, i * dims : (i + 1) * dims] = f * r, f * m


def tap_list(dims, pw, e_ref, f_ref):
    e0, e1, f = e_ref[:dims], e_ref[dims:], f_ref[...]
    out = []
    for d in range(STEP):
        row = jnp.sum(f * (e0 * pw[d][0] - e1 * pw[d][1]), axis=0, keepdims=True)
        out.append(jnp.broadcast_to(row, (8, LANES)))
    return out


def chunk_sums(groups, dims, table, source, out, sign):
    def pair(jp, carry):
        acc = [None] * groups
        for i in range(STEP):
            c = [broadcast_row(table.at[p], i * dims + jp * 2 + k) for k in range(2) for p in range(2)]
            for g in range(groups):
                h = source[g * STEP + i]
                terms = [v * h for v in c]
                acc[g] = terms if i == 0 else [u + v for u, v in zip(acc[g], terms)]
        for g in range(groups):
            for k in range(2):
                at = (g * dims + jp * 2 + k) * 2
                out[at] = acc[g][2 * k]
                out[at + 1] = acc[g][2 * k + 1] if sign > 0 else -acc[g][2 * k + 1]
        return carry

    lax.fori_loop(0, dims // 2, pair, 0)


def position_sums(groups, dims, table, states, mask, out, base, sign):
    block = 4

    def some(iq, carry):
        acc = [[None] * block for _ in range(groups)]
        for j in range(dims):
            here = [(states[(g * dims + j) * 2], states[(g * dims + j) * 2 + 1]) for g in range(groups)]
            for i in range(block):
                cr = broadcast_row(table.at[0], (iq * block + i) * dims + j)
                ci = broadcast_row(table.at[1], (iq * block + i) * dims + j)
                for g in range(groups):
                    u, v = cr * here[g][0], ci * here[g][1]
                    term = u - v if sign < 0 else u + v
                    acc[g][i] = term if j == 0 else acc[g][i] + term
        for g in range(groups):
            for i in range(block):
                at = g * STEP + iq * block + i
                out[base + at] = acc[g][i] * mask[at]
        return carry

    lax.fori_loop(0, STEP // block, some, 0)


def ema_enter(rows, dims, h_ref, kend_ref, q_ref, f_ref, cont_ref, mk_ref, l_ref, end_ref, turn_ref, hm, tb, qs):
    groups = rows // (8 * STEP)
    pw = power_list(dims, q_ref)
    turn_ref[:dims], turn_ref[dims:] = fill_scales(groups, dims, pw, qs)
    fill_feed(dims, pw, f_ref, tb)
    for at in range(groups * STEP):
        hm[at] = h_ref[pl.ds(at, 8, stride=groups * STEP), :] * kend_ref[at]
    chunk_sums(groups, dims, tb, hm, l_ref, 1)

    def one(j, carry):
        zero = jnp.zeros((8, LANES), F32)
        _, ends = scan_states(groups, dims, j, l_ref, qs, cont_ref, mk_ref, zero, zero)
        end_ref[pl.ds(j, 1), :] = ends[0][7:8]
        end_ref[pl.ds(dims + j, 1), :] = ends[1][7:8]
        return carry

    lax.fori_loop(0, dims, one, 0)


def scan_states(groups, dims, j, l_ref, qs, cont_ref, mk_ref, inr, ini):
    qr, qi = broadcast_row(qs, j), broadcast_row(qs, dims + j)
    part = [(l_ref[(g * dims + j) * 2], l_ref[(g * dims + j) * 2 + 1]) for g in range(groups)]

    def through(sr, si):
        starts = []
        for g in range(groups):
            starts.append((sr, si))
            keep = cont_ref[g]
            tr, ti = times(qr, qi, sr, si)
            sr, si = keep * tr + part[g][0], keep * ti + part[g][1]
        return starts, sr, si

    _, er, ei = through(inr, ini)
    for k in range(3):
        base = 2 * dims * (k + 1)
        wr, wi = broadcast_row(qs, base + j), broadcast_row(qs, base + dims + j)
        pr, pi = times(wr, wi, rotate(er, 1 << k), rotate(ei, 1 << k))
        keep = mk_ref[k]
        er, ei = er + keep * pr, ei + keep * pi
    first = lax.broadcasted_iota(jnp.int32, (8, LANES), 0) == 0
    starts, _, _ = through(jnp.where(first, inr, rotate(er, 1)), jnp.where(first, ini, rotate(ei, 1)))
    return starts, (er, ei)


def ema_read(
    rows, dims, h_ref, seg_ref, k0_ref, q_ref, f_ref, e_ref, cont_ref, mk_ref, l_ref, in_ref, skip_ref,
    out_ref, m_ref, s_ref, hs, ta, qs
):
    groups = rows // (8 * STEP)
    first = lax.broadcasted_iota(jnp.int32, (8, LANES), 0) == 0
    pw = power_list(dims, q_ref)
    fill_scales(groups, dims, pw, qs)
    fill_read(dims, pw, e_ref, ta)
    taps = tap_list(dims, pw, e_ref, f_ref)

    def one(j, carry):
        inr = jnp.where(first, broadcast_row(in_ref, j), 0.0)
        ini = jnp.where(first, broadcast_row(in_ref, dims + j), 0.0)
        starts, _ = scan_states(groups, dims, j, l_ref, qs, cont_ref, mk_ref, inr, ini)
        for g in range(groups):
            s_ref[(g * dims + j) * 2] = starts[g][0]
            s_ref[(g * dims + j) * 2 + 1] = starts[g][1]
        return carry

    lax.fori_loop(0, dims, one, 0)
    for at in range(groups * STEP):
        hs[at] = h_ref[pl.ds(at, 8, stride=groups * STEP), :]
    position_sums(groups, dims, ta, s_ref, k0_ref, hs, groups * STEP, -1)
    tap0 = taps[0] + jnp.broadcast_to(skip_ref[...], (8, LANES))
    for g in range(groups):
        for i in range(STEP):
            at = g * STEP + i
            seg = seg_ref[at]
            out = hs[groups * STEP + at] + tap0 * hs[at]
            for s in range(i):
                src = g * STEP + s
                out = out + taps[i - s] * jnp.where(seg_ref[src] == seg, hs[src], 0.0)
            out_ref[pl.ds(at, 8, stride=groups * STEP), :] = out
    m_ref[...] = silu_of(out_ref[...]).astype(m_ref.dtype)


def reverse_states(groups, dims, j, g_ref, qs, cont_ref, mkr_ref, inr, ini):
    qr, qi = broadcast_row(qs, j), broadcast_row(qs, dims + j)
    part = [(g_ref[(g * dims + j) * 2], g_ref[(g * dims + j) * 2 + 1]) for g in range(groups)]

    def through(yr, yi):
        ends = [None] * groups
        for g in reversed(range(groups)):
            ends[g] = (yr, yi)
            keep = cont_ref[g]
            tr, ti = qr * yr + qi * yi, qr * yi - qi * yr
            yr, yi = keep * tr + part[g][0], keep * ti + part[g][1]
        return ends, yr, yi

    _, fr, fi = through(inr, ini)
    for k in range(3):
        base = 2 * dims * (k + 1)
        wr, wi = broadcast_row(qs, base + j), broadcast_row(qs, base + dims + j)
        pr, pi = rotate(fr, -(1 << k)), rotate(fi, -(1 << k))
        keep = mkr_ref[k]
        fr, fi = fr + keep * (wr * pr + wi * pi), fi + keep * (wr * pi - wi * pr)
    last = lax.broadcasted_iota(jnp.int32, (8, LANES), 0) == 7
    ends, _, _ = through(jnp.where(last, inr, rotate(fr, -1)), jnp.where(last, ini, rotate(fi, -1)))
    return ends, (fr, fi)


def ema_leave(rows, dims, de_ref, k0_ref, q_ref, e_ref, cont_ref, mkr_ref, g_ref, head_ref, dm, ta, qs):
    groups = rows // (8 * STEP)
    pw = power_list(dims, q_ref)
    fill_scales(groups, dims, pw, qs)
    fill_read(dims, pw, e_ref, ta)
    for at in range(groups * STEP):
        dm[at] = de_ref[pl.ds(at, 8, stride=groups * STEP), :] * k0_ref[at]
    chunk_sums(groups, dims, ta, dm, g_ref, -1)

    def one(j, carry):
        zero = jnp.zeros((8, LANES), F32)
        _, heads = reverse_states(groups, dims, j, g_ref, qs, cont_ref, mkr_ref, zero, zero)
        head_ref[pl.ds(j, 1), :] = heads[0][0:1]
        head_ref[pl.ds(dims + j, 1), :] = heads[1][0:1]
        return carry

    lax.fori_loop(0, dims, one, 0)


def ema_grads(
    rows, dims, h_ref, de_ref, seg_ref, kend_ref, rk0_ref, rkend_ref, q_ref, f_ref, e_ref, root_ref, feed_ref, cont_ref,
    mkr_ref, g_ref, in_ref, s_ref, skip_ref, dh_ref, ge_ref, gf_ref, gr_ref, ga_ref, gs_ref, hs, ds, la, tb, qs, pf, red, hn, dn
):
    groups = rows // (8 * STEP)
    last = lax.broadcasted_iota(jnp.int32, (8, LANES), 0) == 7
    pw = power_list(dims, q_ref)
    fill_scales(groups, dims, pw, qs)
    fill_feed(dims, pw, f_ref, tb)
    taps = tap_list(dims, pw, e_ref, f_ref)
    for i in range(STEP):
        at = slice(i * dims, (i + 1) * dims)
        pf[0, at], pf[1, at] = pw[i + 1]
        pf[2, at], pf[3, at] = pw[STEP - 1 - i]

    def one(j, carry):
        inr = jnp.where(last, broadcast_row(in_ref, j), 0.0)
        ini = jnp.where(last, broadcast_row(in_ref, dims + j), 0.0)
        ends, _ = reverse_states(groups, dims, j, g_ref, qs, cont_ref, mkr_ref, inr, ini)
        qr = jnp.zeros((8, LANES), F32)
        qi = jnp.zeros((8, LANES), F32)
        for g in range(groups):
            yr, yi = ends[g]
            la[(g * dims + j) * 2] = yr
            la[(g * dims + j) * 2 + 1] = yi
            keep = cont_ref[g]
            sr, si = s_ref[(g * dims + j) * 2], s_ref[(g * dims + j) * 2 + 1]
            qr = qr + keep * (yr * sr + yi * si)
            qi = qi + keep * (yi * sr - yr * si)
        red[0, pl.ds(j, 1), :] = jnp.sum(qr, axis=0, keepdims=True)
        red[1, pl.ds(j, 1), :] = jnp.sum(qi, axis=0, keepdims=True)
        return carry

    lax.fori_loop(0, dims, one, 0)
    total = jnp.zeros((8, LANES), F32)
    for at in range(groups * STEP):
        h = h_ref[pl.ds(at, 8, stride=groups * STEP), :]
        d = de_ref[pl.ds(at, 8, stride=groups * STEP), :]
        hs[at] = h
        ds[at] = d
        total = total + h * d
    gs_ref[...] = jnp.sum(total, axis=0, keepdims=True)
    position_sums(groups, dims, tb, la, kend_ref, hs, groups * STEP, 1)
    tap0 = taps[0] + jnp.broadcast_to(skip_ref[...], (8, LANES))
    kacc = [jnp.zeros((8, LANES), F32) for _ in range(STEP)]
    kacc[0] = total
    for g in range(groups):
        for s in range(STEP):
            at = g * STEP + s
            seg = seg_ref[at]
            h = hs[at]
            out = hs[groups * STEP + at] + tap0 * ds[at]
            for t in range(s + 1, STEP):
                d = jnp.where(seg_ref[g * STEP + t] == seg, ds[g * STEP + t], 0.0)
                out = out + taps[t - s] * d
                kacc[t - s] = kacc[t - s] + h * d
            dh_ref[pl.ds(at, 8, stride=groups * STEP), :] = out

    hn[...] = h_ref[...] * rkend_ref[...]
    dn[...] = de_ref[...] * rk0_ref[...]
    width = 4
    place = (lax.broadcasted_iota(jnp.int32, (STEP, LANES), 0) + 1).astype(F32)

    def tables(jq, carry):
        def chunk(n, acc):
            sub, g = n // groups, n % groups
            d0, d1 = (dn[pl.ds(pl.multiple_of(n * STEP + 8 * p, 8), 8), :] for p in range(2))
            h0, h1 = (hn[pl.ds(pl.multiple_of(n * STEP + 8 * p, 8), 8), :] for p in range(2))
            out = []
            for k in range(width):
                at = (g * dims + jq * width + k) * 2
                sr, si = (s_ref[at + p, pl.ds(sub, 8, stride=0), :] for p in range(2))
                yr, yi = (la[at + p, pl.ds(sub, 8, stride=0), :] for p in range(2))
                a = acc[8 * k : 8 * k + 8]
                out += [a[0] + d0 * sr, a[1] + d1 * sr, a[2] - d0 * si, a[3] - d1 * si]
                out += [a[4] + h0 * yr, a[5] + h1 * yr, a[6] + h0 * yi, a[7] + h1 * yi]
            return tuple(out)

        acc = lax.fori_loop(0, 8 * groups, chunk, (jnp.zeros((8, LANES), F32),) * (8 * width))
        for k in range(width):
            j = jq * width + k
            ar, ai, br, bi = (
                jnp.concatenate([acc[8 * k + 2 * p], acc[8 * k + 2 * p + 1]], axis=0) for p in range(4)
            )
            pr, pi, wr, wi = (pf[p, pl.ds(j, STEP, stride=dims), :] for p in range(4))
            ur, ui = ar * pr + ai * pi, ai * pr - ar * pi
            vr, vi = br * wr + bi * wi, bi * wr - br * wi
            rest = STEP - place
            sums = (ur, ui, place * ur, place * ui, vr, rest * vr, rest * vi)
            for p, v in enumerate(sums):
                red[2 + p, pl.ds(j, 1), :] = jnp.sum(v, axis=0, keepdims=True)
        return carry

    lax.fori_loop(0, dims // width, tables, 0)
    e0, e1, f = e_ref[:dims], e_ref[dims:], f_ref[...]
    zero = jnp.zeros((dims, LANES), F32)
    tr, ti, ur, ui = zero, zero, zero, zero
    for d in range(STEP):
        tap = jnp.broadcast_to(jnp.sum(kacc[d], axis=0, keepdims=True), (dims, LANES))
        r, m = tap * pw[d][0], tap * pw[d][1]
        tr, ti = tr + r, ti - m
        if d > 0:
            ur, ui = ur + d * r, ui - d * m
    ge_ref[:dims] = red[2] + f * tr
    ge_ref[dims:] = red[3] + f * ti
    gf = red[6] + e0 * tr + e1 * ti
    xr, xi = red[4] + f * ur, red[5] + f * ui
    lr = e0 * xr + e1 * xi + f * red[7]
    li = e0 * xi - e1 * xr + f * red[8]
    zr, zi = pw[STEP]
    lr = lr + STEP * (red[0] * zr + red[1] * zi)
    li = li + STEP * (red[1] * zr - red[0] * zi)
    root = root_ref[...]
    gf_ref[...] = gf * root
    gr_ref[...] = gf * feed_ref[...] * (1.0 - root * root) / root - lr
    ga_ref[...] = li


def col(rows):
    return pl.BlockSpec((rows, LANES), lambda i: (0, i))


def col3(a, b):
    return pl.BlockSpec((a, b, LANES), lambda i: (0, 0, i))


def whole(*shape):
    return pl.BlockSpec(shape, lambda i: (0,) * len(shape))


def ema_call(body, rows, dims, width, ins, outs, scratch, name, flops):
    specs = [s for _, s in ins]
    return pl.pallas_call(
        functools.partial(body, rows, dims),
        grid=(width // LANES,),
        in_specs=specs,
        out_specs=[s for _, s in outs],
        out_shape=[o for o, _ in outs],
        scratch_shapes=scratch,
        compiler_params=pltpu.CompilerParams(vmem_limit_bytes=48 << 20),
        cost_estimate=pl.CostEstimate(flops=flops, bytes_accessed=16 << 20, transcendentals=0),
        name=name,
    )(*[a for a, _ in ins])


def spread(v):
    return jnp.broadcast_to(v[..., None], v.shape + (LANES,))


def row_masks(seg, before):
    rows = seg.shape[0]
    groups = rows // (8 * STEP)
    cube = seg.reshape(8, groups, STEP)
    chunk_last = cube[:, :, -1]
    prior = jnp.concatenate([before[None], chunk_last.reshape(-1)[:-1]]).reshape(8, groups)
    keep0 = (cube == prior[:, :, None]).astype(F32)
    kend = (cube == chunk_last[:, :, None]).astype(F32)
    order = lambda v: spread(v.transpose(1, 2, 0).reshape(groups * STEP, 8))
    cont = spread((chunk_last == prior).astype(F32).transpose(1, 0))
    ends = jnp.concatenate([before[None], chunk_last[:, -1]])
    sub = jnp.arange(8)
    ahead, behind = [], []
    for k in range(3):
        w = 1 << k
        a = jnp.take(ends, jnp.maximum(sub + 1 - w, 0))
        ahead.append(((ends[1:] == a) & (sub >= w)).astype(F32))
        b = jnp.take(ends, jnp.minimum(sub + w, 8))
        behind.append(((ends[:8] == b) & (sub + w <= 7)).astype(F32))
    return dict(
        seg=order(cube.astype(F32)), keep0=order(keep0), kend=order(kend), cont=cont,
        mk=spread(jnp.stack(ahead)), mkr=spread(jnp.stack(behind)),
        rk0=spread(keep0.reshape(rows)), rkend=spread(kend.reshape(rows)),
    )


def merged(ref):
    v = ref[...]
    return v.reshape(-1, v.shape[-1])


def attend_kernel(
    halo, q_ref, k_ref, seg_ref, segk_ref, h_ref, m_ref, x_ref, gain_ref, wv_ref, wg_ref, wo_ref,
    p_ref, vp_ref, v_ref, gp_ref, o_ref, g_ref, y_ref, n_ref, pb_ref,
):
    t = pl.program_id(0)

    @pl.when(t == 0)
    def _():
        rows, keys = pb_ref.shape
        scores = dot32(q_ref[...], k_ref[...], NT) * (1.0 / math.sqrt(q_ref.shape[1]))
        at_row = lax.broadcasted_iota(jnp.int32, (rows, keys), 0)
        at_key = lax.broadcasted_iota(jnp.int32, (rows, keys), 1)
        allowed = (at_key <= at_row + halo) & (segk_ref[...] == seg_ref[...])
        scores = jnp.where(allowed, scores, -1e30)
        raw = jnp.exp(scores - jnp.max(scores, axis=1, keepdims=True))
        p = raw / jnp.sum(raw, axis=1, keepdims=True)
        p_ref[...] = p
        pb_ref[...] = p.astype(BF16)
        y_ref[...] = x_ref[...].astype(F32)

    vp = dot32(h_ref[...], merged(wv_ref))
    v = silu_of(vp).astype(BF16)
    vp_ref[...] = vp.astype(BF16)
    v_ref[...] = v
    gp = dot32(m_ref[...], merged(wg_ref))
    gp_ref[...] = gp.astype(BF16)
    o = dot32(pb_ref[...], v)
    o_ref[...] = o.astype(BF16)
    g = (silu_of(gp) * o).astype(BF16)
    g_ref[...] = g
    y_ref[...] += dot32(g, merged(wo_ref), NT)

    @pl.when(t == pl.num_programs(0) - 1)
    def _():
        y = y_ref[...]
        rr = lax.rsqrt(jnp.mean(y * y, axis=1, keepdims=True) + EPSILON)
        n_ref[...] = (y * rr * gain_ref[...]).astype(BF16)


def ffn_kernel(
    y_ref, n_ref, og_ref, gain_ref, w1_ref, w3_ref, w2_ref, out_ref, dy_ref, branch_ref, gain_grad_ref, grads_ref,
    acc, dn,
):
    t = pl.program_id(0)

    @pl.when(t == 0)
    def _():
        acc[...] = y_ref[...]
        dn[...] = jnp.zeros_like(dn)

    w1, w3, w2 = merged(w1_ref), merged(w3_ref), merged(w2_ref)
    nn, og = n_ref[...], og_ref[...]
    u1, u3 = dot32(nn, w1), dot32(nn, w3)
    sg = jax.nn.sigmoid(u1)
    act = u1 * sg
    hd = (act * u3).astype(BF16)
    acc[...] += dot32(hd, w2, NT)
    dh = dot32(og, w2)
    d1 = (dh * u3 * (sg * (1.0 + u1 * (1.0 - sg)))).astype(BF16)
    d3 = (dh * act).astype(BF16)
    dn[...] += dot32(d1, w1, NT) + dot32(d3, w3, NT)
    depth = grads_ref.shape[3]
    for k, (a, b) in enumerate(((nn, d1), (nn, d3), (og, hd))):
        grads_ref[:, 0, k] = dot32(a, b, TN).astype(BF16).reshape(-1, depth, b.shape[1])

    @pl.when(t == pl.num_programs(0) - 1)
    def _():
        out_ref[...] = acc[...].astype(BF16)
        y = y_ref[...]
        rr = lax.rsqrt(jnp.mean(y * y, axis=1, keepdims=True) + EPSILON)
        nh = y * rr
        g = dn[...]
        gain_grad_ref[...] = jnp.sum(nh * g, axis=0, keepdims=True)
        scaled = g * gain_ref[...]
        dy = og.astype(F32) + rr * (scaled - nh * jnp.mean(nh * scaled, axis=1, keepdims=True))
        dy_ref[...] = dy
        branch_ref[...] = dy.astype(BF16)


def attend_back_kernel(
    halo, br_ref, p_ref, h_ref, m_ref, q_ref, k_ref, vp_ref, v_ref, gp_ref, o_ref, g_ref, wv_ref, wg_ref, wo_ref,
    dq_ref, dkn_ref, dk_ref, dhn_ref, dh_ref, dm_ref, grads_ref, dp, dhv, pb_ref,
):
    t = pl.program_id(0)

    @pl.when(t == 0)
    def _():
        pb_ref[...] = p_ref[...].astype(BF16)
        dp[...] = jnp.zeros_like(dp)
        dhv[...] = jnp.zeros_like(dhv)
        dm_ref[...] = jnp.zeros_like(dm_ref)

    branch, pb = br_ref[...], pb_ref[...]
    dg = dot32(branch, merged(wo_ref))
    gp = gp_ref[...].astype(F32)
    sg = jax.nn.sigmoid(gp)
    da = (dg * (gp * sg)).astype(BF16)
    dr = (dg * o_ref[...].astype(F32) * (sg * (1.0 + gp * (1.0 - sg)))).astype(BF16)
    dp[...] += dot32(da, v_ref[...], NT)
    dv = dot32(pb, da, TN)
    dvp = (dv * silu_slope(vp_ref[...].astype(F32))).astype(BF16)
    dhv[...] += dot32(dvp, merged(wv_ref), NT)
    dm_ref[...] += dot32(dr, merged(wg_ref), NT)
    depth = grads_ref.shape[3]
    for k, (a, b) in enumerate(((h_ref[...], dvp), (m_ref[...], dr), (branch, g_ref[...]))):
        grads_ref[:, 0, k] = dot32(a, b, TN).astype(BF16).reshape(-1, depth, b.shape[1])

    @pl.when(t == pl.num_programs(0) - 1)
    def _():
        scale = 1.0 / math.sqrt(q_ref.shape[1])
        p = p_ref[...]
        d = dp[...]
        ds = (p * (d - jnp.sum(p * d, axis=1, keepdims=True))).astype(BF16)
        dq_ref[...] = dot32(ds, k_ref[...]) * scale
        dk = dot32(ds, q_ref[...], TN) * scale
        dkn_ref[...] = dk[:halo].astype(BF16)
        dk_ref[...] = dk[halo:]
        dhn_ref[...] = dhv[:halo, :].astype(BF16)
        dh_ref[...] = dhv[halo:, :]


def stage_call(body, steps, ins, outs, scratch, name, flops):
    def spec(v, how):
        if how == "all":
            return pl.BlockSpec(v.shape, lambda t: (0,) * v.ndim)
        if how == "col":
            return pl.BlockSpec((v.shape[0], v.shape[1] // steps), lambda t: (0, t))
        return how

    outs = [(jax.ShapeDtypeStruct(s, d), how) for s, d, how in outs]
    return pl.pallas_call(
        body,
        grid=(steps,),
        in_specs=[spec(v, how) for v, how in ins],
        out_specs=[spec(v, how) for v, how in outs],
        out_shape=[v for v, _ in outs],
        scratch_shapes=scratch,
        compiler_params=pltpu.CompilerParams(vmem_limit_bytes=60 << 20),
        cost_estimate=pl.CostEstimate(flops=flops, bytes_accessed=48 << 20, transcendentals=0),
        name=name,
    )(*[v for v, _ in ins])


def small_sums_kernel(bits, small_ref, block_ref, out_ref, own_ref, acc, cube, buf, cbuf, sems):
    d, t = lax.axis_index("dp"), lax.axis_index("tensor")

    def mine(axis, k):
        return ((d if axis == "dp" else t) // (1 << k)) % 2

    def partner(axis, k):
        step = (1 - 2 * mine(axis, k)) * (1 << k)
        return (d + step, t) if axis == "dp" else (d, t + step)

    barrier = pltpu.get_barrier_semaphore()
    for bit in bits:
        pl.semaphore_signal(barrier, inc=1, device_id=partner(*bit), device_id_type=pl.DeviceIdType.MESH)
    pl.semaphore_wait(barrier, len(bits))

    def send(n, which, src, dst, bit):
        copy = pltpu.make_async_remote_copy(
            src_ref=src, dst_ref=dst, send_sem=sems.at[0, which, n], recv_sem=sems.at[1, which, n],
            device_id=partner(*bit), device_id_type=pl.DeviceIdType.MESH,
        )
        copy.start()
        return copy

    acc[...] = small_ref[...]
    cube[...] = block_ref[...]
    start, length, cstart, clength = 0, acc.shape[0], 0, cube.shape[0]
    at, cat = 0, 0
    trail = []
    for n, bit in enumerate(bits):
        axis, k = bit
        half = length // 2
        keep = pl.multiple_of(start + mine(axis, k) * half, 8)
        give = pl.multiple_of(start + (1 - mine(axis, k)) * half, 8)
        copies = [send(n, 0, acc.at[pl.ds(give, half)], buf.at[pl.ds(at, half)], bit)]
        if axis == "dp":
            chalf = clength // 2
            ckeep = pl.multiple_of(cstart + mine(axis, k) * chalf, 8)
            cgive = pl.multiple_of(cstart + (1 - mine(axis, k)) * chalf, 8)
        else:
            chalf, ckeep, cgive = clength, cstart, cstart
        copies.append(send(n, 1, cube.at[pl.ds(cgive, chalf)], cbuf.at[pl.ds(cat, chalf)], bit))
        for copy in copies:
            copy.wait()
        acc[pl.ds(keep, half)] += buf[pl.ds(at, half)]
        cube[pl.ds(ckeep, chalf)] += cbuf[pl.ds(cat, chalf)]
        trail.append((start, length))
        start, length, cstart, clength = keep, half, ckeep, chalf
        at, cat = at + half, cat + chalf
    own_ref[...] = cube[pl.ds(cstart, clength)]
    out_ref[pl.ds(start, length)] = acc[pl.ds(start, length)]
    for n, bit in reversed(list(enumerate(bits))):
        copy = send(n, 2, out_ref.at[pl.ds(start, length)], out_ref.at[pl.ds(start, length)], bit)
        copy.wait()
        start, length = trail[n]


def small_sums_call(small, block, replicas, parts):
    bits = [("dp", k) for k in range(replicas.bit_length() - 1)]
    bits += [("tensor", k) for k in range(parts.bit_length() - 1)]
    own = block.shape[0] // replicas
    got = sum(block.shape[0] >> (k + 1) for k in range(replicas.bit_length() - 1))
    got += own * (parts.bit_length() - 1)
    vmem = pl.BlockSpec(memory_space=pltpu.VMEM)
    return pl.pallas_call(
        functools.partial(small_sums_kernel, bits),
        in_specs=[vmem, vmem],
        out_specs=[vmem, vmem],
        out_shape=[jax.ShapeDtypeStruct(small.shape, F32), jax.ShapeDtypeStruct((own, block.shape[1]), F32)],
        scratch_shapes=[
            pltpu.VMEM(small.shape, F32), pltpu.VMEM(block.shape, F32), pltpu.VMEM(small.shape, F32),
            pltpu.VMEM((got, block.shape[1]), F32), pltpu.SemaphoreType.DMA((2, 3, len(bits))),
        ],
        compiler_params=pltpu.CompilerParams(collective_id=0, has_side_effects=True, vmem_limit_bytes=24 << 20),
        name="small_sums",
    )(small, block)


def on_device(
    block_in, segments, norm_gain, ema_rate, ema_angle, ema_input, ema_output, ema_skip, w_shared, query_gain,
    query_bias, key_gain, w_value, w_gate, w_out, ffn_gain, w_swish, w_up, w_down, out_grad,
):
    parts = lax.axis_size("tensor")
    replicas = lax.axis_size("dp")
    rank = lax.axis_index("tensor")
    rows, width = block_in.shape
    dims = ema_rate.shape[0]
    length = segments.shape[1]
    groups = TN_GROUPS
    span = width // groups
    latent_width = w_shared.shape[1]
    value_width = w_value.shape[1] * parts
    ffn_width = w_swish.shape[1] * parts
    depth = w_value.shape[0]
    halo = -(-REACH // LANES) * LANES
    hops = [min(rows, halo - h * rows) for h in range(-(-halo // rows))]

    def from_earlier(x, hop):
        return lax.ppermute(x, "tensor", [(i, i + hop) for i in range(parts - hop)])

    def from_later(x, hop):
        return lax.ppermute(x, "tensor", [(i + hop, i) for i in range(parts - hop)])

    def halo_of(x):
        pieces = [from_earlier(x[rows - n :], h + 1) for h, n in enumerate(hops)]
        return jnp.concatenate(pieces[::-1] + [x], axis=0)

    def give_back(total, x):
        end = halo
        for h, n in enumerate(hops):
            got = from_later(x[end - n : end], h + 1).astype(F32)
            total = total.at[rows - n :].add(got)
            end -= n
        return total

    piece = depth // parts
    shared_piece = lax.dynamic_slice_in_dim(w_shared, rank * piece, piece, 0)
    low = lambda w: w.astype(BF16)
    vw, fw = value_width // parts, ffn_width // parts
    pack_a = jnp.concatenate(
        [low(w_value), low(w_gate), low(w_out.T), low(shared_piece).reshape(-1, vw)], axis=0
    )
    pack_f = jnp.concatenate([low(w_swish), low(w_up), low(w_down.T)], axis=0)
    all_a = lax.all_gather(pack_a, BOTH, axis=0)
    all_a = all_a.reshape(replicas, parts, -1, vw)
    pack_f = with_layout_constraint(pack_f, Layout((0, 1)))
    all_f = lax.all_gather(pack_f, BOTH, axis=0).reshape(replicas, parts, 3 * depth, fw)
    shared_b = all_a[:, :, 3 * depth :].reshape(width, latent_width)

    def part(k, columns):
        return pl.BlockSpec((replicas, 1, depth, columns), lambda t: (0, t, k, 0))

    seg_all = segments[0]
    padded = jnp.concatenate([jnp.full((halo,), -1, jnp.int32), seg_all, jnp.full((halo,), -2, jnp.int32)])
    near = lax.dynamic_slice_in_dim(padded, rank * rows, halo + rows + halo, 0)
    seg_keys = near[: halo + rows]
    seg = near[halo : halo + rows]
    before = near[halo - 1]
    masks = row_masks(seg, before)
    index = rank * rows + jnp.arange(rows, dtype=jnp.int32)
    start = jnp.sum((seg_all[None, :] < seg[:, None]).astype(jnp.int32), axis=1)
    count = (index - start + 1).astype(F32)[:, None] * span
    tri = jnp.arange(rows)
    same = seg[:, None] == seg[None, :]
    lower = (same & (tri[:, None] >= tri[None, :])).astype(F32)
    link1 = (seg[0] == before).astype(F32)
    link2 = (before == near[halo - rows - 1]).astype(F32)
    last = seg[-1]
    next1 = (near[halo + rows] == last).astype(F32)
    next2 = ((near[halo + 2 * rows - 1] == last) & (near[halo + 2 * rows] == last)).astype(F32) if halo > rows else 0.0
    heads = (seg == before).astype(F32)[:, None]
    tails = (seg == last).astype(F32)[:, None]

    x = block_in.astype(F32)
    gather = (jnp.arange(width)[:, None] // span == jnp.arange(groups)[None, :]).astype(F32)
    sums_of = lambda v: dot32(v, gather, precision=HIGHEST)
    spread_of = lambda v: dot32(v, gather, NT, precision=HIGHEST)
    sums = jnp.concatenate([dot32(block_in, gather.astype(BF16)), sums_of(x * x)], axis=1)
    running = dot32(lower, sums, precision=HIGHEST)
    tail = running[-1:]
    carry = from_earlier(tail, 1) + link2 * from_earlier(tail, 2)
    running = running + heads * carry
    mean = running[:, :groups] / count
    var = running[:, groups:] / count - mean * mean
    rho = lax.rsqrt(var + EPSILON)
    mean_full, rho_full = spread_of(mean), spread_of(rho)
    centred = (x - mean_full) * rho_full
    hidden = centred * norm_gain
    hidden_b = low(hidden)

    size = jnp.exp(-ema_rate)
    unit = jnp.concatenate([size * jnp.cos(ema_angle), size * jnp.sin(ema_angle)])
    root = jnp.sqrt(1.0 - size * size)
    feed = ema_input * root
    reads = ema_output.reshape(2 * dims, width)
    skip = ema_skip[None]
    gcount = rows // (8 * STEP)
    nstate = gcount * dims * 2
    at_rows = gcount * STEP
    state_shape = (jax.ShapeDtypeStruct((nstate, 8, width), F32), col3(nstate, 8))
    edge_shape = (jax.ShapeDtypeStruct((2 * dims, width), F32), col(2 * dims))
    dim_shape = (jax.ShapeDtypeStruct((dims, width), F32), col(dims))
    rows_shape = (jax.ShapeDtypeStruct((rows, width), F32), col(rows))
    mask_spec = whole(at_rows, 8, LANES)
    cont, mk, mkr = (
        (masks["cont"], whole(gcount, 8, LANES)), (masks["mk"], whole(3, 8, LANES)), (masks["mkr"], whole(3, 8, LANES))
    )
    kend, keep0, seg8 = ((masks[k], mask_spec) for k in ("kend", "keep0", "seg"))
    pair, single = col(2 * dims), col(dims)
    vm = lambda n: pltpu.VMEM((n, 8, LANES), F32)
    flat_vm = lambda *n: pltpu.VMEM((*n, LANES), F32)
    table_vm, scale_vm = flat_vm(2, STEP * dims), flat_vm(8 * dims)
    mac = rows * width * dims * 4
    entering, end, turn = ema_call(
        ema_enter, rows, dims, width,
        [(hidden, col(rows)), kend, (unit, pair), (feed, single), cont, mk],
        [state_shape, edge_shape, edge_shape], [vm(at_rows), table_vm, scale_vm], "ema_enter", mac,
    )

    def turned(v, sign):
        r, i = times(turn[:dims], sign * turn[dims:], v[:dims], v[dims:])
        return jnp.concatenate([r, i])

    state_in = from_earlier(end, 1) + link2 * turned(from_earlier(end, 2), 1.0)
    ema_out, mixed, states = ema_call(
        ema_read, rows, dims, width,
        [(hidden, col(rows)), seg8, keep0, (unit, pair), (feed, single), (reads, pair), cont, mk,
         (entering, col3(nstate, 8)), (state_in, pair), (skip, col(1))],
        [rows_shape, (jax.ShapeDtypeStruct((rows, width), BF16), col(rows)), state_shape],
        [vm(2 * at_rows), table_vm, scale_vm], "ema_read", mac,
    )

    hidden_near = halo_of(hidden_b)
    near_rows = halo + rows
    latent = dot32(mixed, shared_b)
    queries = low(latent * query_gain + query_bias)
    keys_near = halo_of(low(latent * key_gain))
    one = lambda v: v[None]
    matmul = rows * width * vw * 2 * parts
    col_v = lambda n: ((n, value_width), BF16, "col")
    probs, value_pre, values, gate_pre, attended, gated, residual, norm_in = stage_call(
        functools.partial(attend_kernel, halo), parts,
        [(queries, "all"), (keys_near, "all"), (seg[:, None], "all"), (one(seg_keys), "all"), (hidden_near, "all"),
         (mixed, "all"), (block_in, "all"), (one(ffn_gain), "all"), (all_a, part(0, vw)), (all_a, part(1, vw)),
         (all_a, part(2, vw))],
        [((rows, near_rows), F32, "all"), col_v(near_rows), col_v(near_rows), col_v(rows), col_v(rows), col_v(rows),
         ((rows, width), F32, "all"), ((rows, width), BF16, "all")],
        [pltpu.VMEM((rows, near_rows), BF16)], "attend", 6 * matmul,
    )

    row_vm = lambda n: pltpu.VMEM((n, width), F32)
    block_out, grad_residual, branch, grad_ffn_gain, ffn_grads = stage_call(
        ffn_kernel, parts,
        [(residual, "all"), (norm_in, "all"), (out_grad, "all"), (one(ffn_gain), "all"), (all_f, part(0, fw)),
         (all_f, part(1, fw)), (all_f, part(2, fw))],
        [((rows, width), BF16, "all"), ((rows, width), F32, "all"), ((rows, width), BF16, "all"),
         ((1, width), F32, "all"),
         ((replicas, parts, 3, depth, fw), BF16,
          pl.BlockSpec((replicas, 1, 3, depth, fw), lambda t: (0, t, 0, 0, 0)))],
        [row_vm(rows), row_vm(rows)], "ffn", 11 * matmul,
    )

    def summed(g):
        g = g.reshape(replicas, parts, -1, g.shape[-1])
        g = lax.psum_scatter(g, "dp", scatter_dimension=0, tiled=False)
        return lax.psum_scatter(g, "tensor", scatter_dimension=0, tiled=False).astype(F32)

    ffn_sum = summed(ffn_grads)

    grad_queries, keys_back, keys_own, hidden_back, hidden_own, grad_mixed, attn_grads = stage_call(
        functools.partial(attend_back_kernel, halo), parts,
        [(branch, "all"), (probs, "all"), (hidden_near, "all"), (mixed, "all"), (queries, "all"), (keys_near, "all"),
         (value_pre, "col"), (values, "col"), (gate_pre, "col"), (attended, "col"), (gated, "col"),
         (all_a, part(0, vw)), (all_a, part(1, vw)), (all_a, part(2, vw))],
        [((rows, latent_width), F32, "all"), ((halo, latent_width), BF16, "all"), ((rows, latent_width), F32, "all"),
         ((halo, width), BF16, "all"), ((rows, width), F32, "all"), ((rows, width), F32, "all"),
         ((replicas, parts, 3, depth, vw), BF16,
          pl.BlockSpec((replicas, 1, 3, depth, vw), lambda t: (0, t, 0, 0, 0)))],
        [pltpu.VMEM((rows, near_rows), F32), row_vm(near_rows), pltpu.VMEM((rows, near_rows), BF16)], "attend_back", 12 * matmul,
    )
    grad_keys = give_back(keys_own, keys_back)
    grad_hidden = give_back(hidden_own, hidden_back)
    grad_query_gain = jnp.sum(latent * grad_queries, axis=0)
    grad_query_bias = jnp.sum(grad_queries, axis=0)
    grad_key_gain = jnp.sum(latent * grad_keys, axis=0)
    grad_latent = low(grad_queries * query_gain + grad_keys * key_gain)
    grad_shared = dot32(mixed, grad_latent, TN)
    attn_sum = summed(attn_grads)
    grad_ema = (dot32(grad_latent, shared_b, NT) + grad_mixed) * silu_slope(ema_out)

    pulls, head = ema_call(
        ema_leave, rows, dims, width,
        [(grad_ema, col(rows)), keep0, (unit, pair), (reads, pair), cont, mkr],
        [state_shape, edge_shape], [vm(at_rows), table_vm, scale_vm], "ema_leave", mac,
    )
    cross = (near[halo + 2 * rows - 1] == last).astype(F32)
    pull_in = from_later(head, 1) + cross * turned(from_later(head, 2), -1.0)
    grad_hidden_ema, output_grad, input_grad, rate_grad, angle_grad, grad_skip = ema_call(
        ema_grads, rows, dims, width,
        [(hidden, col(rows)), (grad_ema, col(rows)), seg8, kend, (masks["rk0"], whole(rows, LANES)),
         (masks["rkend"], whole(rows, LANES)), (unit, pair), (feed, single), (reads, pair), (root, single),
         (ema_input, single), cont, mkr, (pulls, col3(nstate, 8)), (pull_in, pair), (states, col3(nstate, 8)),
         (skip, col(1))],
        [rows_shape, edge_shape, dim_shape, dim_shape, dim_shape, (jax.ShapeDtypeStruct((1, width), F32), col(1))],
        [vm(2 * at_rows), vm(at_rows), vm(nstate), table_vm, scale_vm, flat_vm(4, STEP * dims), flat_vm(9, dims),
         flat_vm(rows), flat_vm(rows)], "ema_grads", 3 * mac,
    )

    grad_hidden = grad_hidden + grad_hidden_ema
    gain_grad = jnp.sum(centred * grad_hidden, axis=0)
    spread_grad = grad_hidden * norm_gain
    sum_a = rho * sums_of(spread_grad)
    sum_b = sums_of(spread_grad * (x - mean_full))
    cube = sum_b * rho * rho * rho
    push = jnp.concatenate([(cube * mean - sum_a) / count, -cube / (2.0 * count)], axis=1)
    backed = dot32(lower, push, TN, precision=HIGHEST)
    first = backed[:1]
    carry = next1 * from_later(first, 1) + next2 * from_later(first, 2)
    backed = backed + tails * carry
    grad_x = spread_grad * rho_full + spread_of(backed[:, :groups]) + 2.0 * x * spread_of(backed[:, groups:])
    in_grad = grad_residual + grad_x

    small = [gain_grad, rate_grad, angle_grad, input_grad, output_grad, grad_skip, grad_query_gain,
             grad_query_bias, grad_key_gain, grad_ffn_gain]
    sizes = [v.size for v in small]
    total = sum(sizes)
    members = parts * replicas
    unit = members * 8 * LANES
    packed = jnp.concatenate([v.reshape(-1) for v in small] + [jnp.zeros((-total % unit,), F32)])
    packed = packed.reshape(-1, LANES)
    levels = replicas.bit_length() - 1
    mirror = lambda v: v.transpose(tuple(reversed(range(levels))) + (levels, levels + 1))
    block = mirror(grad_shared.reshape((2,) * levels + (depth, latent_width)))
    packed, shared_sum = small_sums_call(packed, block.reshape(width, latent_width), replicas, parts)
    packed = packed.reshape(-1)
    small_sums, at = [], 0
    for n in sizes:
        small_sums.append(packed[at : at + n])
        at += n
    shape = lambda k, like: small_sums[k].reshape(like.shape)

    cut = lambda g, k: g[k * depth : (k + 1) * depth]
    return (
        block_out, in_grad, shape(0, norm_gain), shape(1, ema_rate), shape(2, ema_angle), shape(3, ema_input),
        shape(4, ema_output), shape(5, ema_skip), shared_sum, shape(6, query_gain), shape(7, query_bias),
        shape(8, key_gain), cut(attn_sum, 0), cut(attn_sum, 1), cut(attn_sum, 2).T, shape(9, ffn_gain),
        cut(ffn_sum, 0), cut(ffn_sum, 1), cut(ffn_sum, 2).T,
    )


def solution(mesh):
    rows, dp, copy = P(BOTH, None), P("dp", None), P()
    wide, tall = P("dp", "tensor"), P("tensor", "dp")
    return jax.shard_map(
        on_device,
        mesh=mesh,
        in_specs=(
            rows, dp, copy, copy, copy, copy, copy, copy, dp, copy, copy, copy, wide, wide, tall, copy, wide, wide,
            tall, rows,
        ),
        out_specs=(
            rows, rows, copy, copy, copy, copy, copy, copy, dp, copy, copy, copy, wide, wide, tall, copy, wide, wide,
            tall,
        ),
        check_vma=False,
    )
```

time: 974 us -> 672 us (0.69)
  local copies, waits for them, and re-layouts: 231 us -> 32.3 us
  Pallas kernels: 94.6 us -> 264 us
  blocking collectives: 166 us -> 0 us
  matrix products: 146 us -> 17.2 us
  other arithmetic: 79.1 us -> 27.3 us
  waiting for transfers between devices: 189 us -> 233 us
  starting transfers between devices: 38.7 us -> 68.8 us
    all_gather x3 -> x0, blocking collectives: 166 us -> none  [the longest x1 77.7 us: on_device(): all_s = lax.all_gather(low(shared_piece), BOTH, axis=0, tiled=True)]
    pallas_call x0 -> x4, Pallas kernels: none -> 165 us  [the longest x3 108 us: stage_call(): pl.pallas_call(body, grid=(steps,), in_specs=[spec(v, how) for v, how in...]
    dot_general x37 -> x13, matrix products: 146 us -> 17.2 us  [dot32(): lax.dot_general(a, b, (dims, ((), ())), precision=precision, preferred_el...]
    unnamed x8 -> x6, waiting for transfers between devices: 109 us -> 0.6 us
    reshape x22 -> x3, local copies, waits for them, and re-layouts: 83.3 us -> 2.1 us  [the longest x1 2.02 us: on_device(): shared_b = all_a[:, :, 3 * depth:].reshape(width, latent_width)]
    transpose x8 -> x0, local copies, waits for them, and re-layouts: 70.2 us -> none  [on_device(): flat = lambda w, k: w[:, :, k].transpose(0, 2, 1, 3).reshape(width, -1)]
    ppermute x8, waiting for transfers between devices: 20.9 us -> 71.1 us  [from_earlier(): return lax.ppermute(x, 'tensor', [(i, i + hop) for i in range(parts - hop)])]
    all_gather x2, waiting for transfers between devices: 0.01 us -> 48.8 us  [the longest x1 48.8 us: on_device(): lax.all_gather(pack_f, BOTH, axis=0).reshape(replicas, parts, 3 * depth, fw)]
  transfers between devices with their start and end apart: 23 -> 22, of which waited for: 8 -> 10; matrix products, arithmetic and copies ran while one was open for 34% -> 10% of each run, Pallas kernels for 10% -> 27%
where the time goes in v2:
time: 672 us; the launch traced here: 663 us
  Pallas kernels  264 us (39%)
  waiting for transfers between devices  233 us (35%)
  starting transfers between devices  68.8 us (10%)
  local copies, waits for them, and re-layouts  32.3 us (5%)
  other arithmetic  27.3 us (4%)
  between operations  20.7 us (3%)
  matrix products  17.2 us (3%)
    pallas_call x3, Pallas kernels, stage_call(): pl.pallas_call(body, grid=(steps,), in_specs=[spec(v, how) for v, how in...  108 us
    pallas_call x4, Pallas kernels, ema_call(): pl.pallas_call(functools.partial(body, rows, dims), grid=(width // LANES,...  98.8 us
    ppermute x8, waiting for transfers between devices, from_later(): return lax.ppermute(x, 'tensor', [(i + hop, i) for i in range(parts - hop)])  77.8 us
    ppermute x8, waiting for transfers between devices, from_earlier(): return lax.ppermute(x, 'tensor', [(i, i + hop) for i in range(parts - hop)])  71.1 us
    ppermute x8, starting transfers between devices, from_earlier(): return lax.ppermute(x, 'tensor', [(i, i + hop) for i in range(parts - hop)])  57.8 us
    pallas_call x1, Pallas kernels, small_sums_call(): pl.pallas_call(functools.partial(small_sums_kernel, bits), in_specs=[vmem...  57.3 us
    all_gather x1, waiting for transfers between devices, on_device(): lax.all_gather(pack_f, BOTH, axis=0).reshape(replicas, parts, 3 * depth, fw)  48.8 us
    reduce_scatter x2, waiting for transfers between devices, summed(): g = lax.psum_scatter(g, 'dp', scatter_dimension=0, tiled=False)  19.4 us
  transfers between devices with their start and end apart: 22, of which 10 were waited for; matrix products, arithmetic and copies ran while one was open for 10% of the time, Pallas kernels for 27%

profile of v2, /device:TPU:0, one launch (start us, length us, event | category | flops | bytes accessed | tf_op | source)
XLA Modules:
  0.0 663.4 jit_solution(4562757004571449873)
XLA Ops:
  8.1 1.1 copy.86
  9.2 1.0 convert_element_type.129
  10.2 1.0 convert_element_type.128
  13.3 1.2 fusion
  15.8 4.9 collective-permute-start
  20.8 4.5 collective-permute-start.1
  32.7 1.3 compare_convert_fusion
  34.4 1.2 fusion.31
  35.7 3.6 fusion.66
  39.2 2.3 collective-permute-start.7
  41.5 0.9 slice.346
  42.7 12.9 %ema_enter.1 = (f32[128,8,1024]{2,1,0:T(8,128)}, f32[32,1024]{1,0:T(8,128)S(1)}, f32[32,1024]{1,0:T(8,128)S(1)}) custom-call(f32[512,1024]{1,0:T(8,128)S(1)} %get-tuple-element.219.h_ref, f32[64,8,128]{2,1,0:T(8,128)S(1)} %broadcast_in_dim.108.kend_ref, f32[32,1024]{1,0:T(8,128)S(1)} %pad_maximum_fusion.4.q_ref, f32[16,1024]{1,0:T(8,128)S(1)} %get-tuple-element.246.f_ref, ...), custom_call_target="tpu_custom_call" | custom-call | flops 33554432 | bytes 16777216 | tf_op jit(solution)/shard_map/ema_enter/pallas_call | solution.py:394
  55.6 1.3 collective-permute-start.3
  56.9 2.2 collective-permute-start.6
  60.8 1.5 collective-permute-start.2
  62.3 22.8 %collective-permute-done.3 = f32[32,1024]{1,0:T(8,128)S(1)} collective-permute-done((f32[32,1024]{1,0:T(8,128)S(1)}, f32[32,1024]{1,0:T(8,128)S(1)}, u32[]{:S(2)}, u32[]{:S(2)}) %collective-permute-start.3) | collective-permute-done | bytes 131104 | tf_op jit(solution)/shard_map/ppermute | solution.py:682
  85.1 37.8 %collective-permute-done.2 = f32[32,1024]{1,0:T(8,128)S(1)} collective-permute-done((f32[32,1024]{1,0:T(8,128)S(1)}, f32[32,1024]{1,0:T(8,128)S(1)}, u32[]{:S(2)}, u32[]{:S(2)}) %collective-permute-start.2) | collective-permute-done | bytes 131104 | tf_op jit(solution)/shard_map/ppermute | solution.py:682
  123.3 18.9 %ema_read.1 = (f32[512,1024]{1,0:T(8,128)S(1)}, bf16[512,1024]{1,0:T(8,128)(2,1)S(1)}, f32[128,8,1024]{2,1,0:T(8,128)}) custom-call(f32[512,1024]{1,0:T(8,128)} %copy-done.2, f32[64,8,128]{2,1,0:T(8,128)S(1)} %broadcast_in_dim.48.seg_ref, f32[64,8,128]{2,1,0:T(8,128)S(1)} %broadcast_in_dim.51.k0_ref, f32[32,1024]{1,0:T(8,128)S(1)} %pad_maximum_fusion.4.q_ref, ...), custom_call_target="tpu_custom_call" | custom-call | flops 33554432 | bytes 16777216 | tf_op jit(solution)/shard_map/ema_read/pallas_call | solution.py:394
  142.2 1.3 copy-done.7
  143.6 2.3 slice.343
  145.8 2.0 reshape.326
  147.9 2.4 multiply_convert_fusion
  150.2 37.1 %collective-permute-start.5 = (bf16[512,256]{1,0:T(8,128)(2,1)S(1)}, bf16[512,256]{1,0:T(8,128)(2,1)S(1)}, u32[]{:S(2)}, u32[]{:S(2)}) collective-permute-start(bf16[512,256]{1,0:T(8,128)(2,1)S(1)} %get-tuple-element.228), channel_id=1, source_target_pairs={{0,1},{1,2},{2,3},{4,5},{5,6},{6,7},{8,9},{9,10},{10,11},{12,13},{... | collective-permute-start | bytes 786440 | tf_op jit(solution)/shard_map/ppermute | solution.py:682
  187.4 4.0 collective-permute-start.4
  191.4 3.5 pad_maximum_fusion.h_ref
  194.9 10.5 %collective-permute-done.4 = bf16[384,256]{1,0:T(8,128)(2,1)S(1)} collective-permute-done((bf16[384,256]{1,0:T(8,128)(2,1)S(1)}, bf16[384,256]{1,0:T(8,128)(2,1)S(1)}, u32[]{:S(2)}, u32[]{:S(2)}) %collective-permute-start.4) | collective-permute-done | bytes 196640 | tf_op jit(solution)/shard_map/ppermute | solution.py:682
  206.3 25.1 %attend.1 = (f32[512,1408]{1,0:T(8,128)}, bf16[1408,2048]{1,0:T(8,128)(2,1)}, bf16[1408,2048]{1,0:T(8,128)(2,1)}, bf16[512,2048]{1,0:T(8,128)(2,1)}, bf16[512,20...) custom-call(bf16[512,256]{1,0:T(8,128)(2,1)} %get-tuple-element.229.q_ref, ...), custom_call_target="tpu_custom_call" | custom-call | flops 12884901888 | bytes 50331648 | tf_op jit(solution)/shard_map/attend/pallas_call | solution.py:572
  231.5 48.8 %all-gather.7.cloned.1.call-done = bf16[12288,640]{1,0:T(8,128)(2,1)} async-done(((bf16[384,640]{1,0:T(8,128)(2,1)}), bf16[12288,640]{1,0:T(8,128)(2,1)}) %all-gather.7.cloned.1.call-update) | async-done | bytes 15728656 | tf_op jit(solution)/shard_map/all_gather | solution.py:710
  280.2 39.8 %ffn.1 = (bf16[512,1024]{1,0:T(8,128)(2,1)}, f32[512,1024]{1,0:T(8,128)}, bf16[512,1024]{1,0:T(8,128)(2,1)}, f32[1,1024]{1,0:T(1,128)}, bf16[8,4,3,128,640]{4,3,2,1,0:T(8,128)(2,1)}) custom-call(f32[512,1024]{1,0:T(8,128)} %get-tuple-element.124.y_ref, bf16[512,1024]{1,0:T(8,128)(2,1)} %get-tuple-element.125.n_ref, bf16[512,1024]{1,0:T(8,128)(2,1)} %og_ref.1, ...), custom_call_target="tpu_custom_call" | custom-call | flops 23622320128 | bytes 50331648 | tf_op jit(solution)/shard_map/ffn/pallas_call | solution.py:572
  320.0 42.8 %attend_back.1 = (f32[512,256]{1,0:T(8,128)}, bf16[896,256]{1,0:T(8,128)(2,1)}, f32[512,256]{1,0:T(8,128)}, bf16[896,1024]{1,0:T(8,128)(2,1)}, f32[512,1024]{1,0...) custom-call(bf16[512,1024]{1,0:T(8,128)(2,1)} %get-tuple-element.128.br_ref, ...), custom_call_target="tpu_custom_call" | custom-call | flops 25769803776 | bytes 50331648 | tf_op jit(solution)/shard_map/attend_back/pallas_call | solution.py:572
  364.2 1.2 gather_fusion.4
  365.4 1.2 gather_fusion.5
  370.5 1.1 slice.281
  371.6 1.4 collective-permute-start.10
  373.7 1.1 slice.278
  374.9 0.9 slice.280
  375.8 1.1 slice.283
  376.9 1.4 collective-permute-start.8
  378.3 1.3 collective-permute-start.9
  379.6 1.3 collective-permute-start.11
  380.9 1.2 collective-permute-done.10
  382.2 66.1 %collective-permute-done.11 = bf16[384,256]{1,0:T(8,128)(2,1)S(1)} collective-permute-done((bf16[384,256]{1,0:T(8,128)(2,1)S(1)}, bf16[384,256]{1,0:T(8,128)(2,1)S(1)}, u32[]{:S(2)}, u32[]{:S(2)}) %collective-permute-start.11) | collective-permute-done | bytes 196640 | tf_op jit(solution)/shard_map/ppermute | solution.py:685
  449.3 1.8 fusion.71
  451.1 2.6 reduce-scatter.5.cloned.1.call-done
  453.7 3.0 multiply_multiply_fusion.de_ref
  456.9 13.6 %ema_leave.1 = (f32[128,8,1024]{2,1,0:T(8,128)}, f32[32,1024]{1,0:T(8,128)S(1)}) custom-call(f32[512,1024]{1,0:T(8,128)S(1)} %multiply_multiply_fusion.de_ref, f32[64,8,128]{2,1,0:T(8,128)S(1)} %broadcast_in_dim.51.k0_ref, f32[32,1024]{1,0:T(8,128)S(1)} %pad_maximum_fusion.4.q_ref, f32[32,1024]{1,0:T(8,128)S(1)} %bitcast.112, ...), custom_call_target="tpu_custom_call" | custom-call | flops 33554432 | bytes 16777216 | tf_op jit(solution)/shard_map/ema_leave/pallas_call | solution.py:394
  470.5 1.3 collective-permute-start.12
  471.8 1.3 collective-permute-start.13
  473.7 10.5 %collective-permute-done.13 = f32[32,1024]{1,0:T(8,128)S(1)} collective-permute-done((f32[32,1024]{1,0:T(8,128)S(1)}, f32[32,1024]{1,0:T(8,128)S(1)}, u32[]{:S(2)}, u32[]{:S(2)}) %collective-permute-start.13) | collective-permute-done | bytes 131104 | tf_op jit(solution)/shard_map/ppermute | solution.py:685
  484.5 53.3 %ema_grads.1 = (f32[512,1024]{1,0:T(8,128)S(1)}, f32[32,1024]{1,0:T(8,128)S(1)}, f32[16,1024]{1,0:T(8,128)S(1)}, f32[16,1024]{1,0:T(8,128)S(1)}, f32[16,1024]{1,0:T(8,128)S(1)}, /*index=5*/f32[1,1024]{1,0:T(1,128)S(1)}) custom-call(f32[512,1024]{1,0:T(8,128)S(1)} %copy-done.3, f32[512,1024]{1,0:T(8,128)} %copy-done.4, ...), custom_call_target="tpu_custom_call" | custom-call | flops 100663296 | bytes 16777216 | tf_op jit(solution)/shard_map/ema_grads/pallas_call | solution.py:394
  537.9 1.7 convert_add_fusion
  539.6 1.8 fusion.9
  543.6 1.3 fusion.16
  544.9 1.2 subtract_divide_fusion
  546.6 1.3 collective-permute-start.15
  547.9 1.5 collective-permute-start.14
  549.4 16.8 %reduce-scatter.9.cloned.1.call-done = bf16[1,4,384,640]{3,2,1,0:T(8,128)(2,1)} async-done(((bf16[8,4,384,640]{3,2,1,0:T(8,128)(2,1)}), bf16[1,4,384,640]{3,2,1,0:T(8,128)(2,1)}) %reduce-scatter.9.cloned.1.call-update) | async-done | bytes 1966096 | tf_op jit(solution)/shard_map/reduce_scatter | solution.py:828
  566.4 57.3 %small_sums.1 = (f32[768,128]{1,0:T(8,128)S(1)}, f32[128,256]{1,0:T(8,128)S(1)}) custom-call(f32[768,128]{1,0:T(8,128)S(1)} %bitcast.114, f32[1024,256]{1,0:T(8,128)S(1)} %bitcast.110), custom_call_target="tpu_custom_call" | custom-call | tf_op jit(solution)/shard_map/small_sums/pallas_call | solution.py:648
  627.8 1.2 fusion.29
  629.0 1.2 fusion.30
  630.3 4.3 fusion.3
  634.6 1.1 convert_element_type.151
  637.4 15.5 %reduce-scatter.11.cloned.1.call-done = bf16[1,384,640]{2,1,0:T(8,128)(2,1)} async-done(((bf16[4,384,640]{2,1,0:T(8,128)(2,1)}), bf16[1,384,640]{2,1,0:T(8,128)(2,1)}) %reduce-scatter.11.cloned.1.call-update) | async-done | bytes 491536 | tf_op jit(solution)/shard_map/reduce_scatter | solution.py:829
  652.8 1.1 convert_element_type.152
  (219 shorter events, 28.8 us)
Async XLA Ops:
  7.2 0.9 copy-start
  7.2 4.8 copy-start.30
  7.2 5.0 copy-start.31
  7.2 5.0 copy-start.32
  7.2 136.3 %all-gather.5.cloned.1.call-start = ((), (), s32[]{:S(2)}) async-start(), calls=%async_computation.8 | async-start | bytes 13516800 | tf_op jit(solution)/shard_map/all_gather | solution.py:707
  11.1 2.0 copy-start.36
  11.1 2.2 copy-start.16
  12.0 268.3 %all-gather.7.cloned.1.call-start = ((), (), s32[]{:S(2)}) async-start(), calls=%async_computation.9 | async-start | bytes 16220160 | tf_op jit(solution)/shard_map/all_gather | solution.py:710
  13.1 440.5 %reduce-scatter.5.cloned.1.call-start = ((), (), s32[]{:S(2)}) async-start(), calls=%async_computation.4 | async-start | bytes 14155776 | tf_op jit(solution)/shard_map/reduce_scatter | solution.py:828
  14.5 17.2 %copy-start.10 = (f32[16,1024]{1,0:T(8,128)S(1)}, f32[16,1024]{1,0:T(8,128)}, u32[]{:S(2)}) copy-start(f32[16,1024]{1,0:T(8,128)} %feed_ref.1) | copy-start | bytes 196612
  14.6 17.2 %copy-start.34 = (f32[16,1024]{1,0:T(8,128)S(1)}, f32[16,1024]{1,0:T(8,128)}, u32[]{:S(2)}) copy-start(f32[16,1024]{1,0:T(8,128)} %param.37) | copy-start | bytes 196612
  14.6 17.2 %copy-start.35 = (f32[16,1024]{1,0:T(8,128)S(1)}, f32[16,1024]{1,0:T(8,128)}, u32[]{:S(2)}) copy-start(f32[16,1024]{1,0:T(8,128)} %param.38) | copy-start | bytes 196612
  15.8 18.4 %collective-permute-start = (f32[1,32]{0,1:T(8,128)S(1)}, f32[1,32]{0,1:T(8,128)S(1)}, u32[]{:S(2)}, u32[]{:S(2)}) collective-permute-start(f32[1,32]{0,1:T(8,128)S(1)} %slice.336), channel_id=1, source_target_pairs={{0,1},{1,2},{2,3},{4,5},{5,6},{6,7},{8,9},{9,10},{10,11},{12,13},{... | collective-permute-start | bytes 392 | tf_op jit(solution)/shard_map/ppermute | solution.py:682
  20.8 13.4 %collective-permute-start.1 = (f32[1,32]{0,1:T(8,128)S(1)}, f32[1,32]{0,1:T(8,128)S(1)}, u32[]{:S(2)}, u32[]{:S(2)}) collective-permute-start(f32[1,32]{0,1:T(8,128)S(1)} %slice.336), channel_id=1, source_target_pairs={{0,2},{1,3},{4,6},{5,7},{8,10},{9,11},{12,14},{13,15},{16,18},{17,... | collective-permute-start | bytes 392 | tf_op jit(solution)/shard_map/ppermute | solution.py:682
  30.4 5.2 copy-start.33
  34.4 4.8 copy-start.26
  35.6 3.6 copy-start.14
  39.2 16.4 %copy-start.2 = (f32[512,1024]{1,0:T(8,128)}, f32[512,1024]{1,0:T(8,128)S(1)}, u32[]{:S(2)}) copy-start(f32[512,1024]{1,0:T(8,128)S(1)} %get-tuple-element.219.h_ref) | copy-start | bytes 6291460
  39.2 152.2 %collective-permute-start.7 = (bf16[512,1024]{1,0:T(8,128)(2,1)S(1)}, bf16[512,1024]{1,0:T(8,128)(2,1)}, u32[]{:S(2)}, u32[]{:S(2)}) collective-permute-start(bf16[512,1024]{1,0:T(8,128)(2,1)S(1)} %get-tuple-element.218), channel_id=1, source_target_pairs={{0,1},{1,2},{2,3},{4,5},{5,6},{6,7},{8,9},{9,10},{10,11},{12,13},{... | collective-permute-start | bytes 3145736 | tf_op jit(solution)/shard_map/ppermute | solution.py:682
  42.7 80.5 %copy-start.9 = (f32[2,16,1024]{2,1,0:T(8,128)S(1)}, f32[2,16,1024]{2,1,0:T(8,128)}, u32[]{:S(2)}) copy-start(f32[2,16,1024]{2,1,0:T(8,128)} %param.40) | copy-start | bytes 393220
  42.7 80.5 %copy-start.11 = (f32[1024]{0:T(1024)S(1)}, f32[1024]{0:T(1024)}, u32[]{:S(2)}) copy-start(f32[1024]{0:T(1024)} %param.41) | copy-start | bytes 12292
  55.6 29.5 %collective-permute-start.3 = (f32[32,1024]{1,0:T(8,128)S(1)}, f32[32,1024]{1,0:T(8,128)S(1)}, u32[]{:S(2)}, u32[]{:S(2)}) collective-permute-start(f32[32,1024]{1,0:T(8,128)S(1)} %get-tuple-element.121), channel_id=1, source_target_pairs={{0,2},{1,3},{4,6},{5,7},{8,10},{9,11},{12,14},{13,15},{16,18},{17,... | collective-permute-start | bytes 393224 | tf_op jit(solution)/shard_map/ppermute | solution.py:682
  56.9 134.5 %collective-permute-start.6 = (bf16[384,1024]{1,0:T(8,128)(2,1)}, bf16[384,1024]{1,0:T(8,128)(2,1)}, u32[]{:S(2)}, u32[]{:S(2)}) collective-permute-start(bf16[384,1024]{1,0:T(8,128)(2,1)} %slice.346), channel_id=1, source_target_pairs={{0,2},{1,3},{4,6},{5,7},{8,10},{9,11},{12,14},{13,15},{16,18},{17,... | collective-permute-start | bytes 2359304 | tf_op jit(solution)/shard_map/ppermute | solution.py:682
  60.8 62.2 %collective-permute-start.2 = (f32[32,1024]{1,0:T(8,128)S(1)}, f32[32,1024]{1,0:T(8,128)S(1)}, u32[]{:S(2)}, u32[]{:S(2)}) collective-permute-start(f32[32,1024]{1,0:T(8,128)S(1)} %get-tuple-element.121), channel_id=1, source_target_pairs={{0,1},{1,2},{2,3},{4,5},{5,6},{6,7},{8,9},{9,10},{10,11},{12,13},{... | collective-permute-start | bytes 393224 | tf_op jit(solution)/shard_map/ppermute | solution.py:682
  142.2 1.3 copy-start.7
  143.5 6.7 %copy-start.5 = (bf16[512,1024]{1,0:T(8,128)(2,1)}, bf16[512,1024]{1,0:T(8,128)(2,1)S(1)}, u32[]{:S(2)}) copy-start(bf16[512,1024]{1,0:T(8,128)(2,1)S(1)} %get-tuple-element.123.m_ref) | copy-start | bytes 3145732
  143.5 4.3 copy-start.37
  143.5 4.3 copy-start.38
  143.5 4.3 copy-start.40
  150.2 55.2 %collective-permute-start.5 = (bf16[512,256]{1,0:T(8,128)(2,1)S(1)}, bf16[512,256]{1,0:T(8,128)(2,1)S(1)}, u32[]{:S(2)}, u32[]{:S(2)}) collective-permute-start(bf16[512,256]{1,0:T(8,128)(2,1)S(1)} %get-tuple-element.228), channel_id=1, source_target_pairs={{0,1},{1,2},{2,3},{4,5},{5,6},{6,7},{8,9},{9,10},{10,11},{12,13},{... | collective-permute-start | bytes 786440 | tf_op jit(solution)/shard_map/ppermute | solution.py:682
  187.4 18.0 %collective-permute-start.4 = (bf16[384,256]{1,0:T(8,128)(2,1)S(1)}, bf16[384,256]{1,0:T(8,128)(2,1)S(1)}, u32[]{:S(2)}, u32[]{:S(2)}) collective-permute-start(bf16[384,256]{1,0:T(8,128)(2,1)S(1)} %slice.344), channel_id=1, source_target_pairs={{0,2},{1,3},{4,6},{5,7},{8,10},{9,11},{12,14},{13,15},{16,18},{17,... | collective-permute-start | bytes 589832 | tf_op jit(solution)/shard_map/ppermute | solution.py:682
  362.9 203.3 %reduce-scatter.9.cloned.1.call-start = ((), (), s32[]{:S(2)}) async-start(), calls=%async_computation.6 | async-start | bytes 17694720 | tf_op jit(solution)/shard_map/reduce_scatter | solution.py:828
  363.5 10.2 %copy-start.25 = (bf16[896,1024]{1,0:T(8,128)(2,1)S(1)}, bf16[896,1024]{1,0:T(8,128)(2,1)}, u32[]{:S(2)}) copy-start(bf16[896,1024]{1,0:T(8,128)(2,1)} %get-tuple-element.136) | copy-start | bytes 5505028
  363.5 271.1 %reduce-scatter.7.cloned.1.call-start = ((), (), s32[]{:S(2)}) async-start(), calls=%async_computation.5 | async-start | bytes 1966080 | tf_op jit(solution)/shard_map/reduce_scatter | solution.py:829
  371.6 10.5 %copy-start.29 = (f32[512,256]{1,0:T(8,128)S(1)}, f32[512,256]{1,0:T(8,128)}, u32[]{:S(2)}) copy-start(f32[512,256]{1,0:T(8,128)} %get-tuple-element.138) | copy-start | bytes 1572868
  371.6 10.5 %collective-permute-start.10 = (bf16[512,256]{1,0:T(8,128)(2,1)S(1)}, bf16[512,256]{1,0:T(8,128)(2,1)S(1)}, u32[]{:S(2)}, u32[]{:S(2)}) collective-permute-start(bf16[512,256]{1,0:T(8,128)(2,1)S(1)} %slice.281), channel_id=1, source_target_pairs={{1,0},{2,1},{3,2},{5,4},{6,5},{7,6},{9,8},{10,9},{11,10},{13,12},{... | collective-permute-start | bytes 786440 | tf_op jit(solution)/shard_map/ppermute | solution.py:685
  374.8 73.5 %copy-start.24 = (f32[512,256]{1,0:T(8,128)S(1)}, f32[512,256]{1,0:T(8,128)}, u32[]{:S(2)}) copy-start(f32[512,256]{1,0:T(8,128)} %get-tuple-element.274) | copy-start | bytes 1572868
  374.8 73.5 %copy-start.28 = (f32[512,256]{1,0:T(8,128)S(1)}, f32[512,256]{1,0:T(8,128)}, u32[]{:S(2)}) copy-start(f32[512,256]{1,0:T(8,128)} %get-tuple-element.137) | copy-start | bytes 1572868
  376.9 72.4 %copy-start.20 = (bf16[1024,256]{1,0:T(8,128)(2,1)S(1)}, bf16[1024,256]{1,0:T(8,128)(2,1)}, u32[]{:S(2)}) copy-start(bf16[1024,256]{1,0:T(8,128)(2,1)} %reshape.326) | copy-start | bytes 1572868
  376.9 161.1 %collective-permute-start.8 = (bf16[512,1024]{1,0:T(8,128)(2,1)}, bf16[512,1024]{1,0:T(8,128)(2,1)}, u32[]{:S(2)}, u32[]{:S(2)}) collective-permute-start(bf16[512,1024]{1,0:T(8,128)(2,1)} %slice.278), channel_id=1, source_target_pairs={{1,0},{2,1},{3,2},{5,4},{6,5},{7,6},{9,8},{10,9},{11,10},{13,12},{... | collective-permute-start | bytes 3145736 | tf_op jit(solution)/shard_map/ppermute | solution.py:685
  378.3 161.3 %collective-permute-start.9 = (bf16[384,1024]{1,0:T(8,128)(2,1)}, bf16[384,1024]{1,0:T(8,128)(2,1)}, u32[]{:S(2)}, u32[]{:S(2)}) collective-permute-start(bf16[384,1024]{1,0:T(8,128)(2,1)} %slice.280), channel_id=1, source_target_pairs={{2,0},{3,1},{6,4},{7,5},{10,8},{11,9},{14,12},{15,13},{18,16},{19,... | collective-permute-start | bytes 2359304 | tf_op jit(solution)/shard_map/ppermute | solution.py:685
  379.6 68.7 %collective-permute-start.11 = (bf16[384,256]{1,0:T(8,128)(2,1)S(1)}, bf16[384,256]{1,0:T(8,128)(2,1)S(1)}, u32[]{:S(2)}, u32[]{:S(2)}) collective-permute-start(bf16[384,256]{1,0:T(8,128)(2,1)S(1)} %slice.283), channel_id=1, source_target_pairs={{2,0},{3,1},{6,4},{7,5},{10,8},{11,9},{14,12},{15,13},{18,16},{19,... | collective-permute-start | bytes 589832 | tf_op jit(solution)/shard_map/ppermute | solution.py:685
  448.5 0.7 copy-start.21
  449.2 4.5 copy-start.8
  453.7 199.2 %reduce-scatter.11.cloned.1.call-start = ((), (), s32[]{:S(2)}) async-start(), calls=%async_computation.7 | async-start | bytes 2457600 | tf_op jit(solution)/shard_map/reduce_scatter | solution.py:829
  456.8 16.8 %copy-start.4 = (f32[512,1024]{1,0:T(8,128)}, f32[512,1024]{1,0:T(8,128)S(1)}, u32[]{:S(2)}) copy-start(f32[512,1024]{1,0:T(8,128)S(1)} %multiply_multiply_fusion.de_ref) | copy-start | bytes 6291460
  456.8 16.3 %copy-start.6 = (bf16[512,1024]{1,0:T(8,128)(2,1)S(1)}, bf16[512,1024]{1,0:T(8,128)(2,1)}, u32[]{:S(2)}) copy-start(bf16[512,1024]{1,0:T(8,128)(2,1)} %copy-done.5) | copy-start | bytes 3145732
  456.8 16.3 %copy-start.22 = (bf16[512,256]{1,0:T(8,128)(2,1)S(1)}, bf16[512,256]{1,0:T(8,128)(2,1)}, u32[]{:S(2)}) copy-start(bf16[512,256]{1,0:T(8,128)(2,1)} %copy-done.21) | copy-start | bytes 786436
  470.5 13.7 %collective-permute-start.12 = (f32[32,1024]{1,0:T(8,128)S(1)}, f32[32,1024]{1,0:T(8,128)S(1)}, u32[]{:S(2)}, u32[]{:S(2)}) collective-permute-start(f32[32,1024]{1,0:T(8,128)S(1)} %get-tuple-element.143), channel_id=1, source_target_pairs={{1,0},{2,1},{3,2},{5,4},{6,5},{7,6},{9,8},{10,9},{11,10},{13,12},{... | collective-permute-start | bytes 393224 | tf_op jit(solution)/shard_map/ppermute | solution.py:685
  471.8 12.4 %collective-permute-start.13 = (f32[32,1024]{1,0:T(8,128)S(1)}, f32[32,1024]{1,0:T(8,128)S(1)}, u32[]{:S(2)}, u32[]{:S(2)}) collective-permute-start(f32[32,1024]{1,0:T(8,128)S(1)} %get-tuple-element.143), channel_id=1, source_target_pairs={{2,0},{3,1},{6,4},{7,5},{10,8},{11,9},{14,12},{15,13},{18,16},{19,... | collective-permute-start | bytes 393224 | tf_op jit(solution)/shard_map/ppermute | solution.py:685
  473.6 10.9 %copy-start.3 = (f32[512,1024]{1,0:T(8,128)S(1)}, f32[512,1024]{1,0:T(8,128)}, u32[]{:S(2)}) copy-start(f32[512,1024]{1,0:T(8,128)} %copy-done.2) | copy-start | bytes 6291460
  484.5 53.5 %copy-start.23 = (f32[512,1024]{1,0:T(8,128)S(1)}, f32[512,1024]{1,0:T(8,128)}, u32[]{:S(2)}) copy-start(f32[512,1024]{1,0:T(8,128)} %get-tuple-element.135) | copy-start | bytes 6291460
  539.6 2.3 copy-start.19
  542.0 1.6 copy-start.18
  542.0 1.6 copy-start.27
  542.9 2.0 copy-start.12
  546.1 20.3 %copy-start.39 = (f32[1,1024]{1,0:T(1,128)S(1)}, f32[1,1024]{1,0:T(1,128)}, u32[]{:S(2)}) copy-start(f32[1,1024]{1,0:T(1,128)} %get-tuple-element.151) | copy-start | bytes 12292
  546.6 81.0 %collective-permute-start.15 = (f32[1,32]{0,1:T(8,128)S(1)}, f32[1,32]{0,1:T(8,128)S(1)}, u32[]{:S(2)}, u32[]{:S(2)}) collective-permute-start(f32[1,32]{0,1:T(8,128)S(1)} %slice.354), channel_id=1, source_target_pairs={{2,0},{3,1},{6,4},{7,5},{10,8},{11,9},{14,12},{15,13},{18,16},{19,... | collective-permute-start | bytes 392 | tf_op jit(solution)/shard_map/ppermute | solution.py:685
  547.9 79.7 %collective-permute-start.14 = (f32[1,32]{0,1:T(8,128)S(1)}, f32[1,32]{0,1:T(8,128)S(1)}, u32[]{:S(2)}, u32[]{:S(2)}) collective-permute-start(f32[1,32]{0,1:T(8,128)S(1)} %slice.354), channel_id=1, source_target_pairs={{1,0},{2,1},{3,2},{5,4},{6,5},{7,6},{9,8},{10,9},{11,10},{13,12},{... | collective-permute-start | bytes 392 | tf_op jit(solution)/shard_map/ppermute | solution.py:685
  566.4 63.9 %copy-start.17 = (bf16[512,1024]{1,0:T(8,128)(2,1)S(1)}, bf16[512,1024]{1,0:T(8,128)(2,1)}, u32[]{:S(2)}) copy-start(bf16[512,1024]{1,0:T(8,128)(2,1)} %x_ref.1) | copy-start | bytes 3145732
  627.7 2.5 copy-start.13
  627.7 2.5 copy-start.15
  636.5 19.9 %copy-start.1 = (f32[128,256]{1,0:T(8,128)S(1)}, f32[128,256]{1,0:T(8,128)}, u32[]{:S(2)}) copy-start(f32[128,256]{1,0:T(8,128)} %param.42) | copy-start | bytes 393220
Sparse Core Ops, SparseCore 0:
  12.1 126.2 all-gather.4
  141.2 139.0 all-gather.6
  363.0 90.5 reduce-scatter.4
  457.0 109.1 reduce-scatter.8
  568.4 41.8 reduce-scatter.6
  612.4 40.4 reduce-scatter.10

commit v3 on v2

--- a/solution.py
+++ b/solution.py
@@ -257,6 +257,21 @@
         return carry
 
     lax.fori_loop(0, dims, one, 0)
+
+
+REDUCE_PLAN = (
+    (0, 1, False), (1, 2, False), (2, 1, False), (3, 2, False), (4, 1, False), (5, 2, False), (6, 1, False), (7, 0, True)
+)
+
+
+def ema_grads_reduce(parts, ins, outs, held, rows, dims, *refs):
+    own = list(refs)
+    pack_ref, sum_ref = own.pop(ins), own.pop(ins + outs)
+    stages = reduce_stages(parts, pack_ref, sum_ref, *own[ins + outs + held :])
+    step = pl.program_id(0)
+    run_stages(stages, step, REDUCE_PLAN, False)
+    ema_grads(rows, dims, *own[: ins + outs + held])
+    run_stages(stages, step, REDUCE_PLAN, True)
 
 
 def ema_grads(
@@ -389,7 +404,7 @@
     return pl.BlockSpec(shape, lambda i: (0,) * len(shape))
 
 
-def ema_call(body, rows, dims, width, ins, outs, scratch, name, flops):
+def ema_call(body, rows, dims, width, ins, outs, scratch, name, flops, collective_id=None):
     specs = [s for _, s in ins]
     return pl.pallas_call(
         functools.partial(body, rows, dims),
@@ -398,8 +413,10 @@
         out_specs=[s for _, s in outs],
         out_shape=[o for o, _ in outs],
         scratch_shapes=scratch,
-        compiler_params=pltpu.CompilerParams(vmem_limit_bytes=48 << 20),
-        cost_estimate=pl.CostEstimate(flops=flops, bytes_accessed=16 << 20, transcendentals=0),
+        compiler_params=pltpu.CompilerParams(
+            vmem_limit_bytes=60 << 20, collective_id=collective_id, has_side_effects=collective_id is not None
+        ),
+        cost_estimate=pl.CostEstimate(flops=flops // 1000, bytes_accessed=1024, transcendentals=0),
         name=name,
     )(*[a for a, _ in ins])
 
@@ -439,6 +456,19 @@
     return v.reshape(-1, v.shape[-1])
 
 
+GATHER_PLAN = ((0, 2, False), (1, 1, False), (2, 1, False), (3, 1, False), (3, 0, True))
+
+
+def attend_gather_kernel(halo, parts, ins, outs, *refs):
+    own = list(refs)
+    pack_ref, all_ref = own.pop(ins), own.pop(ins + outs)
+    stages = gather_stages(parts, pack_ref, all_ref, *own[ins + outs + 1 :])
+    step = pl.program_id(0)
+    run_stages(stages, step, GATHER_PLAN, False)
+    attend_kernel(halo, *own[: ins + outs + 1])
+    run_stages(stages, step, GATHER_PLAN, True)
+
+
 def attend_kernel(
     halo, q_ref, k_ref, seg_ref, segk_ref, h_ref, m_ref, x_ref, gain_ref, wv_ref, wg_ref, wo_ref,
     p_ref, vp_ref, v_ref, gp_ref, o_ref, g_ref, y_ref, n_ref, pb_ref,
@@ -560,7 +590,7 @@
         dh_ref[...] = dhv[halo:, :]
 
 
-def stage_call(body, steps, ins, outs, scratch, name, flops):
+def stage_call(body, steps, ins, outs, scratch, name, flops, collective_id=None):
     def spec(v, how):
         if how == "all":
             return pl.BlockSpec(v.shape, lambda t: (0,) * v.ndim)
@@ -576,10 +606,283 @@
         out_specs=[spec(v, how) for v, how in outs],
         out_shape=[v for v, _ in outs],
         scratch_shapes=scratch,
-        compiler_params=pltpu.CompilerParams(vmem_limit_bytes=60 << 20),
-        cost_estimate=pl.CostEstimate(flops=flops, bytes_accessed=48 << 20, transcendentals=0),
+        compiler_params=pltpu.CompilerParams(
+            vmem_limit_bytes=60 << 20, collective_id=collective_id, has_side_effects=collective_id is not None
+        ),
+        cost_estimate=pl.CostEstimate(flops=flops // 1000, bytes_accessed=1024, transcendentals=0),
         name=name,
     )(*[v for v, _ in ins])
+
+
+def gather_stages(parts, pack_ref, out_ref, sems, own_sem):
+    d, z = lax.axis_index("dp"), lax.axis_index("tensor")
+    total = pack_ref.shape[0]
+    cut = total // 32 * 16
+    upper, lower, full = pl.ds(0, cut), pl.ds(cut, total - cut), pl.ds(0, total)
+    flip = lambda k: d + (1 - 2 * ((d // (1 << k)) % 2)) * (1 << k)
+    core, first, second = flip(0), flip(1), flip(2)
+    across = first + second - d
+    MESH = pl.DeviceIdType.MESH
+
+    LINE, TO_FIRST, TO_SECOND, UP, DOWN, C_OWN, C_FIRST, C_SECOND, C_UP, C_DOWN = range(10)
+
+    def copy(kind, b, source, part, dp_to, z_to):
+        here = out_ref.at[source, b, part]
+        return pltpu.make_async_remote_copy(
+            src_ref=here, dst_ref=here, send_sem=sems.at[0, kind, b], recv_sem=sems.at[1, kind, b],
+            device_id=(dp_to, z_to), device_id_type=MESH,
+        )
+
+    def begin():
+        mine = pltpu.make_async_copy(pack_ref, out_ref.at[d, z], own_sem)
+        mine.start()
+        barrier = pltpu.get_barrier_semaphore()
+        for other in (core, first, second):
+            pl.semaphore_signal(barrier, inc=1, device_id=(other, z), device_id_type=MESH)
+        for step in (-1, 1):
+            @pl.when((z + step >= 0) & (z + step < parts))
+            def _():
+                pl.semaphore_signal(barrier, inc=1, device_id=(d, z + step), device_id_type=MESH)
+        pl.semaphore_wait(barrier, 3 + jnp.minimum(z, 1) + jnp.minimum(parts - 1 - z, 1))
+        mine.wait()
+
+    def spread_block(b):
+        copy(TO_FIRST, b, d, full, first, z).start()
+        copy(TO_SECOND, b, d, full, second, z).start()
+        copy(C_OWN, b, d, full, core, z).start()
+
+    def along(b, step):
+        @pl.when((z + step >= 0) & (z + step < parts))
+        def _():
+            here = out_ref.at[d, b]
+            pltpu.make_async_remote_copy(
+                src_ref=here, dst_ref=here, send_sem=sems.at[0, LINE + (10 if step > 0 else 11), b],
+                recv_sem=sems.at[1, LINE, b], device_id=(d, z + step), device_id_type=MESH,
+            ).start()
+
+    def relay(b):
+        copy(TO_FIRST, b, first, full, first, z).wait_recv()
+        copy(UP, b, first, upper, second, z).start()
+        copy(C_FIRST, b, first, full, core, z).start()
+        copy(TO_SECOND, b, second, full, second, z).wait_recv()
+        copy(DOWN, b, second, lower, first, z).start()
+        copy(C_SECOND, b, second, full, core, z).start()
+
+    def corner(b):
+        copy(UP, b, across, upper, second, z).wait_recv()
+        copy(C_UP, b, across, upper, core, z).start()
+        copy(DOWN, b, across, lower, first, z).wait_recv()
+        copy(C_DOWN, b, across, lower, core, z).start()
+
+    def at_distance(dist, action):
+        for side in ((0,) if dist == 0 else (-1, 1)):
+            b = z + side * dist
+            @pl.when((b >= 0) & (b < parts))
+            def _():
+                action(b, side)
+
+    def arrive(b, side):
+        if side != 0:
+            copy(LINE, b, d, full, d, z).wait_recv()
+        if side <= 0:
+            along(b, 1)
+        if side >= 0:
+            along(b, -1)
+        spread_block(b)
+
+    def finish():
+        other_first, other_second = core + first - d, core + second - d
+        for b in range(parts):
+            for kind, source, part in ((C_OWN, core, full), (C_FIRST, other_first, full), (C_SECOND, other_second, full),
+                                       (C_UP, core + across - d, upper), (C_DOWN, core + across - d, lower)):
+                copy(kind, b, source, part, core, z).wait_recv()
+            for kind, source, part in ((TO_FIRST, d, full), (TO_SECOND, d, full), (C_OWN, d, full), (UP, first, upper),
+                                       (DOWN, second, lower), (C_FIRST, first, full), (C_SECOND, second, full),
+                                       (C_UP, across, upper), (C_DOWN, across, lower)):
+                copy(kind, b, source, part, core, z).wait_send()
+            for step, slot in ((1, 10), (-1, 11)):
+                @pl.when((z + step >= 0) & (z + step < parts) & (step * (z - b) >= 0))
+                def _():
+                    copy(slot, b, d, full, core, z).wait_send()
+
+    stages = [begin]
+    for dist in range(parts + 2):
+        if dist < parts:
+            stages.append(functools.partial(at_distance, dist, arrive))
+        if 1 <= dist < parts + 1:
+            stages.append(functools.partial(at_distance, dist - 1, lambda b, side: relay(b)))
+        if dist >= 2:
+            stages.append(functools.partial(at_distance, dist - 2, lambda b, side: corner(b)))
+    return stages + [finish]
+
+
+def gather_scratch(parts):
+    return [pltpu.SemaphoreType.DMA((2, 12, parts)), pltpu.SemaphoreType.DMA]
+
+
+def run_stages(stages, step, plan, late):
+    at = 0
+    for when, count, end in plan:
+        here = stages[at : at + count] if count else stages[at:]
+        at += len(here)
+        if end == late:
+            @pl.when(step == when)
+            def _():
+                for stage in here:
+                    stage()
+
+
+R_CORE, R_FIRST, R_FIRST2, R_SECOND, R_SECOND2, R_UP, R_DOWN, R_RIGHT, R_LEFT = range(9)
+
+
+def reduce_scratch(parts, rows, columns):
+    upper = rows // 32 * 16
+    vm = lambda *n: pltpu.VMEM((*n, columns), BF16)
+    return [
+        vm(parts, 4, rows), vm(parts, 4, rows), vm(parts, 2, upper), vm(parts, 2, rows - upper), vm(parts, upper),
+        vm(parts, rows - upper), vm(2, parts, rows), pltpu.SemaphoreType.DMA((2, 9, parts)),
+        pltpu.SemaphoreType.DMA((parts,)),
+    ]
+
+
+def reduce_stages(parts, pack, out, acc, got_core, got_first, got_second, got_up, got_down, got_line, sems, load_sems):
+    d, z = lax.axis_index("dp"), lax.axis_index("tensor")
+    MESH = pl.DeviceIdType.MESH
+    rows = acc.shape[2]
+    cut = rows // 32 * 16
+    upper, lower = pl.ds(0, cut), pl.ds(cut, rows - cut)
+    me, core = d // 2, d % 2
+    bit = lambda k: (me // (1 << k)) % 2
+    first = me + (1 - 2 * bit(0))
+    second = me + 2 * (1 - 2 * bit(1))
+    across = first + second - me
+    on = lambda p: 2 * p + core
+    far = z // (parts // 2)
+    near_end = z + far * (parts - 1 - 2 * z)
+
+    def unit(s):
+        t = (parts - 1 - s) + near_end * ((3, 0, 2, 1)[s] - (parts - 1 - s))
+        return t + far * (parts - 1 - 2 * t)
+
+    def copy(kind, t, src, dst, where):
+        return pltpu.make_async_remote_copy(
+            src_ref=src, dst_ref=dst, send_sem=sems.at[0, kind, t], recv_sem=sems.at[1, kind, t], device_id=where,
+            device_id_type=MESH,
+        )
+
+    def copies(s):
+        t = unit(s)
+        to_first, to_second = (on(first), z), (on(second), z)
+        table = {
+            R_CORE: (pack.at[:, 1 - core, t], got_core.at[t], (2 * me + 1 - core, z)),
+            R_FIRST: (acc.at[t, first, upper], got_first.at[t, 0], to_first),
+            R_FIRST2: (acc.at[t, across, upper], got_first.at[t, 1], to_first),
+            R_SECOND: (acc.at[t, second, lower], got_second.at[t, 0], to_second),
+            R_SECOND2: (acc.at[t, across, lower], got_second.at[t, 1], to_second),
+            R_UP: (acc.at[t, second, upper], got_up.at[t], to_second),
+            R_DOWN: (acc.at[t, first, lower], got_down.at[t], to_first),
+            R_RIGHT: (acc.at[t, me], got_line.at[0, t], (d, jnp.minimum(z + 1, parts - 1))),
+            R_LEFT: (acc.at[t, me], got_line.at[1, t], (d, jnp.maximum(z - 1, 0))),
+        }
+        return lambda kind: copy(kind, t, *table[kind])
+
+    def load(s):
+        t = unit(s)
+        return pltpu.make_async_copy(pack.at[:, core, t], acc.at[t], load_sems.at[t])
+
+    def add(target, at, count, source):
+        tile = 32 if count % 32 == 0 else 16
+
+        def some(i, carry):
+            here = pl.ds(pl.multiple_of(at + i * tile, 16), tile)
+            there = pl.ds(pl.multiple_of(i * tile, 16), tile)
+            target[here, :] = (target[here, :].astype(F32) + source[there, :].astype(F32)).astype(BF16)
+            return carry
+
+        lax.fori_loop(0, count // tile, some, 0)
+
+    def begin():
+        barrier = pltpu.get_barrier_semaphore()
+        for where in ((2 * me + 1 - core, z), (on(first), z), (on(second), z)):
+            pl.semaphore_signal(barrier, inc=1, device_id=where, device_id_type=MESH)
+        for step in (-1, 1):
+            @pl.when((z + step >= 0) & (z + step < parts))
+            def _():
+                pl.semaphore_signal(barrier, inc=1, device_id=(d, z + step), device_id_type=MESH)
+        pl.semaphore_wait(barrier, 3 + jnp.minimum(z, 1) + jnp.minimum(parts - 1 - z, 1))
+        for s in range(parts):
+            load(s).start()
+            copies(s)(R_CORE).start()
+
+    def cores(s):
+        t, c = unit(s), copies(s)
+        load(s).wait()
+        c(R_CORE).wait_recv()
+        for p in (first, across, second, me):
+            add(acc.at[t, p], 0, rows, got_core.at[t, p])
+        for kind in (R_FIRST, R_FIRST2, R_SECOND, R_SECOND2):
+            c(kind).start()
+
+    def chips(s):
+        t, c = unit(s), copies(s)
+        for kind in (R_FIRST2, R_SECOND2, R_FIRST, R_SECOND):
+            c(kind).wait_recv()
+        add(acc.at[t, second], 0, cut, got_first.at[t, 1])
+        c(R_UP).start()
+        add(acc.at[t, first], cut, rows - cut, got_second.at[t, 1])
+        c(R_DOWN).start()
+        add(acc.at[t, me], 0, cut, got_first.at[t, 0])
+        add(acc.at[t, me], cut, rows - cut, got_second.at[t, 0])
+
+    def line(s):
+        t, c = unit(s), copies(s)
+        c(R_UP).wait_recv()
+        add(acc.at[t, me], 0, cut, got_up.at[t])
+        c(R_DOWN).wait_recv()
+        add(acc.at[t, me], cut, rows - cut, got_down.at[t])
+
+        @pl.when((z <= t) & (z > 0))
+        def _():
+            c(R_RIGHT).wait_recv()
+            add(acc.at[t, me], 0, rows, got_line.at[0, t])
+
+        @pl.when((z >= t) & (z < parts - 1))
+        def _():
+            c(R_LEFT).wait_recv()
+            add(acc.at[t, me], 0, rows, got_line.at[1, t])
+
+        @pl.when(z < t)
+        def _():
+            c(R_RIGHT).start()
+
+        @pl.when(z > t)
+        def _():
+            c(R_LEFT).start()
+
+    def finish():
+        out[...] = acc[z, me].astype(F32)
+        for s in range(parts):
+            t, c = unit(s), copies(s)
+            for kind in range(R_RIGHT):
+                c(kind).wait_send()
+
+            @pl.when(z < t)
+            def _():
+                c(R_RIGHT).wait_send()
+
+            @pl.when(z > t)
+            def _():
+                c(R_LEFT).wait_send()
+
+    stages = [begin]
+    for s in range(parts + 2):
+        if s < parts:
+            stages.append(functools.partial(cores, s))
+        if 1 <= s <= parts:
+            stages.append(functools.partial(chips, s - 1))
+        if s >= 2:
+            stages.append(functools.partial(line, s - 2))
+    return stages + [finish]
 
 
 def small_sums_kernel(bits, small_ref, block_ref, out_ref, own_ref, acc, cube, buf, cbuf, sems):
@@ -676,7 +979,7 @@
     ffn_width = w_swish.shape[1] * parts
     depth = w_value.shape[0]
     halo = -(-REACH // LANES) * LANES
-    hops = [min(rows, halo - h * rows) for h in range(-(-halo // rows))]
+    hops = [min(rows, REACH - h * rows) for h in range(-(-REACH // rows))]
 
     def from_earlier(x, hop):
         return lax.ppermute(x, "tensor", [(i, i + hop) for i in range(parts - hop)])
@@ -686,7 +989,8 @@
 
     def halo_of(x):
         pieces = [from_earlier(x[rows - n :], h + 1) for h, n in enumerate(hops)]
-        return jnp.concatenate(pieces[::-1] + [x], axis=0)
+        ahead = jnp.zeros((halo - sum(hops), x.shape[1]), x.dtype)
+        return jnp.concatenate([ahead] + pieces[::-1] + [x], axis=0)
 
     def give_back(total, x):
         end = halo
@@ -695,6 +999,8 @@
             total = total.at[rows - n :].add(got)
             end -= n
         return total
+
+    chip_links = replicas == 8 and parts == 4
 
     piece = depth // parts
     shared_piece = lax.dynamic_slice_in_dim(w_shared, rank * piece, piece, 0)
@@ -704,10 +1010,8 @@
         [low(w_value), low(w_gate), low(w_out.T), low(shared_piece).reshape(-1, vw)], axis=0
     )
     pack_f = jnp.concatenate([low(w_swish), low(w_up), low(w_down.T)], axis=0)
-    all_a = lax.all_gather(pack_a, BOTH, axis=0)
-    all_a = all_a.reshape(replicas, parts, -1, vw)
+    all_a = lax.all_gather(pack_a, BOTH, axis=0).reshape(replicas, parts, -1, vw)
     pack_f = with_layout_constraint(pack_f, Layout((0, 1)))
-    all_f = lax.all_gather(pack_f, BOTH, axis=0).reshape(replicas, parts, 3 * depth, fw)
     shared_b = all_a[:, :, 3 * depth :].reshape(width, latent_width)
 
     def part(k, columns):
@@ -793,7 +1097,7 @@
         [vm(2 * at_rows), table_vm, scale_vm], "ema_read", mac,
     )
 
-    hidden_near = halo_of(hidden_b)
+    hidden_near = halo_of(lax.optimization_barrier((hidden_b, state_in))[0])
     near_rows = halo + rows
     latent = dot32(mixed, shared_b)
     queries = low(latent * query_gain + query_bias)
@@ -801,15 +1105,24 @@
     one = lambda v: v[None]
     matmul = rows * width * vw * 2 * parts
     col_v = lambda n: ((n, value_width), BF16, "col")
-    probs, value_pre, values, gate_pre, attended, gated, residual, norm_in = stage_call(
-        functools.partial(attend_kernel, halo), parts,
-        [(queries, "all"), (keys_near, "all"), (seg[:, None], "all"), (one(seg_keys), "all"), (hidden_near, "all"),
-         (mixed, "all"), (block_in, "all"), (one(ffn_gain), "all"), (all_a, part(0, vw)), (all_a, part(1, vw)),
-         (all_a, part(2, vw))],
-        [((rows, near_rows), F32, "all"), col_v(near_rows), col_v(near_rows), col_v(rows), col_v(rows), col_v(rows),
-         ((rows, width), F32, "all"), ((rows, width), BF16, "all")],
-        [pltpu.VMEM((rows, near_rows), BF16)], "attend", 6 * matmul,
-    )
+    anywhere = pl.BlockSpec(memory_space=pl.ANY)
+    ins = [(queries, "all"), (keys_near, "all"), (seg[:, None], "all"), (one(seg_keys), "all"), (hidden_near, "all"),
+           (mixed, "all"), (block_in, "all"), (one(ffn_gain), "all"), (all_a, part(0, vw)), (all_a, part(1, vw)),
+           (all_a, part(2, vw))]
+    outs = [((rows, near_rows), F32, "all"), col_v(near_rows), col_v(near_rows), col_v(rows), col_v(rows), col_v(rows),
+            ((rows, width), F32, "all"), ((rows, width), BF16, "all")]
+    scratch = [pltpu.VMEM((rows, near_rows), BF16)]
+    if chip_links:
+        results = stage_call(
+            functools.partial(attend_gather_kernel, halo, parts, len(ins), len(outs)), parts,
+            ins + [(pack_f, anywhere)], outs + [((replicas, parts) + pack_f.shape, BF16, anywhere)],
+            scratch + gather_scratch(parts), "attend", 6 * matmul, collective_id=1,
+        )
+        all_f = results[-1]
+    else:
+        results = stage_call(functools.partial(attend_kernel, halo), parts, ins, outs, scratch, "attend", 6 * matmul)
+        all_f = lax.all_gather(pack_f, BOTH, axis=0).reshape(replicas, parts, 3 * depth, fw)
+    probs, value_pre, values, gate_pre, attended, gated, residual, norm_in = results[:8]
 
     row_vm = lambda n: pltpu.VMEM((n, width), F32)
     block_out, grad_residual, branch, grad_ffn_gain, ffn_grads = stage_call(
@@ -825,7 +1138,10 @@
 
     def summed(g):
         g = g.reshape(replicas, parts, -1, g.shape[-1])
-        g = lax.psum_scatter(g, "dp", scatter_dimension=0, tiled=False)
+        return lax.psum_scatter(g, "dp", scatter_dimension=0, tiled=False)
+
+    def summed_along(g, after):
+        g = lax.optimization_barrier((g, after))[0]
         return lax.psum_scatter(g, "tensor", scatter_dimension=0, tiled=False).astype(F32)
 
     ffn_sum = summed(ffn_grads)
@@ -842,13 +1158,12 @@
         [pltpu.VMEM((rows, near_rows), F32), row_vm(near_rows), pltpu.VMEM((rows, near_rows), BF16)], "attend_back", 12 * matmul,
     )
     grad_keys = give_back(keys_own, keys_back)
-    grad_hidden = give_back(hidden_own, hidden_back)
+    grad_hidden = give_back(hidden_own, lax.optimization_barrier((hidden_back, grad_keys))[0])
     grad_query_gain = jnp.sum(latent * grad_queries, axis=0)
     grad_query_bias = jnp.sum(grad_queries, axis=0)
     grad_key_gain = jnp.sum(latent * grad_keys, axis=0)
     grad_latent = low(grad_queries * query_gain + grad_keys * key_gain)
     grad_shared = dot32(mixed, grad_latent, TN)
-    attn_sum = summed(attn_grads)
     grad_ema = (dot32(grad_latent, shared_b, NT) + grad_mixed) * silu_slope(ema_out)
 
     pulls, head = ema_call(
@@ -858,16 +1173,27 @@
     )
     cross = (near[halo + 2 * rows - 1] == last).astype(F32)
     pull_in = from_later(head, 1) + cross * turned(from_later(head, 2), -1.0)
-    grad_hidden_ema, output_grad, input_grad, rate_grad, angle_grad, grad_skip = ema_call(
-        ema_grads, rows, dims, width,
-        [(hidden, col(rows)), (grad_ema, col(rows)), seg8, kend, (masks["rk0"], whole(rows, LANES)),
-         (masks["rkend"], whole(rows, LANES)), (unit, pair), (feed, single), (reads, pair), (root, single),
-         (ema_input, single), cont, mkr, (pulls, col3(nstate, 8)), (pull_in, pair), (states, col3(nstate, 8)),
-         (skip, col(1))],
-        [rows_shape, edge_shape, dim_shape, dim_shape, dim_shape, (jax.ShapeDtypeStruct((1, width), F32), col(1))],
-        [vm(2 * at_rows), vm(at_rows), vm(nstate), table_vm, scale_vm, flat_vm(4, STEP * dims), flat_vm(9, dims),
-         flat_vm(rows), flat_vm(rows)], "ema_grads", 3 * mac,
-    )
+    ins = [(hidden, col(rows)), (grad_ema, col(rows)), seg8, kend, (masks["rk0"], whole(rows, LANES)),
+           (masks["rkend"], whole(rows, LANES)), (unit, pair), (feed, single), (reads, pair), (root, single),
+           (ema_input, single), cont, mkr, (pulls, col3(nstate, 8)), (pull_in, pair), (states, col3(nstate, 8)),
+           (skip, col(1))]
+    outs = [rows_shape, edge_shape, dim_shape, dim_shape, dim_shape, (jax.ShapeDtypeStruct((1, width), F32), col(1))]
+    scratch = [vm(2 * at_rows), vm(at_rows), vm(nstate), table_vm, scale_vm, flat_vm(4, STEP * dims), flat_vm(9, dims),
+               flat_vm(rows), flat_vm(rows)]
+    if chip_links:
+        results = ema_call(
+            functools.partial(ema_grads_reduce, parts, len(ins), len(outs), len(scratch)), rows, dims, width,
+            ins + [(attn_grads.reshape(replicas // 2, 2, parts, 3 * depth, vw), anywhere)],
+            outs + [(jax.ShapeDtypeStruct((3 * depth, vw), F32), whole(3 * depth, vw))],
+            scratch + reduce_scratch(parts, 3 * depth, vw), "ema_grads", 3 * mac, collective_id=2,
+        )
+        attn_sum = results[-1]
+    else:
+        results = ema_call(ema_grads, rows, dims, width, ins, outs, scratch, "ema_grads", 3 * mac)
+        attn_sum = summed_along(summed(attn_grads), results[-1])
+    grad_hidden_ema, output_grad, input_grad, rate_grad, angle_grad, grad_skip = results[:6]
+
+    ffn_sum = summed_along(ffn_sum, grad_skip)
 
     grad_hidden = grad_hidden + grad_hidden_ema
     gain_grad = jnp.sum(centred * grad_hidden, axis=0)

time: 672 us -> 626 us (0.932)
  waiting for transfers between devices: 233 us -> 82.3 us
  Pallas kernels: 264 us -> 381 us
  starting transfers between devices: 68.8 us -> 41.9 us
  local copies, waits for them, and re-layouts: 32.3 us -> 42.1 us
  other arithmetic: 27.3 us -> 34.3 us
    pallas_call x3, Pallas kernels: 108 us -> 188 us  [stage_call(): pl.pallas_call(body, grid=(steps,), in_specs=[spec(v, how) for v, how in...]
    ppermute x8, waiting for transfers between devices: 71.1 us -> 8.43 us  [from_earlier(): return lax.ppermute(x, 'tensor', [(i, i + hop) for i in range(parts - hop)])]
    ppermute x8, waiting for transfers between devices: 77.8 us -> 33.2 us  [from_later(): return lax.ppermute(x, 'tensor', [(i + hop, i) for i in range(parts - hop)])]
    reduce_scatter x4 -> x2, waiting for transfers between devices: 34.9 us -> 0.02 us  [the longest x1 0.02 us: summed(): return lax.psum_scatter(g, 'dp', scatter_dimension=0, tiled=False)]
    ppermute x8, starting transfers between devices: 57.8 us -> 30.9 us  [from_earlier(): return lax.ppermute(x, 'tensor', [(i, i + hop) for i in range(parts - hop)])]
    pallas_call x4, Pallas kernels: 98.8 us -> 122 us  [ema_call(): pl.pallas_call(functools.partial(body, rows, dims), grid=(width // LANES,...]
    pallas_call x1, Pallas kernels: 57.3 us -> 71.5 us  [small_sums_call(): pl.pallas_call(functools.partial(small_sums_kernel, bits), in_specs=[vmem...]
    all_gather x2 -> x1, waiting for transfers between devices: 48.8 us -> 40.6 us  [on_device(): lax.all_gather(pack_a, BOTH, axis=0).reshape(replicas, parts, -1, vw)]
  transfers between devices with their start and end apart: 22 -> 19, of which waited for: 10 -> 7; matrix products, arithmetic and copies ran while one was open for 10% -> 13% of each run, Pallas kernels for 27% -> 39%
where the time goes in v3:
time: 626 us; the launch traced here: 618 us
  Pallas kernels  381 us (61%)
  waiting for transfers between devices  82.3 us (13%)
  local copies, waits for them, and re-layouts  42.1 us (7%)
  starting transfers between devices  41.9 us (7%)
  other arithmetic  34.3 us (5%)
  between operations  20.4 us (3%)
  matrix products  15.6 us (2%)
    pallas_call x3, Pallas kernels, stage_call(): pl.pallas_call(body, grid=(steps,), in_specs=[spec(v, how) for v, how in...  188 us
    pallas_call x4, Pallas kernels, ema_call(): pl.pallas_call(functools.partial(body, rows, dims), grid=(width // LANES,...  122 us
    pallas_call x1, Pallas kernels, small_sums_call(): pl.pallas_call(functools.partial(small_sums_kernel, bits), in_specs=[vmem...  71.5 us
    all_gather x1, waiting for transfers between devices, on_device(): lax.all_gather(pack_a, BOTH, axis=0).reshape(replicas, parts, -1, vw)  40.6 us
    ppermute x8, waiting for transfers between devices, from_later(): return lax.ppermute(x, 'tensor', [(i + hop, i) for i in range(parts - hop)])  33.2 us
    ppermute x8, starting transfers between devices, from_earlier(): return lax.ppermute(x, 'tensor', [(i, i + hop) for i in range(parts - hop)])  30.9 us
    dot_general x13, matrix products, dot32(): lax.dot_general(a, b, (dims, ((), ())), precision=precision, preferred_el...  15.6 us
    unnamed x103, local copies, waits for them, and re-layouts  13.3 us
  transfers between devices with their start and end apart: 19, of which 7 were waited for; matrix products, arithmetic and copies ran while one was open for 13% of the time, Pallas kernels for 39%

profile of v3, /device:TPU:0, one launch (start us, length us, event | category | flops | bytes accessed | tf_op | source)
XLA Modules:
  0.0 618.1 jit_solution(14434715369167325697)
XLA Ops:
  8.1 1.1 copy.86
  9.2 1.0 convert_element_type.125
  10.2 1.0 convert_element_type.124
  12.2 1.2 fusion
  14.7 4.9 collective-permute-start
  19.6 4.5 collective-permute-start.1
  34.0 1.9 compare_convert_fusion
  36.2 1.2 fusion.31
  37.5 4.6 fusion.66
  44.2 13.8 %ema_enter.1 = (f32[128,8,1024]{2,1,0:T(8,128)}, f32[32,1024]{1,0:T(8,128)}, f32[32,1024]{1,0:T(8,128)}) custom-call(f32[512,1024]{1,0:T(8,128)} %get-tuple-element.248.h_ref.refs_0_, f32[64,8,128]{2,1,0:T(8,128)} %broadcast_in_dim.114.kend_ref.refs_3_, f32[32,1024]{1,0:T(8,128)} %pad_maximum_fusion.4.q_ref.refs_6_, ...), custom_call_target="tpu_custom_call" | custom-call | flops 33554 | bytes 1024 | tf_op jit(solution)/shard_map/ema_enter/pallas_call | solution.py:409
  58.0 1.4 collective-permute-start.3
  59.5 1.3 collective-permute-start.2
  60.8 5.4 collective-permute-done.3
  67.1 1.8 collective-permute-done.2
  69.6 6.2 %collective-permute-start.7 = (bf16[512,1024]{1,0:T(8,128)(2,1)}, bf16[512,1024]{1,0:T(8,128)(2,1)S(1)}, u32[]{:S(2)}, u32[]{:S(2)}) collective-permute-start(bf16[512,1024]{1,0:T(8,128)(2,1)} %get-tuple-element.129), channel_id=1, source_target_pairs={{0,1},{1,2},{2,3},{4,5},{5,6},{6,7},{8,9},{9,10},{10,11},{12,13},{... | collective-permute-start | bytes 3145736 | tf_op jit(solution)/shard_map/ppermute | solution.py:985
  75.8 2.1 slice.268
  77.9 4.4 collective-permute-start.6
  86.7 18.7 %ema_read.1 = (f32[512,1024]{1,0:T(8,128)}, bf16[512,1024]{1,0:T(8,128)(2,1)}, f32[128,8,1024]{2,1,0:T(8,128)}) custom-call(f32[512,1024]{1,0:T(8,128)} %get-tuple-element.248.h_ref.refs_0_, f32[64,8,128]{2,1,0:T(8,128)} %broadcast_in_dim.52.seg_ref.refs_2_, f32[64,8,128]{2,1,0:T(8,128)} %broadcast_in_dim.55.k0_ref, ...), custom_call_target="tpu_custom_call" | custom-call | flops 33554 | bytes 1024 | tf_op jit(solution)/shard_map/ema_read/pallas_call | solution.py:409
  105.5 40.6 %all-gather.3.cloned.1.call-done = bf16[12800,512]{1,0:T(8,128)(2,1)} async-done(((bf16[400,512]{1,0:T(8,128)(2,1)}), bf16[12800,512]{1,0:T(8,128)(2,1)}) %all-gather.3.cloned.1.call-update) | async-done | bytes 13107216 | tf_op jit(solution)/shard_map/all_gather | solution.py:1013
  146.1 1.1 slice.331
  147.4 1.1 multiply_convert_fusion
  148.5 6.6 %collective-permute-start.5 = (bf16[512,256]{1,0:T(8,128)(2,1)S(1)}, bf16[512,256]{1,0:T(8,128)(2,1)S(1)}, u32[]{:S(2)}, u32[]{:S(2)}) collective-permute-start(bf16[512,256]{1,0:T(8,128)(2,1)S(1)} %get-tuple-element.257), channel_id=1, source_target_pairs={{0,1},{1,2},{2,3},{4,5},{5,6},{6,7},{8,9},{9,10},{10,11},{12,13},{... | collective-permute-start | bytes 786440 | tf_op jit(solution)/shard_map/ppermute | solution.py:985
  155.2 1.6 collective-permute-start.4
  156.8 6.3 %pad_maximum_fusion.refs_4_.h_ref = bf16[1408,1024]{1,0:T(8,128)(2,1)} fusion(bf16[512,1024]{1,0:T(8,128)(2,1)} %get-tuple-element.129, bf16[512,1024]{1,0:T(8,128)(2,1)S(1)} %collective-permute-done.7, bf16[288,1024]{1,0:T(8,128)(2,1)} %collective-permute-done.6, bf16[1408]{0:T(1024)(128)(2,1)S(1)} %pad.24.clone), kind=kLoop, calls=%fused_computation.10 | loop fusion | flops 11534336 | bytes 5573376 | tf_op jit(solution)/shard_map/concatenate | solution.py:993
  163.1 1.2 collective-permute-done.4
  164.3 1.2 pad_maximum_fusion.1.refs_1_.k_ref
  165.5 100.8 %attend.1 = (f32[512,1408]{1,0:T(8,128)}, bf16[1408,2048]{1,0:T(8,128)(2,1)}, bf16[1408,2048]{1,0:T(8,128)(2,1)}, bf16[512,2048]{1,0:T(8,128)(2,1)}, bf16[512,20...) custom-call(bf16[512,256]{1,0:T(8,128)(2,1)} %get-tuple-element.258., ...), custom_call_target="tpu_custom_call" | custom-call | flops 12884901 | bytes 1024 | tf_op jit(solution)/shard_map/attend/pallas_call | solution.py:602
  266.3 40.3 %ffn.1 = (bf16[512,1024]{1,0:T(8,128)(2,1)}, f32[512,1024]{1,0:T(8,128)}, bf16[512,1024]{1,0:T(8,128)(2,1)}, f32[1,1024]{1,0:T(1,128)}, bf16[8,4,3,128,640]{4,3,2,1,0:T(8,128)(2,1)}) custom-call(f32[512,1024]{1,0:T(8,128)} %get-tuple-element.130.y_ref, bf16[512,1024]{1,0:T(8,128)(2,1)} %get-tuple-element.131.n_ref, bf16[512,1024]{1,0:T(8,128)(2,1)} %og_ref.1, ...), custom_call_target="tpu_custom_call" | custom-call | flops 23622320 | bytes 1024 | tf_op jit(solution)/shard_map/ffn/pallas_call | solution.py:602
  313.2 46.9 %attend_back.1 = (f32[512,256]{1,0:T(8,128)}, bf16[896,256]{1,0:T(8,128)(2,1)}, f32[512,256]{1,0:T(8,128)}, bf16[896,1024]{1,0:T(8,128)(2,1)}, f32[512,1024]{1,0...) custom-call(bf16[512,1024]{1,0:T(8,128)(2,1)} %get-tuple-element.135.br_ref, ...), custom_call_target="tpu_custom_call" | custom-call | flops 25769804 | bytes 1024 | tf_op jit(solution)/shard_map/attend_back/pallas_call | solution.py:602
  360.1 1.1 slice.269
  361.2 1.3 collective-permute-start.8
  362.6 0.9 slice.271
  363.5 1.4 collective-permute-start.9
  364.9 8.1 %collective-permute-done.8 = bf16[512,256]{1,0:T(8,128)(2,1)S(1)} collective-permute-done((bf16[512,256]{1,0:T(8,128)(2,1)S(1)}, bf16[512,256]{1,0:T(8,128)(2,1)S(1)}, u32[]{:S(2)}, u32[]{:S(2)}) %collective-permute-start.8) | collective-permute-done | bytes 262176 | tf_op jit(solution)/shard_map/ppermute | solution.py:988
  373.0 1.1 convert_add_fusion.1
  374.1 3.0 collective-permute-done.9
  377.1 1.1 slice.272
  378.2 1.3 collective-permute-start.10
  381.7 2.1 multiply_multiply_fusion.de_ref.refs_1_
  384.5 14.0 %ema_leave.1 = (f32[128,8,1024]{2,1,0:T(8,128)}, f32[32,1024]{1,0:T(8,128)}) custom-call(f32[512,1024]{1,0:T(8,128)} %multiply_multiply_fusion.de_ref.refs_1_, f32[64,8,128]{2,1,0:T(8,128)} %broadcast_in_dim.55.k0_ref, f32[32,1024]{1,0:T(8,128)} %pad_maximum_fusion.4.q_ref.refs_6_, f32[32,1024]{1,0:T(8,128)} %bitcast.116, ...), custom_call_target="tpu_custom_call" | custom-call | flops 33554 | bytes 1024 | tf_op jit(solution)/shard_map/ema_leave/pallas_call | solution.py:409
  398.5 1.3 collective-permute-start.12
  399.8 1.5 collective-permute-start.13
  401.8 2.0 slice.274
  403.8 1.3 collective-permute-start.11
  405.2 22.1 %collective-permute-done.13 = f32[32,1024]{1,0:T(8,128)S(1)} collective-permute-done((f32[32,1024]{1,0:T(8,128)}, f32[32,1024]{1,0:T(8,128)S(1)}, u32[]{:S(2)}, u32[]{:S(2)}) %collective-permute-start.13) | collective-permute-done | bytes 131104 | tf_op jit(solution)/shard_map/ppermute | solution.py:988
  429.8 75.2 %ema_grads.1 = (f32[512,1024]{1,0:T(8,128)}, f32[32,1024]{1,0:T(8,128)}, f32[16,1024]{1,0:T(8,128)}, f32[16,1024]{1,0:T(8,128)}, f32[16,1024]{1,0:T(8,128)}, /*index=5*/f32[1,1024]{1,0:T(1,128)}, f32[384,512]{1,0:T(8,128)}) custom-call(f32[512,1024]{1,0:T(8,128)} %get-tuple-element.248.h_ref.refs_0_, f32[512,1024]{1,0:T(8,128)} %multiply_multiply_fusion.de_ref.refs_1_, ...), custom_call_target="tpu_custom_call" | custom-call | flops 100663 | bytes 1024 | tf_op jit(solution)/shard_map/ema_grads/pallas_call | solution.py:409
  505.0 1.6 copy.95
  506.6 1.5 copy.96
  508.1 1.5 copy.97
  509.6 1.6 copy.98
  511.2 1.9 slice_bitcast_fusion.3
  514.0 1.8 convert_add_fusion
  515.8 1.5 fusion.9
  517.6 0.9 multiply_reduce_fusion
  519.2 1.3 fusion.16
  520.5 1.2 subtract_divide_fusion
  522.2 1.3 collective-permute-start.15
  523.5 1.5 collective-permute-start.14
  525.4 71.5 %small_sums.1 = (f32[768,128]{1,0:T(8,128)S(1)}, f32[128,256]{1,0:T(8,128)S(1)}) custom-call(f32[768,128]{1,0:T(8,128)S(1)} %bitcast.103, f32[1024,256]{1,0:T(8,128)S(1)} %bitcast.102), custom_call_target="tpu_custom_call" | custom-call | tf_op jit(solution)/shard_map/small_sums/pallas_call | solution.py:951
  600.9 1.2 fusion.29
  602.2 1.2 fusion.30
  603.4 4.3 fusion.3
  607.8 1.1 convert_element_type.147
  608.9 0.9 slice_bitcast_fusion
  (213 shorter events, 36.7 us)
Async XLA Ops:
  7.2 0.9 copy-start
  7.2 4.8 copy-start.30
  7.2 4.9 copy-start.8
  7.2 138.8 %all-gather.3.cloned.1.call-start = ((), (), s32[]{:S(2)}) async-start(), calls=%async_computation.4 | async-start | bytes 13516800 | tf_op jit(solution)/shard_map/all_gather | solution.py:1013
  12.0 513.1 %reduce-scatter.3.cloned.1.call-start = ((), (), s32[]{:S(2)}) async-start(), calls=%async_computation.2 | async-start | bytes 17694720 | tf_op jit(solution)/shard_map/reduce_scatter | solution.py:1141
  13.4 17.8 %copy-start.23 = (f32[16,1024]{1,0:T(8,128)S(1)}, f32[16,1024]{1,0:T(8,128)}, u32[]{:S(2)}) copy-start(f32[16,1024]{1,0:T(8,128)} %refs_10_.1) | copy-start | bytes 196612
  13.4 17.8 %copy-start.28 = (f32[16,1024]{1,0:T(8,128)S(1)}, f32[16,1024]{1,0:T(8,128)}, u32[]{:S(2)}) copy-start(f32[16,1024]{1,0:T(8,128)} %param.37) | copy-start | bytes 196612
  13.4 17.8 %copy-start.29 = (f32[16,1024]{1,0:T(8,128)S(1)}, f32[16,1024]{1,0:T(8,128)}, u32[]{:S(2)}) copy-start(f32[16,1024]{1,0:T(8,128)} %param.38) | copy-start | bytes 196612
  14.7 21.3 %collective-permute-start = (f32[1,32]{0,1:T(8,128)S(1)}, f32[1,32]{0,1:T(8,128)S(1)}, u32[]{:S(2)}, u32[]{:S(2)}) collective-permute-start(f32[1,32]{0,1:T(8,128)S(1)} %slice.324), channel_id=1, source_target_pairs={{0,1},{1,2},{2,3},{4,5},{5,6},{6,7},{8,9},{9,10},{10,11},{12,13},{... | collective-permute-start | bytes 392 | tf_op jit(solution)/shard_map/ppermute | solution.py:985
  19.6 16.4 %collective-permute-start.1 = (f32[1,32]{0,1:T(8,128)S(1)}, f32[1,32]{0,1:T(8,128)S(1)}, u32[]{:S(2)}, u32[]{:S(2)}) collective-permute-start(f32[1,32]{0,1:T(8,128)S(1)} %slice.324), channel_id=1, source_target_pairs={{0,2},{1,3},{4,6},{5,7},{8,10},{9,11},{12,14},{13,15},{16,18},{17,... | collective-permute-start | bytes 392 | tf_op jit(solution)/shard_map/ppermute | solution.py:985
  29.3 8.2 %copy-start.27 = (f32[1024]{0:T(1024)S(1)}, f32[1024]{0:T(1024)}, u32[]{:S(2)}) copy-start(f32[1024]{0:T(1024)} %param.36) | copy-start | bytes 12292
  37.5 4.6 copy-start.4
  44.2 39.7 %copy-start.20 = (f32[640,128]{1,0:T(8,128)S(1)}, f32[640,128]{1,0:T(8,128)}, u32[]{:S(2)}) copy-start(f32[640,128]{1,0:T(8,128)} %param.52) | copy-start | bytes 983044
  44.2 39.8 %copy-start.21 = (f32[128,640]{1,0:T(8,128)S(1)}, f32[128,640]{1,0:T(8,128)}, u32[]{:S(2)}) copy-start(f32[128,640]{1,0:T(8,128)} %param.51) | copy-start | bytes 983044
  58.0 26.1 %copy-start.22 = (f32[128,640]{1,0:T(8,128)S(1)}, f32[128,640]{1,0:T(8,128)}, u32[]{:S(2)}) copy-start(f32[128,640]{1,0:T(8,128)} %param.50) | copy-start | bytes 983044
  58.0 8.1 %collective-permute-start.3 = (f32[32,1024]{1,0:T(8,128)}, f32[32,1024]{1,0:T(8,128)S(1)}, u32[]{:S(2)}, u32[]{:S(2)}) collective-permute-start(f32[32,1024]{1,0:T(8,128)} %get-tuple-element.126), channel_id=1, source_target_pairs={{0,2},{1,3},{4,6},{5,7},{8,10},{9,11},{12,14},{13,15},{16,18},{17,... | collective-permute-start | bytes 393224 | tf_op jit(solution)/shard_map/ppermute | solution.py:985
  59.5 9.4 %collective-permute-start.2 = (f32[32,1024]{1,0:T(8,128)}, f32[32,1024]{1,0:T(8,128)S(1)}, u32[]{:S(2)}, u32[]{:S(2)}) collective-permute-start(f32[32,1024]{1,0:T(8,128)} %get-tuple-element.126), channel_id=1, source_target_pairs={{0,1},{1,2},{2,3},{4,5},{5,6},{6,7},{8,9},{9,10},{10,11},{12,13},{... | collective-permute-start | bytes 393224 | tf_op jit(solution)/shard_map/ppermute | solution.py:985
  69.6 87.2 %collective-permute-start.7 = (bf16[512,1024]{1,0:T(8,128)(2,1)}, bf16[512,1024]{1,0:T(8,128)(2,1)S(1)}, u32[]{:S(2)}, u32[]{:S(2)}) collective-permute-start(bf16[512,1024]{1,0:T(8,128)(2,1)} %get-tuple-element.129), channel_id=1, source_target_pairs={{0,1},{1,2},{2,3},{4,5},{5,6},{6,7},{8,9},{9,10},{10,11},{12,13},{... | collective-permute-start | bytes 3145736 | tf_op jit(solution)/shard_map/ppermute | solution.py:985
  77.9 78.8 %collective-permute-start.6 = (bf16[288,1024]{1,0:T(8,128)(2,1)}, bf16[288,1024]{1,0:T(8,128)(2,1)}, u32[]{:S(2)}, u32[]{:S(2)}) collective-permute-start(bf16[288,1024]{1,0:T(8,128)(2,1)} %slice.268), channel_id=1, source_target_pairs={{0,2},{1,3},{4,6},{5,7},{8,10},{9,11},{12,14},{13,15},{16,18},{17,... | collective-permute-start | bytes 1769480 | tf_op jit(solution)/shard_map/ppermute | solution.py:985
  105.4 41.9 %copy-start.6 = (bf16[512,1024]{1,0:T(8,128)(2,1)S(1)}, bf16[512,1024]{1,0:T(8,128)(2,1)}, u32[]{:S(2)}) copy-start(bf16[512,1024]{1,0:T(8,128)(2,1)} %get-tuple-element.128.refs_5_.m_ref) | copy-start | bytes 3145732
  105.4 41.9 %copy-start.33 = (f32[256]{0:T(256)S(1)}, f32[256]{0:T(256)}, u32[]{:S(2)}) copy-start(f32[256]{0:T(256)} %param.45) | copy-start | bytes 3076
  105.4 41.9 %copy-start.34 = (f32[256]{0:T(256)S(1)}, f32[256]{0:T(256)}, u32[]{:S(2)}) copy-start(f32[256]{0:T(256)} %param.43) | copy-start | bytes 3076
  105.4 41.9 %copy-start.40 = (f32[256]{0:T(256)S(1)}, f32[256]{0:T(256)}, u32[]{:S(2)}) copy-start(f32[256]{0:T(256)} %param.44) | copy-start | bytes 3076
  148.5 15.8 %collective-permute-start.5 = (bf16[512,256]{1,0:T(8,128)(2,1)S(1)}, bf16[512,256]{1,0:T(8,128)(2,1)S(1)}, u32[]{:S(2)}, u32[]{:S(2)}) collective-permute-start(bf16[512,256]{1,0:T(8,128)(2,1)S(1)} %get-tuple-element.257), channel_id=1, source_target_pairs={{0,1},{1,2},{2,3},{4,5},{5,6},{6,7},{8,9},{9,10},{10,11},{12,13},{... | collective-permute-start | bytes 786440 | tf_op jit(solution)/shard_map/ppermute | solution.py:985
  155.2 9.1 %collective-permute-start.4 = (bf16[288,256]{1,0:T(8,128)(2,1)S(1)}, bf16[288,256]{1,0:T(8,128)(2,1)S(1)}, u32[]{:S(2)}, u32[]{:S(2)}) collective-permute-start(bf16[288,256]{1,0:T(8,128)(2,1)S(1)} %slice.332), channel_id=1, source_target_pairs={{0,2},{1,3},{4,6},{5,7},{8,10},{9,11},{12,14},{13,15},{16,18},{17,... | collective-permute-start | bytes 442376 | tf_op jit(solution)/shard_map/ppermute | solution.py:985
  306.7 0.6 copy-start.41
  306.7 301.1 %reduce-scatter.5.cloned.1.call-start = ((), (), s32[]{:S(2)}) async-start(), calls=%async_computation.3 | async-start | bytes 2457600 | tf_op jit(solution)/shard_map/reduce_scatter | solution.py:1145
  360.1 17.0 %copy-start.16 = (bf16[896,1024]{1,0:T(8,128)(2,1)S(1)}, bf16[896,1024]{1,0:T(8,128)(2,1)}, u32[]{:S(2)}) copy-start(bf16[896,1024]{1,0:T(8,128)(2,1)} %get-tuple-element.146) | copy-start | bytes 5505028
  361.2 11.8 %collective-permute-start.8 = (bf16[512,256]{1,0:T(8,128)(2,1)S(1)}, bf16[512,256]{1,0:T(8,128)(2,1)S(1)}, u32[]{:S(2)}, u32[]{:S(2)}) collective-permute-start(bf16[512,256]{1,0:T(8,128)(2,1)S(1)} %slice.269), channel_id=1, source_target_pairs={{1,0},{2,1},{3,2},{5,4},{6,5},{7,6},{9,8},{10,9},{11,10},{13,12},{... | collective-permute-start | bytes 786440 | tf_op jit(solution)/shard_map/ppermute | solution.py:988
  363.5 16.0 %copy-start.17 = (f32[512,256]{1,0:T(8,128)S(1)}, f32[512,256]{1,0:T(8,128)}, u32[]{:S(2)}) copy-start(f32[512,256]{1,0:T(8,128)} %get-tuple-element.147) | copy-start | bytes 1572868
  363.5 13.6 %collective-permute-start.9 = (bf16[288,256]{1,0:T(8,128)(2,1)S(1)}, bf16[288,256]{1,0:T(8,128)(2,1)S(1)}, u32[]{:S(2)}, u32[]{:S(2)}) collective-permute-start(bf16[288,256]{1,0:T(8,128)(2,1)S(1)} %slice.271), channel_id=1, source_target_pairs={{2,0},{3,1},{6,4},{7,5},{10,8},{11,9},{14,12},{15,13},{18,16},{19,... | collective-permute-start | bytes 442376 | tf_op jit(solution)/shard_map/ppermute | solution.py:988
  378.2 135.8 %collective-permute-start.10 = (bf16[512,1024]{1,0:T(8,128)(2,1)}, bf16[512,1024]{1,0:T(8,128)(2,1)}, u32[]{:S(2)}, u32[]{:S(2)}) collective-permute-start(bf16[512,1024]{1,0:T(8,128)(2,1)} %slice.272), channel_id=1, source_target_pairs={{1,0},{2,1},{3,2},{5,4},{6,5},{7,6},{9,8},{10,9},{11,10},{13,12},{... | collective-permute-start | bytes 3145736 | tf_op jit(solution)/shard_map/ppermute | solution.py:988
  379.5 1.6 copy-start.13
  379.5 2.2 copy-start.14
  383.9 17.5 %copy-start.7 = (bf16[512,1024]{1,0:T(8,128)(2,1)S(1)}, bf16[512,1024]{1,0:T(8,128)(2,1)}, u32[]{:S(2)}) copy-start(bf16[512,1024]{1,0:T(8,128)(2,1)} %get-tuple-element.128.refs_5_.m_ref) | copy-start | bytes 3145732
  398.5 28.9 %collective-permute-start.12 = (f32[32,1024]{1,0:T(8,128)}, f32[32,1024]{1,0:T(8,128)S(1)}, u32[]{:S(2)}, u32[]{:S(2)}) collective-permute-start(f32[32,1024]{1,0:T(8,128)} %get-tuple-element.151), channel_id=1, source_target_pairs={{1,0},{2,1},{3,2},{5,4},{6,5},{7,6},{9,8},{10,9},{11,10},{13,12},{... | collective-permute-start | bytes 393224 | tf_op jit(solution)/shard_map/ppermute | solution.py:988
  399.8 27.5 %collective-permute-start.13 = (f32[32,1024]{1,0:T(8,128)}, f32[32,1024]{1,0:T(8,128)S(1)}, u32[]{:S(2)}, u32[]{:S(2)}) collective-permute-start(f32[32,1024]{1,0:T(8,128)} %get-tuple-element.151), channel_id=1, source_target_pairs={{2,0},{3,1},{6,4},{7,5},{10,8},{11,9},{14,12},{15,13},{18,16},{19,... | collective-permute-start | bytes 393224 | tf_op jit(solution)/shard_map/ppermute | solution.py:988
  401.8 25.6 %copy-start.18 = (f32[32,1024]{1,0:T(8,128)S(1)}, f32[32,1024]{1,0:T(8,128)}, u32[]{:S(2)}) copy-start(f32[32,1024]{1,0:T(8,128)} %get-tuple-element.127) | copy-start | bytes 393220
  403.8 112.0 %collective-permute-start.11 = (bf16[288,1024]{1,0:T(8,128)(2,1)}, bf16[288,1024]{1,0:T(8,128)(2,1)}, u32[]{:S(2)}, u32[]{:S(2)}) collective-permute-start(bf16[288,1024]{1,0:T(8,128)(2,1)} %slice.274), channel_id=1, source_target_pairs={{2,0},{3,1},{6,4},{7,5},{10,8},{11,9},{14,12},{15,13},{18,16},{19,... | collective-permute-start | bytes 1769480 | tf_op jit(solution)/shard_map/ppermute | solution.py:988
  505.0 9.0 %copy-start.12 = (f32[512,1024]{1,0:T(8,128)S(1)}, f32[512,1024]{1,0:T(8,128)}, u32[]{:S(2)}) copy-start(f32[512,1024]{1,0:T(8,128)} %get-tuple-element.142) | copy-start | bytes 6291460
  514.0 3.4 copy-start.15
  515.8 1.8 copy-start.11
  517.6 1.6 copy-start.10
  518.5 1.9 copy-start.2
  519.2 1.3 copy-start.32
  520.5 4.7 copy-start.26
  520.5 4.7 copy-start.25
  521.7 3.5 copy-start.24
  521.7 3.6 copy-start.19
  521.7 3.6 copy-start.39
  521.7 3.6 copy-start.37
  521.7 3.6 copy-start.36
  521.7 3.6 copy-start.35
  521.7 3.6 copy-start.38
  522.2 78.5 %collective-permute-start.15 = (f32[1,32]{0,1:T(8,128)S(1)}, f32[1,32]{0,1:T(8,128)S(1)}, u32[]{:S(2)}, u32[]{:S(2)}) collective-permute-start(f32[1,32]{0,1:T(8,128)S(1)} %slice.341), channel_id=1, source_target_pairs={{2,0},{3,1},{6,4},{7,5},{10,8},{11,9},{14,12},{15,13},{18,16},{19,... | collective-permute-start | bytes 392 | tf_op jit(solution)/shard_map/ppermute | solution.py:988
  523.5 77.2 %collective-permute-start.14 = (f32[1,32]{0,1:T(8,128)S(1)}, f32[1,32]{0,1:T(8,128)S(1)}, u32[]{:S(2)}, u32[]{:S(2)}) collective-permute-start(f32[1,32]{0,1:T(8,128)S(1)} %slice.341), channel_id=1, source_target_pairs={{1,0},{2,1},{3,2},{5,4},{6,5},{7,6},{9,8},{10,9},{11,10},{13,12},{... | collective-permute-start | bytes 392 | tf_op jit(solution)/shard_map/ppermute | solution.py:988
  525.1 75.7 %copy-start.31 = (f32[512]{0:T(512)S(1)}, f32[512]{0:T(512)}, u32[]{:S(2)}) copy-start(f32[512]{0:T(512)} %get-tuple-element.284) | copy-start | bytes 6148
  525.2 78.2 %copy-start.9 = (bf16[512,1024]{1,0:T(8,128)(2,1)S(1)}, bf16[512,1024]{1,0:T(8,128)(2,1)}, u32[]{:S(2)}) copy-start(bf16[512,1024]{1,0:T(8,128)(2,1)} %refs_6_.1) | copy-start | bytes 3145732
  600.9 2.5 copy-start.3
  600.9 2.5 copy-start.5
  603.4 7.9 %copy-start.1 = (f32[128,256]{1,0:T(8,128)S(1)}, f32[128,256]{1,0:T(8,128)}, u32[]{:S(2)}) copy-start(f32[128,256]{1,0:T(8,128)} %param.42) | copy-start | bytes 393220
Sparse Core Ops, SparseCore 0:
  12.1 133.9 all-gather.2
  306.8 108.3 reduce-scatter.2
  525.3 59.5 reduce-scatter.4

commit v4 on v3

--- a/solution.py
+++ b/solution.py
@@ -134,25 +134,6 @@
     lax.fori_loop(0, STEP // block, some, 0)
 
 
-def ema_enter(rows, dims, h_ref, kend_ref, q_ref, f_ref, cont_ref, mk_ref, l_ref, end_ref, turn_ref, hm, tb, qs):
-    groups = rows // (8 * STEP)
-    pw = power_list(dims, q_ref)
-    turn_ref[:dims], turn_ref[dims:] = fill_scales(groups, dims, pw, qs)
-    fill_feed(dims, pw, f_ref, tb)
-    for at in range(groups * STEP):
-        hm[at] = h_ref[pl.ds(at, 8, stride=groups * STEP), :] * kend_ref[at]
-    chunk_sums(groups, dims, tb, hm, l_ref, 1)
-
-    def one(j, carry):
-        zero = jnp.zeros((8, LANES), F32)
-        _, ends = scan_states(groups, dims, j, l_ref, qs, cont_ref, mk_ref, zero, zero)
-        end_ref[pl.ds(j, 1), :] = ends[0][7:8]
-        end_ref[pl.ds(dims + j, 1), :] = ends[1][7:8]
-        return carry
-
-    lax.fori_loop(0, dims, one, 0)
-
-
 def scan_states(groups, dims, j, l_ref, qs, cont_ref, mk_ref, inr, ini):
     qr, qi = broadcast_row(qs, j), broadcast_row(qs, dims + j)
     part = [(l_ref[(g * dims + j) * 2], l_ref[(g * dims + j) * 2 + 1]) for g in range(groups)]
@@ -178,14 +159,132 @@
     return starts, (er, ei)
 
 
+ENTER_PLAN = (
+    (0, 2, False), (8, 1, False), (9, 1, False), (10, 1, False), (11, 2, False), (12, 1, False), (13, 1, False),
+    (14, 2, False), (15, 0, True),
+)
+
+
+def shifted_rows(parts, halo, hops, rows, source, near, zeros, sems, local_sems):
+    z = lax.axis_index("tensor")
+    moves, fills, end = [], [], halo
+    for h, n in enumerate(hops):
+        place = near.at[pl.ds(end - n, n)]
+        moves.append(Along(parts, h + 1, source.at[pl.ds(rows - n, n)], place, sems.at[0, h], sems.at[1, h]))
+        fills.append((z <= h, zeros.at[pl.ds(0, n)], place, local_sems.at[h]))
+        end -= n
+    own = [(source, near.at[pl.ds(halo, rows)], local_sems.at[len(hops)])]
+    if end > 0:
+        own.append((zeros.at[pl.ds(0, end)], near.at[pl.ds(0, end)], local_sems.at[len(hops) + 1]))
+
+    def each(action):
+        for copy in own:
+            action(pltpu.make_async_copy(*copy))
+        for condition, *copy in fills:
+            @pl.when(condition)
+            def _():
+                action(pltpu.make_async_copy(*copy))
+
+    def start():
+        for move in moves:
+            move.start()
+        each(lambda c: c.start())
+
+    def wait():
+        for move in moves:
+            move.wait_recv()
+            move.wait_send()
+        each(lambda c: c.wait())
+
+    return start, wait
+
+
+def ema_forward(
+    rows, dims, parts, halo, hops, hosted, h_ref, kend_ref, seg_ref, k0_ref, q_ref, f_ref, e_ref, cont_ref, mk_ref,
+    link_ref, skip_ref, low_ref, zeros_ref, *refs
+):
+    refs = list(refs)
+    pack_ref = refs.pop(0) if hosted else None
+    out_ref, m_ref, s_ref, near_ref = (refs.pop(0) for _ in range(4))
+    all_ref = refs.pop(0) if hosted else None
+    hs, table, qs, parts_all, ends, got, entry, state_sems, near_sems, local_sems, *rest = refs
+    groups = rows // (8 * STEP)
+    step = pl.program_id(0)
+    blocks = parts_all.shape[0]
+    k = step % blocks
+    stages = gather_stages(parts, pack_ref, all_ref, *rest) if hosted else []
+    near_start, near_wait = shifted_rows(parts, halo, hops, rows, low_ref, near_ref, zeros_ref, near_sems, local_sems)
+    states = lambda hop, at: Along(
+        parts, hop, ends.at[at], got.at[hop - 1, at], state_sems.at[0, hop - 1, at], state_sems.at[1, hop - 1, at]
+    )
+
+    @pl.when(step == 0)
+    def _():
+        greet(parts, 3 if hosted else 0)
+
+    @pl.when(step == blocks)
+    def _():
+        near_start()
+
+    if hosted:
+        run_stages(stages, step, ENTER_PLAN, False)
+    pw = power_list(dims, q_ref)
+    turn = fill_scales(groups, dims, pw, qs)
+
+    @pl.when(step < blocks)
+    def _():
+        fill_feed(dims, pw, f_ref, table)
+        for at in range(groups * STEP):
+            hs[at] = h_ref[pl.ds(at, 8, stride=groups * STEP), :] * kend_ref[at]
+        chunk_sums(groups, dims, table, hs, parts_all.at[k], 1)
+
+        def one(j, carry):
+            zero = jnp.zeros((8, LANES), F32)
+            _, last = scan_states(groups, dims, j, parts_all.at[k], qs, cont_ref, mk_ref, zero, zero)
+            ends[k, pl.ds(j, 1), :] = last[0][7:8]
+            ends[k, pl.ds(dims + j, 1), :] = last[1][7:8]
+            return carry
+
+        lax.fori_loop(0, dims, one, 0)
+        for hop in (1, 2):
+            states(hop, k).start()
+
+    @pl.when(step >= blocks)
+    def _():
+        entry[...] = jnp.zeros_like(entry)
+
+        def near_one():
+            entry[...] = got[0, k]
+
+        def far_one():
+            link = link_ref[...]
+            r, i = times(*turn, got[1, k, :dims], got[1, k, dims:])
+            entry[:dims] += link * r
+            entry[dims:] += link * i
+
+        states(1, k).wait_recv(near_one)
+        states(2, k).wait_recv(far_one)
+        ema_read(
+            groups, dims, h_ref, seg_ref, k0_ref, pw, f_ref, e_ref, cont_ref, mk_ref, parts_all.at[k], entry, skip_ref,
+            out_ref, m_ref, s_ref, hs, table, qs,
+        )
+
+    @pl.when(step == 2 * blocks - 1)
+    def _():
+        for at in range(blocks):
+            for hop in (1, 2):
+                states(hop, at).wait_send()
+        near_wait()
+
+    if hosted:
+        run_stages(stages, step, ENTER_PLAN, True)
+
+
 def ema_read(
-    rows, dims, h_ref, seg_ref, k0_ref, q_ref, f_ref, e_ref, cont_ref, mk_ref, l_ref, in_ref, skip_ref,
-    out_ref, m_ref, s_ref, hs, ta, qs
+    groups, dims, h_ref, seg_ref, k0_ref, pw, f_ref, e_ref, cont_ref, mk_ref, l_ref, in_ref, skip_ref, out_ref, m_ref,
+    s_ref, hs, ta, qs
 ):
-    groups = rows // (8 * STEP)
     first = lax.broadcasted_iota(jnp.int32, (8, LANES), 0) == 0
-    pw = power_list(dims, q_ref)
-    fill_scales(groups, dims, pw, qs)
     fill_read(dims, pw, e_ref, ta)
     taps = tap_list(dims, pw, e_ref, f_ref)
 
@@ -240,48 +339,118 @@
     return ends, (fr, fi)
 
 
-def ema_leave(rows, dims, de_ref, k0_ref, q_ref, e_ref, cont_ref, mkr_ref, g_ref, head_ref, dm, ta, qs):
+REDUCE_PLAN = (
+    (0, 1, False), (4, 1, False), (5, 1, False), (7, 1, False), (8, 2, False), (9, 1, False), (10, 1, False),
+    (11, 1, False), (12, 1, False), (13, 1, False), (14, 1, False), (15, 0, True),
+)
+
+
+def ema_backward(
+    rows, dims, parts, halo, hops, hosted, h_ref, de_ref, seg_ref, kend_ref, k0_ref, rk0_ref, rkend_ref, q_ref, f_ref,
+    e_ref, root_ref, feed_ref, cont_ref, mkr_ref, s_ref, cross_ref, skip_ref, back_ref, zeros_ref, *refs
+):
+    refs = list(refs)
+    pack_ref = refs.pop(0) if hosted else None
+    outs = [refs.pop(0) for _ in range(6)]
+    back = [refs.pop(0) for _ in hops]
+    sum_ref = refs.pop(0) if hosted else None
+    pulls, heads, got, entry, state_sems, back_sems, local_sems, *rest = refs
+    held, rest = rest[:9], rest[9:]
+    hs, ds, la, table, qs = held[:5]
     groups = rows // (8 * STEP)
+    step = pl.program_id(0)
+    z = lax.axis_index("tensor")
+    blocks = pulls.shape[0]
+    k = step % blocks
+    stages = reduce_stages(parts, pack_ref, sum_ref, *rest) if hosted else []
+    states = lambda hop, at: Along(
+        parts, -hop, heads.at[at], got.at[hop - 1, at], state_sems.at[0, hop - 1, at], state_sems.at[1, hop - 1, at]
+    )
+    moves, fills, end = [], [], halo
+    for h, n in enumerate(hops):
+        moves.append(Along(parts, -h - 1, back_ref.at[pl.ds(end - n, n)], back[h], back_sems.at[0, h], back_sems.at[1, h]))
+        fills.append((z + h + 1 >= parts, (zeros_ref.at[pl.ds(0, n)], back[h], local_sems.at[h])))
+        end -= n
+
+    def filling(action):
+        for condition, copy in fills:
+            @pl.when(condition)
+            def _():
+                action(pltpu.make_async_copy(*copy))
+
+    @pl.when(step == 0)
+    def _():
+        greet(parts, 3 if hosted else 0)
+        filling(lambda c: c.start())
+
+    @pl.when(step == blocks)
+    def _():
+        for move in moves:
+            move.start()
+
+    if hosted:
+        run_stages(stages, step, REDUCE_PLAN, False)
     pw = power_list(dims, q_ref)
-    fill_scales(groups, dims, pw, qs)
-    fill_read(dims, pw, e_ref, ta)
-    for at in range(groups * STEP):
-        dm[at] = de_ref[pl.ds(at, 8, stride=groups * STEP), :] * k0_ref[at]
-    chunk_sums(groups, dims, ta, dm, g_ref, -1)
-
-    def one(j, carry):
-        zero = jnp.zeros((8, LANES), F32)
-        _, heads = reverse_states(groups, dims, j, g_ref, qs, cont_ref, mkr_ref, zero, zero)
-        head_ref[pl.ds(j, 1), :] = heads[0][0:1]
-        head_ref[pl.ds(dims + j, 1), :] = heads[1][0:1]
-        return carry
-
-    lax.fori_loop(0, dims, one, 0)
-
-
-REDUCE_PLAN = (
-    (0, 1, False), (1, 2, False), (2, 1, False), (3, 2, False), (4, 1, False), (5, 2, False), (6, 1, False), (7, 0, True)
-)
-
-
-def ema_grads_reduce(parts, ins, outs, held, rows, dims, *refs):
-    own = list(refs)
-    pack_ref, sum_ref = own.pop(ins), own.pop(ins + outs)
-    stages = reduce_stages(parts, pack_ref, sum_ref, *own[ins + outs + held :])
-    step = pl.program_id(0)
-    run_stages(stages, step, REDUCE_PLAN, False)
-    ema_grads(rows, dims, *own[: ins + outs + held])
-    run_stages(stages, step, REDUCE_PLAN, True)
+    turn = fill_scales(groups, dims, pw, qs)
+
+    @pl.when(step < blocks)
+    def _():
+        fill_read(dims, pw, e_ref, table)
+        for at in range(groups * STEP):
+            ds[at] = de_ref[pl.ds(at, 8, stride=groups * STEP), :] * k0_ref[at]
+        chunk_sums(groups, dims, table, ds, pulls.at[k], -1)
+
+        def one(j, carry):
+            zero = jnp.zeros((8, LANES), F32)
+            _, head = reverse_states(groups, dims, j, pulls.at[k], qs, cont_ref, mkr_ref, zero, zero)
+            heads[k, pl.ds(j, 1), :] = head[0][0:1]
+            heads[k, pl.ds(dims + j, 1), :] = head[1][0:1]
+            return carry
+
+        lax.fori_loop(0, dims, one, 0)
+        for hop in (1, 2):
+            states(hop, k).start()
+
+    @pl.when(step >= blocks)
+    def _():
+        entry[...] = jnp.zeros_like(entry)
+
+        def near_one():
+            entry[...] = got[0, k]
+
+        def far_one():
+            cross = cross_ref[...]
+            r, i = times(turn[0], -turn[1], got[1, k, :dims], got[1, k, dims:])
+            entry[:dims] += cross * r
+            entry[dims:] += cross * i
+
+        states(1, k).wait_recv(near_one)
+        states(2, k).wait_recv(far_one)
+        ema_grads(
+            groups, dims, h_ref, de_ref, seg_ref, kend_ref, rk0_ref, rkend_ref, pw, f_ref, e_ref, root_ref, feed_ref,
+            cont_ref, mkr_ref, pulls.at[k], entry, s_ref, skip_ref, *outs, *held,
+        )
+
+    @pl.when(step == 2 * blocks - 1)
+    def _():
+        for at in range(blocks):
+            for hop in (1, 2):
+                states(hop, at).wait_send()
+        for move in moves:
+            move.wait_recv()
+            move.wait_send()
+        filling(lambda c: c.wait())
+
+    if hosted:
+        run_stages(stages, step, REDUCE_PLAN, True)
 
 
 def ema_grads(
-    rows, dims, h_ref, de_ref, seg_ref, kend_ref, rk0_ref, rkend_ref, q_ref, f_ref, e_ref, root_ref, feed_ref, cont_ref,
-    mkr_ref, g_ref, in_ref, s_ref, skip_ref, dh_ref, ge_ref, gf_ref, gr_ref, ga_ref, gs_ref, hs, ds, la, tb, qs, pf, red, hn, dn
+    groups, dims, h_ref, de_ref, seg_ref, kend_ref, rk0_ref, rkend_ref, pw, f_ref, e_ref, root_ref, feed_ref, cont_ref,
+    mkr_ref, g_ref, in_ref, s_ref, skip_ref, dh_ref, ge_ref, gf_ref, gr_ref, ga_ref, gs_ref, hs, ds, la, tb, qs, pf,
+    red, hn, dn
 ):
-    groups = rows // (8 * STEP)
     last = lax.broadcasted_iota(jnp.int32, (8, LANES), 0) == 7
-    pw = power_list(dims, q_ref)
-    fill_scales(groups, dims, pw, qs)
     fill_feed(dims, pw, f_ref, tb)
     taps = tap_list(dims, pw, e_ref, f_ref)
     for i in range(STEP):
@@ -392,29 +561,20 @@
     ga_ref[...] = li
 
 
-def col(rows):
-    return pl.BlockSpec((rows, LANES), lambda i: (0, i))
-
-
-def col3(a, b):
-    return pl.BlockSpec((a, b, LANES), lambda i: (0, 0, i))
-
-
 def whole(*shape):
     return pl.BlockSpec(shape, lambda i: (0,) * len(shape))
 
 
-def ema_call(body, rows, dims, width, ins, outs, scratch, name, flops, collective_id=None):
-    specs = [s for _, s in ins]
+def ema_call(body, width, ins, outs, scratch, name, flops, collective_id):
     return pl.pallas_call(
-        functools.partial(body, rows, dims),
-        grid=(width // LANES,),
-        in_specs=specs,
+        body,
+        grid=(2 * (width // LANES),),
+        in_specs=[s for _, s in ins],
         out_specs=[s for _, s in outs],
         out_shape=[o for o, _ in outs],
         scratch_shapes=scratch,
         compiler_params=pltpu.CompilerParams(
-            vmem_limit_bytes=60 << 20, collective_id=collective_id, has_side_effects=collective_id is not None
+            vmem_limit_bytes=60 << 20, collective_id=collective_id, has_side_effects=True
         ),
         cost_estimate=pl.CostEstimate(flops=flops // 1000, bytes_accessed=1024, transcendentals=0),
         name=name,
@@ -464,6 +624,11 @@
     pack_ref, all_ref = own.pop(ins), own.pop(ins + outs)
     stages = gather_stages(parts, pack_ref, all_ref, *own[ins + outs + 1 :])
     step = pl.program_id(0)
+
+    @pl.when(step == 0)
+    def _():
+        greet(parts, 3)
+
     run_stages(stages, step, GATHER_PLAN, False)
     attend_kernel(halo, *own[: ins + outs + 1])
     run_stages(stages, step, GATHER_PLAN, True)
@@ -614,13 +779,56 @@
     )(*[v for v, _ in ins])
 
 
+def flipped(d, k):
+    return d + (1 - 2 * ((d // (1 << k)) % 2)) * (1 << k)
+
+
+def greet(parts, dp_bits):
+    d, z = lax.axis_index("dp"), lax.axis_index("tensor")
+    barrier = pltpu.get_barrier_semaphore()
+    for k in range(dp_bits):
+        pl.semaphore_signal(barrier, inc=1, device_id=(flipped(d, k), z), device_id_type=pl.DeviceIdType.MESH)
+    for step in (-2, -1, 1, 2):
+        @pl.when((z + step >= 0) & (z + step < parts))
+        def _():
+            pl.semaphore_signal(barrier, inc=1, device_id=(d, z + step), device_id_type=pl.DeviceIdType.MESH)
+    pl.semaphore_wait(barrier, dp_bits + jnp.minimum(z, 2) + jnp.minimum(parts - 1 - z, 2))
+
+
+class Along:
+    def __init__(self, parts, hop, src, dst, send_sem, recv_sem):
+        d, z = lax.axis_index("dp"), lax.axis_index("tensor")
+        to = z + hop
+        self.sends = (to >= 0) & (to < parts)
+        self.gets = (z - hop >= 0) & (z - hop < parts)
+        self.make = lambda: pltpu.make_async_remote_copy(
+            src_ref=src, dst_ref=dst, send_sem=send_sem, recv_sem=recv_sem,
+            device_id=(d, jnp.clip(to, 0, parts - 1)), device_id_type=pl.DeviceIdType.MESH,
+        )
+
+    def start(self):
+        @pl.when(self.sends)
+        def _():
+            self.make().start()
+
+    def wait_send(self):
+        @pl.when(self.sends)
+        def _():
+            self.make().wait_send()
+
+    def wait_recv(self, then=lambda: None):
+        @pl.when(self.gets)
+        def _():
+            self.make().wait_recv()
+            then()
+
+
 def gather_stages(parts, pack_ref, out_ref, sems, own_sem):
     d, z = lax.axis_index("dp"), lax.axis_index("tensor")
     total = pack_ref.shape[0]
     cut = total // 32 * 16
     upper, lower, full = pl.ds(0, cut), pl.ds(cut, total - cut), pl.ds(0, total)
-    flip = lambda k: d + (1 - 2 * ((d // (1 << k)) % 2)) * (1 << k)
-    core, first, second = flip(0), flip(1), flip(2)
+    core, first, second = (flipped(d, k) for k in range(3))
     across = first + second - d
     MESH = pl.DeviceIdType.MESH
 
@@ -636,14 +844,6 @@
     def begin():
         mine = pltpu.make_async_copy(pack_ref, out_ref.at[d, z], own_sem)
         mine.start()
-        barrier = pltpu.get_barrier_semaphore()
-        for other in (core, first, second):
-            pl.semaphore_signal(barrier, inc=1, device_id=(other, z), device_id_type=MESH)
-        for step in (-1, 1):
-            @pl.when((z + step >= 0) & (z + step < parts))
-            def _():
-                pl.semaphore_signal(barrier, inc=1, device_id=(d, z + step), device_id_type=MESH)
-        pl.semaphore_wait(barrier, 3 + jnp.minimum(z, 1) + jnp.minimum(parts - 1 - z, 1))
         mine.wait()
 
     def spread_block(b):
@@ -802,14 +1002,6 @@
         lax.fori_loop(0, count // tile, some, 0)
 
     def begin():
-        barrier = pltpu.get_barrier_semaphore()
-        for where in ((2 * me + 1 - core, z), (on(first), z), (on(second), z)):
-            pl.semaphore_signal(barrier, inc=1, device_id=where, device_id_type=MESH)
-        for step in (-1, 1):
-            @pl.when((z + step >= 0) & (z + step < parts))
-            def _():
-                pl.semaphore_signal(barrier, inc=1, device_id=(d, z + step), device_id_type=MESH)
-        pl.semaphore_wait(barrier, 3 + jnp.minimum(z, 1) + jnp.minimum(parts - 1 - z, 1))
         for s in range(parts):
             load(s).start()
             copies(s)(R_CORE).start()
@@ -874,92 +1066,262 @@
             def _():
                 c(R_LEFT).wait_send()
 
-    stages = [begin]
-    for s in range(parts + 2):
-        if s < parts:
-            stages.append(functools.partial(cores, s))
-        if 1 <= s <= parts:
-            stages.append(functools.partial(chips, s - 1))
-        if s >= 2:
-            stages.append(functools.partial(line, s - 2))
-    return stages + [finish]
-
-
-def small_sums_kernel(bits, small_ref, block_ref, out_ref, own_ref, acc, cube, buf, cbuf, sems):
-    d, t = lax.axis_index("dp"), lax.axis_index("tensor")
+    order = [(cores, 0), (cores, 1), (cores, 2), (chips, 0), (cores, 3), (chips, 1), (line, 0), (chips, 2), (line, 1),
+             (chips, 3), (line, 2), (line, 3)]
+    return [begin] + [functools.partial(f, s) for f, s in order] + [finish]
+
+
+def parts_of(v, count):
+    out = []
+    for _ in range(count):
+        out.append(v.astype(BF16))
+        v = v - out[-1].astype(F32)
+    return out
+
+
+def group_table(width, groups):
+    low = lax.broadcasted_iota(jnp.int32, (width, groups), 1) * (width // groups)
+    at = lax.broadcasted_iota(jnp.int32, (width, groups), 0)
+    return ((at >= low) & (at < low + width // groups)).astype(BF16)
+
+
+def add_rows(target, source, other, count, columns):
+    def some(i, carry):
+        here = pl.ds(pl.multiple_of(i * 32, 32), 32)
+        target[here, :] = (source[here, :].astype(F32) + other[here, :].astype(F32)).astype(BF16)
+        return carry
+
+    lax.fori_loop(0, count // 32 if count % 32 == 0 else 0, some, 0)
+    if count % 32:
+        target[...] = (source[...].astype(F32) + other[...].astype(F32)).astype(BF16)
+
+
+def end_kernel(
+    bits, parts, replicas, per_tile, hops, x_ref, mean_ref, rho_ref, count_ref, gain_ref, own_ref, ema_ref, back0_ref,
+    back1_ref, res_ref, segc_ref, segr_ref, next_ref, block_ref, *refs
+):
+    pieces, (ffn_ref, in_ref), outs, (own_sum_ref, ffn_sum_ref), scratch = (
+        refs[:6], refs[6:8], refs[8:15], refs[15:17], refs[17:]
+    )
+    (gh, cen, rf, backed, head, head_got, total, acc, cube, buf, cbuf, summed, chain, chain_got,
+     sems, head_sems, chain_sems) = scratch
+    d, z = lax.axis_index("dp"), lax.axis_index("tensor")
+    MESH = pl.DeviceIdType.MESH
+    rows, width = x_ref.shape
+    groups = mean_ref.shape[1]
+    tiles = width // LANES
+    greet(parts, sum(axis == "dp" for axis, _ in bits))
+
+    far = z // (parts // 2)
+    near_end = z + far * (parts - 1 - 2 * z)
+
+    def unit(s):
+        t = (parts - 1 - s) + near_end * ((3, 0, 2, 1)[s] - (parts - 1 - s))
+        return t + far * (parts - 1 - 2 * t)
+
+    def line_copy(s, side):
+        t = unit(s)
+        to = jnp.clip(z + (1 if side == 0 else -1), 0, parts - 1)
+        return pltpu.make_async_remote_copy(
+            src_ref=chain.at[t], dst_ref=chain_got.at[side, t], send_sem=chain_sems.at[0, side, t],
+            recv_sem=chain_sems.at[1, side, t], device_id=(d, to), device_id_type=MESH,
+        )
+
+    def along(s):
+        t = unit(s)
+        span, columns = chain.shape[1:]
+        from_left, from_right = (z <= t) & (z > 0), (z >= t) & (z < parts - 1)
+
+        @pl.when(from_left)
+        def _():
+            line_copy(s, 0).wait_recv()
+            add_rows(chain.at[t], ffn_ref.at[t], chain_got.at[0, t], span, columns)
+
+        @pl.when(jnp.logical_not(from_left))
+        def _():
+            chain[t] = ffn_ref[t]
+
+        @pl.when(from_right)
+        def _():
+            line_copy(s, 1).wait_recv()
+            add_rows(chain.at[t], chain.at[t], chain_got.at[1, t], span, columns)
+
+        @pl.when(z < t)
+        def _():
+            line_copy(s, 0).start()
+
+        @pl.when(z > t)
+        def _():
+            line_copy(s, 1).start()
 
     def mine(axis, k):
-        return ((d if axis == "dp" else t) // (1 << k)) % 2
+        return ((d if axis == "dp" else z) // (1 << k)) % 2
 
     def partner(axis, k):
         step = (1 - 2 * mine(axis, k)) * (1 << k)
-        return (d + step, t) if axis == "dp" else (d, t + step)
-
-    barrier = pltpu.get_barrier_semaphore()
-    for bit in bits:
-        pl.semaphore_signal(barrier, inc=1, device_id=partner(*bit), device_id_type=pl.DeviceIdType.MESH)
-    pl.semaphore_wait(barrier, len(bits))
-
-    def send(n, which, src, dst, bit):
-        copy = pltpu.make_async_remote_copy(
+        return (d + step, z) if axis == "dp" else (d, z + step)
+
+    def copy(n, which, src, dst):
+        return pltpu.make_async_remote_copy(
             src_ref=src, dst_ref=dst, send_sem=sems.at[0, which, n], recv_sem=sems.at[1, which, n],
-            device_id=partner(*bit), device_id_type=pl.DeviceIdType.MESH,
+            device_id=partner(*bits[n]), device_id_type=MESH,
         )
-        copy.start()
-        return copy
-
-    acc[...] = small_ref[...]
-    cube[...] = block_ref[...]
-    start, length, cstart, clength = 0, acc.shape[0], 0, cube.shape[0]
-    at, cat = 0, 0
-    trail = []
-    for n, bit in enumerate(bits):
-        axis, k = bit
+
+    plan = []
+    start, length, cstart, clength, at, cat = 0, acc.shape[0], 0, cube.shape[0], 0, 0
+    for axis, k in bits:
         half = length // 2
         keep = pl.multiple_of(start + mine(axis, k) * half, 8)
         give = pl.multiple_of(start + (1 - mine(axis, k)) * half, 8)
-        copies = [send(n, 0, acc.at[pl.ds(give, half)], buf.at[pl.ds(at, half)], bit)]
         if axis == "dp":
             chalf = clength // 2
-            ckeep = pl.multiple_of(cstart + mine(axis, k) * chalf, 8)
-            cgive = pl.multiple_of(cstart + (1 - mine(axis, k)) * chalf, 8)
+            ckeep = pl.multiple_of(cstart + mine(axis, k) * chalf, 16)
+            cgive = pl.multiple_of(cstart + (1 - mine(axis, k)) * chalf, 16)
         else:
             chalf, ckeep, cgive = clength, cstart, cstart
-        copies.append(send(n, 1, cube.at[pl.ds(cgive, chalf)], cbuf.at[pl.ds(cat, chalf)], bit))
-        for copy in copies:
-            copy.wait()
-        acc[pl.ds(keep, half)] += buf[pl.ds(at, half)]
-        cube[pl.ds(ckeep, chalf)] += cbuf[pl.ds(cat, chalf)]
-        trail.append((start, length))
+        plan.append((start, length, half, keep, give, chalf, ckeep, cgive, at, cat))
         start, length, cstart, clength = keep, half, ckeep, chalf
         at, cat = at + half, cat + chalf
-    own_ref[...] = cube[pl.ds(cstart, clength)]
-    out_ref[pl.ds(start, length)] = acc[pl.ds(start, length)]
-    for n, bit in reversed(list(enumerate(bits))):
-        copy = send(n, 2, out_ref.at[pl.ds(start, length)], out_ref.at[pl.ds(start, length)], bit)
-        copy.wait()
-        start, length = trail[n]
-
-
-def small_sums_call(small, block, replicas, parts):
+
+    def exchange(n):
+        _, _, half, _, give, chalf, _, cgive, at, cat = plan[n]
+        return (copy(n, 0, acc.at[pl.ds(give, half)], buf.at[pl.ds(at, half)]),
+                copy(n, 1, cube.at[pl.ds(cgive, chalf)], cbuf.at[pl.ds(cat, chalf)]))
+
+    def send(n):
+        for c in exchange(n):
+            c.start()
+
+    def receive(n):
+        for c in exchange(n):
+            c.wait()
+        _, _, half, keep, _, chalf, ckeep, _, at, cat = plan[n]
+        acc[pl.ds(keep, half)] += buf[pl.ds(at, half)]
+        both = cube[pl.ds(ckeep, chalf)].astype(F32) + cbuf[pl.ds(cat, chalf)].astype(F32)
+        cube[pl.ds(ckeep, chalf)] = both.astype(BF16)
+
+    along(0)
+
+    table = group_table(width, groups)
+    spread_of = lambda v: sum(dot32(p, table, NT) for p in parts_of(v, 3))
+    sums_of = lambda v: sum(dot32(p, table) for p in parts_of(v, 2))
+    gh[...] = own_ref[...] + ema_ref[...] + back0_ref[...].astype(F32)
+    gh[rows - hops[1] :, :] += back1_ref[...].astype(F32)
+    mean, rho, count = mean_ref[...], rho_ref[...], count_ref[...]
+    rf[...] = spread_of(rho)
+    cen[...] = x_ref[...].astype(F32) - spread_of(mean)
+    gain_grad = jnp.sum(cen[...] * rf[...] * gh[...], axis=0, keepdims=True)
+    last_rows = jnp.zeros((per_tile - sum(p.shape[0] for p in pieces) - 1, LANES), F32)
+    for tile in range(tiles):
+        lanes = slice(tile * LANES, (tile + 1) * LANES)
+        row = tile * per_tile
+        for p in pieces:
+            acc[row : row + p.shape[0], :] = p[:, lanes]
+            row += p.shape[0]
+        acc[row : row + 1, :] = gain_grad[:, lanes]
+        acc[row + 1 : (tile + 1) * per_tile, :] = last_rows
+    depth = block_ref.shape[0] // replicas
+    levels = replicas.bit_length() - 1
+    for b in range(replicas):
+        m = sum(((b >> k) & 1) << (levels - 1 - k) for k in range(levels))
+        cube[m * depth : (m + 1) * depth, :] = block_ref[b * depth : (b + 1) * depth, :].astype(BF16)
+    send(0)
+
+    gh[...] = gh[...] * gain_ref[...]
+    sum_a, sum_b = rho * sums_of(gh[...]), sums_of(gh[...] * cen[...])
+    third = sum_b * rho * rho * rho
+    lower = (segc_ref[...] == segr_ref[...]) & (
+        lax.broadcasted_iota(jnp.int32, (rows, rows), 0) >= lax.broadcasted_iota(jnp.int32, (rows, rows), 1)
+    )
+    lower = lower.astype(F32).astype(BF16)
+    back = lambda v: sum(dot32(lower, p, TN) for p in parts_of(v, 3))
+    backed[0] = back((third * mean - sum_a) / count)
+    backed[1] = back(-third / (2.0 * count))
+    for half in range(2):
+        head[half, :, :groups] = backed[half, 0:8, :]
+    to_heads = [Along(parts, -hop, head, head_got.at[hop - 1], head_sems.at[0, hop - 1], head_sems.at[1, hop - 1])
+                for hop in (1, 2)]
+    for move in to_heads:
+        move.start()
+    receive(0)
+    send(1)
+    along(1)
+    total[...] = jnp.zeros_like(total)
+    for hop, move in enumerate(to_heads):
+        def arrived(hop=hop):
+            total[...] += next_ref[hop : hop + 1, :] * head_got[hop]
+        move.wait_recv(arrived)
+    tails = (segc_ref[...] == segc_ref[rows - 1 : rows, :]).astype(F32)
+    first, second = (backed[half] + tails * total[half, 0:1, :groups] for half in range(2))
+    in_ref[...] = res_ref[...] + gh[...] * rf[...] + spread_of(first) + 2.0 * x_ref[...].astype(F32) * spread_of(second)
+
+    for n in range(1, len(bits)):
+        receive(n)
+        if n + 1 < len(bits):
+            send(n + 1)
+        if n + 1 < parts:
+            along(n + 1)
+    clast = pl.multiple_of(plan[-1][6], 16)
+    own_sum_ref[...] = cube[pl.ds(clast, clength)].astype(F32)
+    summed[pl.ds(start, length)] = acc[pl.ds(start, length)]
+    for n in reversed(range(len(bits))):
+        here = summed.at[pl.ds(start, length)]
+        copy(n, 2, here, here).start()
+        copy(n, 2, here, here).wait()
+        start, length = plan[n][:2]
+    for tile in range(tiles):
+        lanes = slice(tile * LANES, (tile + 1) * LANES)
+        row = tile * per_tile
+        for out in outs:
+            out[:, lanes] = summed[row : row + out.shape[0], :]
+            row += out.shape[0]
+    ffn_sum_ref[...] = chain[z].astype(F32)
+    for s in range(parts):
+        @pl.when(z < unit(s))
+        def _():
+            line_copy(s, 0).wait_send()
+
+        @pl.when(z > unit(s))
+        def _():
+            line_copy(s, 1).wait_send()
+    for move in to_heads:
+        move.wait_send()
+
+
+def end_call(replicas, parts, hops, per_row, pieces, ffn):
     bits = [("dp", k) for k in range(replicas.bit_length() - 1)]
     bits += [("tensor", k) for k in range(parts.bit_length() - 1)]
+    x, block = per_row[0], per_row[-1]
+    rows, width = x.shape
+    tiles = width // LANES
+    wanted = tiles * (sum(p.shape[0] for p in pieces) + 1)
+    unit = max(replicas * parts * 8, tiles * 8)
+    per_tile = -(-wanted // unit) * unit // tiles
+    small = (tiles * per_tile, LANES)
     own = block.shape[0] // replicas
     got = sum(block.shape[0] >> (k + 1) for k in range(replicas.bit_length() - 1))
     got += own * (parts.bit_length() - 1)
-    vmem = pl.BlockSpec(memory_space=pltpu.VMEM)
+    groups = per_row[1].shape[1]
+    vm = pltpu.VMEM
+    dma = lambda *n: pltpu.SemaphoreType.DMA(n)
+    shape = jax.ShapeDtypeStruct
+    ins = (*per_row, *pieces, ffn)
+    outs = ([shape((rows, width), F32)] + [shape(p.shape, F32) for p in pieces]
+            + [shape((1, width), F32), shape((own, block.shape[1]), F32), shape(ffn.shape[1:], F32)])
     return pl.pallas_call(
-        functools.partial(small_sums_kernel, bits),
-        in_specs=[vmem, vmem],
-        out_specs=[vmem, vmem],
-        out_shape=[jax.ShapeDtypeStruct(small.shape, F32), jax.ShapeDtypeStruct((own, block.shape[1]), F32)],
+        functools.partial(end_kernel, bits, parts, replicas, per_tile, hops),
+        in_specs=[pl.BlockSpec(memory_space=vm)] * len(ins),
+        out_specs=[pl.BlockSpec(memory_space=vm)] * len(outs),
+        out_shape=outs,
         scratch_shapes=[
-            pltpu.VMEM(small.shape, F32), pltpu.VMEM(block.shape, F32), pltpu.VMEM(small.shape, F32),
-            pltpu.VMEM((got, block.shape[1]), F32), pltpu.SemaphoreType.DMA((2, 3, len(bits))),
+            vm((rows, width), F32), vm((rows, width), F32), vm((rows, width), F32), vm((2, rows, groups), F32),
+            vm((2, 8, LANES), F32), vm((2, 2, 8, LANES), F32), vm((2, 8, LANES), F32), vm(small, F32),
+            vm(block.shape, BF16), vm(small, F32), vm((got, block.shape[1]), BF16), vm(small, F32),
+            vm(ffn.shape, BF16), vm((2,) + ffn.shape, BF16), dma(2, 3, len(bits)), dma(2, 2), dma(2, 2, parts),
         ],
-        compiler_params=pltpu.CompilerParams(collective_id=0, has_side_effects=True, vmem_limit_bytes=24 << 20),
-        name="small_sums",
-    )(small, block)
+        compiler_params=pltpu.CompilerParams(collective_id=0, has_side_effects=True, vmem_limit_bytes=60 << 20),
+        name="ending",
+    )(*ins)
 
 
 def on_device(
@@ -1009,10 +1371,11 @@
     pack_a = jnp.concatenate(
         [low(w_value), low(w_gate), low(w_out.T), low(shared_piece).reshape(-1, vw)], axis=0
     )
-    pack_f = jnp.concatenate([low(w_swish), low(w_up), low(w_down.T)], axis=0)
-    all_a = lax.all_gather(pack_a, BOTH, axis=0).reshape(replicas, parts, -1, vw)
-    pack_f = with_layout_constraint(pack_f, Layout((0, 1)))
-    shared_b = all_a[:, :, 3 * depth :].reshape(width, latent_width)
+    pack_f1 = low(w_swish)
+    pack_f2 = jnp.concatenate([low(w_up), low(w_down.T)], axis=0)
+    gathered = lambda v: lax.all_gather(v, BOTH, axis=0).reshape(replicas, parts, *v.shape)
+    all_f1 = gathered(pack_f1)
+    pack_f2 = with_layout_constraint(pack_f2, Layout((0, 1)))
 
     def part(k, columns):
         return pl.BlockSpec((replicas, 1, depth, columns), lambda t: (0, t, k, 0))
@@ -1064,48 +1427,47 @@
     gcount = rows // (8 * STEP)
     nstate = gcount * dims * 2
     at_rows = gcount * STEP
-    state_shape = (jax.ShapeDtypeStruct((nstate, 8, width), F32), col3(nstate, 8))
-    edge_shape = (jax.ShapeDtypeStruct((2 * dims, width), F32), col(2 * dims))
-    dim_shape = (jax.ShapeDtypeStruct((dims, width), F32), col(dims))
-    rows_shape = (jax.ShapeDtypeStruct((rows, width), F32), col(rows))
+    blocks = width // LANES
+    col = lambda n: pl.BlockSpec((n, LANES), lambda i: (0, i % blocks))
+    late = lambda n: pl.BlockSpec((n, LANES), lambda i: (0, jnp.maximum(i - blocks, 0)))
+    late3 = lambda n, m: pl.BlockSpec((n, m, LANES), lambda i: (0, 0, jnp.maximum(i - blocks, 0)))
+    anywhere = pl.BlockSpec(memory_space=pl.ANY)
+    shape_of = jax.ShapeDtypeStruct
     mask_spec = whole(at_rows, 8, LANES)
     cont, mk, mkr = (
         (masks["cont"], whole(gcount, 8, LANES)), (masks["mk"], whole(3, 8, LANES)), (masks["mkr"], whole(3, 8, LANES))
     )
     kend, keep0, seg8 = ((masks[k], mask_spec) for k in ("kend", "keep0", "seg"))
-    pair, single = col(2 * dims), col(dims)
-    vm = lambda n: pltpu.VMEM((n, 8, LANES), F32)
+    lane = lambda v: (jnp.full((1, LANES), v, F32), whole(1, LANES))
+    vm = lambda *n: pltpu.VMEM((*n, 8, LANES), F32)
     flat_vm = lambda *n: pltpu.VMEM((*n, LANES), F32)
+    dma = lambda *n: pltpu.SemaphoreType.DMA(n)
     table_vm, scale_vm = flat_vm(2, STEP * dims), flat_vm(8 * dims)
+    state_vms = [vm(blocks, nstate), flat_vm(blocks, 2 * dims), flat_vm(2, blocks, 2 * dims), flat_vm(2 * dims),
+                 dma(2, 2, blocks), dma(2, 2), dma(4)]
     mac = rows * width * dims * 4
-    entering, end, turn = ema_call(
-        ema_enter, rows, dims, width,
-        [(hidden, col(rows)), kend, (unit, pair), (feed, single), cont, mk],
-        [state_shape, edge_shape, edge_shape], [vm(at_rows), table_vm, scale_vm], "ema_enter", mac,
+    zeros = (jnp.zeros((rows, width), BF16), anywhere)
+    near_rows = halo + rows
+    results = ema_call(
+        functools.partial(ema_forward, rows, dims, parts, halo, hops, chip_links), width,
+        [(hidden, col(rows)), kend, seg8, keep0, (unit, col(2 * dims)), (feed, col(dims)), (reads, col(2 * dims)), cont,
+         mk, lane(link2), (skip, col(1)), (hidden_b, anywhere), zeros] + [(pack_a, anywhere)] * chip_links,
+        [(shape_of((rows, width), F32), late(rows)), (shape_of((rows, width), BF16), late(rows)),
+         (shape_of((nstate, 8, width), F32), late3(nstate, 8)), (shape_of((near_rows, width), BF16), anywhere)]
+        + [(shape_of((replicas, parts) + pack_a.shape, BF16), anywhere)] * chip_links,
+        [vm(2 * at_rows), table_vm, scale_vm] + state_vms + (gather_scratch(parts) if chip_links else []),
+        "ema_forward", 2 * mac, 3,
     )
-
-    def turned(v, sign):
-        r, i = times(turn[:dims], sign * turn[dims:], v[:dims], v[dims:])
-        return jnp.concatenate([r, i])
-
-    state_in = from_earlier(end, 1) + link2 * turned(from_earlier(end, 2), 1.0)
-    ema_out, mixed, states = ema_call(
-        ema_read, rows, dims, width,
-        [(hidden, col(rows)), seg8, keep0, (unit, pair), (feed, single), (reads, pair), cont, mk,
-         (entering, col3(nstate, 8)), (state_in, pair), (skip, col(1))],
-        [rows_shape, (jax.ShapeDtypeStruct((rows, width), BF16), col(rows)), state_shape],
-        [vm(2 * at_rows), table_vm, scale_vm], "ema_read", mac,
-    )
-
-    hidden_near = halo_of(lax.optimization_barrier((hidden_b, state_in))[0])
-    near_rows = halo + rows
+    ema_out, mixed, states, hidden_near = results[:4]
+    all_a = results[-1] if chip_links else gathered(pack_a)
+    shared_b = all_a[:, :, 3 * depth :].reshape(width, latent_width)
+
     latent = dot32(mixed, shared_b)
     queries = low(latent * query_gain + query_bias)
     keys_near = halo_of(low(latent * key_gain))
     one = lambda v: v[None]
     matmul = rows * width * vw * 2 * parts
     col_v = lambda n: ((n, value_width), BF16, "col")
-    anywhere = pl.BlockSpec(memory_space=pl.ANY)
     ins = [(queries, "all"), (keys_near, "all"), (seg[:, None], "all"), (one(seg_keys), "all"), (hidden_near, "all"),
            (mixed, "all"), (block_in, "all"), (one(ffn_gain), "all"), (all_a, part(0, vw)), (all_a, part(1, vw)),
            (all_a, part(2, vw))]
@@ -1115,20 +1477,20 @@
     if chip_links:
         results = stage_call(
             functools.partial(attend_gather_kernel, halo, parts, len(ins), len(outs)), parts,
-            ins + [(pack_f, anywhere)], outs + [((replicas, parts) + pack_f.shape, BF16, anywhere)],
+            ins + [(pack_f2, anywhere)], outs + [((replicas, parts) + pack_f2.shape, BF16, anywhere)],
             scratch + gather_scratch(parts), "attend", 6 * matmul, collective_id=1,
         )
-        all_f = results[-1]
+        all_f2 = results[-1]
     else:
         results = stage_call(functools.partial(attend_kernel, halo), parts, ins, outs, scratch, "attend", 6 * matmul)
-        all_f = lax.all_gather(pack_f, BOTH, axis=0).reshape(replicas, parts, 3 * depth, fw)
+        all_f2 = gathered(pack_f2)
     probs, value_pre, values, gate_pre, attended, gated, residual, norm_in = results[:8]
 
     row_vm = lambda n: pltpu.VMEM((n, width), F32)
     block_out, grad_residual, branch, grad_ffn_gain, ffn_grads = stage_call(
         ffn_kernel, parts,
-        [(residual, "all"), (norm_in, "all"), (out_grad, "all"), (one(ffn_gain), "all"), (all_f, part(0, fw)),
-         (all_f, part(1, fw)), (all_f, part(2, fw))],
+        [(residual, "all"), (norm_in, "all"), (out_grad, "all"), (one(ffn_gain), "all"), (all_f1, part(0, fw)),
+         (all_f2, part(0, fw)), (all_f2, part(1, fw))],
         [((rows, width), BF16, "all"), ((rows, width), F32, "all"), ((rows, width), BF16, "all"),
          ((1, width), F32, "all"),
          ((replicas, parts, 3, depth, fw), BF16,
@@ -1158,7 +1520,6 @@
         [pltpu.VMEM((rows, near_rows), F32), row_vm(near_rows), pltpu.VMEM((rows, near_rows), BF16)], "attend_back", 12 * matmul,
     )
     grad_keys = give_back(keys_own, keys_back)
-    grad_hidden = give_back(hidden_own, lax.optimization_barrier((hidden_back, grad_keys))[0])
     grad_query_gain = jnp.sum(latent * grad_queries, axis=0)
     grad_query_bias = jnp.sum(grad_queries, axis=0)
     grad_key_gain = jnp.sum(latent * grad_keys, axis=0)
@@ -1166,74 +1527,45 @@
     grad_shared = dot32(mixed, grad_latent, TN)
     grad_ema = (dot32(grad_latent, shared_b, NT) + grad_mixed) * silu_slope(ema_out)
 
-    pulls, head = ema_call(
-        ema_leave, rows, dims, width,
-        [(grad_ema, col(rows)), keep0, (unit, pair), (reads, pair), cont, mkr],
-        [state_shape, edge_shape], [vm(at_rows), table_vm, scale_vm], "ema_leave", mac,
+    cross = (near[halo + 2 * rows - 1] == last).astype(F32)
+    dim_late = late(dims)
+    results = ema_call(
+        functools.partial(ema_backward, rows, dims, parts, halo, hops, chip_links), width,
+        [(hidden, late(rows)), (grad_ema, col(rows)), seg8, kend, keep0, (masks["rk0"], whole(rows, LANES)),
+         (masks["rkend"], whole(rows, LANES)), (unit, col(2 * dims)), (feed, dim_late), (reads, col(2 * dims)),
+         (root, dim_late), (ema_input, dim_late), cont, mkr, (states, late3(nstate, 8)), lane(cross), (skip, late(1)),
+         (hidden_back, anywhere), zeros]
+        + [(attn_grads.reshape(replicas // 2, 2, parts, 3 * depth, vw), anywhere)] * chip_links,
+        [(shape_of((rows, width), F32), late(rows)), (shape_of((2 * dims, width), F32), late(2 * dims))]
+        + [(shape_of((dims, width), F32), dim_late)] * 3 + [(shape_of((1, width), F32), late(1))]
+        + [(shape_of((n, width), BF16), anywhere) for n in hops]
+        + [(shape_of((3 * depth, vw), F32), whole(3 * depth, vw))] * chip_links,
+        state_vms + [vm(2 * at_rows), vm(at_rows), vm(nstate), table_vm, scale_vm, flat_vm(4, STEP * dims),
+                     flat_vm(9, dims), flat_vm(rows), flat_vm(rows)]
+        + (reduce_scratch(parts, 3 * depth, vw) if chip_links else []),
+        "ema_backward", 4 * mac, 2,
     )
-    cross = (near[halo + 2 * rows - 1] == last).astype(F32)
-    pull_in = from_later(head, 1) + cross * turned(from_later(head, 2), -1.0)
-    ins = [(hidden, col(rows)), (grad_ema, col(rows)), seg8, kend, (masks["rk0"], whole(rows, LANES)),
-           (masks["rkend"], whole(rows, LANES)), (unit, pair), (feed, single), (reads, pair), (root, single),
-           (ema_input, single), cont, mkr, (pulls, col3(nstate, 8)), (pull_in, pair), (states, col3(nstate, 8)),
-           (skip, col(1))]
-    outs = [rows_shape, edge_shape, dim_shape, dim_shape, dim_shape, (jax.ShapeDtypeStruct((1, width), F32), col(1))]
-    scratch = [vm(2 * at_rows), vm(at_rows), vm(nstate), table_vm, scale_vm, flat_vm(4, STEP * dims), flat_vm(9, dims),
-               flat_vm(rows), flat_vm(rows)]
-    if chip_links:
-        results = ema_call(
-            functools.partial(ema_grads_reduce, parts, len(ins), len(outs), len(scratch)), rows, dims, width,
-            ins + [(attn_grads.reshape(replicas // 2, 2, parts, 3 * depth, vw), anywhere)],
-            outs + [(jax.ShapeDtypeStruct((3 * depth, vw), F32), whole(3 * depth, vw))],
-            scratch + reduce_scratch(parts, 3 * depth, vw), "ema_grads", 3 * mac, collective_id=2,
-        )
-        attn_sum = results[-1]
-    else:
-        results = ema_call(ema_grads, rows, dims, width, ins, outs, scratch, "ema_grads", 3 * mac)
-        attn_sum = summed_along(summed(attn_grads), results[-1])
     grad_hidden_ema, output_grad, input_grad, rate_grad, angle_grad, grad_skip = results[:6]
-
-    ffn_sum = summed_along(ffn_sum, grad_skip)
-
-    grad_hidden = grad_hidden + grad_hidden_ema
-    gain_grad = jnp.sum(centred * grad_hidden, axis=0)
-    spread_grad = grad_hidden * norm_gain
-    sum_a = rho * sums_of(spread_grad)
-    sum_b = sums_of(spread_grad * (x - mean_full))
-    cube = sum_b * rho * rho * rho
-    push = jnp.concatenate([(cube * mean - sum_a) / count, -cube / (2.0 * count)], axis=1)
-    backed = dot32(lower, push, TN, precision=HIGHEST)
-    first = backed[:1]
-    carry = next1 * from_later(first, 1) + next2 * from_later(first, 2)
-    backed = backed + tails * carry
-    grad_x = spread_grad * rho_full + spread_of(backed[:, :groups]) + 2.0 * x * spread_of(backed[:, groups:])
-    in_grad = grad_residual + grad_x
-
-    small = [gain_grad, rate_grad, angle_grad, input_grad, output_grad, grad_skip, grad_query_gain,
-             grad_query_bias, grad_key_gain, grad_ffn_gain]
-    sizes = [v.size for v in small]
-    total = sum(sizes)
-    members = parts * replicas
-    unit = members * 8 * LANES
-    packed = jnp.concatenate([v.reshape(-1) for v in small] + [jnp.zeros((-total % unit,), F32)])
-    packed = packed.reshape(-1, LANES)
-    levels = replicas.bit_length() - 1
-    mirror = lambda v: v.transpose(tuple(reversed(range(levels))) + (levels, levels + 1))
-    block = mirror(grad_shared.reshape((2,) * levels + (depth, latent_width)))
-    packed, shared_sum = small_sums_call(packed, block.reshape(width, latent_width), replicas, parts)
-    packed = packed.reshape(-1)
-    small_sums, at = [], 0
-    for n in sizes:
-        small_sums.append(packed[at : at + n])
-        at += n
-    shape = lambda k, like: small_sums[k].reshape(like.shape)
+    attn_sum = results[-1] if chip_links else summed_along(summed(attn_grads), grad_skip)
+    zero = jnp.zeros((1, width - 3 * latent_width), F32)
+    latents = jnp.concatenate([grad_query_gain[None], grad_query_bias[None], grad_key_gain[None], zero], axis=1)
+    nexts = jnp.stack([next1, jnp.asarray(next2, F32)])[:, None] * jnp.ones((1, LANES), F32)
+    results = end_call(
+        replicas, parts, hops,
+        (block_in, mean, rho, count, norm_gain[None], hidden_own, grad_hidden_ema, results[6], results[7],
+         grad_residual, seg[:, None], seg[None], nexts, grad_shared),
+        (output_grad, input_grad, rate_grad, angle_grad, grad_skip,
+         jnp.concatenate([grad_ffn_gain, latents], axis=0)),
+        ffn_sum,
+    )
+    in_grad, output_grad, input_grad, rate_grad, angle_grad, skip_grad, two, gain_grad, shared_sum, ffn_sum = results
+    latents = two[1].reshape(-1, latent_width)
 
     cut = lambda g, k: g[k * depth : (k + 1) * depth]
     return (
-        block_out, in_grad, shape(0, norm_gain), shape(1, ema_rate), shape(2, ema_angle), shape(3, ema_input),
-        shape(4, ema_output), shape(5, ema_skip), shared_sum, shape(6, query_gain), shape(7, query_bias),
-        shape(8, key_gain), cut(attn_sum, 0), cut(attn_sum, 1), cut(attn_sum, 2).T, shape(9, ffn_gain),
-        cut(ffn_sum, 0), cut(ffn_sum, 1), cut(ffn_sum, 2).T,
+        block_out, in_grad, gain_grad[0], rate_grad, angle_grad, input_grad, output_grad.reshape(ema_output.shape),
+        skip_grad[0], shared_sum, latents[0], latents[1], latents[2], cut(attn_sum, 0), cut(attn_sum, 1),
+        cut(attn_sum, 2).T, two[0], cut(ffn_sum, 0), cut(ffn_sum, 1), cut(ffn_sum, 2).T,
     )
 
 

time: 626 us -> 593 us (0.947)
  Pallas kernels: 381 us -> 459 us
  waiting for transfers between devices: 82.3 us -> 11.4 us
  other arithmetic: 34.3 us -> 12.9 us
  starting transfers between devices: 41.9 us -> 32.2 us
  local copies, waits for them, and re-layouts: 42.1 us -> 34.7 us
    pallas_call x5 -> x3, Pallas kernels: 193 us -> 301 us  [the longest x2 226 us: ema_call(): pl.pallas_call(body, grid=(2 * (width // LANES),), in_specs=[s for _, s i...]
    all_gather x1, waiting for transfers between devices: 40.6 us -> 0.02 us  [on_device(): lax.all_gather(v, BOTH, axis=0).reshape(replicas, parts, *v.shape)]
    pallas_call x3, Pallas kernels: 188 us -> 158 us  [stage_call(): pl.pallas_call(body, grid=(steps,), in_specs=[spec(v, how) for v, how in...]
    ppermute x8 -> x2, waiting for transfers between devices: 33.2 us -> 10.6 us  [from_later(): return lax.ppermute(x, 'tensor', [(i + hop, i) for i in range(parts - hop)])]
    ppermute x8 -> x2, starting transfers between devices: 10.9 us -> 2.72 us  [from_later(): return lax.ppermute(x, 'tensor', [(i + hop, i) for i in range(parts - hop)])]
    ppermute x8 -> x4, waiting for transfers between devices: 8.43 us -> 0.76 us  [from_earlier(): return lax.ppermute(x, 'tensor', [(i, i + hop) for i in range(parts - hop)])]
    concatenate x2 -> x1, other arithmetic: 7.5 us -> 1.14 us  [halo_of(): return jnp.concatenate([ahead] + pieces[::-1] + [x], axis=0)]
    unnamed x103 -> x78, local copies, waits for them, and re-layouts: 13.3 us -> 7.85 us
  transfers between devices with their start and end apart: 19 -> 8, of which waited for: 7 -> 3; matrix products, arithmetic and copies ran while one was open for 13% -> 8% of each run, Pallas kernels for 39% -> 59%
where the time goes in v4:
time: 593 us; the launch traced here: 585 us
  Pallas kernels  459 us (77%)
  local copies, waits for them, and re-layouts  34.7 us (6%)
  starting transfers between devices  32.2 us (5%)
  between operations  20.1 us (3%)
  matrix products  13.9 us (2%)
  other arithmetic  12.9 us (2%)
  waiting for transfers between devices  11.4 us (2%)
    pallas_call x2, Pallas kernels, ema_call(): pl.pallas_call(body, grid=(2 * (width // LANES),), in_specs=[s for _, s i...  226 us
    pallas_call x3, Pallas kernels, stage_call(): pl.pallas_call(body, grid=(steps,), in_specs=[spec(v, how) for v, how in...  158 us
    pallas_call x1, Pallas kernels, end_call(): pl.pallas_call(functools.partial(end_kernel, bits, parts, replicas, per_t...  74.9 us
    ppermute x4, starting transfers between devices, from_earlier(): return lax.ppermute(x, 'tensor', [(i, i + hop) for i in range(parts - hop)])  29.4 us
    dot_general x8, matrix products, dot32(): lax.dot_general(a, b, (dims, ((), ())), precision=precision, preferred_el...  13.9 us
  transfers between devices with their start and end apart: 8, of which 3 were waited for; matrix products, arithmetic and copies ran while one was open for 8% of the time, Pallas kernels for 59%

profile of v4, /device:TPU:0, one launch (start us, length us, event | category | flops | bytes accessed | tf_op | source)
XLA Modules:
  0.0 584.5 jit_solution(351721406167977569)
XLA Ops:
  7.3 1.7 convert_element_type.126
  9.0 0.8 fusion.21
  9.8 1.8 convolution_bitcast_fusion
  11.7 2.5 fusion
  14.9 4.9 collective-permute-start
  19.8 4.5 collective-permute-start.1
  25.5 0.7 pad_add_fusion
  28.2 0.7 pad_add_fusion.1
  29.0 0.6 gather_fusion
  29.6 0.6 gather_fusion.1
  30.3 0.6 gather_fusion.2
  31.4 0.9 subtract_sqrt_fusion
  32.3 0.7 pad_maximum_fusion.3.q_ref
  33.0 0.8 pad_maximum_fusion.1.refs_0_
  34.4 0.7 compare_convert_fusion
  35.7 1.1 fusion.6
  36.8 3.0 fusion.29
  39.9 0.7 broadcast_in_dim.135.mk_ref
  40.5 0.8 broadcast_in_dim.128.kend_ref
  41.4 0.8 broadcast_in_dim.133.k0_ref
  42.2 0.7 broadcast_in_dim.134.cont_ref
  43.4 0.8 broadcast_in_dim.130.seg_ref
  44.2 1.1 broadcast_in_dim.138.zeros_ref
  45.3 123.4 %ema_forward.1 = (f32[512,1024]{1,0:T(8,128)}, bf16[512,1024]{1,0:T(8,128)(2,1)}, f32[128,8,1024]{2,1,0:T(8,128)}, bf16[1408,1024]{1,0:T(8,128)(2,1)}, bf16[8,4,400,512]{3,2,1,0:T(8,128)(2,1)}) custom-call(f32[512,1024]{1,0:T(8,128)} %get-tuple-element.261.h_ref, f32[64,8,128]{2,1,0:T(8,128)} %broadcast_in_dim.128.kend_ref, ...), custom_call_target="tpu_custom_call" | custom-call | flops 67108 | bytes 1024 | tf_op jit(solution)/shard_map/ema_forward/pallas_call | solution.py:569
  168.8 1.2 slice.148
  170.2 1.1 multiply_convert_fusion
  171.3 1.3 collective-permute-start.3
  172.7 18.7 %collective-permute-start.2 = (bf16[288,256]{1,0:T(8,128)(2,1)S(1)}, bf16[288,256]{1,0:T(8,128)(2,1)S(1)}, u32[]{:S(2)}, u32[]{:S(2)}) collective-permute-start(bf16[288,256]{1,0:T(8,128)(2,1)S(1)} %slice.188), channel_id=1, source_target_pairs={{0,2},{1,3},{4,6},{5,7},{8,10},{9,11},{12,14},{13,15},{16,18},{17,... | collective-permute-start | bytes 442376 | tf_op jit(solution)/shard_map/ppermute | solution.py:1347
  191.4 0.9 copy.85.refs_2_.segc_ref
  193.1 0.8 pad_maximum_fusion.2.refs_11_
  193.9 0.8 collective-permute-done.2
  194.6 1.1 pad_maximum_fusion.refs_1_.k_ref
  195.8 71.1 %attend.1 = (f32[512,1408]{1,0:T(8,128)}, bf16[1408,2048]{1,0:T(8,128)(2,1)}, bf16[1408,2048]{1,0:T(8,128)(2,1)}, bf16[512,2048]{1,0:T(8,128)(2,1)}, bf16[512,20...) custom-call(bf16[512,256]{1,0:T(8,128)(2,1)} %get-tuple-element.231., ...), custom_call_target="tpu_custom_call" | custom-call | flops 12884901 | bytes 1024 | tf_op jit(solution)/shard_map/attend/pallas_call | solution.py:767
  266.9 40.0 %ffn.1 = (bf16[512,1024]{1,0:T(8,128)(2,1)}, f32[512,1024]{1,0:T(8,128)}, bf16[512,1024]{1,0:T(8,128)(2,1)}, f32[1,1024]{1,0:T(1,128)}, bf16[8,4,3,128,640]{4,3,2,1,0:T(8,128)(2,1)}) custom-call(f32[512,1024]{1,0:T(8,128)} %get-tuple-element.100.y_ref, bf16[512,1024]{1,0:T(8,128)(2,1)} %get-tuple-element.101.n_ref, bf16[512,1024]{1,0:T(8,128)(2,1)} %og_ref.1, ...), custom_call_target="tpu_custom_call" | custom-call | flops 23622320 | bytes 1024 | tf_op jit(solution)/shard_map/ffn/pallas_call | solution.py:767
  307.0 0.6 gather_fusion.4
  307.6 0.6 gather_fusion.5
  308.3 0.6 gather_fusion.3
  312.8 47.0 %attend_back.1 = (f32[512,256]{1,0:T(8,128)}, bf16[896,256]{1,0:T(8,128)(2,1)}, f32[512,256]{1,0:T(8,128)}, bf16[896,1024]{1,0:T(8,128)(2,1)}, f32[512,1024]{1,0...) custom-call(bf16[512,1024]{1,0:T(8,128)(2,1)} %get-tuple-element.104.br_ref, ...), custom_call_target="tpu_custom_call" | custom-call | flops 25769804 | bytes 1024 | tf_op jit(solution)/shard_map/attend_back/pallas_call | solution.py:767
  359.8 1.0 slice.151
  360.8 1.3 collective-permute-start.4
  362.3 0.8 convert_multiply_fusion.2.count_ref
  363.1 1.1 slice.153
  364.2 1.4 collective-permute-start.5
  365.6 7.0 %collective-permute-done.4 = bf16[512,256]{1,0:T(8,128)(2,1)S(1)} collective-permute-done((bf16[512,256]{1,0:T(8,128)(2,1)S(1)}, bf16[512,256]{1,0:T(8,128)(2,1)S(1)}, u32[]{:S(2)}, u32[]{:S(2)}) %collective-permute-start.4) | collective-permute-done | bytes 262176 | tf_op jit(solution)/shard_map/ppermute | solution.py:1350
  372.7 1.1 convert_add_fusion
  373.8 3.6 collective-permute-done.5
  377.6 2.3 multiply_multiply_fusion.de_ref
  379.9 0.7 broadcast_in_dim.146.mkr_ref
  380.6 0.8 broadcast_in_dim.144.rk0_ref
  381.4 0.8 broadcast_in_dim.145.rkend_ref
  382.8 102.7 %ema_backward.1 = (f32[512,1024]{1,0:T(8,128)}, f32[32,1024]{1,0:T(8,128)}, f32[16,1024]{1,0:T(8,128)}, f32[16,1024]{1,0:T(8,128)}, f32[16,1024]{1,0:T(8,128)}, ...) custom-call(f32[512,1024]{1,0:T(8,128)} %get-tuple-element.261.h_ref, ...), custom_call_target="tpu_custom_call" | custom-call | flops 134217 | bytes 1024 | tf_op jit(solution)/shard_map/ema_backward/pallas_call | solution.py:569
  485.5 2.0 slice_bitcast_fusion.1
  487.6 0.8 copy.89
  489.0 1.5 fusion.30.block_ref
  490.5 0.6 mul.145.next_ref
  491.1 74.9 %ending.1 = (f32[512,1024]{1,0:T(8,128)}, f32[32,1024]{1,0:T(8,128)}, f32[16,1024]{1,0:T(8,128)}, f32[16,1024]{1,0:T(8,128)}, f32[16,1024]{1,0:T(8,128)}, /*inde...) custom-call(bf16[512,1024]{1,0:T(8,128)(2,1)} %x_ref.1, ...), custom_call_target="tpu_custom_call" | custom-call | tf_op jit(solution)/shard_map/ending/pallas_call | solution.py:1311
  566.0 1.4 slice.165
  567.5 1.3 fusion.28
  568.7 2.1 slice_bitcast_fusion
  570.8 0.9 copy.90
  571.7 1.3 copy.106
  574.3 0.6 copy.109
  575.6 0.7 copy.111
  576.8 0.7 copy.113
  (144 shorter events, 10.0 us)
Async XLA Ops:
  7.2 23.9 %copy-start = (f32[128,256]{1,0:T(8,128)S(1)}, f32[128,256]{1,0:T(8,128)}, u32[]{:S(2)}) copy-start(f32[128,256]{1,0:T(8,128)} %param.36) | copy-start | bytes 393220
  7.2 259.7 %all-gather.3.cloned.1.call-start = ((), (), s32[]{:S(2)}) async-start(), calls=%async_computation.2 | async-start | bytes 5406720 | tf_op jit(solution)/shard_map/all_gather | solution.py:1376
  9.0 481.5 %reduce-scatter.2.cloned.1.call-start = ((), (), s32[]{:S(2)}) async-start(), calls=%async_computation.1 | async-start | bytes 17694720 | tf_op jit(solution)/shard_map/reduce_scatter | solution.py:1503
  9.8 181.6 %copy-start.22 = (s32[512]{0:T(512)}, s32[512]{0:T(512)S(1)}, u32[]{:S(2)}) copy-start(s32[512]{0:T(512)S(1)} %slice.181) | copy-start | bytes 6148
  11.7 19.5 %copy-start.12 = (f32[512,128]{1,0:T(8,128)S(1)}, f32[512,128]{1,0:T(8,128)}, u32[]{:S(2)}) copy-start(f32[512,128]{1,0:T(8,128)} %param.42) | copy-start | bytes 786436
  11.7 19.6 %copy-start.13 = (f32[128,512]{1,0:T(8,128)S(1)}, f32[128,512]{1,0:T(8,128)}, u32[]{:S(2)}) copy-start(f32[128,512]{1,0:T(8,128)} %param.40) | copy-start | bytes 786436
  14.2 17.1 %copy-start.14 = (f32[128,512]{1,0:T(8,128)S(1)}, f32[128,512]{1,0:T(8,128)}, u32[]{:S(2)}) copy-start(f32[128,512]{1,0:T(8,128)} %param.41) | copy-start | bytes 786436
  14.2 17.2 %copy-start.11 = (f32[16,1024]{1,0:T(8,128)S(1)}, f32[16,1024]{1,0:T(8,128)}, u32[]{:S(2)}) copy-start(f32[16,1024]{1,0:T(8,128)} %feed_ref.1) | copy-start | bytes 196612
  14.2 17.2 %copy-start.17 = (f32[16,1024]{1,0:T(8,128)S(1)}, f32[16,1024]{1,0:T(8,128)}, u32[]{:S(2)}) copy-start(f32[16,1024]{1,0:T(8,128)} %param.31) | copy-start | bytes 196612
  14.2 17.2 %copy-start.18 = (f32[16,1024]{1,0:T(8,128)S(1)}, f32[16,1024]{1,0:T(8,128)}, u32[]{:S(2)}) copy-start(f32[16,1024]{1,0:T(8,128)} %param.32) | copy-start | bytes 196612
  14.9 20.4 %collective-permute-start = (f32[1,32]{0,1:T(8,128)S(1)}, f32[1,32]{0,1:T(8,128)S(1)}, u32[]{:S(2)}, u32[]{:S(2)}) collective-permute-start(f32[1,32]{0,1:T(8,128)S(1)} %slice.183), channel_id=1, source_target_pairs={{0,1},{1,2},{2,3},{4,5},{5,6},{6,7},{8,9},{9,10},{10,11},{12,13},{... | collective-permute-start | bytes 392 | tf_op jit(solution)/shard_map/ppermute | solution.py:1347
  19.8 15.4 %collective-permute-start.1 = (f32[1,32]{0,1:T(8,128)S(1)}, f32[1,32]{0,1:T(8,128)S(1)}, u32[]{:S(2)}, u32[]{:S(2)}) collective-permute-start(f32[1,32]{0,1:T(8,128)S(1)} %slice.183), channel_id=1, source_target_pairs={{0,2},{1,3},{4,6},{5,7},{8,10},{9,11},{12,14},{13,15},{16,18},{17,... | collective-permute-start | bytes 392 | tf_op jit(solution)/shard_map/ppermute | solution.py:1347
  29.6 4.1 copy-start.23
  33.8 3.1 copy-start.4
  33.8 3.1 copy-start.24
  35.7 4.2 copy-start.5
  35.7 4.1 copy-start.6
  168.7 1.4 copy-start.2
  168.7 1.4 copy-start.25
  168.8 1.4 copy-start.26
  168.8 1.4 copy-start.30
  170.0 22.9 %copy-start.9 = (f32[640,128]{1,0:T(8,128)S(1)}, f32[640,128]{1,0:T(8,128)}, u32[]{:S(2)}) copy-start(f32[640,128]{1,0:T(8,128)} %param.46) | copy-start | bytes 983044
  170.1 22.9 %copy-start.10 = (f32[128,640]{1,0:T(8,128)S(1)}, f32[128,640]{1,0:T(8,128)}, u32[]{:S(2)}) copy-start(f32[128,640]{1,0:T(8,128)} %param.45) | copy-start | bytes 983044
  171.3 23.3 %collective-permute-start.3 = (bf16[512,256]{1,0:T(8,128)(2,1)S(1)}, bf16[512,256]{1,0:T(8,128)(2,1)S(1)}, u32[]{:S(2)}, u32[]{:S(2)}) collective-permute-start(bf16[512,256]{1,0:T(8,128)(2,1)S(1)} %get-tuple-element.230), channel_id=1, source_target_pairs={{0,1},{1,2},{2,3},{4,5},{5,6},{6,7},{8,9},{9,10},{10,11},{12,13},{... | collective-permute-start | bytes 786440 | tf_op jit(solution)/shard_map/ppermute | solution.py:1347
  172.7 21.9 %collective-permute-start.2 = (bf16[288,256]{1,0:T(8,128)(2,1)S(1)}, bf16[288,256]{1,0:T(8,128)(2,1)S(1)}, u32[]{:S(2)}, u32[]{:S(2)}) collective-permute-start(bf16[288,256]{1,0:T(8,128)(2,1)S(1)} %slice.188), channel_id=1, source_target_pairs={{0,2},{1,3},{4,6},{5,7},{8,10},{9,11},{12,14},{13,15},{16,18},{17,... | collective-permute-start | bytes 442376 | tf_op jit(solution)/shard_map/ppermute | solution.py:1347
  359.8 17.7 %copy-start.8 = (f32[512,256]{1,0:T(8,128)S(1)}, f32[512,256]{1,0:T(8,128)}, u32[]{:S(2)}) copy-start(f32[512,256]{1,0:T(8,128)} %get-tuple-element.112) | copy-start | bytes 1572868
  360.8 11.8 %collective-permute-start.4 = (bf16[512,256]{1,0:T(8,128)(2,1)S(1)}, bf16[512,256]{1,0:T(8,128)(2,1)S(1)}, u32[]{:S(2)}, u32[]{:S(2)}) collective-permute-start(bf16[512,256]{1,0:T(8,128)(2,1)S(1)} %slice.151), channel_id=1, source_target_pairs={{1,0},{2,1},{3,2},{5,4},{6,5},{7,6},{9,8},{10,9},{11,10},{13,12},{... | collective-permute-start | bytes 786440 | tf_op jit(solution)/shard_map/ppermute | solution.py:1350
  363.1 14.5 %copy-start.31 = (f32[512,1024]{1,0:T(8,128)S(1)}, f32[512,1024]{1,0:T(8,128)}, u32[]{:S(2)}) copy-start(f32[512,1024]{1,0:T(8,128)} %get-tuple-element.116) | copy-start | bytes 6291460
  363.1 14.5 %copy-start.32 = (f32[512,1024]{1,0:T(8,128)S(1)}, f32[512,1024]{1,0:T(8,128)}, u32[]{:S(2)}) copy-start(f32[512,1024]{1,0:T(8,128)} %get-tuple-element.115) | copy-start | bytes 6291460
  364.2 13.2 %collective-permute-start.5 = (bf16[288,256]{1,0:T(8,128)(2,1)S(1)}, bf16[288,256]{1,0:T(8,128)(2,1)S(1)}, u32[]{:S(2)}, u32[]{:S(2)}) collective-permute-start(bf16[288,256]{1,0:T(8,128)(2,1)S(1)} %slice.153), channel_id=1, source_target_pairs={{2,0},{3,1},{6,4},{7,5},{10,8},{11,9},{14,12},{15,13},{18,16},{19,... | collective-permute-start | bytes 442376 | tf_op jit(solution)/shard_map/ppermute | solution.py:1350
  485.5 2.9 copy-start.29
  485.5 3.5 copy-start.3
  566.0 5.7 copy-start.7
  571.7 5.8 copy-start.1
  571.7 1.4 copy-start.28
  571.7 2.0 copy-start.21
  571.7 2.6 copy-start.20
  571.7 3.2 copy-start.19
  571.7 3.8 copy-start.16
  571.7 4.5 copy-start.27
  571.7 5.1 copy-start.15
Sparse Core Ops, SparseCore 0:
  10.9 76.3 all-gather.2
  307.1 123.7 reduce-scatter.1

commit v5 on v4

--- a/solution.py
+++ b/solution.py
@@ -159,6 +159,28 @@
     return starts, (er, ei)
 
 
+def fill_masks(groups, seg_ref, before, seg, kend, keep0, cont, ahead, reverse):
+    sub = lax.broadcasted_iota(jnp.int32, (8, LANES), 0)
+    for at in range(groups * STEP):
+        seg[at] = seg_ref[pl.ds(at, 8, stride=groups * STEP), :]
+    ends = [seg[g * STEP + STEP - 1] for g in range(groups)]
+    start = jnp.where(sub == 0, before, rotate(ends[-1], 1))
+    prior = [start] + ends[:-1]
+    same = lambda a, b: (a == b).astype(F32)
+    for g in range(groups):
+        cont[g] = same(ends[g], prior[g])
+        for i in range(STEP):
+            here = seg[g * STEP + i]
+            keep0[g * STEP + i] = same(here, prior[g])
+            kend[g * STEP + i] = same(here, ends[g])
+    for k in range(3):
+        w = 1 << k
+        if reverse:
+            ahead[k] = jnp.where(sub + w <= 7, same(start, rotate(start, -w)), 0.0)
+        else:
+            ahead[k] = jnp.where(sub >= w, same(ends[-1], rotate(ends[-1], w)), 0.0)
+
+
 ENTER_PLAN = (
     (0, 2, False), (8, 1, False), (9, 1, False), (10, 1, False), (11, 2, False), (12, 1, False), (13, 1, False),
     (14, 2, False), (15, 0, True),
@@ -167,53 +189,105 @@
 
 def shifted_rows(parts, halo, hops, rows, source, near, zeros, sems, local_sems):
     z = lax.axis_index("tensor")
-    moves, fills, end = [], [], halo
-    for h, n in enumerate(hops):
-        place = near.at[pl.ds(end - n, n)]
-        moves.append(Along(parts, h + 1, source.at[pl.ds(rows - n, n)], place, sems.at[0, h], sems.at[1, h]))
-        fills.append((z <= h, zeros.at[pl.ds(0, n)], place, local_sems.at[h]))
-        end -= n
-    own = [(source, near.at[pl.ds(halo, rows)], local_sems.at[len(hops)])]
-    if end > 0:
-        own.append((zeros.at[pl.ds(0, end)], near.at[pl.ds(0, end)], local_sems.at[len(hops) + 1]))
+    late = hops[1]
+    early = rows - late
+    cut = halo - late
+    move = lambda n, src, at, count, first: Along(
+        parts, 1, src, near.at[pl.ds(at, count)], sems.at[0, n], sems.at[1, n], first
+    )
+    last = move(0, source.at[pl.ds(early, late)], cut, late, 0)
+    other = move(1, source.at[pl.ds(0, early)], halo - rows, early, 0)
+    onward = move(2, near.at[pl.ds(cut, late)], halo - rows - late, late, 1)
+    ahead = halo - rows - late
+    fills = [(z < 1, rows, halo - rows), (z < 2, late, ahead)]
+    if ahead > 0:
+        fills.append((z < parts, ahead, 0))
 
     def each(action):
-        for copy in own:
-            action(pltpu.make_async_copy(*copy))
-        for condition, *copy in fills:
+        action(pltpu.make_async_copy(source, near.at[pl.ds(halo, rows)], local_sems.at[3]))
+        for n, (condition, count, at) in enumerate(fills):
             @pl.when(condition)
             def _():
-                action(pltpu.make_async_copy(*copy))
-
-    def start():
-        for move in moves:
-            move.start()
+                action(pltpu.make_async_copy(zeros.at[pl.ds(0, count)], near.at[pl.ds(at, count)], local_sems.at[n]))
+
+    def begin():
+        last.start()
         each(lambda c: c.start())
 
+    def relay():
+        last.wait_recv()
+        onward.start()
+
     def wait():
-        for move in moves:
-            move.wait_recv()
-            move.wait_send()
+        other.wait_recv()
+        onward.wait_recv()
+        for one in (last, other, onward):
+            one.wait_send()
         each(lambda c: c.wait())
 
-    return start, wait
+    return begin, other.start, relay, wait
+
+
+def normalize(
+    parts, x_ref, gain_ref, seg_ref, segc_ref, segr_ref, count_ref, edge_ref, mean_ref, rho_ref, hid, low, tail,
+    tail_got, tail_total, tail_sems
+):
+    rows, width = x_ref.shape
+    groups = mean_ref.shape[1]
+    table = group_table(width, groups)
+    spread_of = lambda v: sum(dot32(p, table, NT) for p in parts_of(v, 3))
+    lower = (segc_ref[...] == segr_ref[...]) & (
+        lax.broadcasted_iota(jnp.int32, (rows, rows), 0) >= lax.broadcasted_iota(jnp.int32, (rows, rows), 1)
+    )
+    lower = lower.astype(F32).astype(BF16)
+    running_of = lambda v: sum(dot32(lower, p) for p in parts_of(v, 3))
+    x = x_ref[...].astype(F32)
+    running = [
+        running_of(dot32(x_ref[...], table)),
+        running_of(sum(dot32(p, table) for p in parts_of(x * x, 2))),
+    ]
+    for half in range(2):
+        tail[half, :, :groups] = running[half][rows - 8 :]
+    moves = [Along(parts, hop, tail, tail_got.at[hop - 1], tail_sems.at[0, hop - 1], tail_sems.at[1, hop - 1])
+             for hop in (1, 2)]
+    for move in moves:
+        move.start()
+    tail_total[...] = jnp.zeros_like(tail_total)
+    for hop, move in enumerate(moves):
+        def arrived(hop=hop):
+            tail_total[...] += edge_ref[1 + hop : 2 + hop, :] * tail_got[hop]
+        move.wait_recv(arrived)
+    heads = (seg_ref[:, 0:1] == edge_ref[0:1, 0:1]).astype(F32)
+    count = count_ref[...]
+    first, second = (running[half] + heads * tail_total[half, 7:8, :groups] for half in range(2))
+    mean = first / count
+    rho = lax.rsqrt(second / count - mean * mean + EPSILON)
+    mean_ref[...] = mean
+    rho_ref[...] = rho
+    hidden = (x - spread_of(mean)) * spread_of(rho) * gain_ref[...]
+    low[...] = hidden.astype(BF16)
+    for k in range(width // LANES):
+        hid[k] = hidden[:, k * LANES : (k + 1) * LANES]
+    for move in moves:
+        move.wait_send()
 
 
 def ema_forward(
-    rows, dims, parts, halo, hops, hosted, h_ref, kend_ref, seg_ref, k0_ref, q_ref, f_ref, e_ref, cont_ref, mk_ref,
-    link_ref, skip_ref, low_ref, zeros_ref, *refs
+    rows, dims, parts, halo, hops, hosted, x_ref, gain_ref, seg_ref, segc_ref, segr_ref, count_ref, edge_ref, q_ref,
+    f_ref, e_ref, skip_ref, zeros_ref, *refs
 ):
     refs = list(refs)
     pack_ref = refs.pop(0) if hosted else None
-    out_ref, m_ref, s_ref, near_ref = (refs.pop(0) for _ in range(4))
+    out_ref, m_ref, s_ref, hidden_ref, mean_ref, rho_ref, near_ref = (refs.pop(0) for _ in range(7))
     all_ref = refs.pop(0) if hosted else None
+    hid, low, tail, tail_got, tail_total, tail_sems, seg, kend, keep0, cont, ahead = (refs.pop(0) for _ in range(11))
     hs, table, qs, parts_all, ends, got, entry, state_sems, near_sems, local_sems, *rest = refs
     groups = rows // (8 * STEP)
     step = pl.program_id(0)
     blocks = parts_all.shape[0]
     k = step % blocks
     stages = gather_stages(parts, pack_ref, all_ref, *rest) if hosted else []
-    near_start, near_wait = shifted_rows(parts, halo, hops, rows, low_ref, near_ref, zeros_ref, near_sems, local_sems)
+    near_begin, near_more, near_relay, near_wait = shifted_rows(parts, halo, hops, rows, low, near_ref, zeros_ref, near_sems, local_sems)
     states = lambda hop, at: Along(
         parts, hop, ends.at[at], got.at[hop - 1, at], state_sems.at[0, hop - 1, at], state_sems.at[1, hop - 1, at]
     )
@@ -224,10 +298,24 @@
 
     @pl.when(step == blocks)
     def _():
-        near_start()
+        near_more()
+
+    @pl.when(step == blocks + 2)
+    def _():
+        near_relay()
 
     if hosted:
         run_stages(stages, step, ENTER_PLAN, False)
+
+    @pl.when(step == 0)
+    def _():
+        normalize(
+            parts, x_ref, gain_ref, seg_ref, segc_ref, segr_ref, count_ref, edge_ref, mean_ref, rho_ref, hid, low,
+            tail, tail_got, tail_total, tail_sems,
+        )
+        near_begin()
+        fill_masks(groups, seg_ref, edge_ref[0:1, :], seg, kend, keep0, cont, ahead, False)
+
     pw = power_list(dims, q_ref)
     turn = fill_scales(groups, dims, pw, qs)
 
@@ -235,12 +323,12 @@
     def _():
         fill_feed(dims, pw, f_ref, table)
         for at in range(groups * STEP):
-            hs[at] = h_ref[pl.ds(at, 8, stride=groups * STEP), :] * kend_ref[at]
+            hs[at] = hid[k, pl.ds(at, 8, stride=groups * STEP), :] * kend[at]
         chunk_sums(groups, dims, table, hs, parts_all.at[k], 1)
 
         def one(j, carry):
             zero = jnp.zeros((8, LANES), F32)
-            _, last = scan_states(groups, dims, j, parts_all.at[k], qs, cont_ref, mk_ref, zero, zero)
+            _, last = scan_states(groups, dims, j, parts_all.at[k], qs, cont, ahead, zero, zero)
             ends[k, pl.ds(j, 1), :] = last[0][7:8]
             ends[k, pl.ds(dims + j, 1), :] = last[1][7:8]
             return carry
@@ -251,13 +339,14 @@
 
     @pl.when(step >= blocks)
     def _():
+        hidden_ref[...] = hid[k]
         entry[...] = jnp.zeros_like(entry)
 
         def near_one():
             entry[...] = got[0, k]
 
         def far_one():
-            link = link_ref[...]
+            link = edge_ref[2:3, :]
             r, i = times(*turn, got[1, k, :dims], got[1, k, dims:])
             entry[:dims] += link * r
             entry[dims:] += link * i
@@ -265,7 +354,7 @@
         states(1, k).wait_recv(near_one)
         states(2, k).wait_recv(far_one)
         ema_read(
-            groups, dims, h_ref, seg_ref, k0_ref, pw, f_ref, e_ref, cont_ref, mk_ref, parts_all.at[k], entry, skip_ref,
+            groups, dims, hid.at[k], seg, keep0, pw, f_ref, e_ref, cont, ahead, parts_all.at[k], entry, skip_ref,
             out_ref, m_ref, s_ref, hs, table, qs,
         )
 
@@ -302,7 +391,8 @@
         hs[at] = h_ref[pl.ds(at, 8, stride=groups * STEP), :]
     position_sums(groups, dims, ta, s_ref, k0_ref, hs, groups * STEP, -1)
     tap0 = taps[0] + jnp.broadcast_to(skip_ref[...], (8, LANES))
-    for g in range(groups):
+
+    def within(g, carry):
         for i in range(STEP):
             at = g * STEP + i
             seg = seg_ref[at]
@@ -311,6 +401,9 @@
                 src = g * STEP + s
                 out = out + taps[i - s] * jnp.where(seg_ref[src] == seg, hs[src], 0.0)
             out_ref[pl.ds(at, 8, stride=groups * STEP), :] = out
+        return carry
+
+    lax.fori_loop(0, groups, within, 0)
     m_ref[...] = silu_of(out_ref[...]).astype(m_ref.dtype)
 
 
@@ -346,14 +439,15 @@
 
 
 def ema_backward(
-    rows, dims, parts, halo, hops, hosted, h_ref, de_ref, seg_ref, kend_ref, k0_ref, rk0_ref, rkend_ref, q_ref, f_ref,
-    e_ref, root_ref, feed_ref, cont_ref, mkr_ref, s_ref, cross_ref, skip_ref, back_ref, zeros_ref, *refs
+    rows, dims, parts, halo, hops, hosted, h_ref, de_ref, rows_seg_ref, edge_ref, q_ref, f_ref, e_ref, root_ref,
+    feed_ref, s_ref, skip_ref, back_ref, zeros_ref, *refs
 ):
     refs = list(refs)
     pack_ref = refs.pop(0) if hosted else None
     outs = [refs.pop(0) for _ in range(6)]
     back = [refs.pop(0) for _ in hops]
     sum_ref = refs.pop(0) if hosted else None
+    seg_ref, kend_ref, k0_ref, cont_ref, mkr_ref = (refs.pop(0) for _ in range(5))
     pulls, heads, got, entry, state_sems, back_sems, local_sems, *rest = refs
     held, rest = rest[:9], rest[9:]
     hs, ds, la, table, qs = held[:5]
@@ -382,6 +476,7 @@
     def _():
         greet(parts, 3 if hosted else 0)
         filling(lambda c: c.start())
+        fill_masks(groups, rows_seg_ref, edge_ref[0:1, :], seg_ref, kend_ref, k0_ref, cont_ref, mkr_ref, True)
 
     @pl.when(step == blocks)
     def _():
@@ -419,7 +514,7 @@
             entry[...] = got[0, k]
 
         def far_one():
-            cross = cross_ref[...]
+            cross = edge_ref[3:4, :]
             r, i = times(turn[0], -turn[1], got[1, k, :dims], got[1, k, dims:])
             entry[:dims] += cross * r
             entry[dims:] += cross * i
@@ -427,7 +522,7 @@
         states(1, k).wait_recv(near_one)
         states(2, k).wait_recv(far_one)
         ema_grads(
-            groups, dims, h_ref, de_ref, seg_ref, kend_ref, rk0_ref, rkend_ref, pw, f_ref, e_ref, root_ref, feed_ref,
+            groups, dims, h_ref, de_ref, seg_ref, kend_ref, k0_ref, pw, f_ref, e_ref, root_ref, feed_ref,
             cont_ref, mkr_ref, pulls.at[k], entry, s_ref, skip_ref, *outs, *held,
         )
 
@@ -446,7 +541,7 @@
 
 
 def ema_grads(
-    groups, dims, h_ref, de_ref, seg_ref, kend_ref, rk0_ref, rkend_ref, pw, f_ref, e_ref, root_ref, feed_ref, cont_ref,
+    groups, dims, h_ref, de_ref, seg_ref, kend_ref, k0_ref, pw, f_ref, e_ref, root_ref, feed_ref, cont_ref,
     mkr_ref, g_ref, in_ref, s_ref, skip_ref, dh_ref, ge_ref, gf_ref, gr_ref, ga_ref, gs_ref, hs, ds, la, tb, qs, pf,
     red, hn, dn
 ):
@@ -483,13 +578,15 @@
         d = de_ref[pl.ds(at, 8, stride=groups * STEP), :]
         hs[at] = h
         ds[at] = d
+        hn[pl.ds(at, 8, stride=groups * STEP), :] = h * kend_ref[at]
+        dn[pl.ds(at, 8, stride=groups * STEP), :] = d * k0_ref[at]
         total = total + h * d
     gs_ref[...] = jnp.sum(total, axis=0, keepdims=True)
     position_sums(groups, dims, tb, la, kend_ref, hs, groups * STEP, 1)
     tap0 = taps[0] + jnp.broadcast_to(skip_ref[...], (8, LANES))
-    kacc = [jnp.zeros((8, LANES), F32) for _ in range(STEP)]
-    kacc[0] = total
-    for g in range(groups):
+
+    def within(g, kacc):
+        kacc = list(kacc)
         for s in range(STEP):
             at = g * STEP + s
             seg = seg_ref[at]
@@ -500,9 +597,10 @@
                 out = out + taps[t - s] * d
                 kacc[t - s] = kacc[t - s] + h * d
             dh_ref[pl.ds(at, 8, stride=groups * STEP), :] = out
-
-    hn[...] = h_ref[...] * rkend_ref[...]
-    dn[...] = de_ref[...] * rk0_ref[...]
+        return tuple(kacc)
+
+    kacc = lax.fori_loop(0, groups, within, (total,) + (jnp.zeros((8, LANES), F32),) * (STEP - 1))
+
     width = 4
     place = (lax.broadcasted_iota(jnp.int32, (STEP, LANES), 0) + 1).astype(F32)
 
@@ -581,36 +679,6 @@
     )(*[a for a, _ in ins])
 
 
-def spread(v):
-    return jnp.broadcast_to(v[..., None], v.shape + (LANES,))
-
-
-def row_masks(seg, before):
-    rows = seg.shape[0]
-    groups = rows // (8 * STEP)
-    cube = seg.reshape(8, groups, STEP)
-    chunk_last = cube[:, :, -1]
-    prior = jnp.concatenate([before[None], chunk_last.reshape(-1)[:-1]]).reshape(8, groups)
-    keep0 = (cube == prior[:, :, None]).astype(F32)
-    kend = (cube == chunk_last[:, :, None]).astype(F32)
-    order = lambda v: spread(v.transpose(1, 2, 0).reshape(groups * STEP, 8))
-    cont = spread((chunk_last == prior).astype(F32).transpose(1, 0))
-    ends = jnp.concatenate([before[None], chunk_last[:, -1]])
-    sub = jnp.arange(8)
-    ahead, behind = [], []
-    for k in range(3):
-        w = 1 << k
-        a = jnp.take(ends, jnp.maximum(sub + 1 - w, 0))
-        ahead.append(((ends[1:] == a) & (sub >= w)).astype(F32))
-        b = jnp.take(ends, jnp.minimum(sub + w, 8))
-        behind.append(((ends[:8] == b) & (sub + w <= 7)).astype(F32))
-    return dict(
-        seg=order(cube.astype(F32)), keep0=order(keep0), kend=order(kend), cont=cont,
-        mk=spread(jnp.stack(ahead)), mkr=spread(jnp.stack(behind)),
-        rk0=spread(keep0.reshape(rows)), rkend=spread(kend.reshape(rows)),
-    )
-
-
 def merged(ref):
     v = ref[...]
     return v.reshape(-1, v.shape[-1])
@@ -619,33 +687,57 @@
 GATHER_PLAN = ((0, 2, False), (1, 1, False), (2, 1, False), (3, 1, False), (3, 0, True))
 
 
-def attend_gather_kernel(halo, parts, ins, outs, *refs):
-    own = list(refs)
-    pack_ref, all_ref = own.pop(ins), own.pop(ins + outs)
-    stages = gather_stages(parts, pack_ref, all_ref, *own[ins + outs + 1 :])
-    step = pl.program_id(0)
-
-    @pl.when(step == 0)
-    def _():
-        greet(parts, 3)
-
-    run_stages(stages, step, GATHER_PLAN, False)
-    attend_kernel(halo, *own[: ins + outs + 1])
-    run_stages(stages, step, GATHER_PLAN, True)
-
-
-def attend_kernel(
-    halo, q_ref, k_ref, seg_ref, segk_ref, h_ref, m_ref, x_ref, gain_ref, wv_ref, wg_ref, wo_ref,
-    p_ref, vp_ref, v_ref, gp_ref, o_ref, g_ref, y_ref, n_ref, pb_ref,
-):
+def attend_kernel(halo, parts, hops, hosted, q_ref, own_k_ref, seg_ref, segk_ref, h_ref, m_ref, x_ref, gain_ref, wv_ref, wg_ref,
+                  wo_ref, *refs):
+    refs = list(refs)
+    pack_ref = refs.pop(0) if hosted else None
+    p_ref, vp_ref, v_ref, gp_ref, o_ref, g_ref, y_ref, n_ref, k_ref = (refs.pop(0) for _ in range(9))
+    all_ref = refs.pop(0) if hosted else None
+    pb_ref, keys, key_sems, *rest = refs
     t = pl.program_id(0)
+    z = lax.axis_index("tensor")
+    rows = q_ref.shape[0]
+    stages = gather_stages(parts, pack_ref, all_ref, *rest) if hosted else []
+    moves, places, end = [], [], halo
+    for h, n in enumerate(hops):
+        place = pl.ds(end - n, n)
+        moves.append(Along(parts, h + 1, own_k_ref.at[pl.ds(rows - n, n)], keys.at[place], key_sems.at[0, h], key_sems.at[1, h]))
+        places.append((h + 1, slice(end - n, end)))
+        end -= n
 
     @pl.when(t == 0)
     def _():
-        rows, keys = pb_ref.shape
-        scores = dot32(q_ref[...], k_ref[...], NT) * (1.0 / math.sqrt(q_ref.shape[1]))
-        at_row = lax.broadcasted_iota(jnp.int32, (rows, keys), 0)
-        at_key = lax.broadcasted_iota(jnp.int32, (rows, keys), 1)
+        greet(parts, 3 if hosted else 0)
+        for move in moves:
+            move.start()
+        keys[halo:, :] = own_k_ref[...]
+        if end > 0:
+            keys[:end, :] = jnp.zeros((end, keys.shape[1]), BF16)
+        for first, place in places:
+            @pl.when(z < first)
+            def _():
+                keys[place, :] = jnp.zeros((place.stop - place.start, keys.shape[1]), BF16)
+
+    if hosted:
+        run_stages(stages, t, GATHER_PLAN, False)
+
+    vp = dot32(h_ref[...], merged(wv_ref))
+    v = silu_of(vp).astype(BF16)
+    vp_ref[...] = vp.astype(BF16)
+    v_ref[...] = v
+    gp = dot32(m_ref[...], merged(wg_ref))
+    gp_ref[...] = gp.astype(BF16)
+
+    @pl.when(t == 0)
+    def _():
+        for move in moves:
+            move.wait_recv()
+            move.wait_send()
+        k_ref[...] = keys[...]
+        count = keys.shape[0]
+        scores = dot32(q_ref[...], keys[...], NT) * (1.0 / math.sqrt(q_ref.shape[1]))
+        at_row = lax.broadcasted_iota(jnp.int32, (rows, count), 0)
+        at_key = lax.broadcasted_iota(jnp.int32, (rows, count), 1)
         allowed = (at_key <= at_row + halo) & (segk_ref[...] == seg_ref[...])
         scores = jnp.where(allowed, scores, -1e30)
         raw = jnp.exp(scores - jnp.max(scores, axis=1, keepdims=True))
@@ -654,12 +746,6 @@
         pb_ref[...] = p.astype(BF16)
         y_ref[...] = x_ref[...].astype(F32)
 
-    vp = dot32(h_ref[...], merged(wv_ref))
-    v = silu_of(vp).astype(BF16)
-    vp_ref[...] = vp.astype(BF16)
-    v_ref[...] = v
-    gp = dot32(m_ref[...], merged(wg_ref))
-    gp_ref[...] = gp.astype(BF16)
     o = dot32(pb_ref[...], v)
     o_ref[...] = o.astype(BF16)
     g = (silu_of(gp) * o).astype(BF16)
@@ -671,6 +757,9 @@
         y = y_ref[...]
         rr = lax.rsqrt(jnp.mean(y * y, axis=1, keepdims=True) + EPSILON)
         n_ref[...] = (y * rr * gain_ref[...]).astype(BF16)
+
+    if hosted:
+        run_stages(stages, t, GATHER_PLAN, True)
 
 
 def ffn_kernel(
@@ -714,13 +803,19 @@
 
 
 def attend_back_kernel(
-    halo, br_ref, p_ref, h_ref, m_ref, q_ref, k_ref, vp_ref, v_ref, gp_ref, o_ref, g_ref, wv_ref, wg_ref, wo_ref,
-    dq_ref, dkn_ref, dk_ref, dhn_ref, dh_ref, dm_ref, grads_ref, dp, dhv, pb_ref,
+    halo, parts, hops, br_ref, p_ref, h_ref, m_ref, q_ref, k_ref, vp_ref, v_ref, gp_ref, o_ref, g_ref, wv_ref, wg_ref, wo_ref,
+    dq_ref, dk_ref, dhn_ref, dh_ref, dm_ref, grads_ref, dp, dhv, pb_ref, give, got, key_sems,
 ):
     t = pl.program_id(0)
+    rows = br_ref.shape[0]
+    moves, end = [], halo
+    for h, n in enumerate(hops):
+        moves.append((n, Along(parts, -h - 1, give.at[pl.ds(end - n, n)], got.at[h, pl.ds(0, n)], key_sems.at[0, h], key_sems.at[1, h])))
+        end -= n
 
     @pl.when(t == 0)
     def _():
+        greet(parts, 0)
         pb_ref[...] = p_ref[...].astype(BF16)
         dp[...] = jnp.zeros_like(dp)
         dhv[...] = jnp.zeros_like(dhv)
@@ -733,6 +828,20 @@
     da = (dg * (gp * sg)).astype(BF16)
     dr = (dg * o_ref[...].astype(F32) * (sg * (1.0 + gp * (1.0 - sg)))).astype(BF16)
     dp[...] += dot32(da, v_ref[...], NT)
+
+    @pl.when(t == pl.num_programs(0) - 1)
+    def _():
+        scale = 1.0 / math.sqrt(q_ref.shape[1])
+        p = p_ref[...]
+        d = dp[...]
+        ds = (p * (d - jnp.sum(p * d, axis=1, keepdims=True))).astype(BF16)
+        dk = dot32(ds, q_ref[...], TN) * scale
+        give[...] = dk[:halo].astype(BF16)
+        for _, move in moves:
+            move.start()
+        dk_ref[...] = dk[halo:]
+        dq_ref[...] = dot32(ds, k_ref[...]) * scale
+
     dv = dot32(pb, da, TN)
     dvp = (dv * silu_slope(vp_ref[...].astype(F32))).astype(BF16)
     dhv[...] += dot32(dvp, merged(wv_ref), NT)
@@ -743,16 +852,13 @@
 
     @pl.when(t == pl.num_programs(0) - 1)
     def _():
-        scale = 1.0 / math.sqrt(q_ref.shape[1])
-        p = p_ref[...]
-        d = dp[...]
-        ds = (p * (d - jnp.sum(p * d, axis=1, keepdims=True))).astype(BF16)
-        dq_ref[...] = dot32(ds, k_ref[...]) * scale
-        dk = dot32(ds, q_ref[...], TN) * scale
-        dkn_ref[...] = dk[:halo].astype(BF16)
-        dk_ref[...] = dk[halo:]
         dhn_ref[...] = dhv[:halo, :].astype(BF16)
         dh_ref[...] = dhv[halo:, :]
+        for h, (n, move) in enumerate(moves):
+            def arrived(h=h, n=n):
+                dk_ref[rows - n :, :] += got[h, :n, :].astype(F32)
+            move.wait_recv(arrived)
+            move.wait_send()
 
 
 def stage_call(body, steps, ins, outs, scratch, name, flops, collective_id=None):
@@ -796,11 +902,11 @@
 
 
 class Along:
-    def __init__(self, parts, hop, src, dst, send_sem, recv_sem):
+    def __init__(self, parts, hop, src, dst, send_sem, recv_sem, first=0):
         d, z = lax.axis_index("dp"), lax.axis_index("tensor")
         to = z + hop
-        self.sends = (to >= 0) & (to < parts)
-        self.gets = (z - hop >= 0) & (z - hop < parts)
+        self.sends = (to >= 0) & (to < parts) & (z >= first)
+        self.gets = (z - hop >= first) & (z - hop < parts)
         self.make = lambda: pltpu.make_async_remote_copy(
             src_ref=src, dst_ref=dst, send_sem=send_sem, recv_sem=recv_sem,
             device_id=(d, jnp.clip(to, 0, parts - 1)), device_id_type=pl.DeviceIdType.MESH,
@@ -1343,25 +1449,6 @@
     halo = -(-REACH // LANES) * LANES
     hops = [min(rows, REACH - h * rows) for h in range(-(-REACH // rows))]
 
-    def from_earlier(x, hop):
-        return lax.ppermute(x, "tensor", [(i, i + hop) for i in range(parts - hop)])
-
-    def from_later(x, hop):
-        return lax.ppermute(x, "tensor", [(i + hop, i) for i in range(parts - hop)])
-
-    def halo_of(x):
-        pieces = [from_earlier(x[rows - n :], h + 1) for h, n in enumerate(hops)]
-        ahead = jnp.zeros((halo - sum(hops), x.shape[1]), x.dtype)
-        return jnp.concatenate([ahead] + pieces[::-1] + [x], axis=0)
-
-    def give_back(total, x):
-        end = halo
-        for h, n in enumerate(hops):
-            got = from_later(x[end - n : end], h + 1).astype(F32)
-            total = total.at[rows - n :].add(got)
-            end -= n
-        return total
-
     chip_links = replicas == 8 and parts == 4
 
     piece = depth // parts
@@ -1374,7 +1461,6 @@
     pack_f1 = low(w_swish)
     pack_f2 = jnp.concatenate([low(w_up), low(w_down.T)], axis=0)
     gathered = lambda v: lax.all_gather(v, BOTH, axis=0).reshape(replicas, parts, *v.shape)
-    all_f1 = gathered(pack_f1)
     pack_f2 = with_layout_constraint(pack_f2, Layout((0, 1)))
 
     def part(k, columns):
@@ -1386,37 +1472,17 @@
     seg_keys = near[: halo + rows]
     seg = near[halo : halo + rows]
     before = near[halo - 1]
-    masks = row_masks(seg, before)
     index = rank * rows + jnp.arange(rows, dtype=jnp.int32)
     start = jnp.sum((seg_all[None, :] < seg[:, None]).astype(jnp.int32), axis=1)
     count = (index - start + 1).astype(F32)[:, None] * span
     tri = jnp.arange(rows)
-    same = seg[:, None] == seg[None, :]
-    lower = (same & (tri[:, None] >= tri[None, :])).astype(F32)
-    link1 = (seg[0] == before).astype(F32)
     link2 = (before == near[halo - rows - 1]).astype(F32)
     last = seg[-1]
     next1 = (near[halo + rows] == last).astype(F32)
     next2 = ((near[halo + 2 * rows - 1] == last) & (near[halo + 2 * rows] == last)).astype(F32) if halo > rows else 0.0
-    heads = (seg == before).astype(F32)[:, None]
-    tails = (seg == last).astype(F32)[:, None]
-
-    x = block_in.astype(F32)
-    gather = (jnp.arange(width)[:, None] // span == jnp.arange(groups)[None, :]).astype(F32)
-    sums_of = lambda v: dot32(v, gather, precision=HIGHEST)
-    spread_of = lambda v: dot32(v, gather, NT, precision=HIGHEST)
-    sums = jnp.concatenate([dot32(block_in, gather.astype(BF16)), sums_of(x * x)], axis=1)
-    running = dot32(lower, sums, precision=HIGHEST)
-    tail = running[-1:]
-    carry = from_earlier(tail, 1) + link2 * from_earlier(tail, 2)
-    running = running + heads * carry
-    mean = running[:, :groups] / count
-    var = running[:, groups:] / count - mean * mean
-    rho = lax.rsqrt(var + EPSILON)
-    mean_full, rho_full = spread_of(mean), spread_of(rho)
-    centred = (x - mean_full) * rho_full
-    hidden = centred * norm_gain
-    hidden_b = low(hidden)
+    cross = near[halo + 2 * rows - 1] == last
+    edge = jnp.stack([before.astype(F32), jnp.float32(1.0), link2, cross.astype(F32)])[:, None] * jnp.ones((1, LANES), F32)
+    seg_lanes = jnp.broadcast_to(seg.astype(F32)[:, None], (rows, LANES))
 
     size = jnp.exp(-ema_rate)
     unit = jnp.concatenate([size * jnp.cos(ema_angle), size * jnp.sin(ema_angle)])
@@ -1433,58 +1499,57 @@
     late3 = lambda n, m: pl.BlockSpec((n, m, LANES), lambda i: (0, 0, jnp.maximum(i - blocks, 0)))
     anywhere = pl.BlockSpec(memory_space=pl.ANY)
     shape_of = jax.ShapeDtypeStruct
-    mask_spec = whole(at_rows, 8, LANES)
-    cont, mk, mkr = (
-        (masks["cont"], whole(gcount, 8, LANES)), (masks["mk"], whole(3, 8, LANES)), (masks["mkr"], whole(3, 8, LANES))
-    )
-    kend, keep0, seg8 = ((masks[k], mask_spec) for k in ("kend", "keep0", "seg"))
-    lane = lambda v: (jnp.full((1, LANES), v, F32), whole(1, LANES))
     vm = lambda *n: pltpu.VMEM((*n, 8, LANES), F32)
     flat_vm = lambda *n: pltpu.VMEM((*n, LANES), F32)
     dma = lambda *n: pltpu.SemaphoreType.DMA(n)
     table_vm, scale_vm = flat_vm(2, STEP * dims), flat_vm(8 * dims)
     state_vms = [vm(blocks, nstate), flat_vm(blocks, 2 * dims), flat_vm(2, blocks, 2 * dims), flat_vm(2 * dims),
-                 dma(2, 2, blocks), dma(2, 2), dma(4)]
+                 dma(2, 2, blocks), dma(2, 3), dma(4)]
     mac = rows * width * dims * 4
     zeros = (jnp.zeros((rows, width), BF16), anywhere)
     near_rows = halo + rows
+    full = lambda v: (v, whole(*v.shape))
+    norm_shape = (shape_of((rows, groups), F32), whole(rows, groups))
+    rows_late = (shape_of((rows, width), F32), late(rows))
+    mask_vms = [vm(at_rows), vm(at_rows), vm(at_rows), vm(gcount), vm(3)]
     results = ema_call(
         functools.partial(ema_forward, rows, dims, parts, halo, hops, chip_links), width,
-        [(hidden, col(rows)), kend, seg8, keep0, (unit, col(2 * dims)), (feed, col(dims)), (reads, col(2 * dims)), cont,
-         mk, lane(link2), (skip, col(1)), (hidden_b, anywhere), zeros] + [(pack_a, anywhere)] * chip_links,
-        [(shape_of((rows, width), F32), late(rows)), (shape_of((rows, width), BF16), late(rows)),
-         (shape_of((nstate, 8, width), F32), late3(nstate, 8)), (shape_of((near_rows, width), BF16), anywhere)]
+        [full(block_in), full(norm_gain[None]), full(seg_lanes), full(seg[:, None]), full(seg[None]), full(count),
+         full(edge), (unit, col(2 * dims)), (feed, col(dims)), (reads, col(2 * dims)), (skip, col(1)), zeros]
+        + [(pack_a, anywhere)] * chip_links,
+        [rows_late, (shape_of((rows, width), BF16), late(rows)), (shape_of((nstate, 8, width), F32), late3(nstate, 8)),
+         rows_late, norm_shape, norm_shape, (shape_of((near_rows, width), BF16), anywhere)]
         + [(shape_of((replicas, parts) + pack_a.shape, BF16), anywhere)] * chip_links,
-        [vm(2 * at_rows), table_vm, scale_vm] + state_vms + (gather_scratch(parts) if chip_links else []),
+        [flat_vm(blocks, rows), pltpu.VMEM((rows, width), BF16), vm(2), vm(2, 2), vm(2), dma(2, 2)] + mask_vms
+        + [vm(2 * at_rows), table_vm, scale_vm] + state_vms + (gather_scratch(parts) if chip_links else []),
         "ema_forward", 2 * mac, 3,
     )
-    ema_out, mixed, states, hidden_near = results[:4]
+    ema_out, mixed, states, hidden, mean, rho, hidden_near = results[:7]
+    all_f1 = gathered(lax.optimization_barrier((pack_f1, mixed))[0])
     all_a = results[-1] if chip_links else gathered(pack_a)
     shared_b = all_a[:, :, 3 * depth :].reshape(width, latent_width)
 
     latent = dot32(mixed, shared_b)
     queries = low(latent * query_gain + query_bias)
-    keys_near = halo_of(low(latent * key_gain))
+    keys_own = low(latent * key_gain)
     one = lambda v: v[None]
     matmul = rows * width * vw * 2 * parts
     col_v = lambda n: ((n, value_width), BF16, "col")
-    ins = [(queries, "all"), (keys_near, "all"), (seg[:, None], "all"), (one(seg_keys), "all"), (hidden_near, "all"),
+    ins = [(queries, "all"), (keys_own, "all"), (seg[:, None], "all"), (one(seg_keys), "all"), (hidden_near, "all"),
            (mixed, "all"), (block_in, "all"), (one(ffn_gain), "all"), (all_a, part(0, vw)), (all_a, part(1, vw)),
            (all_a, part(2, vw))]
     outs = [((rows, near_rows), F32, "all"), col_v(near_rows), col_v(near_rows), col_v(rows), col_v(rows), col_v(rows),
-            ((rows, width), F32, "all"), ((rows, width), BF16, "all")]
-    scratch = [pltpu.VMEM((rows, near_rows), BF16)]
-    if chip_links:
-        results = stage_call(
-            functools.partial(attend_gather_kernel, halo, parts, len(ins), len(outs)), parts,
-            ins + [(pack_f2, anywhere)], outs + [((replicas, parts) + pack_f2.shape, BF16, anywhere)],
-            scratch + gather_scratch(parts), "attend", 6 * matmul, collective_id=1,
-        )
-        all_f2 = results[-1]
-    else:
-        results = stage_call(functools.partial(attend_kernel, halo), parts, ins, outs, scratch, "attend", 6 * matmul)
-        all_f2 = gathered(pack_f2)
-    probs, value_pre, values, gate_pre, attended, gated, residual, norm_in = results[:8]
+            ((rows, width), F32, "all"), ((rows, width), BF16, "all"), ((near_rows, latent_width), BF16, "all")]
+    results = stage_call(
+        functools.partial(attend_kernel, halo, parts, hops, chip_links), parts,
+        ins + [(pack_f2, anywhere)] * chip_links,
+        outs + [((replicas, parts) + pack_f2.shape, BF16, anywhere)] * chip_links,
+        [pltpu.VMEM((rows, near_rows), BF16), pltpu.VMEM((near_rows, latent_width), BF16), dma(2, len(hops))]
+        + (gather_scratch(parts) if chip_links else []),
+        "attend", 6 * matmul, collective_id=1,
+    )
+    all_f2 = results[-1] if chip_links else gathered(pack_f2)
+    probs, value_pre, values, gate_pre, attended, gated, residual, norm_in, keys_near = results[:9]
 
     row_vm = lambda n: pltpu.VMEM((n, width), F32)
     block_out, grad_residual, branch, grad_ffn_gain, ffn_grads = stage_call(
@@ -1508,18 +1573,19 @@
 
     ffn_sum = summed(ffn_grads)
 
-    grad_queries, keys_back, keys_own, hidden_back, hidden_own, grad_mixed, attn_grads = stage_call(
-        functools.partial(attend_back_kernel, halo), parts,
+    grad_queries, grad_keys, hidden_back, hidden_own, grad_mixed, attn_grads = stage_call(
+        functools.partial(attend_back_kernel, halo, parts, hops), parts,
         [(branch, "all"), (probs, "all"), (hidden_near, "all"), (mixed, "all"), (queries, "all"), (keys_near, "all"),
          (value_pre, "col"), (values, "col"), (gate_pre, "col"), (attended, "col"), (gated, "col"),
          (all_a, part(0, vw)), (all_a, part(1, vw)), (all_a, part(2, vw))],
-        [((rows, latent_width), F32, "all"), ((halo, latent_width), BF16, "all"), ((rows, latent_width), F32, "all"),
+        [((rows, latent_width), F32, "all"), ((rows, latent_width), F32, "all"),
          ((halo, width), BF16, "all"), ((rows, width), F32, "all"), ((rows, width), F32, "all"),
          ((replicas, parts, 3, depth, vw), BF16,
           pl.BlockSpec((replicas, 1, 3, depth, vw), lambda t: (0, t, 0, 0, 0)))],
-        [pltpu.VMEM((rows, near_rows), F32), row_vm(near_rows), pltpu.VMEM((rows, near_rows), BF16)], "attend_back", 12 * matmul,
+        [pltpu.VMEM((rows, near_rows), F32), row_vm(near_rows), pltpu.VMEM((rows, near_rows), BF16),
+         pltpu.VMEM((halo, latent_width), BF16), pltpu.VMEM((len(hops), rows, latent_width), BF16), dma(2, len(hops))],
+        "attend_back", 12 * matmul, collective_id=4,
     )
-    grad_keys = give_back(keys_own, keys_back)
     grad_query_gain = jnp.sum(latent * grad_queries, axis=0)
     grad_query_bias = jnp.sum(grad_queries, axis=0)
     grad_key_gain = jnp.sum(latent * grad_keys, axis=0)
@@ -1527,20 +1593,18 @@
     grad_shared = dot32(mixed, grad_latent, TN)
     grad_ema = (dot32(grad_latent, shared_b, NT) + grad_mixed) * silu_slope(ema_out)
 
-    cross = (near[halo + 2 * rows - 1] == last).astype(F32)
     dim_late = late(dims)
     results = ema_call(
         functools.partial(ema_backward, rows, dims, parts, halo, hops, chip_links), width,
-        [(hidden, late(rows)), (grad_ema, col(rows)), seg8, kend, keep0, (masks["rk0"], whole(rows, LANES)),
-         (masks["rkend"], whole(rows, LANES)), (unit, col(2 * dims)), (feed, dim_late), (reads, col(2 * dims)),
-         (root, dim_late), (ema_input, dim_late), cont, mkr, (states, late3(nstate, 8)), lane(cross), (skip, late(1)),
-         (hidden_back, anywhere), zeros]
+        [(hidden, late(rows)), (grad_ema, col(rows)), full(seg_lanes), full(edge), (unit, col(2 * dims)),
+         (feed, dim_late), (reads, col(2 * dims)), (root, dim_late), (ema_input, dim_late),
+         (states, late3(nstate, 8)), (skip, late(1)), (hidden_back, anywhere), zeros]
         + [(attn_grads.reshape(replicas // 2, 2, parts, 3 * depth, vw), anywhere)] * chip_links,
         [(shape_of((rows, width), F32), late(rows)), (shape_of((2 * dims, width), F32), late(2 * dims))]
         + [(shape_of((dims, width), F32), dim_late)] * 3 + [(shape_of((1, width), F32), late(1))]
         + [(shape_of((n, width), BF16), anywhere) for n in hops]
         + [(shape_of((3 * depth, vw), F32), whole(3 * depth, vw))] * chip_links,
-        state_vms + [vm(2 * at_rows), vm(at_rows), vm(nstate), table_vm, scale_vm, flat_vm(4, STEP * dims),
+        mask_vms + state_vms + [vm(2 * at_rows), vm(at_rows), vm(nstate), table_vm, scale_vm, flat_vm(4, STEP * dims),
                      flat_vm(9, dims), flat_vm(rows), flat_vm(rows)]
         + (reduce_scratch(parts, 3 * depth, vw) if chip_links else []),
         "ema_backward", 4 * mac, 2,

time: 593 us -> 545 us (0.919)
  starting transfers between devices: 32.2 us -> 0.25 us
  Pallas kernels: 459 us -> 477 us
  local copies, waits for them, and re-layouts: 34.7 us -> 22.3 us
  waiting for transfers between devices: 11.4 us -> 0.06 us
  matrix products: 13.9 us -> 6.59 us
    pallas_call x3, Pallas kernels: 158 us -> 201 us  [stage_call(): pl.pallas_call(body, grid=(steps,), in_specs=[spec(v, how) for v, how in...]
    ppermute x6 -> x0, starting transfers between devices: 32.2 us -> none  [the longest x4 29.4 us: from_earlier(): return lax.ppermute(x, 'tensor', [(i, i + hop) for i in range(parts - hop)])]
    pallas_call x2, Pallas kernels: 226 us -> 202 us  [ema_call(): pl.pallas_call(body, grid=(2 * (width // LANES),), in_specs=[s for _, s i...]
    ppermute x6 -> x0, waiting for transfers between devices: 11.4 us -> none  [the longest x2 10.6 us: from_later(): return lax.ppermute(x, 'tensor', [(i + hop, i) for i in range(parts - hop)])]
    dot_general x8 -> x3, matrix products: 13.9 us -> 6.59 us  [dot32(): lax.dot_general(a, b, (dims, ((), ())), precision=precision, preferred_el...]
    broadcast_in_dim x15 -> x2, local copies, waits for them, and re-layouts: 8.32 us -> 1.69 us  [the longest x1 0.86 us: on_device(): seg[:, None]]
  transfers between devices with their start and end apart: 8 -> 2, of which waited for: 3 -> 0; matrix products, arithmetic and copies ran while one was open for 8% -> 3% of each run, Pallas kernels for 59% -> 50%
where the time goes in v5:
time: 545 us; the launch traced here: 538 us
  Pallas kernels  477 us (88%)
  local copies, waits for them, and re-layouts  22.3 us (4%)
  between operations  20.4 us (4%)
  other arithmetic  11.7 us (2%)
  matrix products  6.59 us (1%)
    pallas_call x2, Pallas kernels, ema_call(): pl.pallas_call(body, grid=(2 * (width // LANES),), in_specs=[s for _, s i...  202 us
    pallas_call x3, Pallas kernels, stage_call(): pl.pallas_call(body, grid=(steps,), in_specs=[spec(v, how) for v, how in...  201 us
    pallas_call x1, Pallas kernels, end_call(): pl.pallas_call(functools.partial(end_kernel, bits, parts, replicas, per_t...  73.4 us
  transfers between devices with their start and end apart: 2, of which 0 were waited for; matrix products, arithmetic and copies ran while one was open for 3% of the time, Pallas kernels for 50%

profile of v5, /device:TPU:0, one launch (start us, length us, event | category | flops | bytes accessed | tf_op | source)
XLA Modules:
  0.0 538.2 jit_solution(1959311607727797314)
XLA Ops:
  7.2 0.0 copy-start
  7.2 0.0 copy-start.7
  7.2 0.0 all-gather.3.cloned.1.call-start
  7.3 0.8 fusion.1
  8.1 0.6 fusion.3
  12.0 1.3 convert_reduce_fusion
  13.2 0.0 copy-done
  13.3 1.0 convert_element_type.74
  14.3 1.0 convert_element_type.75
  15.2 1.1 copy.61
  16.3 1.7 convert_element_type.84
  18.0 0.1 copy.60
  18.1 0.8 convert_multiply_fusion.count_ref
  18.9 0.9 copy.62.segc_ref.seg_ref
  19.7 0.0 copy-done.11
  19.7 0.9 subtract_sqrt_fusion
  20.6 0.7 pad_maximum_fusion.2.q_ref
  21.3 0.1 pad_maximum_fusion.3
  21.4 0.8 pad_maximum_fusion.refs_0_
  22.2 0.6 mul.81.edge_ref
  22.8 0.8 broadcast_in_dim.62.seg_ref.rows_seg_ref
  23.6 1.1 broadcast_in_dim.66.zeros_ref
  24.8 93.7 %ema_forward.1 = (f32[512,1024]{1,0:T(8,128)}, bf16[512,1024]{1,0:T(8,128)(2,1)}, f32[128,8,1024]{2,1,0:T(8,128)}, f32[512,1024]{1,0:T(8,128)}, f32[512,16]{1,0:...) custom-call(bf16[512,1024]{1,0:T(8,128)(2,1)} %x_ref.5, ...), custom_call_target="tpu_custom_call" | custom-call | flops 67108 | bytes 1024 | tf_op jit(solution)/shard_map/ema_forward/pallas_call | solution.py:667
  118.5 0.0 copy-start.16
  118.5 0.0 copy-start.17
  118.5 0.0 copy-start.21
  118.5 0.0 all-gather.3.cloned.1.call-update
  118.6 0.2 reduce-scatter.2.cloned.1.call-start
  118.8 0.6 broadcast_in_dim.67.segk_ref
  119.4 0.0 copy-done.6
  119.4 0.2 copy.63
  119.6 1.1 slice.71
  120.7 0.2 reshape.113
  120.9 0.8 pad_maximum_fusion.1.refs_0_
  121.6 0.0 copy-done.2
  121.6 1.2 multiply_convert_fusion
  122.9 104.0 %attend.1 = (f32[512,1408]{1,0:T(8,128)}, bf16[1408,2048]{1,0:T(8,128)(2,1)}, bf16[1408,2048]{1,0:T(8,128)(2,1)}, bf16[512,2048]{1,0:T(8,128)(2,1)}, bf16[512,20...) custom-call(bf16[512,256]{1,0:T(8,128)(2,1)} %get-tuple-element.204., ...), custom_call_target="tpu_custom_call" | custom-call | flops 12884901 | bytes 1024 | tf_op jit(solution)/shard_map/attend/pallas_call | solution.py:873
  226.9 0.0 all-gather.3.cloned.1.call-done
  226.9 40.0 %ffn.1 = (bf16[512,1024]{1,0:T(8,128)(2,1)}, f32[512,1024]{1,0:T(8,128)}, bf16[512,1024]{1,0:T(8,128)(2,1)}, f32[1,1024]{1,0:T(1,128)}, bf16[8,4,3,128,640]{4,3,2,1,0:T(8,128)(2,1)}) custom-call(f32[512,1024]{1,0:T(8,128)} %get-tuple-element.71.y_ref, bf16[512,1024]{1,0:T(8,128)(2,1)} %get-tuple-element.72.n_ref, bf16[512,1024]{1,0:T(8,128)(2,1)} %og_ref.1, ...), custom_call_target="tpu_custom_call" | custom-call | flops 23622320 | bytes 1024 | tf_op jit(solution)/shard_map/ffn/pallas_call | solution.py:873
  266.9 0.0 reduce-scatter.2.cloned.1.call-update
  269.5 0.1 add_convert_fusion.2
  269.6 57.1 %attend_back.1 = (f32[512,256]{1,0:T(8,128)}, f32[512,256]{1,0:T(8,128)}, bf16[896,1024]{1,0:T(8,128)(2,1)}, f32[512,1024]{1,0:T(8,128)}, f32[512,1024]{1,0:T(8,128)}, /*index=5*/bf16[8,4,3,128,512]{4,3,2,1,0:T(8,128)(2,1)}) custom-call(bf16[512,1024]{1,0:T(8,128)(2,1)} %get-tuple-element.78.br_ref, f32[512,1408]{1,0:T(8,128)} %get-tuple-element.79.p_ref, ...), custom_call_target="tpu_custom_call" | custom-call | flops 25769804 | bytes 1024 | tf_op jit(solution)/shard_map/attend_back/pallas_call | solution.py:873
  326.6 1.4 multiply_reduce_fusion.1
  328.0 3.9 multiply_multiply_fusion.de_ref
  331.9 108.8 %ema_backward.1 = (f32[512,1024]{1,0:T(8,128)}, f32[32,1024]{1,0:T(8,128)}, f32[16,1024]{1,0:T(8,128)}, f32[16,1024]{1,0:T(8,128)}, f32[16,1024]{1,0:T(8,128)}, ...) custom-call(f32[512,1024]{1,0:T(8,128)} %get-tuple-element.87.h_ref, ...), custom_call_target="tpu_custom_call" | custom-call | flops 134217 | bytes 1024 | tf_op jit(solution)/shard_map/ema_backward/pallas_call | solution.py:667
  440.7 0.0 copy-start.20
  440.7 2.0 slice_bitcast_fusion.1
  442.8 0.8 copy.66
  443.6 0.6 maximum_maximum_fusion.refs_5_
  444.2 1.4 fusion.6.block_ref
  445.7 0.6 mul.96.next_ref
  446.3 73.4 %ending.1 = (f32[512,1024]{1,0:T(8,128)}, f32[32,1024]{1,0:T(8,128)}, f32[16,1024]{1,0:T(8,128)}, f32[16,1024]{1,0:T(8,128)}, f32[16,1024]{1,0:T(8,128)}, /*inde...) custom-call(bf16[512,1024]{1,0:T(8,128)(2,1)} %x_ref.5, ...), custom_call_target="tpu_custom_call" | custom-call | tf_op jit(solution)/shard_map/ending/pallas_call | solution.py:1417
  519.7 1.4 fusion.5
  521.1 1.3 slice.81
  522.4 2.1 slice_bitcast_fusion
  524.5 0.9 copy.67
  525.5 1.3 copy.79
  526.8 0.6 copy.80
  527.4 0.6 copy.81
  528.0 0.6 copy.82
  528.6 0.6 copy.83
  529.3 0.7 copy.84
  529.9 0.6 copy.85
  530.5 0.7 copy.86
  (45 shorter events, 0.1 us)
Async XLA Ops:
  7.2 6.1 %copy-start = (f32[128,256]{1,0:T(8,128)S(1)}, f32[128,256]{1,0:T(8,128)}, u32[]{:S(2)}) copy-start(f32[128,256]{1,0:T(8,128)} %param.28) | copy-start | bytes 393220
  7.2 12.5 %copy-start.7 = (f32[16,1024]{1,0:T(8,128)S(1)}, f32[16,1024]{1,0:T(8,128)}, u32[]{:S(2)}) copy-start(f32[16,1024]{1,0:T(8,128)} %feed_ref.1) | copy-start | bytes 196612
  7.2 12.5 %copy-start.11 = (f32[16,1024]{1,0:T(8,128)S(1)}, f32[16,1024]{1,0:T(8,128)}, u32[]{:S(2)}) copy-start(f32[16,1024]{1,0:T(8,128)} %param.24) | copy-start | bytes 196612
  7.2 12.5 %copy-start.10 = (f32[16,1024]{1,0:T(8,128)S(1)}, f32[16,1024]{1,0:T(8,128)}, u32[]{:S(2)}) copy-start(f32[16,1024]{1,0:T(8,128)} %param.23) | copy-start | bytes 196612
  7.2 219.7 %all-gather.3.cloned.1.call-start = ((), (), s32[]{:S(2)}) async-start(), calls=%async_computation.2 | async-start | bytes 5406720 | tf_op jit(solution)/shard_map/all_gather | solution.py:1463
  8.7 13.4 %copy-start.15 = (s32[512]{0:T(512)}, s32[512]{0:T(512)S(1)}, u32[]{:S(2)}) copy-start(s32[512]{0:T(512)S(1)} %get-tuple-element.217) | copy-start | bytes 6148
  24.8 94.6 %copy-start.5 = (f32[128,640]{1,0:T(8,128)S(1)}, f32[128,640]{1,0:T(8,128)}, u32[]{:S(2)}) copy-start(f32[128,640]{1,0:T(8,128)} %param.37) | copy-start | bytes 983044
  24.8 94.7 %copy-start.6 = (f32[640,128]{1,0:T(8,128)S(1)}, f32[640,128]{1,0:T(8,128)}, u32[]{:S(2)}) copy-start(f32[640,128]{1,0:T(8,128)} %param.38) | copy-start | bytes 983044
  118.5 3.1 copy-start.2
  118.5 3.1 copy-start.16
  118.5 3.1 copy-start.17
  118.5 3.1 copy-start.21
  118.6 327.1 %reduce-scatter.2.cloned.1.call-start = ((), (), s32[]{:S(2)}) async-start(), calls=%async_computation.1 | async-start | bytes 17694720 | tf_op jit(solution)/shard_map/reduce_scatter | solution.py:1568
  269.6 58.4 %copy-start.22 = (f32[512,1024]{1,0:T(8,128)S(1)}, f32[512,1024]{1,0:T(8,128)}, u32[]{:S(2)}) copy-start(f32[512,1024]{1,0:T(8,128)} %get-tuple-element.91) | copy-start | bytes 6291460
  440.7 2.9 copy-start.20
  440.7 3.5 copy-start.3
  519.7 5.7 %copy-start.4 = (f32[512,1024]{1,0:T(8,128)S(1)}, f32[512,1024]{1,0:T(8,128)}, u32[]{:S(2)}) copy-start(f32[512,1024]{1,0:T(8,128)} %get-tuple-element.243) | copy-start | bytes 6291460
  525.4 5.8 %copy-start.1 = (f32[128,256]{1,0:T(8,128)S(1)}, f32[128,256]{1,0:T(8,128)}, u32[]{:S(2)}) copy-start(f32[128,256]{1,0:T(8,128)} %param.28) | copy-start | bytes 393220
  525.4 1.4 copy-start.19
  525.4 2.0 copy-start.14
  525.4 2.6 copy-start.13
  525.4 3.2 copy-start.12
  525.4 3.8 copy-start.9
  525.4 4.5 copy-start.18
  525.4 5.1 copy-start.8
Sparse Core Ops, SparseCore 0:
  118.7 99.9 all-gather.2
  267.0 134.4 reduce-scatter.1

commit v6 on v5

--- a/solution.py
+++ b/solution.py
@@ -433,8 +433,8 @@
 
 
 REDUCE_PLAN = (
-    (0, 1, False), (4, 1, False), (5, 1, False), (7, 1, False), (8, 2, False), (9, 1, False), (10, 1, False),
-    (11, 1, False), (12, 1, False), (13, 1, False), (14, 1, False), (15, 0, True),
+    (0, 1, False), (5, 1, False), (7, 1, False), (8, 1, False), (9, 1, False), (12, 1, False), (14, 1, False),
+    (15, 0, True),
 )
 
 
@@ -1172,7 +1172,7 @@
             def _():
                 c(R_LEFT).wait_send()
 
-    order = [(cores, 0), (cores, 1), (cores, 2), (chips, 0), (cores, 3), (chips, 1), (line, 0), (chips, 2), (line, 1),
+    order = [(cores, 0), (cores, 1), (cores, 2), (cores, 3), (chips, 0), (chips, 1), (line, 0), (chips, 2), (line, 1),
              (chips, 3), (line, 2), (line, 3)]
     return [begin] + [functools.partial(f, s) for f, s in order] + [finish]
 

time: 545 us -> 539 us (0.989)
  Pallas kernels: 477 us -> 471 us
where the time goes in v6:
time: 539 us; the launch traced here: 532 us
  Pallas kernels  471 us (87%)
  local copies, waits for them, and re-layouts  22.3 us (4%)
  between operations  20.4 us (4%)
  other arithmetic  11.7 us (2%)
  matrix products  6.59 us (1%)
    pallas_call x3, Pallas kernels, stage_call(): pl.pallas_call(body, grid=(steps,), in_specs=[spec(v, how) for v, how in...  201 us
    pallas_call x2, Pallas kernels, ema_call(): pl.pallas_call(body, grid=(2 * (width // LANES),), in_specs=[s for _, s i...  201 us
    pallas_call x1, Pallas kernels, end_call(): pl.pallas_call(functools.partial(end_kernel, bits, parts, replicas, per_t...  69.1 us
  transfers between devices with their start and end apart: 2, of which 0 were waited for; matrix products, arithmetic and copies ran while one was open for 3% of the time, Pallas kernels for 50%

profile of v6, /device:TPU:0, one launch (start us, length us, event | category | flops | bytes accessed | tf_op | source)
XLA Modules:
  0.0 532.0 jit_solution(9220802677806664319)
XLA Ops:
  7.2 0.0 copy-start
  7.2 0.0 copy-start.7
  7.2 0.0 copy-start.11
  7.2 0.0 all-gather.3.cloned.1.call-start
  7.3 0.8 fusion.1
  8.1 0.6 fusion.3
  12.0 1.3 convert_reduce_fusion
  13.3 1.0 convert_element_type.74
  14.3 1.0 convert_element_type.75
  15.2 1.1 copy.61
  16.3 1.7 convert_element_type.84
  18.0 0.1 copy.60
  18.1 0.8 convert_multiply_fusion.count_ref
  18.9 0.9 copy.62.segc_ref.seg_ref
  19.7 0.9 subtract_sqrt_fusion
  20.6 0.7 pad_maximum_fusion.2.q_ref
  21.3 0.1 pad_maximum_fusion.3
  21.4 0.8 pad_maximum_fusion.refs_0_
  22.2 0.6 mul.81.edge_ref
  22.8 0.8 broadcast_in_dim.62.seg_ref.rows_seg_ref
  23.6 1.1 broadcast_in_dim.66.zeros_ref
  24.8 93.7 %ema_forward.1 = (f32[512,1024]{1,0:T(8,128)}, bf16[512,1024]{1,0:T(8,128)(2,1)}, f32[128,8,1024]{2,1,0:T(8,128)}, f32[512,1024]{1,0:T(8,128)}, f32[512,16]{1,0:...) custom-call(bf16[512,1024]{1,0:T(8,128)(2,1)} %x_ref.5, ...), custom_call_target="tpu_custom_call" | custom-call | flops 67108 | bytes 1024 | tf_op jit(solution)/shard_map/ema_forward/pallas_call | solution.py:667
  118.5 0.0 copy-start.2
  118.5 0.0 copy-start.16
  118.5 0.0 copy-start.17
  118.5 0.0 copy-start.21
  118.5 0.0 all-gather.3.cloned.1.call-update
  118.6 0.2 reduce-scatter.2.cloned.1.call-start
  118.8 0.6 broadcast_in_dim.67.segk_ref
  119.4 0.2 copy.63
  119.6 1.1 slice.71
  120.7 0.2 reshape.113
  120.9 0.8 pad_maximum_fusion.1.refs_0_
  121.6 0.0 copy-done.16
  121.6 1.2 multiply_convert_fusion
  122.9 104.0 %attend.1 = (f32[512,1408]{1,0:T(8,128)}, bf16[1408,2048]{1,0:T(8,128)(2,1)}, bf16[1408,2048]{1,0:T(8,128)(2,1)}, bf16[512,2048]{1,0:T(8,128)(2,1)}, bf16[512,20...) custom-call(bf16[512,256]{1,0:T(8,128)(2,1)} %get-tuple-element.204., ...), custom_call_target="tpu_custom_call" | custom-call | flops 12884901 | bytes 1024 | tf_op jit(solution)/shard_map/attend/pallas_call | solution.py:873
  226.9 0.0 all-gather.3.cloned.1.call-done
  226.9 40.0 %ffn.1 = (bf16[512,1024]{1,0:T(8,128)(2,1)}, f32[512,1024]{1,0:T(8,128)}, bf16[512,1024]{1,0:T(8,128)(2,1)}, f32[1,1024]{1,0:T(1,128)}, bf16[8,4,3,128,640]{4,3,2,1,0:T(8,128)(2,1)}) custom-call(f32[512,1024]{1,0:T(8,128)} %get-tuple-element.71.y_ref, bf16[512,1024]{1,0:T(8,128)(2,1)} %get-tuple-element.72.n_ref, bf16[512,1024]{1,0:T(8,128)(2,1)} %og_ref.1, ...), custom_call_target="tpu_custom_call" | custom-call | flops 23622320 | bytes 1024 | tf_op jit(solution)/shard_map/ffn/pallas_call | solution.py:873
  266.9 0.0 reduce-scatter.2.cloned.1.call-update
  269.5 0.1 add_convert_fusion.2
  269.6 57.1 %attend_back.1 = (f32[512,256]{1,0:T(8,128)}, f32[512,256]{1,0:T(8,128)}, bf16[896,1024]{1,0:T(8,128)(2,1)}, f32[512,1024]{1,0:T(8,128)}, f32[512,1024]{1,0:T(8,128)}, /*index=5*/bf16[8,4,3,128,512]{4,3,2,1,0:T(8,128)(2,1)}) custom-call(bf16[512,1024]{1,0:T(8,128)(2,1)} %get-tuple-element.78.br_ref, f32[512,1408]{1,0:T(8,128)} %get-tuple-element.79.p_ref, ...), custom_call_target="tpu_custom_call" | custom-call | flops 25769804 | bytes 1024 | tf_op jit(solution)/shard_map/attend_back/pallas_call | solution.py:873
  326.6 1.4 multiply_reduce_fusion.1
  328.0 3.9 multiply_multiply_fusion.de_ref
  331.9 106.9 %ema_backward.1 = (f32[512,1024]{1,0:T(8,128)}, f32[32,1024]{1,0:T(8,128)}, f32[16,1024]{1,0:T(8,128)}, f32[16,1024]{1,0:T(8,128)}, f32[16,1024]{1,0:T(8,128)}, ...) custom-call(f32[512,1024]{1,0:T(8,128)} %get-tuple-element.87.h_ref, ...), custom_call_target="tpu_custom_call" | custom-call | flops 134217 | bytes 1024 | tf_op jit(solution)/shard_map/ema_backward/pallas_call | solution.py:667
  438.8 0.0 copy-start.20
  438.8 2.0 slice_bitcast_fusion.1
  440.9 0.8 copy.66
  441.7 0.6 maximum_maximum_fusion.refs_5_
  442.3 0.0 copy-done.3
  442.3 1.4 fusion.6.block_ref
  443.8 0.6 mul.96.next_ref
  444.4 69.1 %ending.1 = (f32[512,1024]{1,0:T(8,128)}, f32[32,1024]{1,0:T(8,128)}, f32[16,1024]{1,0:T(8,128)}, f32[16,1024]{1,0:T(8,128)}, f32[16,1024]{1,0:T(8,128)}, /*inde...) custom-call(bf16[512,1024]{1,0:T(8,128)(2,1)} %x_ref.5, ...), custom_call_target="tpu_custom_call" | custom-call | tf_op jit(solution)/shard_map/ending/pallas_call | solution.py:1417
  513.5 1.4 fusion.5
  514.9 1.3 slice.81
  516.2 2.1 slice_bitcast_fusion
  518.3 0.9 copy.67
  519.2 1.3 copy.79
  520.6 0.6 copy.80
  521.2 0.6 copy.81
  521.8 0.6 copy.82
  522.4 0.6 copy.83
  523.1 0.7 copy.84
  523.7 0.6 copy.85
  524.3 0.7 copy.86
  (45 shorter events, 0.1 us)
Async XLA Ops:
  7.2 6.1 %copy-start = (f32[128,256]{1,0:T(8,128)S(1)}, f32[128,256]{1,0:T(8,128)}, u32[]{:S(2)}) copy-start(f32[128,256]{1,0:T(8,128)} %param.28) | copy-start | bytes 393220
  7.2 12.5 %copy-start.7 = (f32[16,1024]{1,0:T(8,128)S(1)}, f32[16,1024]{1,0:T(8,128)}, u32[]{:S(2)}) copy-start(f32[16,1024]{1,0:T(8,128)} %feed_ref.1) | copy-start | bytes 196612
  7.2 12.5 %copy-start.11 = (f32[16,1024]{1,0:T(8,128)S(1)}, f32[16,1024]{1,0:T(8,128)}, u32[]{:S(2)}) copy-start(f32[16,1024]{1,0:T(8,128)} %param.24) | copy-start | bytes 196612
  7.2 12.5 %copy-start.10 = (f32[16,1024]{1,0:T(8,128)S(1)}, f32[16,1024]{1,0:T(8,128)}, u32[]{:S(2)}) copy-start(f32[16,1024]{1,0:T(8,128)} %param.23) | copy-start | bytes 196612
  7.2 219.7 %all-gather.3.cloned.1.call-start = ((), (), s32[]{:S(2)}) async-start(), calls=%async_computation.2 | async-start | bytes 5406720 | tf_op jit(solution)/shard_map/all_gather | solution.py:1463
  8.7 13.4 %copy-start.15 = (s32[512]{0:T(512)}, s32[512]{0:T(512)S(1)}, u32[]{:S(2)}) copy-start(s32[512]{0:T(512)S(1)} %get-tuple-element.217) | copy-start | bytes 6148
  24.8 94.6 %copy-start.5 = (f32[128,640]{1,0:T(8,128)S(1)}, f32[128,640]{1,0:T(8,128)}, u32[]{:S(2)}) copy-start(f32[128,640]{1,0:T(8,128)} %param.37) | copy-start | bytes 983044
  24.8 94.7 %copy-start.6 = (f32[640,128]{1,0:T(8,128)S(1)}, f32[640,128]{1,0:T(8,128)}, u32[]{:S(2)}) copy-start(f32[640,128]{1,0:T(8,128)} %param.38) | copy-start | bytes 983044
  118.5 3.1 copy-start.2
  118.5 3.1 copy-start.16
  118.5 3.1 copy-start.17
  118.5 3.1 copy-start.21
  118.6 325.2 %reduce-scatter.2.cloned.1.call-start = ((), (), s32[]{:S(2)}) async-start(), calls=%async_computation.1 | async-start | bytes 17694720 | tf_op jit(solution)/shard_map/reduce_scatter | solution.py:1568
  269.6 58.4 %copy-start.22 = (f32[512,1024]{1,0:T(8,128)S(1)}, f32[512,1024]{1,0:T(8,128)}, u32[]{:S(2)}) copy-start(f32[512,1024]{1,0:T(8,128)} %get-tuple-element.91) | copy-start | bytes 6291460
  438.8 2.9 copy-start.20
  438.8 3.5 copy-start.3
  513.5 5.7 %copy-start.4 = (f32[512,1024]{1,0:T(8,128)S(1)}, f32[512,1024]{1,0:T(8,128)}, u32[]{:S(2)}) copy-start(f32[512,1024]{1,0:T(8,128)} %get-tuple-element.243) | copy-start | bytes 6291460
  519.2 5.8 %copy-start.1 = (f32[128,256]{1,0:T(8,128)S(1)}, f32[128,256]{1,0:T(8,128)}, u32[]{:S(2)}) copy-start(f32[128,256]{1,0:T(8,128)} %param.28) | copy-start | bytes 393220
  519.2 1.4 copy-start.19
  519.2 2.0 copy-start.14
  519.2 2.6 copy-start.13
  519.2 3.2 copy-start.12
  519.2 3.8 copy-start.9
  519.2 4.5 copy-start.18
  519.2 5.1 copy-start.8
Sparse Core Ops, SparseCore 0:
  118.7 99.9 all-gather.2
  267.0 132.8 reduce-scatter.1
